TPU v7x, 32 devices: a whole 2x2x4 slice. The times are simulated.
32 devices in a mesh: dp: 8 (over y, x, core), seq: 4 (over z).
Axes of the slice: x: 2, y: 2, z: 4, core: 2. Of those that a mesh axis runs over, the one named last changes fastest.
Arguments:
- tokens: bfloat16 [8, 2048, 768], P('dp', 'seq'), may hold values from -6 to 6
- cotangent: bfloat16 [8, 2048, 768], P('dp', 'seq'), may hold values from -6 to 6
- segment_ids: int32 [8, 2048], P('dp', 'seq'), may hold values from 0 to 7, as said below
- doc_starts: int32 [8, 2048], P('dp', 'seq'), may hold values from 0 to 1, as said below
- valid_mask: int32 [8, 2048], P('dp', 'seq'), may hold values from 0 to 1
- step_number: int32 [1], replicated, may hold values from 1 to 64
- learn_rate: float32 [1], replicated, may hold values from 0.001 to 0.004
- norm_gain: float32 [768], replicated, may hold values from 0.5 to 1.5
- in_weight: bfloat16 [768, 3352], replicated, may hold values from -0.21875 to 0.21875
- conv_weight: float32 [4, 1792], replicated, may hold values from -3 to 3
- conv_bias: float32 [1792], replicated, may hold values from -1.75 to 1.75
- dt_bias: float32 [24], replicated, may hold values from -6 to -2
- a_log: float32 [24], replicated, may hold values from -1 to 2.5
- skip_d: float32 [24], replicated, may hold values from 0.5 to 1.5
- gate_gain: float32 [1536], replicated, may hold values from 0.5 to 1.5
- out_weight: bfloat16 [1536, 768], replicated, may hold values from -0.15625 to 0.15625
- in_momentum: float32 [768, 3352], P('seq'), may hold values from -6 to 6
- out_momentum: float32 [1536, 768], P(None, 'seq'), may hold values from -448 to 448
Outputs:
- output: bfloat16 [8, 2048, 768], P('dp', 'seq')
- input_grad: bfloat16 [8, 2048, 768], P('dp', 'seq')
- new_in_weight: bfloat16 [768, 3352], replicated
- new_out_weight: bfloat16 [1536, 768], replicated
- new_in_momentum: float32 [768, 3352], P('seq')
- new_out_momentum: float32 [1536, 768], P(None, 'seq')
- norm_gain_grad: float32 [768], replicated
- conv_weight_grad: float32 [4, 1792], replicated
- conv_bias_grad: float32 [1792], replicated
- dt_bias_grad: float32 [24], replicated
- a_log_grad: float32 [24], replicated
- skip_grad: float32 [24], replicated
- gate_gain_grad: float32 [1536], replicated
- output_rms: float32 [1], replicated
- mixer_rms: float32 [1], replicated
Inputs may be any that keep to these rules, and one draw needn't show every extreme that they name: Within each sequence segment_ids never fall, are 0 at the first position and rise by one exactly where doc_starts is 1; every sequence holds exactly 8 documents. `doc_starts`: 1 at the first position of every sequence; exactly 8 ones in every sequence.
All inputs are finite; a program needn't handle non-finite values.
Results may differ from a plain program's by a relative error of at most 0.0066.
The roundings to bfloat16 on the way count: a program that leaves them out, or rounds other values in their place, can miss the bound.
Values may be sent and summed in bfloat16 or wider, within the bound.
A program may use at most 192 MiB of HBM per device.

v0:
```python
import jax
import jax.numpy as jnp
from jax import lax
from jax.sharding import PartitionSpec as P

epsilon = 1e-05
highest = lax.Precision.HIGHEST


def shifted(block, axis, distance):
    devices = range(lax.axis_size(axis))
    route = [(i - distance, i) for i in devices if i - distance in devices]
    return lax.ppermute(block, axis, route)


def entering(value, axis, join, neutral):
    place = lax.axis_index(axis)
    gathered = jax.tree.map(
        lambda a, kind: lax.all_gather(a.astype(kind), axis), value, (jnp.bfloat16, jnp.bfloat16)
    )
    state = jax.tree.map(lambda a, e: jnp.zeros_like(a) + jnp.asarray(e, a.dtype), value, neutral)

    def one(step, state):
        return join(
            state,
            jax.tree.map(
                lambda a, own: lax.dynamic_index_in_dim(a, step, 0, False).astype(own.dtype),
                gathered,
                value,
            ),
        )

    return lax.fori_loop(0, place, one, state)


def carried_in(value, axis, combine, identity):
    length, mine = (lax.axis_size(axis), lax.axis_index(axis))
    everything = jax.tree.map(lambda part: lax.all_gather(part, axis), value)
    start = jax.tree.map(
        lambda part, zero: jnp.broadcast_to(jnp.asarray(zero, part.dtype), part.shape),
        value,
        identity,
    )

    def step(k, before):
        at = length - 1 - k
        reached = at > mine
        new = combine(before, jax.tree.map(lambda part: part[at], everything))
        return jax.tree.map(lambda a, b: jnp.where(reached, a, b), new, before)

    return lax.fori_loop(0, length, step, start)


def pre_norm(values, gain_values):
    return (
        values
        * lax.rsqrt(jnp.mean(values * values, axis=-1, keepdims=True) + epsilon)
        * gain_values
    )


def compose(earlier, later):
    return (earlier[0] * later[0], later[0][:, :, None, None] * earlier[1] + later[1])


def local(
    tokens,
    cotangent,
    segment_ids,
    doc_starts,
    valid_mask,
    step_number,
    learn_rate,
    norm_gain,
    in_weight,
    conv_weight,
    conv_bias,
    dt_bias,
    a_log,
    skip_d,
    gate_gain,
    out_weight,
    in_momentum,
    out_momentum,
):
    seq_count, piece_size, model_width = tokens.shape
    head_count = dt_bias.shape[0]
    tap_count, channels = conv_weight.shape
    inner_width = gate_gain.shape[0]
    state_width = (channels - inner_width) // 2
    head_width = inner_width // head_count
    proj_width = in_weight.shape[1]
    row_count = seq_count * piece_size
    inputs = tokens.astype(jnp.float32)
    normed_in, back_pre = jax.vjp(pre_norm, inputs, norm_gain)
    normed_low = normed_in.astype(jnp.bfloat16).reshape(row_count, model_width)
    projected = jnp.dot(normed_low, in_weight, preferred_element_type=jnp.float32).reshape(
        seq_count, piece_size, proj_width
    )
    gate_in = projected[:, :, :inner_width]
    conv_in = projected[:, :, inner_width : inner_width + channels]
    dt_raw = projected[:, :, inner_width + channels :]
    seg_float = segment_ids.astype(jnp.float32)
    prev_rows, prev_seg = shifted(
        (conv_in[:, piece_size - tap_count + 1 :], seg_float[:, piece_size - tap_count + 1 :]),
        "seq",
        1,
    )
    padded = jnp.concatenate([prev_rows, conv_in], axis=1)
    seg_pad = jnp.concatenate([prev_seg, seg_float], axis=1)
    masks = [
        (seg_pad[:, k : k + piece_size] == seg_float).astype(jnp.float32)[:, :, None]
        for k in range(tap_count)
    ]

    def conv_part(padded_in, taps_in, bias_in, raw_in, dt_bias_in, a_log_in):
        summed = bias_in + jnp.zeros((seq_count, piece_size, channels), jnp.float32)
        for k in range(tap_count):
            summed = summed + padded_in[:, k : k + piece_size] * masks[k] * taps_in[k]
        activated = jax.nn.silu(summed)
        signal = activated[:, :, :inner_width].reshape(
            seq_count, piece_size, head_count, head_width
        )
        writer = activated[:, :, inner_width : inner_width + state_width]
        reader = activated[:, :, inner_width + state_width :]
        step_size = jax.nn.softplus(raw_in + dt_bias_in)
        return (signal, writer, reader, step_size, -jnp.exp(a_log_in) * step_size)

    (signal, writer, reader, step_size, log_decay), back_conv = jax.vjp(
        conv_part, padded, conv_weight, conv_bias, dt_raw, dt_bias, a_log
    )
    counter = jnp.cumsum(doc_starts, axis=1)
    positions = jnp.arange(piece_size)
    causal = positions[:, None] >= positions[None, :]
    same_doc = (counter[:, :, None] == counter[:, None, :]) & causal[None]
    first_doc = (counter == 0)[:, :, None]
    last_doc = (counter == counter[:, -1:])[:, :, None]
    untouched = (counter[:, -1] == 0)[:, None]

    def end_state(signal_in, writer_in, step_in, decay_in):
        cumulative = jnp.cumsum(decay_in, axis=1)
        final_log = cumulative[:, -1]
        keeping = jnp.where(untouched, jnp.exp(final_log), 0.0)
        tails = jnp.where(last_doc, jnp.exp(final_log[:, None] - cumulative), 0.0) * step_in
        fresh_state = jnp.einsum(
            "slh,slhp,sln->shpn", tails, signal_in, writer_in, precision=highest
        )
        return (keeping, fresh_state)

    def piece_out(signal_in, writer_in, reader_in, step_in, decay_in, incoming_in):
        cumulative = jnp.cumsum(decay_in, axis=1)
        by_head = jnp.transpose(cumulative, (0, 2, 1))
        gaps = by_head[:, :, :, None] - by_head[:, :, None, :]
        decays = jnp.exp(jnp.where(same_doc[:, None], gaps, -1e30))
        scores = jnp.einsum("stn,sun->stu", reader_in, writer_in, precision=highest)
        weighted = scores[:, None] * decays
        inner_part = jnp.einsum(
            "shtu,suhp->sthp", weighted, signal_in * step_in[..., None], precision=highest
        )
        entries = jnp.where(first_doc, jnp.exp(cumulative), 0.0)
        carried = (
            jnp.einsum("stn,shpn->sthp", reader_in, incoming_in, precision=highest)
            * entries[..., None]
        )
        return inner_part + carried

    (keeping, fresh_state), back_end = jax.vjp(end_state, signal, writer, step_size, log_decay)
    identity = (jnp.ones_like(keeping), jnp.zeros_like(fresh_state))
    _, incoming = entering((keeping, fresh_state), "seq", compose, identity)
    ssm_out, back_out = jax.vjp(piece_out, signal, writer, reader, step_size, log_decay, incoming)

    def gate_norm(ssm_in, signal_in, skip_in, gate_values, gain_values):
        mixer_in = (ssm_in + skip_in[:, None] * signal_in).reshape(
            seq_count, piece_size, inner_width
        )
        gated_out = mixer_in * jax.nn.silu(gate_values)
        return (
            gated_out
            * lax.rsqrt(jnp.mean(gated_out * gated_out, axis=-1, keepdims=True) + epsilon)
            * gain_values
        )

    gate_normed, back_gate = jax.vjp(gate_norm, ssm_out, signal, skip_d, gate_in, gate_gain)
    gate_low = gate_normed.astype(jnp.bfloat16).reshape(row_count, inner_width)
    mixed = jnp.dot(gate_low, out_weight, preferred_element_type=jnp.float32).reshape(
        seq_count, piece_size, model_width
    )
    block_out = inputs + mixed
    valid_float = valid_mask.astype(jnp.float32)
    out_square = jnp.sum(valid_float * jnp.sum(block_out * block_out, axis=-1))
    mix_square = jnp.sum(valid_float * jnp.sum(mixed * mixed, axis=-1))
    valid_count = jnp.sum(valid_float)
    out_grad = cotangent.astype(jnp.float32) * valid_float[:, :, None]
    out_low = out_grad.astype(jnp.bfloat16).reshape(row_count, model_width)
    gate_grad = lax.dot_general(
        out_low, out_weight, (((1,), (1,)), ((), ())), preferred_element_type=jnp.float32
    ).reshape(seq_count, piece_size, inner_width)
    ssm_grad, signal_grad_gate, skip_grad, gate_in_grad, gate_gain_grad = back_gate(gate_grad)
    signal_grad_out, writer_grad_out, reader_grad, step_grad_out, decay_grad_out, state_grad = (
        back_out(ssm_grad)
    )
    _, later_grad = carried_in((keeping, state_grad), "seq", compose, identity)
    keeping_grad = jnp.sum(later_grad * incoming, axis=(2, 3))
    signal_grad_end, writer_grad_end, step_grad_end, decay_grad_end = back_end(
        (keeping_grad, later_grad)
    )
    padded_grad, conv_weight_grad, conv_bias_grad, dt_raw_grad, dt_bias_grad, a_log_grad = (
        back_conv(
            (
                signal_grad_gate + signal_grad_out + signal_grad_end,
                writer_grad_out + writer_grad_end,
                reader_grad,
                step_grad_out + step_grad_end,
                decay_grad_out + decay_grad_end,
            )
        )
    )
    rim_grad = shifted(padded_grad[:, : tap_count - 1].astype(jnp.bfloat16), "seq", -1).astype(
        jnp.float32
    )
    conv_in_grad = padded_grad[:, tap_count - 1 :] + jnp.pad(
        rim_grad, ((0, 0), (piece_size - tap_count + 1, 0), (0, 0))
    )
    proj_grad = (
        jnp.concatenate([gate_in_grad, conv_in_grad, dt_raw_grad], axis=2)
        .astype(jnp.bfloat16)
        .reshape(row_count, proj_width)
    )
    normed_grad = lax.dot_general(
        proj_grad, in_weight, (((1,), (1,)), ((), ())), preferred_element_type=jnp.float32
    ).reshape(seq_count, piece_size, model_width)
    input_grad_pre, norm_gain_grad = back_pre(normed_grad)
    input_grad = (out_grad + input_grad_pre).astype(jnp.bfloat16)
    share_rows = model_width // lax.axis_size("seq")
    in_part = lax.dot_general(
        normed_low, proj_grad, (((0,), (0,)), ((), ())), preferred_element_type=jnp.float32
    )
    out_part = lax.dot_general(
        out_low, gate_low, (((0,), (0,)), ((), ())), preferred_element_type=jnp.float32
    )
    whole_grad = lax.psum(jnp.concatenate([in_part, out_part], axis=1), "dp")
    grad_share = lax.psum_scatter(whole_grad, "seq", scatter_dimension=0, tiled=True)
    step_float = step_number[0].astype(jnp.float32)
    rate_now = learn_rate[0] * step_float / (step_float + 16.0)
    new_in_momentum = 0.5 * in_momentum + grad_share[:, :proj_width]
    new_out_momentum = 0.5 * out_momentum + jnp.transpose(grad_share[:, proj_width:])
    first_row = lax.axis_index("seq") * share_rows
    own_in = lax.dynamic_slice_in_dim(in_weight, first_row, share_rows, 0).astype(jnp.float32)
    own_out = lax.dynamic_slice_in_dim(out_weight, first_row, share_rows, 1).astype(jnp.float32)
    new_in_part = (own_in - rate_now * new_in_momentum).astype(jnp.bfloat16)
    new_out_part = (own_out - rate_now * new_out_momentum).astype(jnp.bfloat16)
    new_in_weight, new_out_weight = (
        lax.all_gather(new_in_part, "seq", axis=0, tiled=True),
        lax.all_gather(new_out_part, "seq", axis=1, tiled=True),
    )
    (
        norm_gain_total,
        conv_weight_total,
        conv_bias_total,
        dt_bias_total,
        a_log_total,
        skip_total,
        gate_gain_total,
        out_square_total,
        mix_square_total,
        valid_total,
    ) = lax.psum(
        (
            norm_gain_grad,
            conv_weight_grad,
            conv_bias_grad,
            dt_bias_grad,
            a_log_grad,
            skip_grad,
            gate_gain_grad,
            out_square,
            mix_square,
            valid_count,
        ),
        ("dp", "seq"),
    )
    denominator = jnp.maximum(valid_total, 1.0) * model_width
    output_rms = jnp.sqrt(out_square_total / denominator).reshape(1)
    mixer_rms = jnp.sqrt(mix_square_total / denominator).reshape(1)
    return (
        block_out.astype(jnp.bfloat16),
        input_grad,
        new_in_weight,
        new_out_weight,
        new_in_momentum,
        new_out_momentum,
        norm_gain_total,
        conv_weight_total,
        conv_bias_total,
        dt_bias_total,
        a_log_total,
        skip_total,
        gate_gain_total,
        output_rms,
        mixer_rms,
    )


def solution(mesh):
    placed = (
        P("dp", "seq", None),
        P("dp", "seq", None),
        P("dp", "seq"),
        P("dp", "seq"),
        P("dp", "seq"),
        P(),
        P(),
        P(),
        P(),
        P(),
        P(),
        P(),
        P(),
        P(),
        P(),
        P(),
        P("seq", None),
        P(None, "seq"),
    )
    return jax.shard_map(
        local,
        mesh=mesh,
        in_specs=placed,
        out_specs=(
            P("dp", "seq", None),
            P("dp", "seq", None),
            P(),
            P(),
            P("seq", None),
            P(None, "seq"),
            P(),
            P(),
            P(),
            P(),
            P(),
            P(),
            P(),
            P(),
            P(),
        ),
        check_vma=False,
    )
```

profile of v0, /device:TPU:0, one launch (start us, length us, event | category | flops | bytes accessed | tf_op | source)
XLA Modules:
  0.0 885.2 jit_solution(818629642145929513)
XLA Ops:
  9.2 5.5 convolution_bitcast_fusion
  14.8 4.9 collective-permute-start
  19.9 3.5 collective-permute-start.1
  25.9 4.2 slice.132
  36.3 11.6 %fusion.26 = (f32[1,512,1792]{2,1,0:T(8,128)S(1)}, f32[1,512,1792]{2,1,0:T(8,128)}) fusion(f32[1792]{0:T(1024)S(1)} %get-tuple-element.401, f32[1,512,1792]{2,1,0:T(8,128)} %slice.132, f32[512]{0:T(512)S(1)} %bitcast.377, f32[1792]{0:T(1024)S(1)} %get-tuple-element.402, f32[512]{0:T(512)S(1)} %bitcast.374, f32[1,3,1792]{2,1,0:T(4,128)S(1)} %copy.241, ...), kind=kLoop, calls=%fused_computation.50 | loop fusion | flops 17432576 | bytes 11075584 | tf_op jit(solution)/shard_map/jvp(jit(silu))/mul | solution.py:120
  54.3 4.3 fusion.70
  68.0 3.5 copy.254
  71.5 9.9 %all_gather.26 = bf16[4,1,24]{2,1,0:T(2,128)(2,1)} all-gather(bf16[1,1,24]{2,1,0:T(2,128)(2,1)} %get-tuple-element.453), channel_id=1, replica_groups=mesh['dp'=8,'seq'=4] {'seq'}, dimensions={0}, use_global_device_ids=true | all-gather | bytes 240 | tf_op jit(solution)/shard_map/all_gather | solution.py:19
  87.5 7.6 all-gather.11.cloned.1.call-done
  96.4 4.0 fusion.88
  100.5 29.3 %fusion.30 = f32[1,512,24,64]{1,3,2,0:T(8,128)} fusion(f32[1,512,24,64]{1,3,2,0:T(8,128)S(1)} %bitcast.337, f32[512,24,64]{0,2,1:T(8,128)S(1)} %fusion.88, f32[24]{0:T(128)S(1)} %copy-done.89, f32[512,24]{0,1:T(8,128)S(1)} %copy-done.35, f32[24,512]{1,0:T(8,128)S(1)} %copy-done.45, f32[512,512]{1,0:T(8,128)S(1)} %copy-done.27, ...), kind=kOutput, calls=%fused_computation.59 | convolution fusion | flops 4854644736 | bytes 14041184 | tf_op jit(solution)/shard_map/jvp(shtu,suhp->sthp)/dot_general | solution.py:157
  129.8 3.6 copy.252
  133.4 4.0 multiply_reduce_fusion.7
  141.5 5.6 multiply_reduce_fusion.5
  151.0 12.4 %copy.255 = f32[1,512,1536]{1,2,0:T(8,128)} copy(f32[1,512,1536]{2,1,0:T(8,128)} %mul.669) | data formatting | bytes 6291456 | tf_op jit(solution)/shard_map/transpose(jvp())/mul | solution.py:162
  163.4 5.4 fusion.107
  168.9 17.8 %all_gather.29 = f32[4,1,24]{2,1,0:T(1,128)} all-gather(f32[1,1,24]{2,1,0:T(1,128)S(1)} %copy-done.87), channel_id=1, replica_groups=mesh['dp'=8,'seq'=4] {'seq'}, dimensions={0}, use_global_device_ids=true | all-gather | bytes 480 | tf_op jit(solution)/shard_map/all_gather | solution.py:38
  186.7 3.5 copy.256
  190.2 3.7 multiply_reduce_fusion.6
  194.8 33.7 %fusion.7 = (f32[24,512]{1,0:T(8,128)}, f32[24,512]{1,0:T(8,128)S(1)}, f32[512,512]{1,0:T(8,128)}) fusion(f32[24,512]{1,0:T(8,128)} %bitcast_add_fusion.6, f32[512,512]{1,0:T(8,128)} %fusion.111, pred[512,512]{1,0:T(8,128)(4,1)} %fusion.81, f32[24,64,512]{2,1,0:T(8,128)} %bitcast.346, f32[512,24,64]{0,2,1:T(8,128)S(1)} %bitcast.339, f32[512,24]{0,1:T(8,128)} %copy.243), kind=kOutput, calls=%fused_computation.12 | convolution fusion | flops 4888961024 | bytes 8847360 | tf_op jit(solution)/shard_map/transpose(jvp(shtu,suhp->sthp))/dot_general | solution.py:157
  230.9 3.9 convolution_bitcast_fusion.1
  234.9 7.1 convolution_bitcast_fusion.2
  244.7 3.9 fusion.91
  248.6 22.4 %fusion.2 = f32[24,64,512]{2,1,0:T(8,128)} fusion(f32[24,64,512]{2,1,0:T(8,128)S(1)} %bitcast.347, f32[24,512]{1,0:T(8,128)S(1)} %copy-done.46, f32[512,512]{1,0:T(8,128)S(1)} %copy-done.28, pred[512,512]{1,0:T(8,128)(4,1)S(1)} %copy-done.33), kind=kOutput, calls=%fused_computation.9 | convolution fusion | flops 4850712576 | bytes 7651328 | tf_op jit(solution)/shard_map/transpose(jvp(shtu,suhp->sthp))/dot_general | solution.py:157
  271.0 12.0 %while.29 = (s32[]{:T(128)}, f32[1,24,64,128]{3,2,1,0:T(8,128)}, s32[]{:T(128)}, f32[4,1,24]{2,1,0:T(1,128)}, f32[4,1,24,64,128]{4,3,2,1,0:T(8,128)}, /*index=5*/s32[]{:T(128)}, s32[]{:T(128)}, s32[]{:T(128)}, s32[]{:T(128)}) while((s32[]{:T(128)}, f32[1,24,64,128]{3,2,1,0:T(8,128)}, s32[]{:T(128)}, f32[4,1,24]{2,1,0:T(1,128)}, ...), condition=%wide.region_11.12_spmd.clone, body=%wide.region_10.11_spmd.clone.sunk | while | flops 786440 | bytes 2359751 | solution.py:51
  283.0 4.1 fusion.34
  288.0 5.8 fusion.76
  293.8 4.2 fusion.33
  300.5 11.2 %multiply_reduce_fusion.3 = (f32[1792]{0:T(1024)}, f32[1792]{0:T(1024)S(1)}, f32[1792]{0:T(1024)}, f32[1792]{0:T(1024)S(1)}, f32[1792]{0:T(1024)}, /*index=5*/f32[1,512,1792]{2,1,0:T(8,128)S(1)}) fusion(f32[1,512,1792]{2,1,0:T(8,128)} %slice.132, f32[1,3,1792]{2,1,0:T(4,128)S(1)} %copy.241, f32[512]{0:T(512)S(1)} %bitcast.375, f32[512]{0:T(512)S(1)} %bitcast.369, ...), kind=kLoop, calls=%fused_computation.43 | loop fusion | flops 24763648 | bytes 18415616 | tf_op jit(solution)/shard_map/transpose(jvp())/reduce_sum | solution.py:119
  319.6 5.0 reduce-window.36
  324.8 5.0 reduce-window.34
  334.5 3.1 fusion.68
  337.7 5.8 pad_maximum_fusion
  343.4 15.2 %copy.289 = f32[768,4888]{1,0:T(8,128)} copy(f32[768,4888]{0,1:T(8,128)} %pad_maximum_fusion) | data formatting | bytes 30031872
  358.6 256.6 %reduce-scatter.4.cloned.1.call-done = f32[192,4888]{1,0:T(8,128)} async-done(((f32[768,4888]{1,0:T(8,128)}), f32[192,4888]{1,0:T(8,128)}) %reduce-scatter.4.cloned.1.call-update) | async-done | bytes 3754000
  615.2 5.7 copy.290
  622.9 89.6 %all-reduce.16.cloned.1.call-done = f32[192,4888]{0,1:T(8,128)} async-done(((f32[192,4888]{0,1:T(8,128)}), f32[192,4888]{0,1:T(8,128)}) %all-reduce.16.cloned.1.call-update) | async-done | bytes 3754000 | tf_op jit(solution)/shard_map/psum | solution.py:241
  712.5 3.5 subtract_convert_fusion.1
  717.1 3.6 copy.270
  720.7 6.4 subtract_convert_fusion
  727.1 3.8 copy.272
  731.3 3.3 multiply_reduce_fusion.8
  734.9 7.1 fusion.50
  742.6 42.8 %all-reduce.13 = (f32[768]{0:T(1024)}, f32[4,1792]{1,0:T(4,128)}, f32[1792]{0:T(1024)}, f32[24]{0:T(128)}, f32[24]{0:T(128)}, /*index=5*/f32[24]{0:T(128)}, f32[1536]{0:T(1024)}, f32[]{:T(128)}, f32[]{:T(128)}, f32[]{:T(128)}) all-reduce(f32[768]{0:T(1024)S(1)} %get-tuple-element.396, ...), channel_id=1, replica_groups=mesh['dp'=8,'seq'=4] {'dp','seq'}, use_global_device_ids=true, to_apply=%region_26.27 | all-reduce | flops 11339 | bytes 90712 | tf_op jit(solution)/shard_map/psum | solution.py:267
  787.5 3.3 fusion.52
  796.5 4.3 copy.276
  800.8 66.9 %all-gather.7.cloned.1.call-done = bf16[768,3352]{1,0:T(8,128)(2,1)} async-done(((bf16[192,3352]{1,0:T(8,128)(2,1)}), bf16[768,3352]{1,0:T(8,128)(2,1)}) %all-gather.7.cloned.1.call-update) | async-done | bytes 5148688 | tf_op jit(solution)/shard_map/all_gather | solution.py:253
  867.7 8.0 copy.275
  (306 shorter events, 82.4 us)
Async XLA Ops:
  7.2 88.0 %all-gather.11.cloned.1.call-start = ((), (), s32[]{:S(2)}) async-start(), calls=%async_computation.3 | async-start | bytes 1966080 | tf_op jit(solution)/shard_map/all_gather | solution.py:19
  9.2 5.6 copy-start.69
  9.2 10.6 %copy-start.72 = (s32[1,512]{1,0:T(1,128)S(1)}, s32[1,512]{1,0:T(1,128)}, u32[]{:S(2)}) copy-start(s32[1,512]{1,0:T(1,128)} %param.24) | copy-start | bytes 6148
  9.2 14.2 %copy-start.91 = (f32[24]{0:T(128)S(1)}, f32[24]{0:T(128)}, u32[]{:S(2)}) copy-start(f32[24]{0:T(128)} %param.34) | copy-start | bytes 292
  9.2 14.2 %copy-start.75 = (f32[24]{0:T(128)S(1)}, f32[24]{0:T(128)}, u32[]{:S(2)}) copy-start(f32[24]{0:T(128)} %param.33) | copy-start | bytes 292
  14.8 8.6 copy-start.4
  14.8 21.5 %collective-permute-start = (f32[1,3,1792]{2,0,1:T(1,128)S(1)}, f32[1,3,1792]{2,0,1:T(1,128)S(1)}, u32[]{:S(2)}, u32[]{:S(2)}) collective-permute-start(f32[1,3,1792]{2,0,1:T(1,128)S(1)} %copy.240), channel_id=1, source_target_pairs={{0,1},{1,2},{2,3},{4,5},{5,6},{6,7},{8,9},{9,10},{10,11},{12,13},{... | collective-permute-start | bytes 64520 | tf_op jit(solution)/shard_map/ppermute | solution.py:13
  19.9 16.3 %collective-permute-start.1 = (f32[1,3]{1,0:T(1,128)S(1)}, f32[1,3]{1,0:T(1,128)S(1)}, u32[]{:S(2)}, u32[]{:S(2)}) collective-permute-start(f32[1,3]{1,0:T(1,128)S(1)} %slice.135), channel_id=1, source_target_pairs={{0,1},{1,2},{2,3},{4,5},{5,6},{6,7},{8,9},{9,10},{10,11},{12,13},{... | collective-permute-start | bytes 44 | tf_op jit(solution)/shard_map/ppermute | solution.py:13
  25.8 10.2 %copy-start.63 = (f32[4,1792]{1,0:T(4,128)S(1)}, f32[4,1792]{1,0:T(4,128)}, u32[]{:S(2)}) copy-start(f32[4,1792]{1,0:T(4,128)} %param.31) | copy-start | bytes 86020
  25.8 10.5 %copy-start.74 = (f32[1792]{0:T(1024)S(1)}, f32[1792]{0:T(1024)}, u32[]{:S(2)}) copy-start(f32[1792]{0:T(1024)} %param.32) | copy-start | bytes 21508
  30.0 17.9 %copy-start.57 = (f32[1,512]{1,0:T(1,128)}, f32[1,512]{1,0:T(1,128)S(1)}, u32[]{:S(2)}) copy-start(f32[1,512]{1,0:T(1,128)S(1)} %compare_convert_fusion) | copy-start | bytes 6148
  30.8 17.1 %copy-start.62 = (s32[512]{0:T(512)}, s32[512]{0:T(512)S(1)}, u32[]{:S(2)}) copy-start(s32[512]{0:T(512)S(1)} %get-tuple-element.452) | copy-start | bytes 6148
  36.1 11.8 %copy-start.41 = (f32[1792]{0:T(1024)}, f32[1792]{0:T(1024)S(1)}, u32[]{:S(2)}) copy-start(f32[1792]{0:T(1024)S(1)} %get-tuple-element.401) | copy-start | bytes 21508
  36.2 11.8 %copy-start.43 = (f32[1792]{0:T(1024)}, f32[1792]{0:T(1024)S(1)}, u32[]{:S(2)}) copy-start(f32[1792]{0:T(1024)S(1)} %get-tuple-element.402) | copy-start | bytes 21508
  36.3 11.7 %copy-start.51 = (f32[1,512]{1,0:T(1,128)}, f32[1,512]{1,0:T(1,128)S(1)}, u32[]{:S(2)}) copy-start(f32[1,512]{1,0:T(1,128)S(1)} %get-tuple-element.470) | copy-start | bytes 6148
  36.3 11.7 %copy-start.53 = (f32[1,512]{1,0:T(1,128)}, f32[1,512]{1,0:T(1,128)S(1)}, u32[]{:S(2)}) copy-start(f32[1,512]{1,0:T(1,128)S(1)} %get-tuple-element.471) | copy-start | bytes 6148
  36.3 11.7 %copy-start.55 = (f32[1,512]{1,0:T(1,128)}, f32[1,512]{1,0:T(1,128)S(1)}, u32[]{:S(2)}) copy-start(f32[1,512]{1,0:T(1,128)S(1)} %get-tuple-element.472) | copy-start | bytes 6148
  58.7 212.3 %all-gather.13.cloned.1.call-start = ((), (), s32[]{:S(2)}) async-start(), calls=%async_computation.4 | async-start | bytes 3932160 | tf_op jit(solution)/shard_map/all_gather | solution.py:38
  100.4 29.4 %copy-start.14 = (f32[512,24,64]{0,2,1:T(8,128)}, f32[512,24,64]{0,2,1:T(8,128)S(1)}, u32[]{:S(2)}) copy-start(f32[512,24,64]{0,2,1:T(8,128)S(1)} %fusion.88) | copy-start | bytes 9437188
  141.5 7.3 copy-start.15
  163.4 5.5 copy-start.87
  168.8 446.4 %reduce-scatter.4.cloned.1.call-start = ((), (), s32[]{:S(2)}) async-start(), calls=%async_computation.6 | async-start | bytes 19169280
  230.9 11.1 %copy-start.18 = (f32[512,512]{1,0:T(8,128)S(1)}, f32[512,512]{1,0:T(8,128)}, u32[]{:S(2)}) copy-start(f32[512,512]{1,0:T(8,128)} %get-tuple-element.388) | copy-start | bytes 3145732
  230.9 13.7 %copy-start.7 = (f32[1,512,1536]{2,1,0:T(8,128)S(1)}, f32[1,512,1536]{2,1,0:T(8,128)}, u32[]{:S(2)}) copy-start(f32[1,512,1536]{2,1,0:T(8,128)} %copy-done.6) | copy-start | bytes 9437188
  230.9 13.7 %copy-start.17 = (bf16[1,512,768]{2,1,0:T(8,128)(2,1)S(1)}, bf16[1,512,768]{2,1,0:T(8,128)(2,1)}, u32[]{:S(2)}) copy-start(bf16[1,512,768]{2,1,0:T(8,128)(2,1)} %param.23) | copy-start | bytes 2359300
  230.9 13.7 %copy-start.48 = (f32[1536]{0:T(1024)S(1)}, f32[1536]{0:T(1024)}, u32[]{:S(2)}) copy-start(f32[1536]{0:T(1024)} %param.36) | copy-start | bytes 18436
  230.9 13.7 %copy-start.65 = (f32[512]{0:T(512)S(1)}, f32[512]{0:T(512)}, u32[]{:S(2)}) copy-start(f32[512]{0:T(512)} %copy-done.64) | copy-start | bytes 6148
  283.0 5.0 copy-start.29
  283.0 10.8 %copy-start.21 = (f32[24,64,512]{2,1,0:T(8,128)S(1)}, f32[24,64,512]{2,1,0:T(8,128)}, u32[]{:S(2)}) copy-start(f32[24,64,512]{2,1,0:T(8,128)} %fusion.2) | copy-start | bytes 9437188
  287.2 6.6 copy-start.11
  287.2 6.6 copy-start.37
  287.2 6.6 copy-start.90
  300.5 11.2 %copy-start.42 = (f32[1792]{0:T(1024)S(1)}, f32[1792]{0:T(1024)}, u32[]{:S(2)}) copy-start(f32[1792]{0:T(1024)} %copy-done.41) | copy-start | bytes 21508
  300.5 11.2 %copy-start.44 = (f32[1792]{0:T(1024)S(1)}, f32[1792]{0:T(1024)}, u32[]{:S(2)}) copy-start(f32[1792]{0:T(1024)} %copy-done.43) | copy-start | bytes 21508
  313.3 4.7 copy-start.30
  313.4 6.0 copy-start.86
  316.4 13.7 %copy-start.38 = (f32[512,24]{0,1:T(8,128)S(1)}, f32[512,24]{0,1:T(8,128)}, u32[]{:S(2)}) copy-start(f32[512,24]{0,1:T(8,128)} %get-tuple-element.466) | copy-start | bytes 147460
  316.4 13.9 %copy-start.85 = (f32[24]{0:T(128)S(1)}, f32[24]{0:T(128)}, u32[]{:S(2)}) copy-start(f32[24]{0:T(128)} %copy-done.84) | copy-start | bytes 292
  316.5 15.4 %collective-permute-start.2 = (bf16[1,3,1792]{2,1,0:T(4,128)(2,1)S(1)}, bf16[1,3,1792]{2,1,0:T(4,128)(2,1)S(1)}, u32[]{:S(2)}, u32[]{:S(2)}) collective-permute-start(bf16[1,3,1792]{2,1,0:T(4,128)(2,1)S(1)} %slice.284), channel_id=1, source_target_pairs={{1,0},{2,1},{3,2},{5,4},{6,5},{7,6},{9,8},{10,9},{11,10},{13,12},{... | collective-permute-start | bytes 32264 | tf_op jit(solution)/shard_map/ppermute | solution.py:13
  331.9 5.7 copy-start.39
  331.9 5.7 slice-start
  358.6 353.9 %all-reduce.16.cloned.1.call-start = ((), (), s32[]{:S(2)}) async-start(), calls=%async_computation.5 | async-start | bytes 10010624 | tf_op jit(solution)/shard_map/psum | solution.py:241
  621.0 175.6 %all-gather.9.cloned.1.call-start = ((), (), s32[]{:S(2)}) async-start(), calls=%async_computation.2 | async-start | bytes 2949120 | tf_op jit(solution)/shard_map/all_gather | solution.py:254
  717.1 150.7 %all-gather.7.cloned.1.call-start = ((), (), s32[]{:S(2)}) async-start(), calls=%async_computation.1 | async-start | bytes 6635520 | tf_op jit(solution)/shard_map/all_gather | solution.py:253
  734.8 7.2 copy-start.73
  734.8 7.8 copy-start.71
  734.9 52.6 %copy-start.68 = (f32[512]{0:T(512)S(1)}, f32[512]{0:T(512)}, u32[]{:S(2)}) copy-start(f32[512]{0:T(512)} %copy-done.67) | copy-start | bytes 6148
  742.0 48.8 %copy-start.13 = (f32[192,3352]{0,1:T(8,128)S(1)}, f32[192,3352]{0,1:T(8,128)}, u32[]{:S(2)}) copy-start(f32[192,3352]{0,1:T(8,128)} %get-tuple-element.444) | copy-start | bytes 7723012
  (56 other events, 191.2 us)
Sparse Core Ops, SparseCore 0:
  58.8 36.3 all-gather.10
  169.0 70.9 all-gather.12
  358.7 256.4 reduce-scatter.3
  621.1 91.3 all-reduce.15
  717.2 50.9 all-gather.8
  769.7 98.0 all-gather.6
where the time goes:
time: 895 us; the launch traced here: 885 us
  waiting for transfers between devices  421 us (47%)
  matrix products  151 us (17%)
  local copies, waits for them, and re-layouts  108 us (12%)
  other arithmetic  101 us (11%)
  blocking collectives  70.5 us (8%)
  between operations  23.1 us (3%)
  starting transfers between devices  10.1 us (1%)
    unnamed x7, waiting for transfers between devices  257 us
    psum x1, waiting for transfers between devices, local(): whole_grad = lax.psum(jnp.concatenate([in_part, out_part], axis=1), 'dp')  89.6 us
    dot_general x3, matrix products, piece_out(): jnp.einsum('shtu,suhp->sthp', weighted, signal_in * step_in[..., None], p...  85.3 us
    all_gather x1, waiting for transfers between devices, local(): lax.all_gather(new_in_part, 'seq', axis=0, tiled=True)  66.9 us
    unnamed x198, local copies, waits for them, and re-layouts  51 us
    psum x1, blocking collectives, local(): lax.psum((norm_gain_grad, conv_weight_grad, conv_bias_grad, dt_bias_grad,...  42.8 us
    mul x4, local copies, waits for them, and re-layouts, piece_out(): jnp.einsum('stn,shpn->sthp', reader_in, incoming_in, precision=highest)  20.4 us
  transfers between devices with their start and end apart: 9, of which 4 were waited for; matrix products, arithmetic and copies ran while one was open for 19% of the time, Pallas kernels for 0%

commit v1 on v0

--- a/solution.py
+++ b/solution.py
@@ -1,6 +1,10 @@
+import functools
+
 import jax
 import jax.numpy as jnp
 from jax import lax
+from jax.experimental import pallas as pl
+from jax.experimental.pallas import tpu as pltpu
 from jax.sharding import PartitionSpec as P
 
 epsilon = 1e-05
@@ -61,6 +65,234 @@
 
 def compose(earlier, later):
     return (earlier[0] * later[0], later[0][:, :, None, None] * earlier[1] + later[1])
+
+
+LANES = 128
+
+
+def exchange_kernel(
+    bits,
+    pieces,
+    flows,
+    rate_ref,
+    grad_ref,
+    weight_ref,
+    momentum_ref,
+    small_ref,
+    gathered_ref,
+    small_out_ref,
+    *scratch,
+):
+    halves = scratch[:bits]
+    (piece_parts, small_acc, small_in, small_parts) = scratch[bits : bits + 4]
+    (rs_send, rs_recv, zs_send, zs_recv, zg_send, zg_recv, ag_send, ag_recv) = scratch[
+        bits + 4 : bits + 12
+    ]
+    (sm_send, sm_recv, sz_send, sz_recv) = scratch[bits + 12 :]
+    place = lax.axis_index("dp")
+    turn = lax.axis_index("seq")
+    own = [(place // (1 << b)) % 2 for b in range(bits)]
+    partner = [{"dp": place + (1 - 2 * own[b]) * (1 << b)} for b in range(bits)]
+    others = [{"seq": (turn + j) % pieces} for j in range(pieces)]
+
+    def order_of(f):
+        rest = list(range(1, bits))
+        shift = f % max(len(rest), 1)
+        return ([0] if bits else []) + rest[shift:] + rest[:shift]
+
+    def index_of(fixed):
+        return tuple(fixed.get(b, slice(None)) for b in range(bits - 1, -1, -1))
+
+    barrier = pltpu.get_barrier_semaphore()
+    for target in partner + others[1:]:
+        pl.semaphore_signal(
+            barrier, inc=1, device_id=target, device_id_type=pl.DeviceIdType.MESH
+        )
+    pl.semaphore_wait(barrier, bits + pieces - 1)
+
+    def remote(src, dst, send, recv, target):
+        return pltpu.make_async_remote_copy(
+            src_ref=src,
+            dst_ref=dst,
+            send_sem=send,
+            recv_sem=recv,
+            device_id=target,
+            device_id_type=pl.DeviceIdType.MESH,
+        )
+
+    def held(f, k, other):
+        order = order_of(f)
+        bit = order[k]
+        value = 1 - own[bit] if other else own[bit]
+        if k == 0:
+            return grad_ref.at[(f,) + index_of({bit: value})]
+        free = [b for b in range(bits - 1, -1, -1) if b not in order[:k]]
+        return halves[k - 1].at[
+            (f,) + tuple(value if b == bit else slice(None) for b in free)
+        ]
+
+    def rs_copy(f, k):
+        return remote(
+            held(f, k, True),
+            halves[k].at[f],
+            rs_send.at[f, k],
+            rs_recv.at[f, k],
+            partner[order_of(f)[k]],
+        )
+
+    def rs_add(f, k):
+        kept = held(f, k, False)
+        into = halves[k].at[f]
+        left = bits - k - 1
+        for count in range(1 << left):
+            spot = tuple((count >> (left - 1 - i)) & 1 for i in range(left))
+
+            def body(p, carry):
+                into[spot + (p,)] = (
+                    kept[spot + (p,)].astype(jnp.float32)
+                    + into[spot + (p,)].astype(jnp.float32)
+                ).astype(jnp.bfloat16)
+                return carry
+
+            lax.fori_loop(0, pieces, body, 0)
+
+    mine = index_of({b: own[b] for b in range(bits)})
+
+    def zs_copy(f, j):
+        return remote(
+            halves[bits - 1].at[f, lax.rem(turn + j, pieces)],
+            piece_parts.at[f, j],
+            zs_send.at[f, j],
+            zs_recv.at[f, j],
+            others[j],
+        )
+
+    def zg_copy(f, j):
+        spot = gathered_ref.at[(f,) + mine + (turn,)]
+        return remote(spot, spot, zg_send.at[f, j], zg_recv.at[f, j], others[j])
+
+    def ag_copy(f, k):
+        order = order_of(f)
+        fixed = {order[i]: own[order[i]] for i in range(k + 1)}
+        spot = gathered_ref.at[(f,) + index_of(fixed)]
+        return remote(spot, spot, ag_send.at[f, k], ag_recv.at[f, k], partner[order[k]])
+
+    def sm_copy(k):
+        return remote(small_acc.at[k], small_in.at[k], sm_send.at[k], sm_recv.at[k], partner[k])
+
+    def sz_copy(j):
+        return remote(
+            small_acc.at[bits], small_parts.at[turn], sz_send.at[j], sz_recv.at[j], others[j]
+        )
+
+    def begin(f, k):
+        if k < bits:
+            rs_copy(f, k).start()
+        else:
+            for j in range(1, pieces):
+                zs_copy(f, j).start()
+
+    def begin_back(f, k):
+        if k >= 0:
+            ag_copy(f, k).start()
+
+    small_acc[0] = small_ref[...]
+    if bits:
+        sm_copy(0).start()
+    for f in range(flows):
+        begin(f, 0)
+    for k in range(bits):
+        sm_copy(k).wait_recv()
+        small_acc[k + 1] = small_acc[k] + small_in[k]
+        if k + 1 < bits:
+            sm_copy(k + 1).start()
+        else:
+            for j in range(1, pieces):
+                sz_copy(j).start()
+        for f in range(flows):
+            rs_copy(f, k).wait_recv()
+            rs_add(f, k)
+            begin(f, k + 1)
+    small_parts[turn] = small_acc[bits]
+    rate = rate_ref[0]
+    for f in range(flows):
+        for j in range(1, pieces):
+            zs_copy(f, j).wait_recv()
+        total = halves[bits - 1][f, turn].astype(jnp.float32)
+        for j in range(1, pieces):
+            total = total + piece_parts[f, j].astype(jnp.float32)
+        summed = total.astype(jnp.bfloat16)
+        gathered_ref[(f,) + mine + (pieces,)] = summed
+        moved = 0.5 * momentum_ref[f] + summed.astype(jnp.float32)
+        gathered_ref[(f,) + mine + (turn,)] = (
+            weight_ref[f].astype(jnp.float32) - rate * moved
+        ).astype(jnp.bfloat16)
+        for j in range(1, pieces):
+            zg_copy(f, j).start()
+    for j in range(1, pieces):
+        sz_copy(j).wait_recv()
+    whole = small_parts[0]
+    for j in range(1, pieces):
+        whole = whole + small_parts[j]
+    small_out_ref[...] = whole
+    for f in range(flows):
+        for j in range(1, pieces):
+            zg_copy(f, j).wait_recv()
+        begin_back(f, bits - 1)
+    for k in range(bits - 1, -1, -1):
+        for f in range(flows):
+            ag_copy(f, k).wait_recv()
+            begin_back(f, k - 1)
+    for k in range(bits):
+        sm_copy(k).wait_send()
+        for f in range(flows):
+            rs_copy(f, k).wait_send()
+            ag_copy(f, k).wait_send()
+    for j in range(1, pieces):
+        sz_copy(j).wait_send()
+        for f in range(flows):
+            zs_copy(f, j).wait_send()
+            zg_copy(f, j).wait_send()
+
+
+def exchange(rate, grads, weights, momenta, small):
+    flows, places, pieces, rows, _ = grads.shape
+    bits = places.bit_length() - 1
+    assert places == 1 << bits and bits >= 1 and pieces >= 2
+    twos = (2,) * bits
+    grads = grads.reshape((flows,) + twos + (pieces, rows, LANES))
+    small_rows = small.shape[0]
+    vmem = pl.BlockSpec(memory_space=pltpu.VMEM)
+    dma = pltpu.SemaphoreType.DMA
+    gathered, small_out = pl.pallas_call(
+        functools.partial(exchange_kernel, bits, pieces, flows),
+        out_shape=(
+            jax.ShapeDtypeStruct((flows,) + twos + (pieces + 1, rows, LANES), jnp.bfloat16),
+            jax.ShapeDtypeStruct((small_rows, LANES), jnp.float32),
+        ),
+        in_specs=[pl.BlockSpec(memory_space=pltpu.SMEM)] + [vmem] * 4,
+        out_specs=(vmem, vmem),
+        scratch_shapes=[
+            pltpu.VMEM((flows,) + twos[k + 1 :] + (pieces, rows, LANES), jnp.bfloat16)
+            for k in range(bits)
+        ]
+        + [
+            pltpu.VMEM((flows, pieces, rows, LANES), jnp.bfloat16),
+            pltpu.VMEM((bits + 1, small_rows, LANES), jnp.float32),
+            pltpu.VMEM((bits, small_rows, LANES), jnp.float32),
+            pltpu.VMEM((pieces, small_rows, LANES), jnp.float32),
+        ]
+        + [dma((flows, bits))] * 2
+        + [dma((flows, pieces))] * 4
+        + [dma((flows, bits))] * 2
+        + [dma((bits,))] * 2
+        + [dma((pieces,))] * 2,
+        compiler_params=pltpu.CompilerParams(
+            collective_id=0, has_side_effects=True, vmem_limit_bytes=56 * 1024 * 1024
+        ),
+        name="exchange",
+    )(rate, grads, weights, momenta, small)
+    return gathered.reshape(flows, places, pieces + 1, rows, LANES), small_out
 
 
 def local(
@@ -238,21 +470,73 @@
     out_part = lax.dot_general(
         out_low, gate_low, (((0,), (0,)), ((), ())), preferred_element_type=jnp.float32
     )
-    whole_grad = lax.psum(jnp.concatenate([in_part, out_part], axis=1), "dp")
-    grad_share = lax.psum_scatter(whole_grad, "seq", scatter_dimension=0, tiled=True)
+    places, pieces = lax.axis_size("dp"), lax.axis_size("seq")
+    width = inner_width + proj_width
+    flows = -(-width // (LANES * places))
+    full = flows * places * LANES
+
+    def tiled(block):
+        spread = jnp.pad(block, ((0, 0), (0, full - width)))
+        return spread.reshape(-1, flows * places, LANES)
+
+    whole_grad = jnp.concatenate([out_part, in_part], axis=1).astype(jnp.bfloat16)
+    grads = (
+        tiled(whole_grad)
+        .reshape(pieces, share_rows, flows, places, LANES)
+        .transpose(2, 3, 0, 1, 4)
+    )
     step_float = step_number[0].astype(jnp.float32)
     rate_now = learn_rate[0] * step_float / (step_float + 16.0)
-    new_in_momentum = 0.5 * in_momentum + grad_share[:, :proj_width]
-    new_out_momentum = 0.5 * out_momentum + jnp.transpose(grad_share[:, proj_width:])
     first_row = lax.axis_index("seq") * share_rows
-    own_in = lax.dynamic_slice_in_dim(in_weight, first_row, share_rows, 0).astype(jnp.float32)
-    own_out = lax.dynamic_slice_in_dim(out_weight, first_row, share_rows, 1).astype(jnp.float32)
-    new_in_part = (own_in - rate_now * new_in_momentum).astype(jnp.bfloat16)
-    new_out_part = (own_out - rate_now * new_out_momentum).astype(jnp.bfloat16)
-    new_in_weight, new_out_weight = (
-        lax.all_gather(new_in_part, "seq", axis=0, tiled=True),
-        lax.all_gather(new_out_part, "seq", axis=1, tiled=True),
-    )
+    own_in = lax.dynamic_slice_in_dim(in_weight, first_row, share_rows, 0)
+    own_out = lax.dynamic_slice_in_dim(out_weight, first_row, share_rows, 1)
+    place = lax.axis_index("dp")
+
+    def own_piece(out_rows, in_rows):
+        block = tiled(jnp.concatenate([jnp.transpose(out_rows), in_rows], axis=1))
+        block = block.reshape(share_rows, flows, places, LANES)
+        return jnp.transpose(lax.dynamic_index_in_dim(block, place, 2, False), (1, 0, 2))
+
+    parts = (
+        norm_gain_grad,
+        conv_weight_grad,
+        conv_bias_grad,
+        dt_bias_grad,
+        a_log_grad,
+        skip_grad,
+        gate_gain_grad,
+        out_square,
+        mix_square,
+        valid_count,
+    )
+    flat = jnp.concatenate([p.reshape(-1) for p in parts])
+    small_rows = -(-flat.shape[0] // (8 * LANES)) * 8
+    small = jnp.pad(flat, (0, small_rows * LANES - flat.shape[0])).reshape(small_rows, LANES)
+    gathered, small_total = exchange(
+        rate_now.reshape(1), grads, own_piece(own_out, own_in), own_piece(out_momentum, in_momentum), small
+    )
+
+    def untiled(block):
+        return block.reshape(-1, full)[:, :width]
+
+    summed = untiled(
+        gathered[:, :, pieces].reshape(flows * places, share_rows, LANES).transpose(1, 0, 2)
+    ).astype(jnp.float32)
+    new_in_momentum = 0.5 * in_momentum + summed[:, inner_width:]
+    new_out_momentum = 0.5 * out_momentum + jnp.transpose(summed[:, :inner_width])
+    new_weights = untiled(
+        gathered[:, :, :pieces]
+        .reshape(flows * places, pieces, share_rows, LANES)
+        .transpose(1, 2, 0, 3)
+    )
+    new_in_weight = new_weights[:, inner_width:]
+    new_out_weight = jnp.transpose(new_weights[:, :inner_width])
+    flat_total = small_total.reshape(-1)
+    totals = []
+    at = 0
+    for p in parts:
+        totals.append(flat_total[at : at + p.size].reshape(p.shape))
+        at += p.size
     (
         norm_gain_total,
         conv_weight_total,
@@ -264,21 +548,7 @@
         out_square_total,
         mix_square_total,
         valid_total,
-    ) = lax.psum(
-        (
-            norm_gain_grad,
-            conv_weight_grad,
-            conv_bias_grad,
-            dt_bias_grad,
-            a_log_grad,
-            skip_grad,
-            gate_gain_grad,
-            out_square,
-            mix_square,
-            valid_count,
-        ),
-        ("dp", "seq"),
-    )
+    ) = totals
     denominator = jnp.maximum(valid_total, 1.0) * model_width
     output_rms = jnp.sqrt(out_square_total / denominator).reshape(1)
     mixer_rms = jnp.sqrt(mix_square_total / denominator).reshape(1)

time: 895 us -> 615 us (0.69)
  waiting for transfers between devices: 421 us -> 0.53 us
  Pallas kernels: 0 us -> 130 us
  local copies, waits for them, and re-layouts: 108 us -> 164 us
  blocking collectives: 70.5 us -> 17.5 us
    unnamed x7 -> x2, waiting for transfers between devices: 257 us -> 0.03 us
    pallas_call x0 -> x1, Pallas kernels: none -> 130 us  [exchange(): pl.pallas_call(functools.partial(exchange_kernel, bits, pieces, flows), o...]
    psum x1 -> x0, waiting for transfers between devices: 89.6 us -> none  [local(): whole_grad = lax.psum(jnp.concatenate([in_part, out_part], axis=1), 'dp')]
    all_gather x2 -> x0, waiting for transfers between devices: 66.9 us -> none  [the longest x1 66.9 us: local(): lax.all_gather(new_in_part, 'seq', axis=0, tiled=True)]
    psum x1 -> x0, blocking collectives: 42.8 us -> none  [local(): lax.psum((norm_gain_grad, conv_weight_grad, conv_bias_grad, dt_bias_grad,...]
    slice x1 -> x11, local copies, waits for them, and re-layouts: 0.19 us -> 30.7 us  [the longest x2 20.5 us: local(): gathered[:, :, :pieces].reshape(flows * places, pieces, share_rows, LANES)]
    transpose x0 -> x3, local copies, waits for them, and re-layouts: none -> 12 us  [the longest x1 8.42 us: local(): grads = tiled(whole_grad).reshape(pieces, share_rows, flows, places, LANE...]
    all_gather x1, blocking collectives: 17.8 us -> 8.14 us  [carried_in(): everything = jax.tree.map(lambda part: lax.all_gather(part, axis), value)]
  transfers between devices with their start and end apart: 9 -> 5, of which waited for: 4 -> 1; matrix products, arithmetic and copies ran while one was open for 19% -> 22% of each run, Pallas kernels for 0% -> 0%
where the time goes in v1:
time: 615 us; the launch traced here: 606 us
  local copies, waits for them, and re-layouts  164 us (27%)
  matrix products  158 us (26%)
  Pallas kernels  130 us (21%)
  other arithmetic  104 us (17%)
  between operations  22.4 us (4%)
  blocking collectives  17.5 us (3%)
  starting transfers between devices  9.93 us (2%)
    pallas_call x1, Pallas kernels, exchange(): pl.pallas_call(functools.partial(exchange_kernel, bits, pieces, flows), o...  130 us
    dot_general x3, matrix products, piece_out(): jnp.einsum('shtu,suhp->sthp', weighted, signal_in * step_in[..., None], p...  87.6 us
    unnamed x186, local copies, waits for them, and re-layouts  59.2 us
    slice x2, local copies, waits for them, and re-layouts, local(): gathered[:, :, :pieces].reshape(flows * places, pieces, share_rows, LANES)  20.5 us
    dot_general x3, matrix products, end_state(): jnp.einsum('slh,slhp,sln->shpn', tails, signal_in, writer_in, precision=h...  18.7 us
    dot_general x3, matrix products, piece_out(): jnp.einsum('stn,shpn->sthp', reader_in, incoming_in, precision=highest)  16.1 us
    another operation x10, other arithmetic  13.9 us
  transfers between devices with their start and end apart: 5, of which 1 were waited for; matrix products, arithmetic and copies ran while one was open for 22% of the time, Pallas kernels for 0%

profile of v1, /device:TPU:0, one launch (start us, length us, event | category | flops | bytes accessed | tf_op | source)
XLA Modules:
  0.0 606.0 jit_solution(13977978197669223183)
XLA Ops:
  9.9 5.6 convolution_bitcast_fusion
  15.6 4.9 collective-permute-start
  20.6 3.5 collective-permute-start.1
  26.6 4.1 slice.204
  37.6 11.3 %fusion.29 = (f32[1,512,1792]{2,1,0:T(8,128)S(1)}, f32[1,512,1792]{2,1,0:T(8,128)}) fusion(f32[1792]{0:T(1024)S(1)} %get-tuple-element.390, f32[1,512,1792]{2,1,0:T(8,128)} %slice.204, f32[512]{0:T(512)S(1)} %bitcast.437, f32[1792]{0:T(1024)S(1)} %get-tuple-element.391, f32[512]{0:T(512)S(1)} %bitcast.434, f32[1,3,1792]{2,1,0:T(4,128)S(1)} %copy.246, ...), kind=kLoop, calls=%fused_computation.59 | loop fusion | flops 17432576 | bytes 11075584 | tf_op jit(solution)/shard_map/jvp(jit(silu))/mul | solution.py:352
  53.0 3.5 copy.247
  56.5 5.3 fusion.72
  72.9 3.6 copy.259
  86.1 9.3 %all_gather.20 = bf16[4,1,24]{2,1,0:T(2,128)(2,1)} all-gather(bf16[1,1,24]{2,1,0:T(2,128)(2,1)S(1)} %copy-done.79), channel_id=1, replica_groups=mesh['dp'=8,'seq'=4] {'seq'}, dimensions={0}, use_global_device_ids=true | all-gather | bytes 240 | tf_op jit(solution)/shard_map/all_gather | solution.py:23
  95.5 8.1 %all_gather.23 = f32[4,1,24]{2,1,0:T(1,128)} all-gather(f32[1,1,24]{2,1,0:T(1,128)S(1)} %copy-done.78), channel_id=1, replica_groups=mesh['dp'=8,'seq'=4] {'seq'}, dimensions={0}, use_global_device_ids=true | all-gather | bytes 480 | tf_op jit(solution)/shard_map/all_gather | solution.py:42
  108.3 3.7 fusion.91
  112.1 31.1 %fusion.33 = f32[1,512,24,64]{1,3,2,0:T(8,128)} fusion(f32[1,512,24,64]{1,3,2,0:T(8,128)S(1)} %bitcast.386, f32[512,24,64]{0,2,1:T(8,128)S(1)} %fusion.91, f32[24]{0:T(128)S(1)} %copy-done.82, f32[512,24]{0,1:T(8,128)S(1)} %copy-done.35, f32[24,512]{1,0:T(8,128)} %bitcast_add_fusion.6, f32[512,512]{1,0:T(8,128)S(1)} %copy-done.24, ...), kind=kOutput, calls=%fused_computation.67 | convolution fusion | flops 4854644736 | bytes 14041184 | tf_op jit(solution)/shard_map/jvp(shtu,suhp->sthp)/dot_general | solution.py:389
  143.2 3.5 copy.257
  146.7 3.9 multiply_reduce_fusion.7
  154.8 6.1 %multiply_reduce_fusion.5 = (f32[1536]{0:T(1024)}, f32[1,512,1536]{2,1,0:T(8,128)}, bf16[512,1536]{1,0:T(8,128)(2,1)}) fusion(f32[1,512,1792]{2,1,0:T(8,128)S(1)} %copy-done.5, f32[1,512,3352]{2,1,0:T(8,128)} %copy-done.6, f32[1,512,1536]{2,1,0:T(8,128)S(1)} %get-tuple-element.423, f32[512]{0:T(512)S(1)} %multiply_multiply_fusion.5, f32[512]{0:T(512)S(1)} %fusion.130, ...), kind=kLoop, calls=%fused_computation.81 | loop fusion | flops 15727104 | bytes 20463616 | tf_op jit(solution)/shard_map/transpose(jvp())/reduce_sum | solution.py:405
  160.9 4.0 copy.261
  164.8 5.1 mul.658
  169.9 3.5 copy.260
  173.5 5.4 fusion.109
  178.9 3.7 multiply_reduce_fusion.6
  183.4 34.3 %fusion.7 = (f32[24,512]{1,0:T(8,128)}, f32[24,512]{1,0:T(8,128)S(1)}, f32[512,512]{1,0:T(8,128)}) fusion(f32[24,512]{1,0:T(8,128)} %bitcast_add_fusion.6, f32[512,512]{1,0:T(8,128)} %fusion.113, pred[512,512]{1,0:T(8,128)(4,1)} %fusion.84, f32[24,64,512]{2,1,0:T(8,128)} %bitcast.396, f32[512,24,64]{0,2,1:T(8,128)} %bitcast.382, f32[512,24]{0,1:T(8,128)} %copy.248), kind=kOutput, calls=%fused_computation.12 | convolution fusion | flops 4888961024 | bytes 8847360 | tf_op jit(solution)/shard_map/transpose(jvp(shtu,suhp->sthp))/dot_general | solution.py:389
  221.5 5.2 convolution_convert_fusion.1
  226.7 4.3 copy.275
  231.0 3.9 convolution_bitcast_fusion.1
  234.9 6.9 %convolution_bitcast_fusion.2 = f32[512,128]{1,0:T(8,128)S(1)} fusion(f32[512,24,64]{0,2,1:T(8,128)} %bitcast.394, f32[1,24,64,128]{3,2,1,0:T(8,128)S(1)} %get-tuple-element.193), kind=kOutput, calls=%fused_computation.134 | convolution fusion | flops 1207959552 | bytes 4194304 | tf_op jit(solution)/shard_map/transpose(jvp(stn,shpn->sthp))/dot_general | solution.py:394
  247.7 22.3 %fusion.2 = f32[24,64,512]{2,1,0:T(8,128)} fusion(f32[24,64,512]{2,1,0:T(8,128)S(1)} %bitcast.397, f32[24,512]{1,0:T(8,128)S(1)} %copy-done.42, f32[512,512]{1,0:T(8,128)S(1)} %copy-done.25, pred[512,512]{1,0:T(8,128)(4,1)S(1)} %copy-done.33), kind=kOutput, calls=%fused_computation.9 | convolution fusion | flops 4850712576 | bytes 7651328 | tf_op jit(solution)/shard_map/transpose(jvp(shtu,suhp->sthp))/dot_general | solution.py:389
  270.0 7.9 %while.29 = (s32[]{:T(128)}, f32[1,24,64,128]{3,2,1,0:T(8,128)S(1)}, s32[]{:T(128)}, f32[4,1,24]{2,1,0:T(1,128)}, f32[4,1,24,64,128]{4,3,2,1,0:T(8,128)}, /*index=5*/s32[]{:T(128)}, s32[]{:T(128)}, s32[]{:T(128)}, s32[]{:T(128)}) while((s32[]{:T(128)}, f32[1,24,64,128]{3,2,1,0:T(8,128)S(1)}, s32[]{:T(128)}, ...), condition=%wide.region_11.12_spmd.clone, body=%wide.region_10.11_spmd.clone.sunk | while | flops 786440 | bytes 2359751 | solution.py:55
  277.9 5.6 fusion.37
  286.1 5.4 reduce-window.36
  293.0 5.0 reduce-window.34
  299.5 7.9 %fusion.79 = f32[1,512,128]{2,1,0:T(8,128)} fusion(f32[1,512,128]{2,1,0:T(8,128)S(1)} %copy-done.26, f32[512,24,64]{0,2,1:T(8,128)} %bitcast.384, f32[512,24]{0,1:T(8,128)S(1)} %copy.253, f32[1,24,64,128]{3,2,1,0:T(8,128)S(1)} %get-tuple-element.194), kind=kOutput, calls=%fused_computation.131 | convolution fusion | flops 1208811520 | bytes 4505600 | tf_op jit(solution)/shard_map/transpose(jvp(slh,slhp,sln->shpn))/dot_general | solution.py:377
  307.4 7.4 %fusion.36 = (f32[1,512,24,64]{1,3,2,0:T(8,128)}, f32[512,24]{0,1:T(8,128)S(1)}) fusion(f32[24,64,512]{2,1,0:T(8,128)} %get-tuple-element.456, f32[24,64,512]{2,1,0:T(8,128)} %fusion.2, f32[1,512,24,64]{1,3,2,0:T(8,128)S(1)} %bitcast.398, f32[512,24]{0,1:T(8,128)S(1)} %copy-done.36, f32[24]{0:T(128)S(1)} %copy-done.83, f32[512,24]{0,1:T(8,128)S(1)} %copy.253, ...), kind=kLoop, calls=%fused_computation.73 | loop fusion | flops 5492736 | bytes 15876192 | tf_op jit(solution)/shard_map/add | solution.py:442
  317.2 11.1 %multiply_reduce_fusion.3 = (f32[1792]{0:T(1024)S(1)}, f32[1792]{0:T(1024)S(1)}, f32[1792]{0:T(1024)S(1)}, f32[1792]{0:T(1024)}, f32[1792]{0:T(1024)S(1)}, /*index=5*/f32[1,512,1792]{2,1,0:T(8,128)S(1)}) fusion(f32[1,512,1792]{2,1,0:T(8,128)} %slice.204, f32[1,3,1792]{2,1,0:T(4,128)S(1)} %copy.246, f32[512]{0:T(512)S(1)} %bitcast.435, f32[512]{0:T(512)S(1)} %bitcast.429, ...), kind=kLoop, calls=%fused_computation.52 | loop fusion | flops 24763648 | bytes 18415616 | tf_op jit(solution)/shard_map/transpose(jvp())/reduce_sum | solution.py:351
  346.3 5.3 convolution_convert_fusion
  351.6 4.6 fusion.54
  359.5 5.9 pad_maximum_fusion
  365.5 10.1 %copy.295 = bf16[768,4888]{1,0:T(8,128)(2,1)} copy(bf16[768,4888]{0,1:T(8,128)(2,1)} %pad_maximum_fusion) | data formatting | bytes 15015936
  375.6 7.4 %pad_bitcast_fusion = bf16[96,8,40,128]{3,1,2,0:T(8,128)(2,1)} fusion(bf16[768,4888]{1,0:T(8,128)(2,1)} %copy.295), kind=kLoop, calls=%fused_computation.24 | loop fusion | bytes 15372288
  383.0 8.7 %copy.297 = bf16[96,8,40,128]{3,2,1,0:T(8,128)(2,1)} copy(bf16[96,8,40,128]{3,1,2,0:T(8,128)(2,1)} %pad_bitcast_fusion) | data formatting | bytes 15728640
  391.7 8.4 %copy.277 = bf16[5,8,4,192,128]{4,3,2,1,0:T(8,128)(2,1)} copy(bf16[5,8,4,192,128]{4,1,0,3,2:T(8,128)(2,1)} %bitcast.389) | data formatting | bytes 15728640 | tf_op jit(solution)/shard_map/transpose | solution.py:486
  400.1 129.5 %exchange.1 = (bf16[5,2,2,2,5,192,128]{6,5,4,3,2,1,0:T(8,128)(2,1)}, f32[96,128]{1,0:T(8,128)}) custom-call(f32[1]{0:T(128)S(6)} %div.54.rate_ref, bf16[5,2,2,2,4,192,128]{6,5,4,3,2,1,0:T(8,128)(2,1)} %bitcast.388, bf16[5,192,128]{2,1,0:T(8,128)(2,1)} %bitcast.419, f32[5,192,128]{2,1,0:T(8,128)} %bitcast.414, f32[96,128]{1,0:T(8,128)} %pad_bitcast_fusion.1.small_ref), custom_call_target="tpu_custom_call" | custom-call | tf_op jit(solution)/shard_map/exchange/pallas_call | solution.py:267
  529.6 9.1 %slice.227 = bf16[5,8,4,192,128]{4,3,2,1,0:T(8,128)(2,1)} slice(bf16[5,8,5,192,128]{4,3,2,1,0:T(8,128)(2,1)} %bitcast.401), slice={[0:5], [0:8], [0:4], [0:192], [0:128]} | slice | bytes 15728640 | tf_op jit(solution)/shard_map/slice | solution.py:528
  538.8 11.4 %copy.280 = bf16[5,8,4,192,128]{4,1,0,3,2:T(8,128)(2,1)} copy(bf16[5,8,4,192,128]{4,3,2,1,0:T(8,128)(2,1)} %slice.227) | data formatting | bytes 15728640 | tf_op jit(solution)/shard_map/slice | solution.py:528
  550.1 8.7 %copy.305 = bf16[96,8,40,128]{3,1,2,0:T(8,128)(2,1)} copy(bf16[96,8,40,128]{3,2,1,0:T(8,128)(2,1)} %bitcast.390) | data formatting | bytes 15728640
  558.8 5.2 slice.228
  564.0 3.2 slice_bitcast_fusion
  580.4 8.1 %copy.282 = bf16[768,3352]{0,1:T(8,128)(2,1)} copy(bf16[768,3352]{1,0:T(8,128)(2,1)} %slice.228) | data formatting | bytes 10297344
  588.6 4.3 copy.283
  (305 shorter events, 105.1 us)
Async XLA Ops:
  7.2 54.8 %copy-start = (bf16[1536,768]{1,0:T(8,128)(2,1)S(1)}, bf16[1536,768]{1,0:T(8,128)(2,1)}, u32[]{:S(2)}) copy-start(bf16[1536,768]{1,0:T(8,128)(2,1)} %param.37) | copy-start | bytes 7077892
  7.2 100.9 %all-gather.5.cloned.1.call-start = ((), (), s32[]{:S(2)}) async-start(), calls=%async_computation | async-start | bytes 1966080 | tf_op jit(solution)/shard_map/all_gather | solution.py:23
  9.9 10.6 %copy-start.67 = (s32[1,512]{1,0:T(1,128)S(1)}, s32[1,512]{1,0:T(1,128)}, u32[]{:S(2)}) copy-start(s32[1,512]{1,0:T(1,128)} %param.24) | copy-start | bytes 6148
  9.9 14.1 %copy-start.84 = (f32[24]{0:T(128)S(1)}, f32[24]{0:T(128)}, u32[]{:S(2)}) copy-start(f32[24]{0:T(128)} %param.34) | copy-start | bytes 292
  9.9 14.2 %copy-start.70 = (f32[24]{0:T(128)S(1)}, f32[24]{0:T(128)}, u32[]{:S(2)}) copy-start(f32[24]{0:T(128)} %param.33) | copy-start | bytes 292
  15.5 8.6 %copy-start.6 = (f32[1,512,3352]{2,1,0:T(8,128)}, f32[1,512,3352]{2,1,0:T(8,128)S(1)}, u32[]{:S(2)}) copy-start(f32[1,512,3352]{2,1,0:T(8,128)S(1)} %convolution_bitcast_fusion) | copy-start | bytes 20594692
  15.6 22.0 %collective-permute-start = (f32[1,3,1792]{2,0,1:T(1,128)S(1)}, f32[1,3,1792]{2,0,1:T(1,128)S(1)}, u32[]{:S(2)}, u32[]{:S(2)}) collective-permute-start(f32[1,3,1792]{2,0,1:T(1,128)S(1)} %copy.245), channel_id=1, source_target_pairs={{0,1},{1,2},{2,3},{4,5},{5,6},{6,7},{8,9},{9,10},{10,11},{12,13},{... | collective-permute-start | bytes 64520 | tf_op jit(solution)/shard_map/ppermute | solution.py:17
  20.6 16.8 %collective-permute-start.1 = (f32[1,3]{1,0:T(1,128)S(1)}, f32[1,3]{1,0:T(1,128)S(1)}, u32[]{:S(2)}, u32[]{:S(2)}) collective-permute-start(f32[1,3]{1,0:T(1,128)S(1)} %slice.207), channel_id=1, source_target_pairs={{0,1},{1,2},{2,3},{4,5},{5,6},{6,7},{8,9},{9,10},{10,11},{12,13},{... | collective-permute-start | bytes 44 | tf_op jit(solution)/shard_map/ppermute | solution.py:17
  26.6 10.7 %copy-start.52 = (f32[4,1792]{1,0:T(4,128)S(1)}, f32[4,1792]{1,0:T(4,128)}, u32[]{:S(2)}) copy-start(f32[4,1792]{1,0:T(4,128)} %param.31) | copy-start | bytes 86020
  26.6 11.0 %copy-start.69 = (f32[1792]{0:T(1024)S(1)}, f32[1792]{0:T(1024)}, u32[]{:S(2)}) copy-start(f32[1792]{0:T(1024)} %param.32) | copy-start | bytes 21508
  30.7 18.2 %copy-start.47 = (f32[1,512]{1,0:T(1,128)}, f32[1,512]{1,0:T(1,128)S(1)}, u32[]{:S(2)}) copy-start(f32[1,512]{1,0:T(1,128)S(1)} %compare_convert_fusion) | copy-start | bytes 6148
  31.5 17.4 %copy-start.50 = (s32[512]{0:T(512)}, s32[512]{0:T(512)S(1)}, u32[]{:S(2)}) copy-start(s32[512]{0:T(512)S(1)} %get-tuple-element.427) | copy-start | bytes 6148
  37.4 11.5 %copy-start.37 = (f32[1792]{0:T(1024)}, f32[1792]{0:T(1024)S(1)}, u32[]{:S(2)}) copy-start(f32[1792]{0:T(1024)S(1)} %get-tuple-element.390) | copy-start | bytes 21508
  37.4 11.5 %copy-start.39 = (f32[1792]{0:T(1024)}, f32[1792]{0:T(1024)S(1)}, u32[]{:S(2)}) copy-start(f32[1792]{0:T(1024)S(1)} %get-tuple-element.391) | copy-start | bytes 21508
  37.5 11.4 %copy-start.43 = (f32[1,512]{1,0:T(1,128)}, f32[1,512]{1,0:T(1,128)S(1)}, u32[]{:S(2)}) copy-start(f32[1,512]{1,0:T(1,128)S(1)} %get-tuple-element.452) | copy-start | bytes 6148
  37.5 11.4 %copy-start.45 = (f32[1,512]{1,0:T(1,128)}, f32[1,512]{1,0:T(1,128)S(1)}, u32[]{:S(2)}) copy-start(f32[1,512]{1,0:T(1,128)S(1)} %get-tuple-element.453) | copy-start | bytes 6148
  61.8 208.3 %all-gather.7.cloned.1.call-start = ((), (), s32[]{:S(2)}) async-start(), calls=%async_computation.1 | async-start | bytes 3932160 | tf_op jit(solution)/shard_map/all_gather | solution.py:42
  82.8 12.6 %copy-start.78 = (f32[1,1,24]{2,1,0:T(1,128)S(1)}, f32[1,1,24]{2,1,0:T(1,128)}, u32[]{:S(2)}) copy-start(f32[1,1,24]{2,1,0:T(1,128)} %get-tuple-element.429) | copy-start | bytes 292
  82.9 20.7 %copy-start.34 = (f32[1,24,4,128]{3,2,1,0:T(4,128)S(1)}, f32[1,24,4,128]{3,2,1,0:T(4,128)}, u32[]{:S(2)}) copy-start(f32[1,24,4,128]{3,2,1,0:T(4,128)} %copy.250) | copy-start | bytes 147460
  82.9 21.4 %copy-start.51 = (s32[512]{0:T(512)S(1)}, s32[512]{0:T(512)}, u32[]{:S(2)}) copy-start(s32[512]{0:T(512)} %copy-done.50) | copy-start | bytes 6148
  112.0 31.2 %copy-start.13 = (f32[512,24,64]{0,2,1:T(8,128)}, f32[512,24,64]{0,2,1:T(8,128)S(1)}, u32[]{:S(2)}) copy-start(f32[512,24,64]{0,2,1:T(8,128)S(1)} %fusion.91) | copy-start | bytes 9437188
  231.0 10.9 %copy-start.17 = (f32[512,512]{1,0:T(8,128)S(1)}, f32[512,512]{1,0:T(8,128)}, u32[]{:S(2)}) copy-start(f32[512,512]{1,0:T(8,128)} %get-tuple-element.377) | copy-start | bytes 3145732
  231.0 13.5 %copy-start.12 = (f32[1,512,1536]{2,1,0:T(8,128)S(1)}, f32[1,512,1536]{2,1,0:T(8,128)}, u32[]{:S(2)}) copy-start(f32[1,512,1536]{2,1,0:T(8,128)} %copy-done.11) | copy-start | bytes 9437188
  231.0 13.5 %copy-start.57 = (f32[1536]{0:T(1024)S(1)}, f32[1536]{0:T(1024)}, u32[]{:S(2)}) copy-start(f32[1536]{0:T(1024)} %param.36) | copy-start | bytes 18436
  231.0 13.5 %copy-start.63 = (f32[512]{0:T(512)S(1)}, f32[512]{0:T(512)}, u32[]{:S(2)}) copy-start(f32[512]{0:T(512)} %copy-done.62) | copy-start | bytes 6148
  247.7 22.3 %copy-start.3 = (f32[1,24,64,128]{3,2,1,0:T(8,128)S(1)}, f32[1,24,64,128]{3,2,1,0:T(8,128)}, u32[]{:S(2)}) copy-start(f32[1,24,64,128]{3,2,1,0:T(8,128)} %custom-call) | copy-start | bytes 2359300
  277.9 6.6 %copy-start.29 = (f32[512,24]{1,0:T(8,128)S(1)}, f32[512,24]{1,0:T(8,128)}, u32[]{:S(2)}) copy-start(f32[512,24]{1,0:T(8,128)} %copy.268) | copy-start | bytes 147460
  277.9 6.6 %copy-start.30 = (f32[24,512]{0,1:T(8,128)S(1)}, f32[24,512]{0,1:T(8,128)}, u32[]{:S(2)}) copy-start(f32[24,512]{0,1:T(8,128)} %copy.269) | copy-start | bytes 147460
  277.9 6.6 %copy-start.31 = (f32[24,512]{0,1:T(8,128)S(1)}, f32[24,512]{0,1:T(8,128)}, u32[]{:S(2)}) copy-start(f32[24,512]{0,1:T(8,128)} %copy.270) | copy-start | bytes 147460
  283.5 15.9 %copy-start.26 = (f32[1,512,128]{2,1,0:T(8,128)S(1)}, f32[1,512,128]{2,1,0:T(8,128)}, u32[]{:S(2)}) copy-start(f32[1,512,128]{2,1,0:T(8,128)} %convolution_bitcast_fusion.1) | copy-start | bytes 786436
  284.5 22.9 %copy-start.20 = (f32[512,24]{1,0:T(8,128)}, f32[512,24]{1,0:T(8,128)S(1)}, u32[]{:S(2)}) copy-start(f32[512,24]{1,0:T(8,128)S(1)} %copy.290) | copy-start | bytes 147460
  285.9 21.5 %copy-start.36 = (f32[512,24]{0,1:T(8,128)S(1)}, f32[512,24]{0,1:T(8,128)}, u32[]{:S(2)}) copy-start(f32[512,24]{0,1:T(8,128)} %copy.248) | copy-start | bytes 147460
  285.9 21.5 %copy-start.83 = (f32[24]{0:T(128)S(1)}, f32[24]{0:T(128)}, u32[]{:S(2)}) copy-start(f32[24]{0:T(128)} %param.35) | copy-start | bytes 292
  299.5 7.9 %copy-start.9 = (f32[1,512,1536]{1,2,0:T(8,128)S(1)}, f32[1,512,1536]{1,2,0:T(8,128)}, u32[]{:S(2)}) copy-start(f32[1,512,1536]{1,2,0:T(8,128)} %copy.261) | copy-start | bytes 9437188
  317.2 11.1 %copy-start.38 = (f32[1792]{0:T(1024)S(1)}, f32[1792]{0:T(1024)}, u32[]{:S(2)}) copy-start(f32[1792]{0:T(1024)} %copy-done.37) | copy-start | bytes 21508
  317.2 11.1 %copy-start.40 = (f32[1792]{0:T(1024)S(1)}, f32[1792]{0:T(1024)}, u32[]{:S(2)}) copy-start(f32[1792]{0:T(1024)} %copy-done.39) | copy-start | bytes 21508
  331.0 7.8 %copy-start.65 = (f32[24,4]{0,1:T(4,128)S(1)}, f32[24,4]{0,1:T(4,128)}, u32[]{:S(2)}) copy-start(f32[24,4]{0,1:T(4,128)} %slice_reduce_fusion) | copy-start | bytes 1156
  331.1 7.9 %copy-start.66 = (f32[24,4]{0,1:T(4,128)S(1)}, f32[24,4]{0,1:T(4,128)}, u32[]{:S(2)}) copy-start(f32[24,4]{0,1:T(4,128)} %slice_reduce_fusion.1) | copy-start | bytes 1156
  331.1 8.5 %copy-start.21 = (f32[512,24]{1,0:T(8,128)S(1)}, f32[512,24]{1,0:T(8,128)}, u32[]{:S(2)}) copy-start(f32[512,24]{1,0:T(8,128)} %copy-done.20) | copy-start | bytes 147460
  331.1 8.5 %copy-start.27 = (f32[1,24,4,128]{1,3,2,0:T(8,128)S(1)}, f32[1,24,4,128]{1,3,2,0:T(8,128)}, u32[]{:S(2)}) copy-start(f32[1,24,4,128]{1,3,2,0:T(8,128)} %copy.274) | copy-start | bytes 147460
  331.1 8.5 %copy-start.28 = (f32[1,24,4,128]{1,3,2,0:T(8,128)S(1)}, f32[1,24,4,128]{1,3,2,0:T(8,128)}, u32[]{:S(2)}) copy-start(f32[1,24,4,128]{1,3,2,0:T(8,128)} %copy.272) | copy-start | bytes 147460
  336.7 6.9 %collective-permute-start.2 = (bf16[1,3,1792]{2,1,0:T(4,128)(2,1)}, bf16[1,3,1792]{2,1,0:T(4,128)(2,1)S(1)}, u32[]{:S(2)}, u32[]{:S(2)}) collective-permute-start(bf16[1,3,1792]{2,1,0:T(4,128)(2,1)} %slice.372), channel_id=1, source_target_pairs={{1,0},{2,1},{3,2},{5,4},{6,5},{7,6},{9,8},{10,9},{11,10},{13,12},{... | collective-permute-start | bytes 32264 | tf_op jit(solution)/shard_map/ppermute | solution.py:17
  339.6 6.6 %copy-start.18 = (bf16[1,512,768]{2,1,0:T(8,128)(2,1)S(1)}, bf16[1,512,768]{2,1,0:T(8,128)(2,1)}, u32[]{:S(2)}) copy-start(bf16[1,512,768]{2,1,0:T(8,128)(2,1)} %param.22) | copy-start | bytes 2359300
  339.6 6.6 %copy-start.22 = (bf16[512,1536]{1,0:T(8,128)(2,1)S(1)}, bf16[512,1536]{1,0:T(8,128)(2,1)}, u32[]{:S(2)}) copy-start(bf16[512,1536]{1,0:T(8,128)(2,1)} %get-tuple-element.432) | copy-start | bytes 4718596
  343.7 7.9 %slice-start = ((s8[5148672]{0:T(1024)(128)(4,1)}), s8[4194304]{0:T(1024)(128)(4,1)S(1)}, s32[]{:S(2)}) async-start(s8[5148672]{0:T(1024)(128)(4,1)} %bitcast.420), calls=%async_computation.2 | async-start | bytes 8388608
  346.2 5.3 copy-start.23
  351.6 7.9 %copy-start.15 = (bf16[768,1536]{0,1:T(8,128)(2,1)S(1)}, bf16[768,1536]{0,1:T(8,128)(2,1)}, u32[]{:S(2)}) copy-start(bf16[768,1536]{0,1:T(8,128)(2,1)} %copy.275) | copy-start | bytes 7077892
  580.4 16.2 %copy-start.1 = (bf16[1536,768]{1,0:T(8,128)(2,1)S(1)}, bf16[1536,768]{1,0:T(8,128)(2,1)}, u32[]{:S(2)}) copy-start(bf16[1536,768]{1,0:T(8,128)(2,1)} %param.37) | copy-start | bytes 7077892
  (45 other events, 153.4 us)
Sparse Core Ops, SparseCore 0:
  61.9 36.3 all-gather.4
  179.0 68.3 all-gather.6

commit v2 on v1

--- a/solution.py
+++ b/solution.py
@@ -6,66 +6,6 @@
 from jax.experimental import pallas as pl
 from jax.experimental.pallas import tpu as pltpu
 from jax.sharding import PartitionSpec as P
-
-epsilon = 1e-05
-highest = lax.Precision.HIGHEST
-
-
-def shifted(block, axis, distance):
-    devices = range(lax.axis_size(axis))
-    route = [(i - distance, i) for i in devices if i - distance in devices]
-    return lax.ppermute(block, axis, route)
-
-
-def entering(value, axis, join, neutral):
-    place = lax.axis_index(axis)
-    gathered = jax.tree.map(
-        lambda a, kind: lax.all_gather(a.astype(kind), axis), value, (jnp.bfloat16, jnp.bfloat16)
-    )
-    state = jax.tree.map(lambda a, e: jnp.zeros_like(a) + jnp.asarray(e, a.dtype), value, neutral)
-
-    def one(step, state):
-        return join(
-            state,
-            jax.tree.map(
-                lambda a, own: lax.dynamic_index_in_dim(a, step, 0, False).astype(own.dtype),
-                gathered,
-                value,
-            ),
-        )
-
-    return lax.fori_loop(0, place, one, state)
-
-
-def carried_in(value, axis, combine, identity):
-    length, mine = (lax.axis_size(axis), lax.axis_index(axis))
-    everything = jax.tree.map(lambda part: lax.all_gather(part, axis), value)
-    start = jax.tree.map(
-        lambda part, zero: jnp.broadcast_to(jnp.asarray(zero, part.dtype), part.shape),
-        value,
-        identity,
-    )
-
-    def step(k, before):
-        at = length - 1 - k
-        reached = at > mine
-        new = combine(before, jax.tree.map(lambda part: part[at], everything))
-        return jax.tree.map(lambda a, b: jnp.where(reached, a, b), new, before)
-
-    return lax.fori_loop(0, length, step, start)
-
-
-def pre_norm(values, gain_values):
-    return (
-        values
-        * lax.rsqrt(jnp.mean(values * values, axis=-1, keepdims=True) + epsilon)
-        * gain_values
-    )
-
-
-def compose(earlier, later):
-    return (earlier[0] * later[0], later[0][:, :, None, None] * earlier[1] + later[1])
-
 
 LANES = 128
 
@@ -295,6 +235,889 @@
     return gathered.reshape(flows, places, pieces + 1, rows, LANES), small_out
 
 
+CHUNK = 128
+HALO = 16
+GATE_BLOCK = 256
+EPS = 1e-05
+NEGATIVE = -1e30
+F32, BF16 = jnp.float32, jnp.bfloat16
+
+
+def mm(a, b):
+    return jnp.dot(a, b, preferred_element_type=F32)
+
+
+def mm_nt(a, b):
+    return lax.dot_general(a, b, (((1,), (1,)), ((), ())), preferred_element_type=F32)
+
+
+def mm_tn(a, b):
+    return lax.dot_general(a, b, (((0,), (0,)), ((), ())), preferred_element_type=F32)
+
+
+def split(a):
+    high = a.astype(BF16)
+    return high, (a - high.astype(F32)).astype(BF16)
+
+
+def exact_mm(a, b):
+    return jnp.dot(a, b, preferred_element_type=F32, precision=lax.Precision.HIGHEST)
+
+
+def spread(a, heads_ref):
+    high, low = split(a)
+    return mm(high, heads_ref[...]) + mm(low, heads_ref[...])
+
+
+def gather_heads(a, heads_ref):
+    high, low = split(a)
+    return mm_nt(high, heads_ref[...]) + mm_nt(low, heads_ref[...])
+
+
+def sigmoid(v):
+    return 1.0 / (1.0 + jnp.exp(-v))
+
+
+def softplus(v):
+    return jnp.maximum(v, 0.0) + jnp.log1p(jnp.exp(-jnp.abs(v)))
+
+
+def triangle(size, upper):
+    row = lax.broadcasted_iota(jnp.int32, (size, size), 0)
+    column = lax.broadcasted_iota(jnp.int32, (size, size), 1)
+    return ((row <= column) if upper else (row >= column)).astype(F32)
+
+
+def front_kernel(
+    sizes,
+    tokens_ref,
+    halo_ref,
+    gain_ref,
+    weight_ref,
+    taps_ref,
+    bias_ref,
+    masks_ref,
+    dt_bias_ref,
+    a_log_ref,
+    heads_ref,
+    normed_ref,
+    gate_ref,
+    conv_ref,
+    halo_out_ref,
+    summed_ref,
+    raw_ref,
+    cum_ref,
+    state_ref,
+    keep_ref,
+    padded,
+    product,
+    active,
+):
+    seqs, piece, inner, channels, heads = sizes
+    gate_blocks, conv_blocks = inner // GATE_BLOCK, channels // GATE_BLOCK
+    step = pl.program_id(0)
+    stride = piece + HALO
+
+    @pl.when(step == 0)
+    def _():
+        gain = gain_ref[...]
+        for n in range(seqs):
+            for source, start, to, count in (
+                (halo_ref, n * HALO, n * stride, HALO),
+                (tokens_ref, n * piece, n * stride + HALO, piece),
+            ):
+
+                def body(i, carry):
+                    values = source[pl.ds(pl.multiple_of(start + i * 16, 16), 16)].astype(F32)
+                    scale = lax.rsqrt(jnp.mean(values * values, axis=-1, keepdims=True) + EPS)
+                    low = (values * scale * gain).astype(BF16)
+                    padded[pl.ds(pl.multiple_of(to + i * 16, 16), 16)] = low
+                    return carry
+
+                lax.fori_loop(0, count // 16, body, 0)
+            normed_ref[pl.ds(n * piece, piece)] = padded[pl.ds(n * stride + HALO, piece)]
+
+    product[...] = mm(padded[...], weight_ref[...])
+
+    @pl.when(step < gate_blocks)
+    def _():
+        for n in range(seqs):
+            gate_ref[pl.ds(n * piece, piece)] = product[pl.ds(n * stride + HALO, piece)]
+
+    @pl.when((step >= gate_blocks) & (step < gate_blocks + conv_blocks))
+    def _():
+        at = pl.multiple_of((step - gate_blocks) * GATE_BLOCK, GATE_BLOCK)
+        for n in range(seqs):
+            conv_ref[pl.ds(n * piece, piece)] = product[pl.ds(n * stride + HALO, piece)]
+            halo_out_ref[pl.ds(n * HALO, HALO)] = product[pl.ds(n * stride, HALO)]
+            for i in range(piece // 64):
+                rows = pl.ds(n * piece + i * 64, 64)
+                total = jnp.broadcast_to(bias_ref[...], (64, GATE_BLOCK))
+                for k in range(4):
+                    source = product[pl.ds(n * stride + HALO - 3 + k + i * 64, 64)]
+                    total = total + source * masks_ref[rows, k : k + 1] * taps_ref[k : k + 1]
+                summed_ref[rows] = total
+                active[rows, pl.ds(at, GATE_BLOCK)] = (total * sigmoid(total)).astype(BF16)
+
+    @pl.when(step == gate_blocks + conv_blocks)
+    def _():
+        lane = lax.broadcasted_iota(jnp.int32, (piece, 128), 1)
+        lower = triangle(CHUNK, False)
+        for n in range(seqs):
+            rows = pl.ds(n * piece, piece)
+            raw = jnp.where(lane < heads, product[pl.ds(n * stride + HALO, piece), :128], 0.0)
+            raw = raw + dt_bias_ref[...]
+            raw_ref[rows] = raw
+            steps = jnp.where(lane < heads, softplus(raw), 0.0)
+            decay = -jnp.exp(a_log_ref[...]) * steps
+            total = jnp.zeros((1, 128), F32)
+            pieces = []
+            for c in range(piece // CHUNK):
+                cumulative = exact_mm(lower, decay[c * CHUNK : (c + 1) * CHUNK])
+                cum_ref[pl.ds(n * piece + c * CHUNK, CHUNK)] = cumulative
+                pieces.append(cumulative + total)
+                total = total + cumulative[CHUNK - 1 :]
+            whole = jnp.concatenate(pieces, axis=0) if len(pieces) > 1 else pieces[0]
+            tails = jnp.exp(total - whole) * steps * masks_ref[rows, 7:8]
+            weighted = (spread(tails, heads_ref) * active[rows, :inner].astype(F32)).astype(BF16)
+            state_ref[n] = mm_tn(active[rows, inner : inner + 128], weighted)
+            last = masks_ref[n * piece + piece - 1 : n * piece + piece, 6:7]
+            keep = jnp.exp(total) * last
+            keep_ref[n] = spread(jnp.broadcast_to(keep, (8, 128)), heads_ref)
+
+
+def front(tokens, halo, gain, weight, taps, bias, masks, dt_bias, a_log, heads_map, sizes):
+    seqs, piece, inner, channels, heads = sizes
+    total, model = tokens.shape
+    stride = seqs * (piece + HALO)
+    gate_blocks, conv_blocks = inner // GATE_BLOCK, channels // GATE_BLOCK
+    full = lambda *shape: pl.BlockSpec(shape, lambda j: (0,) * len(shape))
+
+    def conv_at(j):
+        return (0, jnp.clip(j - gate_blocks, 0, conv_blocks - 1))
+
+    return pl.pallas_call(
+        functools.partial(front_kernel, sizes),
+        grid=(gate_blocks + conv_blocks + 1,),
+        in_specs=[
+            full(total, model),
+            full(seqs * HALO, model),
+            full(1, model),
+            pl.BlockSpec((model, GATE_BLOCK), lambda j: (0, j)),
+            pl.BlockSpec((4, GATE_BLOCK), conv_at),
+            pl.BlockSpec((1, GATE_BLOCK), conv_at),
+            full(total, 16),
+            full(1, 128),
+            full(1, 128),
+            full(128, inner),
+        ],
+        out_specs=(
+            full(total, model),
+            pl.BlockSpec((total, GATE_BLOCK), lambda j: (0, jnp.minimum(j, gate_blocks - 1))),
+            pl.BlockSpec((total, GATE_BLOCK), conv_at),
+            pl.BlockSpec((seqs * HALO, GATE_BLOCK), conv_at),
+            pl.BlockSpec((total, GATE_BLOCK), conv_at),
+            full(total, 128),
+            full(total, 128),
+            full(seqs, 128, inner),
+            full(seqs, 8, inner),
+        ),
+        out_shape=(
+            jax.ShapeDtypeStruct((total, model), BF16),
+            jax.ShapeDtypeStruct((total, inner), F32),
+            jax.ShapeDtypeStruct((total, channels), F32),
+            jax.ShapeDtypeStruct((seqs * HALO, channels), F32),
+            jax.ShapeDtypeStruct((total, channels), F32),
+            jax.ShapeDtypeStruct((total, 128), F32),
+            jax.ShapeDtypeStruct((total, 128), F32),
+            jax.ShapeDtypeStruct((seqs, 128, inner), F32),
+            jax.ShapeDtypeStruct((seqs, 8, inner), F32),
+        ),
+        scratch_shapes=[
+            pltpu.VMEM((stride, model), BF16),
+            pltpu.VMEM((stride, GATE_BLOCK), F32),
+            pltpu.VMEM((total, channels), BF16),
+        ],
+        compiler_params=pltpu.CompilerParams(vmem_limit_bytes=48 * 1024 * 1024),
+        name="front",
+    )(tokens, halo, gain, weight, taps, bias, masks, dt_bias, a_log, heads_map)
+
+
+def chain_kernel(ways, blocks, own_ref, keep_ref, out_ref, sent, taken, send, recv):
+    size = lax.axis_size("seq")
+    turn = lax.axis_index("seq")
+    first = turn == (0 if ways > 0 else size - 1)
+    final = turn == (size - 1 if ways > 0 else 0)
+    ahead = {"seq": lax.rem(turn + ways + size, size)}
+    behind = {"seq": lax.rem(turn - ways + size, size)}
+    barrier = pltpu.get_barrier_semaphore()
+
+    @pl.when(jnp.logical_not(first))
+    def _():
+        pl.semaphore_signal(
+            barrier, inc=1, device_id=behind, device_id_type=pl.DeviceIdType.MESH
+        )
+
+    @pl.when(jnp.logical_not(final))
+    def _():
+        pl.semaphore_wait(barrier, 1)
+
+    width = own_ref.shape[2] // blocks
+
+    def copy(c):
+        return pltpu.make_async_remote_copy(
+            src_ref=sent.at[c],
+            dst_ref=taken.at[c],
+            send_sem=send.at[c],
+            recv_sem=recv.at[c],
+            device_id=ahead,
+            device_id_type=pl.DeviceIdType.MESH,
+        )
+
+    @pl.when(first)
+    def _():
+        out_ref[...] = jnp.zeros_like(out_ref)
+        for c in range(blocks):
+            at = slice(c * width, (c + 1) * width)
+            sent[c] = own_ref[:, :, at].astype(BF16)
+            copy(c).start()
+
+    @pl.when(jnp.logical_not(first))
+    def _():
+        for c in range(blocks):
+            at = slice(c * width, (c + 1) * width)
+            copy(c).wait_recv()
+
+            @pl.when(jnp.logical_not(final))
+            def _():
+                sent[c] = (
+                    own_ref[:, :, at] + keep_ref[:, 0:1, at] * taken[c].astype(F32)
+                ).astype(BF16)
+                copy(c).start()
+
+            out_ref[:, :, at] = taken[c].astype(F32)
+
+    @pl.when(jnp.logical_not(final))
+    def _():
+        for c in range(blocks):
+            copy(c).wait_send()
+
+
+def chain(own, keep, ways, blocks=6):
+    seqs, depth, inner = own.shape
+    vmem = pl.BlockSpec(memory_space=pltpu.VMEM)
+    part = (blocks, seqs, depth, inner // blocks)
+    return pl.pallas_call(
+        functools.partial(chain_kernel, ways, blocks),
+        out_shape=jax.ShapeDtypeStruct(own.shape, F32),
+        in_specs=[vmem, vmem],
+        out_specs=vmem,
+        scratch_shapes=[pltpu.VMEM(part, BF16)] * 2 + [pltpu.SemaphoreType.DMA((blocks,))] * 2,
+        compiler_params=pltpu.CompilerParams(
+            collective_id=1 if ways > 0 else 2,
+            has_side_effects=True,
+            vmem_limit_bytes=32 * 1024 * 1024,
+        ),
+        name="chain",
+    )(own, keep)
+
+
+def decays_of(cum, cum_t, bias, h):
+    return jnp.exp(cum[:, h : h + 1] - cum_t[h : h + 1, :] + bias)
+
+
+def mask_bias(seg_col, seg_row):
+    row = lax.broadcasted_iota(jnp.int32, (CHUNK, CHUNK), 0)
+    column = lax.broadcasted_iota(jnp.int32, (CHUNK, CHUNK), 1)
+    return jnp.where((row >= column) & (seg_col == seg_row), 0.0, NEGATIVE)
+
+
+def scores_of(reader, writer):
+    rh, rl = split(reader)
+    wh, wl = split(writer)
+    return mm_nt(rh, wh) + (mm_nt(rh, wl) + mm_nt(rl, wh))
+
+
+def forward_kernel(
+    sizes,
+    chunks,
+    summed_ref,
+    gate_ref,
+    raw_ref,
+    cum_ref,
+    masks_ref,
+    seg_row_ref,
+    incoming_ref,
+    tokens_ref,
+    cot_ref,
+    weight_ref,
+    gain_ref,
+    skip_ref,
+    heads_ref,
+    output_ref,
+    low_ref,
+    out_low_ref,
+    gate_grad_ref,
+    ssm_grad_ref,
+    starts_ref,
+    dot_ref,
+    sums_ref,
+    wide_ref,
+    state_grad_ref,
+    state,
+    prefix,
+    active,
+    mixed_in,
+    factors,
+    grads,
+    inv,
+):
+    seqs, piece, inner, channels, heads = sizes
+    c = pl.program_id(1)
+
+    @pl.when((c == 0) & (pl.program_id(0) == 0))
+    def _():
+        sums_ref[...] = jnp.zeros_like(sums_ref)
+        wide_ref[...] = jnp.zeros_like(wide_ref)
+
+    @pl.when(c == 0)
+    def _():
+        state[...] = incoming_ref[0]
+        prefix[...] = jnp.zeros_like(prefix)
+        state_grad_ref[...] = jnp.zeros_like(state_grad_ref)
+
+    def activate(i, carry):
+        rows = pl.ds(pl.multiple_of(i * 16, 16), 16)
+        values = summed_ref[rows]
+        active[rows] = values * sigmoid(values)
+        return carry
+
+    lax.fori_loop(0, CHUNK // 16, activate, 0)
+    lane = lax.broadcasted_iota(jnp.int32, (CHUNK, 128), 1)
+    steps = jnp.where(lane < heads, softplus(raw_ref[...]), 0.0)
+    cum = cum_ref[...]
+    cum_t = jnp.transpose(cum)
+    final = cum[CHUNK - 1 :]
+    enter = jnp.exp(cum) * masks_ref[:, 4:5]
+    tails = jnp.exp(final - cum) * steps * masks_ref[:, 5:6]
+    from_start = jnp.exp(cum + prefix[0:1]) * masks_ref[:, 6:7]
+    prefix[...] = prefix[...] + final
+    for i, block in enumerate((steps, enter, tails, from_start)):
+        factors[i] = spread(block, heads_ref)
+    writer = active[:, inner : inner + 128]
+    reader = active[:, inner + 128 : inner + 256]
+    scores = scores_of(reader, writer)
+    bias = mask_bias(masks_ref[:, 8:9], seg_row_ref[0:1])
+    half = lax.broadcasted_iota(jnp.int32, (CHUNK, 128), 1) < 64
+    state_low = state[...].astype(BF16)
+    starts_ref[0] = state_low
+    reader_low = reader.astype(BF16)
+    for pair in range(heads // 2):
+        at = slice(pair * 128, (pair + 1) * 128)
+        moved = (active[:, at] * factors[0, :, at]).astype(BF16)
+        zero = jnp.zeros_like(moved)
+        one = (scores * decays_of(cum, cum_t, bias, 2 * pair)).astype(BF16)
+        two = (scores * decays_of(cum, cum_t, bias, 2 * pair + 1)).astype(BF16)
+        both = jnp.concatenate([one, two], axis=1)
+        stacked = jnp.concatenate(
+            [jnp.where(half, moved, zero), jnp.where(half, zero, moved)], axis=0
+        )
+        carried = mm(reader_low, state_low[:, at]) * factors[1, :, at]
+        mixed_in[:, at] = mm(both, stacked) + carried
+    weighted = (active[:, :inner] * factors[2]).astype(BF16)
+    kept = jnp.exp(final) * masks_ref[CHUNK - 1 :, 4:5]
+    kept = spread(jnp.broadcast_to(kept, (8, 128)), heads_ref)[0:1]
+    state[...] = state[...] * kept + mm_tn(writer.astype(BF16), weighted)
+
+    gain = gain_ref[...]
+    skip = skip_ref[...]
+
+    def gating(i, carry):
+        rows = pl.ds(pl.multiple_of(i * 16, 16), 16)
+        gate = gate_ref[rows]
+        mixer = mixed_in[rows] + skip * active[rows, :inner]
+        gated = mixer * gate * sigmoid(gate)
+        scale = lax.rsqrt(jnp.mean(gated * gated, axis=-1, keepdims=True) + EPS)
+        inv[rows] = jnp.broadcast_to(scale, (16, 128))
+        low_ref[rows] = (gated * scale * gain).astype(BF16)
+        return carry
+
+    lax.fori_loop(0, CHUNK // 16, gating, 0)
+    mixed = mm(low_ref[...], weight_ref[...])
+    block_out = tokens_ref[...].astype(F32) + mixed
+    output_ref[...] = block_out.astype(BF16)
+    valid = masks_ref[:, 9:10]
+    sums_ref[0:1] += jnp.sum(valid * block_out * block_out, axis=0, keepdims=True)
+    sums_ref[1:2] += jnp.sum(valid * mixed * mixed, axis=0, keepdims=True)
+    out_low = (cot_ref[...].astype(F32) * valid).astype(BF16)
+    out_low_ref[...] = out_low
+    grads[...] = mm_nt(out_low, weight_ref[...])
+
+    def backing(i, carry):
+        gain_sum, skip_sum = carry
+        rows = pl.ds(pl.multiple_of(i * 16, 16), 16)
+        gate = gate_ref[rows]
+        turned = sigmoid(gate)
+        silu = gate * turned
+        signal = active[rows, :inner]
+        mixer = mixed_in[rows] + skip * signal
+        gated = mixer * silu
+        scale = inv[rows, 0:1]
+        grad = grads[rows]
+        gain_sum = gain_sum + grad * gated * scale
+        grad = grad * gain
+        inside = jnp.mean(grad * gated, axis=-1, keepdims=True)
+        gated_grad = scale * grad - gated * (scale * scale * scale * inside)
+        ssm_grad = gated_grad * silu
+        ssm_grad_ref[rows] = ssm_grad
+        grads[rows] = ssm_grad
+        skip_sum = skip_sum + ssm_grad * signal
+        gate_grad_ref[rows] = (gated_grad * mixer * turned * (1.0 + gate * (1.0 - turned))).astype(
+            BF16
+        )
+        return gain_sum, skip_sum
+
+    start = jnp.zeros((16, inner), F32)
+    gain_sum, skip_sum = lax.fori_loop(0, CHUNK // 16, backing, (start, start))
+    wide_ref[0:1] += jnp.sum(gain_sum, axis=0, keepdims=True)
+    wide_ref[1:2] += jnp.sum(skip_sum, axis=0, keepdims=True)
+    reader_t = jnp.transpose(reader_low)
+    for pair in range(heads // 2):
+        at = slice(pair * 128, (pair + 1) * 128)
+        state_grad_ref[0, :, at] += mm(
+            reader_t, (grads[:, at] * factors[3, :, at]).astype(BF16)
+        )
+        mixed_in[:, at] = mixed_in[:, at] * grads[:, at].astype(BF16).astype(F32)
+    dot_ref[...] = gather_heads(mixed_in[...], heads_ref)
+
+
+def forward(
+    summed, gate, raw, cum, masks, seg_row, incoming, tokens, cot, weight, gain, skip, heads_map, sizes
+):
+    seqs, piece, inner, channels, heads = sizes
+    total, model = tokens.shape
+    chunks = piece // CHUNK
+    full = lambda *shape: pl.BlockSpec(shape, lambda n, c: (0,) * len(shape))
+    rows = lambda width: pl.BlockSpec((CHUNK, width), lambda n, c: (n * chunks + c, 0))
+    each = lambda depth: pl.BlockSpec((1, depth, inner), lambda n, c: (n, 0, 0))
+    shape = jax.ShapeDtypeStruct
+    return pl.pallas_call(
+        functools.partial(forward_kernel, sizes, chunks),
+        grid=(seqs, chunks),
+        in_specs=[
+            rows(channels),
+            rows(inner),
+            rows(128),
+            rows(128),
+            rows(16),
+            pl.BlockSpec((1, CHUNK), lambda n, c: (0, n * chunks + c)),
+            each(128),
+            rows(model),
+            rows(model),
+            full(inner, model),
+            full(1, inner),
+            full(1, inner),
+            full(128, inner),
+        ],
+        out_specs=(
+            rows(model),
+            rows(inner),
+            rows(model),
+            rows(inner),
+            rows(inner),
+            pl.BlockSpec((1, 128, inner), lambda n, c: (n * chunks + c, 0, 0)),
+            rows(128),
+            full(8, model),
+            full(8, inner),
+            each(128),
+        ),
+        out_shape=(
+            shape((total, model), BF16),
+            shape((total, inner), BF16),
+            shape((total, model), BF16),
+            shape((total, inner), BF16),
+            shape((total, inner), F32),
+            shape((seqs * chunks, 128, inner), BF16),
+            shape((total, 128), F32),
+            shape((8, model), F32),
+            shape((8, inner), F32),
+            shape((seqs, 128, inner), F32),
+        ),
+        scratch_shapes=[
+            pltpu.VMEM((128, inner), F32),
+            pltpu.VMEM((8, 128), F32),
+            pltpu.VMEM((CHUNK, channels), F32),
+            pltpu.VMEM((CHUNK, inner), F32),
+            pltpu.VMEM((4, CHUNK, inner), F32),
+            pltpu.VMEM((CHUNK, inner), F32),
+            pltpu.VMEM((CHUNK, 128), F32),
+        ],
+        compiler_params=pltpu.CompilerParams(vmem_limit_bytes=48 * 1024 * 1024),
+        name="forward",
+    )(summed, gate, raw, cum, masks, seg_row, incoming, tokens, cot, weight, gain, skip, heads_map)
+
+
+def backward_kernel(
+    sizes,
+    chunks,
+    summed_ref,
+    conv_ref,
+    halo_ref,
+    raw_ref,
+    cum_ref,
+    masks_ref,
+    seg_row_ref,
+    later_ref,
+    ssm_grad_ref,
+    starts_ref,
+    dot_ref,
+    taps_ref,
+    a_log_ref,
+    skip_ref,
+    heads_ref,
+    proj_grad_ref,
+    tail_ref,
+    rim_ref,
+    conv_sums_ref,
+    head_sums_ref,
+    state_grad,
+    after,
+    active,
+    factors,
+    moved_grad,
+    shifted_rows,
+    all_grad,
+):
+    seqs, piece, inner, channels, heads = sizes
+    c = pl.program_id(1)
+
+    @pl.when((c == 0) & (pl.program_id(0) == 0))
+    def _():
+        conv_sums_ref[...] = jnp.zeros_like(conv_sums_ref)
+        head_sums_ref[...] = jnp.zeros_like(head_sums_ref)
+
+    @pl.when(c == 0)
+    def _():
+        state_grad[...] = later_ref[0]
+        after[...] = jnp.zeros_like(after)
+
+    def activate(i, carry):
+        rows = pl.ds(pl.multiple_of(i * 16, 16), 16)
+        values = summed_ref[rows]
+        active[rows] = values * sigmoid(values)
+        return carry
+
+    lax.fori_loop(0, CHUNK // 16, activate, 0)
+    lane = lax.broadcasted_iota(jnp.int32, (CHUNK, 128), 1)
+    raw = raw_ref[...]
+    steps = jnp.where(lane < heads, softplus(raw), 0.0)
+    cum = cum_ref[...]
+    cum_t = jnp.transpose(cum)
+    final = cum[CHUNK - 1 :]
+    enter = jnp.exp(cum) * masks_ref[:, 4:5]
+    tails = jnp.exp(final - cum) * masks_ref[:, 5:6]
+    for i, block in enumerate((steps, enter, tails)):
+        factors[i] = spread(block, heads_ref)
+    writer = active[:, inner : inner + 128]
+    reader = active[:, inner + 128 : inner + 256]
+    scores = scores_of(reader, writer)
+    bias = mask_bias(masks_ref[:, 8:9], seg_row_ref[0:1])
+    half = lax.broadcasted_iota(jnp.int32, (CHUNK, 128), 1) < 64
+    writer_low, reader_low = writer.astype(BF16), reader.astype(BF16)
+    reader_t = jnp.transpose(reader_low)
+    later = state_grad[...].astype(BF16)
+    kept = jnp.exp(final) * masks_ref[CHUNK - 1 :, 4:5]
+    kept = spread(jnp.broadcast_to(kept, (8, 128)), heads_ref)[0:1]
+    scores_grad = jnp.zeros((CHUNK, CHUNK), F32)
+    reader_grad = jnp.zeros((CHUNK, 128), F32)
+    writer_grad = jnp.zeros((CHUNK, 128), F32)
+    skip = skip_ref[...]
+    for pair in range(heads // 2):
+        at = slice(pair * 128, (pair + 1) * 128)
+        signal = active[:, at]
+        step_x = factors[0, :, at]
+        moved = (signal * step_x).astype(BF16)
+        grad = ssm_grad_ref[:, at]
+        grad_low = grad.astype(BF16)
+        zero = jnp.zeros_like(grad_low)
+        stacked = jnp.concatenate(
+            [jnp.where(half, grad_low, zero), jnp.where(half, zero, grad_low)], axis=0
+        )
+        both_grad = mm_nt(stacked, moved)
+        one = decays_of(cum, cum_t, bias, 2 * pair)
+        two = decays_of(cum, cum_t, bias, 2 * pair + 1)
+        scores_grad = scores_grad + both_grad[:CHUNK] * one + both_grad[CHUNK:] * two
+        both = jnp.concatenate([(scores * one).astype(BF16), (scores * two).astype(BF16)], axis=0)
+        tail_x = factors[2, :, at]
+        from_later = mm(writer_low, later[:, at])
+        total = mm_tn(both, stacked) + from_later * tail_x
+        weighted = (signal * step_x * tail_x).astype(BF16)
+        entered = (grad * factors[1, :, at]).astype(BF16)
+        start = starts_ref[0, :, at]
+        reader_grad = reader_grad + mm_nt(entered, start)
+        writer_grad = writer_grad + mm_nt(weighted, later[:, at])
+        passed = jnp.sum(start.astype(F32) * later[:, at].astype(F32), axis=0, keepdims=True)
+        factors[1, 0:1, at] = kept[:, at] * passed + jnp.sum(
+            moved.astype(F32) * (from_later * tail_x), axis=0, keepdims=True
+        )
+        state_grad[:, at] = state_grad[:, at] * kept[:, at] + mm(reader_t, entered)
+        moved_grad[:, at] = total * signal
+        factors[2, :, at] = total * moved.astype(F32)
+        all_grad[:, at] = total * step_x + skip[:, at] * grad
+    sh, sl = split(scores_grad)
+    reader_grad = reader_grad + mm(sh, writer_low) + mm(sl, writer_low)
+    writer_grad = writer_grad + mm_tn(sh, reader_low) + mm_tn(sl, reader_low)
+    all_grad[:, inner : inner + 128] = writer_grad
+    all_grad[:, inner + 128 : inner + 256] = reader_grad
+    step_grad = gather_heads(moved_grad[...], heads_ref)
+    change = dot_ref[...] - gather_heads(factors[2], heads_ref)
+    at_end = gather_heads(
+        jnp.broadcast_to(factors[1, 0:1], (8, inner)), heads_ref
+    )[0:1]
+    row = lax.broadcasted_iota(jnp.int32, (CHUNK, 128), 0)
+    change = change + jnp.where(row == CHUNK - 1, at_end, 0.0)
+    decay_grad = exact_mm(triangle(CHUNK, True), change)
+    rate = -jnp.exp(a_log_ref[...])
+    raw_grad = jnp.where(lane < heads, (step_grad + decay_grad * rate) * sigmoid(raw), 0.0)
+    head_sums_ref[0:1] += jnp.sum(raw_grad, axis=0, keepdims=True)
+    head_sums_ref[1:2] += jnp.sum(decay_grad * steps * rate, axis=0, keepdims=True)
+    proj_grad_ref[:, channels : channels + 128] = raw_grad.astype(BF16)
+    proj_grad_ref[:, channels + 128 :] = jnp.zeros((CHUNK, 128), BF16)
+
+    for block in range(channels // GATE_BLOCK):
+        at = slice(block * GATE_BLOCK, (block + 1) * GATE_BLOCK)
+        values = summed_ref[:, at]
+        turned = sigmoid(values)
+        grad = all_grad[:, at] * turned * (1.0 + values * (1.0 - turned))
+        conv_sums_ref[4:5, at] += jnp.sum(grad, axis=0, keepdims=True)
+        conv = conv_ref[:, at]
+        result = grad * taps_ref[3:4, at]
+        conv_sums_ref[3:4, at] += jnp.sum(grad * conv, axis=0, keepdims=True)
+        rim = jnp.zeros((8, GATE_BLOCK), F32)
+        shifted_rows[0:8] = jnp.zeros((8, GATE_BLOCK), F32)
+        for k in range(3):
+            shifted_rows[8 : 8 + CHUNK] = grad * masks_ref[:, k : k + 1]
+            shifted_rows[8 + CHUNK :] = after[k, :, at]
+            after[k, :, at] = shifted_rows[8:16]
+            here = shifted_rows[11 - k : 11 - k + CHUNK]
+            result = result + here * taps_ref[k : k + 1, at]
+            conv_sums_ref[k : k + 1, at] += jnp.sum(here * conv, axis=0, keepdims=True)
+            early = shifted_rows[3 - k : 11 - k]
+            rim = rim + early * taps_ref[k : k + 1, at]
+
+            @pl.when(c == chunks - 1)
+            def _():
+                conv_sums_ref[k : k + 1, at] += jnp.sum(
+                    early * halo_ref[HALO - 8 :, at], axis=0, keepdims=True
+                )
+
+        proj_grad_ref[:, at] = result.astype(BF16)
+
+        @pl.when(c == 0)
+        def _():
+            tail_ref[0, :, at] = result[CHUNK - 8 :]
+
+        @pl.when(c == chunks - 1)
+        def _():
+            rim_ref[0, :, at] = rim.astype(BF16)
+
+
+def backward(
+    summed,
+    conv,
+    halo,
+    raw,
+    cum,
+    masks,
+    seg_row,
+    later,
+    ssm_grad,
+    starts,
+    dots,
+    taps,
+    a_log,
+    skip,
+    heads_map,
+    sizes,
+):
+    seqs, piece, inner, channels, heads = sizes
+    total = summed.shape[0]
+    chunks = piece // CHUNK
+    full = lambda *shape: pl.BlockSpec(shape, lambda n, c: (0,) * len(shape))
+    spot = lambda n, c: n * chunks + chunks - 1 - c
+    rows = lambda width: pl.BlockSpec((CHUNK, width), lambda n, c: (spot(n, c), 0))
+    each = lambda depth, width: pl.BlockSpec((1, depth, width), lambda n, c: (n, 0, 0))
+    shape = jax.ShapeDtypeStruct
+    return pl.pallas_call(
+        functools.partial(backward_kernel, sizes, chunks),
+        grid=(seqs, chunks),
+        in_specs=[
+            rows(channels),
+            rows(channels),
+            pl.BlockSpec((HALO, channels), lambda n, c: (n, 0)),
+            rows(128),
+            rows(128),
+            rows(16),
+            pl.BlockSpec((1, CHUNK), lambda n, c: (0, spot(n, c))),
+            each(128, inner),
+            rows(inner),
+            pl.BlockSpec((1, 128, inner), lambda n, c: (spot(n, c), 0, 0)),
+            rows(128),
+            full(4, channels),
+            full(1, 128),
+            full(1, inner),
+            full(128, inner),
+        ],
+        out_specs=(
+            rows(channels + 256),
+            each(8, channels),
+            each(8, channels),
+            full(8, channels),
+            full(8, 128),
+        ),
+        out_shape=(
+            shape((total, channels + 256), BF16),
+            shape((seqs, 8, channels), F32),
+            shape((seqs, 8, channels), BF16),
+            shape((8, channels), F32),
+            shape((8, 128), F32),
+        ),
+        scratch_shapes=[
+            pltpu.VMEM((128, inner), F32),
+            pltpu.VMEM((3, 8, channels), F32),
+            pltpu.VMEM((CHUNK, channels), F32),
+            pltpu.VMEM((3, CHUNK, inner), F32),
+            pltpu.VMEM((CHUNK, inner), F32),
+            pltpu.VMEM((CHUNK + 16, GATE_BLOCK), F32),
+            pltpu.VMEM((CHUNK, channels), F32),
+        ],
+        compiler_params=pltpu.CompilerParams(vmem_limit_bytes=48 * 1024 * 1024),
+        name="backward",
+    )(
+        summed,
+        conv,
+        halo,
+        raw,
+        cum,
+        masks,
+        seg_row,
+        later,
+        ssm_grad,
+        starts,
+        dots,
+        taps,
+        a_log,
+        skip,
+        heads_map,
+    )
+
+
+def input_kernel(
+    tokens_ref, out_low_ref, gate_grad_ref, proj_grad_ref, weight_ref, gain_ref, grad_ref, sums_ref
+):
+    inner = gate_grad_ref.shape[1]
+    rest = weight_ref.shape[1] - inner
+
+    @pl.when(pl.program_id(0) == 0)
+    def _():
+        sums_ref[...] = jnp.zeros_like(sums_ref)
+
+    normed_grad = mm_nt(gate_grad_ref[...], weight_ref[:, :inner]) + mm_nt(
+        proj_grad_ref[:, :rest], weight_ref[:, inner:]
+    )
+    values = tokens_ref[...].astype(F32)
+    scale = lax.rsqrt(jnp.mean(values * values, axis=-1, keepdims=True) + EPS)
+    sums_ref[0:1] += jnp.sum(normed_grad * values * scale, axis=0, keepdims=True)
+    pushed = normed_grad * gain_ref[...]
+    inside = jnp.mean(pushed * values, axis=-1, keepdims=True)
+    grad_ref[...] = (
+        out_low_ref[...].astype(F32)
+        + scale * pushed
+        - values * (scale * scale * scale * inside)
+    ).astype(BF16)
+
+
+def input_gradient(tokens, out_low, gate_grad, proj_grad, weight, gain):
+    total, model = tokens.shape
+    block = 128
+    rows = lambda width: pl.BlockSpec((block, width), lambda i: (i, 0))
+    full = lambda *shape: pl.BlockSpec(shape, lambda i: (0,) * len(shape))
+    return pl.pallas_call(
+        input_kernel,
+        grid=(total // block,),
+        in_specs=[
+            rows(model),
+            rows(model),
+            rows(gate_grad.shape[1]),
+            rows(proj_grad.shape[1]),
+            full(*weight.shape),
+            full(1, model),
+        ],
+        out_specs=(rows(model), full(8, model)),
+        out_shape=(
+            jax.ShapeDtypeStruct((total, model), BF16),
+            jax.ShapeDtypeStruct((8, model), F32),
+        ),
+        compiler_params=pltpu.CompilerParams(vmem_limit_bytes=48 * 1024 * 1024),
+        name="input_gradient",
+    )(tokens, out_low, gate_grad, proj_grad, weight, gain)
+
+
+def weight_kernel(counts, out_low_ref, normed_ref, low_ref, gate_grad_ref, proj_grad_ref, grad_ref, turned):
+    low_count, gate_count = counts
+    step = pl.program_id(0)
+
+    @pl.when(step == 0)
+    def _():
+        turned[0] = jnp.transpose(out_low_ref[...])
+        turned[1] = jnp.transpose(normed_ref[...])
+
+    def put(result):
+        grad_ref[0] = result[:, :LANES].astype(BF16)
+        grad_ref[1] = result[:, LANES:].astype(BF16)
+
+    @pl.when(step < low_count)
+    def _():
+        put(mm(turned[0], low_ref[...]))
+
+    @pl.when((step >= low_count) & (step < low_count + gate_count))
+    def _():
+        put(mm(turned[1], gate_grad_ref[...]))
+
+    @pl.when(step >= low_count + gate_count)
+    def _():
+        put(mm(turned[1], proj_grad_ref[...]))
+
+
+def weight_gradient(out_low, normed, low, gate_grad, proj_grad):
+    total, model = normed.shape
+    wide = 2 * LANES
+    low_count, gate_count, proj_count = (a.shape[1] // wide for a in (low, gate_grad, proj_grad))
+    full = lambda *shape: pl.BlockSpec(shape, lambda j: (0,) * len(shape))
+
+    def columns(before, count):
+        return pl.BlockSpec((total, wide), lambda j: (0, jnp.clip(j - before, 0, count - 1)))
+
+    return pl.pallas_call(
+        functools.partial(weight_kernel, (low_count, gate_count)),
+        grid=(low_count + gate_count + proj_count,),
+        in_specs=[
+            full(total, model),
+            full(total, model),
+            columns(0, low_count),
+            columns(low_count, gate_count),
+            columns(low_count + gate_count, proj_count),
+        ],
+        out_specs=pl.BlockSpec((2, model, LANES), lambda j: (j, 0, 0)),
+        out_shape=jax.ShapeDtypeStruct(
+            (2 * (low_count + gate_count + proj_count), model, LANES), BF16
+        ),
+        scratch_shapes=[pltpu.VMEM((2, model, total), BF16)],
+        compiler_params=pltpu.CompilerParams(vmem_limit_bytes=48 * 1024 * 1024),
+        name="weight_gradient",
+    )(out_low, normed, low, gate_grad, proj_grad)
+
+
 def local(
     tokens,
     cotangent,
@@ -315,176 +1138,145 @@
     in_momentum,
     out_momentum,
 ):
-    seq_count, piece_size, model_width = tokens.shape
-    head_count = dt_bias.shape[0]
+    seqs, piece, model_width = tokens.shape
+    heads = dt_bias.shape[0]
     tap_count, channels = conv_weight.shape
     inner_width = gate_gain.shape[0]
-    state_width = (channels - inner_width) // 2
-    head_width = inner_width // head_count
     proj_width = in_weight.shape[1]
-    row_count = seq_count * piece_size
-    inputs = tokens.astype(jnp.float32)
-    normed_in, back_pre = jax.vjp(pre_norm, inputs, norm_gain)
-    normed_low = normed_in.astype(jnp.bfloat16).reshape(row_count, model_width)
-    projected = jnp.dot(normed_low, in_weight, preferred_element_type=jnp.float32).reshape(
-        seq_count, piece_size, proj_width
+    total = seqs * piece
+    sizes = (seqs, piece, inner_width, channels, heads)
+    places, pieces = lax.axis_size("dp"), lax.axis_size("seq")
+    turn = lax.axis_index("seq")
+    seg = segment_ids.astype(F32)
+    sent = jnp.concatenate(
+        [
+            tokens[:, piece - HALO :],
+            jnp.broadcast_to(seg[:, piece - HALO :, None], (seqs, HALO, LANES)).astype(BF16),
+        ],
+        axis=2,
     )
-    gate_in = projected[:, :, :inner_width]
-    conv_in = projected[:, :, inner_width : inner_width + channels]
-    dt_raw = projected[:, :, inner_width + channels :]
-    seg_float = segment_ids.astype(jnp.float32)
-    prev_rows, prev_seg = shifted(
-        (conv_in[:, piece_size - tap_count + 1 :], seg_float[:, piece_size - tap_count + 1 :]),
-        "seq",
-        1,
+    route = [(i, i + 1) for i in range(pieces - 1)]
+    arrived = lax.ppermute(sent, "seq", route)
+    halo = arrived[:, :, :model_width].reshape(seqs * HALO, model_width)
+    early_seg = jnp.where(turn == 0, -1.0, arrived[:, :, model_width].astype(F32))
+    seg_pad = jnp.concatenate([early_seg, seg], axis=1)
+
+    def same(other):
+        return (other == seg).astype(F32)
+
+    by_chunk = seg.reshape(seqs, piece // CHUNK, CHUNK)
+    before = seg_pad[:, HALO - 1 : HALO - 1 + piece].reshape(by_chunk.shape)[:, :, :1]
+    chunk_first = jnp.broadcast_to(before, by_chunk.shape).reshape(seqs, piece)
+    chunk_last = jnp.broadcast_to(by_chunk[:, :, -1:], by_chunk.shape).reshape(seqs, piece)
+    valid_float = valid_mask.astype(F32)
+    columns = [same(seg_pad[:, HALO - 3 + k : HALO - 3 + k + piece]) for k in range(4)] + [
+        same(chunk_first),
+        same(chunk_last),
+        same(early_seg[:, -1:]),
+        same(seg[:, -1:]),
+        seg,
+        valid_float,
+    ]
+    columns = columns + [jnp.zeros_like(seg)] * (16 - len(columns))
+    masks = jnp.stack(columns, axis=2).reshape(total, 16)
+    seg_row = seg.reshape(1, total)
+    heads_map = (
+        lax.broadcasted_iota(jnp.int32, (LANES, inner_width), 0)
+        == lax.broadcasted_iota(jnp.int32, (LANES, inner_width), 1) // (inner_width // heads)
+    ).astype(BF16)
+
+    def lanes(values):
+        return jnp.pad(values, (0, LANES - heads)).reshape(1, LANES)
+
+    flat_tokens = tokens.reshape(total, model_width)
+    flat_cot = cotangent.reshape(total, model_width)
+    bias_row, decay_row = lanes(dt_bias), lanes(a_log)
+    skip_row = jnp.repeat(skip_d, inner_width // heads).reshape(1, inner_width)
+    gain_row = gate_gain.reshape(1, inner_width)
+    normed, gate, conv, conv_halo, summed, raw, cum, fresh, keep = front(
+        flat_tokens,
+        halo,
+        norm_gain.reshape(1, model_width),
+        in_weight,
+        conv_weight,
+        conv_bias.reshape(1, channels),
+        masks,
+        bias_row,
+        decay_row,
+        heads_map,
+        sizes,
     )
-    padded = jnp.concatenate([prev_rows, conv_in], axis=1)
-    seg_pad = jnp.concatenate([prev_seg, seg_float], axis=1)
-    masks = [
-        (seg_pad[:, k : k + piece_size] == seg_float).astype(jnp.float32)[:, :, None]
-        for k in range(tap_count)
-    ]
-
-    def conv_part(padded_in, taps_in, bias_in, raw_in, dt_bias_in, a_log_in):
-        summed = bias_in + jnp.zeros((seq_count, piece_size, channels), jnp.float32)
-        for k in range(tap_count):
-            summed = summed + padded_in[:, k : k + piece_size] * masks[k] * taps_in[k]
-        activated = jax.nn.silu(summed)
-        signal = activated[:, :, :inner_width].reshape(
-            seq_count, piece_size, head_count, head_width
-        )
-        writer = activated[:, :, inner_width : inner_width + state_width]
-        reader = activated[:, :, inner_width + state_width :]
-        step_size = jax.nn.softplus(raw_in + dt_bias_in)
-        return (signal, writer, reader, step_size, -jnp.exp(a_log_in) * step_size)
-
-    (signal, writer, reader, step_size, log_decay), back_conv = jax.vjp(
-        conv_part, padded, conv_weight, conv_bias, dt_raw, dt_bias, a_log
+    incoming = chain(fresh, keep, 1)
+    output, low, out_low, gate_grad, ssm_grad, starts, dots, squares, wide, state_grad = forward(
+        summed,
+        gate,
+        raw,
+        cum,
+        masks,
+        seg_row,
+        incoming,
+        flat_tokens,
+        flat_cot,
+        out_weight,
+        gain_row,
+        skip_row,
+        heads_map,
+        sizes,
     )
-    counter = jnp.cumsum(doc_starts, axis=1)
-    positions = jnp.arange(piece_size)
-    causal = positions[:, None] >= positions[None, :]
-    same_doc = (counter[:, :, None] == counter[:, None, :]) & causal[None]
-    first_doc = (counter == 0)[:, :, None]
-    last_doc = (counter == counter[:, -1:])[:, :, None]
-    untouched = (counter[:, -1] == 0)[:, None]
-
-    def end_state(signal_in, writer_in, step_in, decay_in):
-        cumulative = jnp.cumsum(decay_in, axis=1)
-        final_log = cumulative[:, -1]
-        keeping = jnp.where(untouched, jnp.exp(final_log), 0.0)
-        tails = jnp.where(last_doc, jnp.exp(final_log[:, None] - cumulative), 0.0) * step_in
-        fresh_state = jnp.einsum(
-            "slh,slhp,sln->shpn", tails, signal_in, writer_in, precision=highest
-        )
-        return (keeping, fresh_state)
-
-    def piece_out(signal_in, writer_in, reader_in, step_in, decay_in, incoming_in):
-        cumulative = jnp.cumsum(decay_in, axis=1)
-        by_head = jnp.transpose(cumulative, (0, 2, 1))
-        gaps = by_head[:, :, :, None] - by_head[:, :, None, :]
-        decays = jnp.exp(jnp.where(same_doc[:, None], gaps, -1e30))
-        scores = jnp.einsum("stn,sun->stu", reader_in, writer_in, precision=highest)
-        weighted = scores[:, None] * decays
-        inner_part = jnp.einsum(
-            "shtu,suhp->sthp", weighted, signal_in * step_in[..., None], precision=highest
-        )
-        entries = jnp.where(first_doc, jnp.exp(cumulative), 0.0)
-        carried = (
-            jnp.einsum("stn,shpn->sthp", reader_in, incoming_in, precision=highest)
-            * entries[..., None]
-        )
-        return inner_part + carried
-
-    (keeping, fresh_state), back_end = jax.vjp(end_state, signal, writer, step_size, log_decay)
-    identity = (jnp.ones_like(keeping), jnp.zeros_like(fresh_state))
-    _, incoming = entering((keeping, fresh_state), "seq", compose, identity)
-    ssm_out, back_out = jax.vjp(piece_out, signal, writer, reader, step_size, log_decay, incoming)
-
-    def gate_norm(ssm_in, signal_in, skip_in, gate_values, gain_values):
-        mixer_in = (ssm_in + skip_in[:, None] * signal_in).reshape(
-            seq_count, piece_size, inner_width
-        )
-        gated_out = mixer_in * jax.nn.silu(gate_values)
-        return (
-            gated_out
-            * lax.rsqrt(jnp.mean(gated_out * gated_out, axis=-1, keepdims=True) + epsilon)
-            * gain_values
-        )
-
-    gate_normed, back_gate = jax.vjp(gate_norm, ssm_out, signal, skip_d, gate_in, gate_gain)
-    gate_low = gate_normed.astype(jnp.bfloat16).reshape(row_count, inner_width)
-    mixed = jnp.dot(gate_low, out_weight, preferred_element_type=jnp.float32).reshape(
-        seq_count, piece_size, model_width
+    later = chain(state_grad, keep, -1)
+    proj_grad, tail, rim, conv_sums, head_sums = backward(
+        summed,
+        conv,
+        conv_halo,
+        raw,
+        cum,
+        masks,
+        seg_row,
+        later,
+        ssm_grad,
+        starts,
+        dots,
+        conv_weight,
+        decay_row,
+        skip_row,
+        heads_map,
+        sizes,
     )
-    block_out = inputs + mixed
-    valid_float = valid_mask.astype(jnp.float32)
-    out_square = jnp.sum(valid_float * jnp.sum(block_out * block_out, axis=-1))
-    mix_square = jnp.sum(valid_float * jnp.sum(mixed * mixed, axis=-1))
-    valid_count = jnp.sum(valid_float)
-    out_grad = cotangent.astype(jnp.float32) * valid_float[:, :, None]
-    out_low = out_grad.astype(jnp.bfloat16).reshape(row_count, model_width)
-    gate_grad = lax.dot_general(
-        out_low, out_weight, (((1,), (1,)), ((), ())), preferred_element_type=jnp.float32
-    ).reshape(seq_count, piece_size, inner_width)
-    ssm_grad, signal_grad_gate, skip_grad, gate_in_grad, gate_gain_grad = back_gate(gate_grad)
-    signal_grad_out, writer_grad_out, reader_grad, step_grad_out, decay_grad_out, state_grad = (
-        back_out(ssm_grad)
+    rim_in = lax.ppermute(rim, "seq", [(b, a) for a, b in route])
+    fixed = (tail + rim_in.astype(F32)).astype(BF16)
+    proj_grad = (
+        proj_grad.reshape(seqs, piece, -1)
+        .at[:, piece - 8 :, :channels]
+        .set(fixed)
+        .reshape(total, -1)
     )
-    _, later_grad = carried_in((keeping, state_grad), "seq", compose, identity)
-    keeping_grad = jnp.sum(later_grad * incoming, axis=(2, 3))
-    signal_grad_end, writer_grad_end, step_grad_end, decay_grad_end = back_end(
-        (keeping_grad, later_grad)
+    input_grad, gain_sums = input_gradient(
+        flat_tokens, out_low, gate_grad, proj_grad, in_weight, norm_gain.reshape(1, model_width)
     )
-    padded_grad, conv_weight_grad, conv_bias_grad, dt_raw_grad, dt_bias_grad, a_log_grad = (
-        back_conv(
-            (
-                signal_grad_gate + signal_grad_out + signal_grad_end,
-                writer_grad_out + writer_grad_end,
-                reader_grad,
-                step_grad_out + step_grad_end,
-                decay_grad_out + decay_grad_end,
-            )
-        )
+    grad_tiles = weight_gradient(out_low, normed, low, gate_grad, proj_grad)
+    share_rows = model_width // pieces
+    width = inner_width + proj_width
+    flows = -(-grad_tiles.shape[0] // places)
+    full = flows * places * LANES
+    grad_tiles = jnp.pad(
+        grad_tiles, ((0, flows * places - grad_tiles.shape[0]), (0, 0), (0, 0))
     )
-    rim_grad = shifted(padded_grad[:, : tap_count - 1].astype(jnp.bfloat16), "seq", -1).astype(
-        jnp.float32
-    )
-    conv_in_grad = padded_grad[:, tap_count - 1 :] + jnp.pad(
-        rim_grad, ((0, 0), (piece_size - tap_count + 1, 0), (0, 0))
-    )
-    proj_grad = (
-        jnp.concatenate([gate_in_grad, conv_in_grad, dt_raw_grad], axis=2)
-        .astype(jnp.bfloat16)
-        .reshape(row_count, proj_width)
-    )
-    normed_grad = lax.dot_general(
-        proj_grad, in_weight, (((1,), (1,)), ((), ())), preferred_element_type=jnp.float32
-    ).reshape(seq_count, piece_size, model_width)
-    input_grad_pre, norm_gain_grad = back_pre(normed_grad)
-    input_grad = (out_grad + input_grad_pre).astype(jnp.bfloat16)
-    share_rows = model_width // lax.axis_size("seq")
-    in_part = lax.dot_general(
-        normed_low, proj_grad, (((0,), (0,)), ((), ())), preferred_element_type=jnp.float32
-    )
-    out_part = lax.dot_general(
-        out_low, gate_low, (((0,), (0,)), ((), ())), preferred_element_type=jnp.float32
-    )
-    places, pieces = lax.axis_size("dp"), lax.axis_size("seq")
-    width = inner_width + proj_width
-    flows = -(-width // (LANES * places))
-    full = flows * places * LANES
+    grads = grad_tiles.reshape(flows, places, pieces, share_rows, LANES)
 
     def tiled(block):
-        spread = jnp.pad(block, ((0, 0), (0, full - width)))
-        return spread.reshape(-1, flows * places, LANES)
-
-    whole_grad = jnp.concatenate([out_part, in_part], axis=1).astype(jnp.bfloat16)
-    grads = (
-        tiled(whole_grad)
-        .reshape(pieces, share_rows, flows, places, LANES)
-        .transpose(2, 3, 0, 1, 4)
-    )
+        spread_out = jnp.pad(block, ((0, 0), (0, full - width)))
+        return spread_out.reshape(-1, flows * places, LANES)
+
+    norm_gain_grad = gain_sums[0]
+    conv_weight_grad = conv_sums[:tap_count]
+    conv_bias_grad = conv_sums[tap_count]
+    dt_bias_grad = head_sums[0, :heads]
+    a_log_grad = head_sums[1, :heads]
+    gate_gain_grad = wide[0]
+    skip_grad = wide[1].reshape(heads, -1).sum(axis=1)
+    out_square = squares[0].sum()
+    mix_square = squares[1].sum()
+    valid_count = valid_float.sum()
     step_float = step_number[0].astype(jnp.float32)
     rate_now = learn_rate[0] * step_float / (step_float + 16.0)
     first_row = lax.axis_index("seq") * share_rows
@@ -553,8 +1345,8 @@
     output_rms = jnp.sqrt(out_square_total / denominator).reshape(1)
     mixer_rms = jnp.sqrt(mix_square_total / denominator).reshape(1)
     return (
-        block_out.astype(jnp.bfloat16),
-        input_grad,
+        output.reshape(tokens.shape),
+        input_grad.reshape(tokens.shape),
         new_in_weight,
         new_out_weight,
         new_in_momentum,

time: 615 us -> 382 us (0.62); the launches traced: 606 us -> 380 us
  matrix products: 158 us -> 0 us
  Pallas kernels: 130 us -> 267 us
  other arithmetic: 104 us -> 11.3 us
  local copies, waits for them, and re-layouts: 164 us -> 84.5 us
  blocking collectives: 17.5 us -> 0 us
  between operations: 22.4 us -> 6.81 us
    dot_general x18 -> x0, matrix products: 158 us -> none  [the longest x3 87.6 us: piece_out(): jnp.einsum('shtu,suhp->sthp', weighted, signal_in * step_in[..., None], p...]
    pallas_call x0 -> x7, Pallas kernels: none -> 142 us  [the longest x1 33.5 us: forward(): pl.pallas_call(functools.partial(forward_kernel, sizes, chunks), grid=(se...]
    reduce_sum x10 -> x3, other arithmetic: 31.7 us -> 2.02 us  [the longest x1 1.29 us: local(): valid_count = valid_float.sum()]
    mul x8 -> x0, other arithmetic: 21.7 us -> none  [the longest x1 11.3 us: conv_part(): activated = jax.nn.silu(summed)]
    unnamed x186 -> x70, local copies, waits for them, and re-layouts: 59.2 us -> 39.2 us
    mul x10 -> x0, local copies, waits for them, and re-layouts: 19.9 us -> none  [the longest x4 11.6 us: piece_out(): jnp.einsum('stn,shpn->sthp', reader_in, incoming_in, precision=highest)]
    all_gather x2 -> x0, blocking collectives: 17.5 us -> none  [the longest x1 9.33 us: entering(): lax.all_gather(a.astype(kind), axis)]
    another operation x10 -> x3, other arithmetic: 13.9 us -> 2.9 us  [local(): masks = jnp.stack(columns, axis=2).reshape(total, 16)]
  transfers between devices with their start and end apart: 5 -> 2, of which waited for: 1 -> 1; matrix products, arithmetic and copies ran while one was open for 22% -> 7% of each run, Pallas kernels for 0% -> 0%
where the time goes in v2:
time: 382 us; the launch traced here: 380 us
  Pallas kernels  267 us (70%)
  local copies, waits for them, and re-layouts  84.5 us (22%)
  other arithmetic  11.3 us (3%)
  between operations  6.81 us (2%)
  starting transfers between devices  6.2 us (2%)
    pallas_call x1, Pallas kernels, exchange(): pl.pallas_call(functools.partial(exchange_kernel, bits, pieces, flows), o...  125 us
    unnamed x70, local copies, waits for them, and re-layouts  39.2 us
    pallas_call x1, Pallas kernels, forward(): pl.pallas_call(functools.partial(forward_kernel, sizes, chunks), grid=(se...  33.5 us
    pallas_call x2, Pallas kernels, chain(): pl.pallas_call(functools.partial(chain_kernel, ways, blocks), out_shape=j...  33.5 us
    pallas_call x1, Pallas kernels, backward(): pl.pallas_call(functools.partial(backward_kernel, sizes, chunks), grid=(s...  28.9 us
    pallas_call x1, Pallas kernels, front(): pl.pallas_call(functools.partial(front_kernel, sizes), grid=(gate_blocks...  21.5 us
    slice x2, local copies, waits for them, and re-layouts, local(): gathered[:, :, :pieces].reshape(flows * places, pieces, share_rows, LANES)  17.4 us
    pallas_call x1, Pallas kernels, weight_gradient(): pl.pallas_call(functools.partial(weight_kernel, (low_count, gate_count)),...  14.9 us
  transfers between devices with their start and end apart: 2, of which 1 were waited for; matrix products, arithmetic and copies ran while one was open for 7% of the time, Pallas kernels for 0%

profile of v2, /device:TPU:0, one launch (start us, length us, event | category | flops | bytes accessed | tf_op | source)
XLA Modules:
  0.0 380.0 jit_solution(17283615297240798664)
XLA Ops:
  0.7 0.8 convert_bitcast_fusion.1
  1.6 0.7 slice.151
  2.4 4.9 %collective-permute-start = (bf16[1,16,896]{2,1,0:T(8,128)(2,1)S(1)}, bf16[1,16,896]{2,1,0:T(8,128)(2,1)S(1)}, u32[]{:S(2)}, u32[]{:S(2)}) collective-permute-start(bf16[1,16,896]{2,1,0:T(8,128)(2,1)S(1)} %pad_maximum_fusion), channel_id=1, source_target_pairs={{0,1},{1,2},{2,3},{4,5},{5,6},{6,7},{8,9},{9,10},{10,11},{12,13},{... | collective-permute-start | bytes 86024 | tf_op jit(solution)/shard_map/ppermute | solution.py:1159
  7.3 0.7 convert_bitcast_fusion
  8.0 1.3 convert_reduce_fusion
  9.3 3.8 constant_dynamic-slice_fusion.2
  13.1 1.6 dynamic-slice_bitcast_fusion
  14.7 1.7 fusion.2
  16.4 2.6 copy.75
  19.5 2.5 constant_dynamic-slice_fusion
  22.1 7.9 %copy.63.weight_ref = bf16[768,3352]{1,0:T(8,128)(2,1)} copy(bf16[768,3352]{0,1:T(8,128)(2,1)} %param.27) | data formatting | bytes 10297344 | tf_op args[8]
  32.3 0.9 copy.73
  33.1 0.8 copy.83
  35.1 1.4 fusion.13
  36.7 0.7 slice_bitcast_fusion.2.halo_ref
  37.5 21.5 %front.1 = (bf16[512,768]{1,0:T(8,128)(2,1)S(1)}, f32[512,1536]{1,0:T(8,128)}, f32[512,1792]{1,0:T(8,128)}, f32[16,1792]{1,0:T(8,128)S(1)}, f32[512,1792]{1,0:T(...) custom-call(bf16[512,768]{1,0:T(8,128)(2,1)S(1)} %bitcast.99, ...), custom_call_target="tpu_custom_call" | custom-call | tf_op jit(solution)/shard_map/front/pallas_call | solution.py:399
  59.0 9.8 %chain.2.incoming_ref = f32[1,128,1536]{2,1,0:T(8,128)S(1)} custom-call(f32[1,128,1536]{2,1,0:T(8,128)S(1)} %get-tuple-element.59.own_ref, f32[1,8,1536]{2,1,0:T(8,128)S(1)} %get-tuple-element.60.keep_ref), custom_call_target="tpu_custom_call" | custom-call | tf_op jit(solution)/shard_map/chain/pallas_call | solution.py:510
  68.8 33.5 %forward.1 = (bf16[512,768]{1,0:T(8,128)(2,1)}, bf16[512,1536]{1,0:T(8,128)(2,1)}, bf16[512,768]{1,0:T(8,128)(2,1)S(1)}, bf16[512,1536]{1,0:T(8,128)(2,1)}, f32[...) custom-call(f32[512,1792]{1,0:T(8,128)} %get-tuple-element.55.summed, ...), custom_call_target="tpu_custom_call" | custom-call | tf_op jit(solution)/shard_map/forward/pallas_call | solution.py:704
  102.3 23.6 %chain.3.later_ref = f32[1,128,1536]{2,1,0:T(8,128)S(1)} custom-call(f32[1,128,1536]{2,1,0:T(8,128)S(1)} %get-tuple-element.66.own_ref, f32[1,8,1536]{2,1,0:T(8,128)S(1)} %get-tuple-element.60.keep_ref), custom_call_target="tpu_custom_call" | custom-call | tf_op jit(solution)/shard_map/chain/pallas_call | solution.py:510
  126.0 28.9 %backward.1 = (bf16[512,2048]{1,0:T(8,128)(2,1)S(1)}, f32[1,8,1792]{2,1,0:T(8,128)S(1)}, bf16[1,8,1792]{2,1,0:T(8,128)(2,1)}, f32[8,1792]{1,0:T(8,128)S(1)}, f32[8,128]{1,0:T(8,128)S(1)}) custom-call(f32[512,1792]{1,0:T(8,128)} %get-tuple-element.55.summed_ref, f32[512,1792]{1,0:T(8,128)} %get-tuple-element.64.conv_ref, ...), custom_call_target="tpu_custom_call" | custom-call | tf_op jit(solution)/shard_map/backward/pallas_call | solution.py:951
  155.5 1.3 collective-permute-start.1
  157.7 3.8 collective-permute-done.1
  161.5 0.8 fusion.7.proj_grad_ref
  162.3 2.2 copy-done.2
  164.5 1.1 copy-done.5
  165.6 10.3 %input_gradient.1 = (bf16[512,768]{1,0:T(8,128)(2,1)}, f32[8,768]{1,0:T(8,128)S(1)}) custom-call(bf16[512,768]{1,0:T(8,128)(2,1)S(1)} %bitcast.101, bf16[512,768]{1,0:T(8,128)(2,1)S(1)} %copy-done.5, bf16[512,1536]{1,0:T(8,128)(2,1)S(1)} %copy-done.2, bf16[512,2048]{1,0:T(8,128)(2,1)S(1)} %fusion.7.proj_grad_ref, bf16[768,3352]{1,0:T(8,128)(2,1)} %copy.63.weight_ref, ...), custom_call_target="tpu_custom_call" | custom-call | tf_op jit(solution)/shard_map/input_gradient/pallas_call | solution.py:1045
  175.9 2.0 concatenate.22
  177.9 0.6 pad_bitcast_fusion.small_ref
  178.5 1.4 copy-done.3
  179.9 1.1 copy-done.6
  181.1 1.4 copy-done.7
  182.5 1.1 copy-done.10
  183.6 14.9 %weight_gradient.1 = bf16[40,768,128]{2,1,0:T(8,128)(2,1)} custom-call(bf16[512,768]{1,0:T(8,128)(2,1)S(1)} %copy-done.6, bf16[512,768]{1,0:T(8,128)(2,1)S(1)} %copy-done.10, bf16[512,1536]{1,0:T(8,128)(2,1)S(1)} %copy-done.7, bf16[512,1536]{1,0:T(8,128)(2,1)S(1)} %copy-done.3, bf16[512,2048]{1,0:T(8,128)(2,1)} %copy-done), custom_call_target="tpu_custom_call" | custom-call | tf_op jit(solution)/shard_map/weight_gradient/pallas_call | solution.py:1101
  198.5 125.0 %exchange.1 = (bf16[5,2,2,2,5,192,128]{6,5,4,3,2,1,0:T(8,128)(2,1)}, f32[96,128]{1,0:T(8,128)}) custom-call(f32[1]{0:T(128)S(6)} %div.27.rate_ref, bf16[5,2,2,2,4,192,128]{6,5,4,3,2,1,0:T(8,128)(2,1)} %bitcast.107, bf16[5,192,128]{2,1,0:T(8,128)(2,1)} %bitcast.120, f32[5,192,128]{2,1,0:T(8,128)} %bitcast.119, f32[96,128]{1,0:T(8,128)} %pad_bitcast_fusion.small_ref), custom_call_target="tpu_custom_call" | custom-call | tf_op jit(solution)/shard_map/exchange/pallas_call | solution.py:207
  323.5 9.2 %slice.198 = bf16[5,8,4,192,128]{4,3,2,1,0:T(8,128)(2,1)} slice(bf16[5,8,5,192,128]{4,3,2,1,0:T(8,128)(2,1)} %bitcast.111), slice={[0:5], [0:8], [0:4], [0:192], [0:128]} | slice | bytes 15728640 | tf_op jit(solution)/shard_map/slice | solution.py:1320
  332.7 8.3 %copy.67 = bf16[5,8,4,192,128]{4,1,0,3,2:T(8,128)(2,1)S(1)} copy(bf16[5,8,4,192,128]{4,3,2,1,0:T(8,128)(2,1)} %slice.198) | data formatting | bytes 15728640 | tf_op jit(solution)/shard_map/slice | solution.py:1320
  340.9 5.5 %copy.81 = bf16[96,8,40,128]{3,1,2,0:T(8,128)(2,1)} copy(bf16[96,8,40,128]{3,2,1,0:T(8,128)(2,1)S(1)} %bitcast.108) | data formatting | bytes 15728640
  346.4 5.2 %slice.199 = bf16[768,3352]{1,0:T(8,128)(2,1)} slice(bf16[768,5120]{1,0:T(8,128)(2,1)} %bitcast.109), slice={[0:768], [1536:4888]} | slice | bytes 10297344 | tf_op jit(solution)/shard_map/slice | solution.py:1324
  351.7 1.8 slice_bitcast_fusion
  353.5 1.7 slice.201
  355.2 1.3 copy.68
  357.1 1.5 copy-done.18
  358.6 1.8 slice_add_fusion
  360.3 1.1 fusion.4
  363.3 0.7 slice.208
  363.9 0.7 fusion.22
  364.6 8.0 %copy.69 = bf16[768,3352]{0,1:T(8,128)(2,1)} copy(bf16[768,3352]{1,0:T(8,128)(2,1)} %slice.199) | data formatting | bytes 10297344
  372.6 2.4 copy.70
  (97 shorter events, 7.5 us)
Async XLA Ops:
  0.6 14.1 %copy-start.17 = (f32[192,3352]{1,0:T(8,128)S(1)}, f32[192,3352]{1,0:T(8,128)}, u32[]{:S(2)}) copy-start(f32[192,3352]{1,0:T(8,128)} %param.35) | copy-start | bytes 7723012
  2.4 31.6 %collective-permute-start = (bf16[1,16,896]{2,1,0:T(8,128)(2,1)S(1)}, bf16[1,16,896]{2,1,0:T(8,128)(2,1)S(1)}, u32[]{:S(2)}, u32[]{:S(2)}) collective-permute-start(bf16[1,16,896]{2,1,0:T(8,128)(2,1)S(1)} %pad_maximum_fusion), channel_id=1, source_target_pairs={{0,1},{1,2},{2,3},{4,5},{5,6},{6,7},{8,9},{9,10},{10,11},{12,13},{... | collective-permute-start | bytes 86024 | tf_op jit(solution)/shard_map/ppermute | solution.py:1159
  16.4 2.6 copy-start.19
  19.0 3.0 copy-start.28
  19.0 3.0 copy-start.29
  22.0 15.4 %copy-start.15 = (f32[1,128]{1,0:T(1,128)}, f32[1,128]{1,0:T(1,128)S(1)}, u32[]{:S(2)}) copy-start(f32[1,128]{1,0:T(1,128)S(1)} %get-tuple-element.137.a_log_ref) | copy-start | bytes 1540
  22.0 8.6 %copy-start.26 = (f32[768]{0:T(1024)S(1)}, f32[768]{0:T(1024)}, u32[]{:S(2)}) copy-start(f32[768]{0:T(1024)} %param.26) | copy-start | bytes 9220
  22.1 8.6 %copy-start.25 = (f32[1792]{0:T(1024)S(1)}, f32[1792]{0:T(1024)}, u32[]{:S(2)}) copy-start(f32[1792]{0:T(1024)} %param.29) | copy-start | bytes 21508
  22.1 8.7 %copy-start.24 = (f32[1536]{0:T(1024)S(1)}, f32[1536]{0:T(1024)}, u32[]{:S(2)}) copy-start(f32[1536]{0:T(1024)} %param.33) | copy-start | bytes 18436
  22.1 8.7 %copy-start.27 = (f32[24]{0:T(128)S(1)}, f32[24]{0:T(128)}, u32[]{:S(2)}) copy-start(f32[24]{0:T(128)} %param.32) | copy-start | bytes 292
  22.1 13.0 %copy-start.23 = (s32[1,512]{1,0:T(1,128)S(1)}, s32[1,512]{1,0:T(1,128)}, u32[]{:S(2)}) copy-start(s32[1,512]{1,0:T(1,128)} %param.22) | copy-start | bytes 6148
  22.1 15.3 %copy-start.12 = (f32[4,1792]{1,0:T(4,128)S(1)}, f32[4,1792]{1,0:T(4,128)}, u32[]{:S(2)}) copy-start(f32[4,1792]{1,0:T(4,128)} %taps_ref.3) | copy-start | bytes 86020
  30.0 7.4 %copy-start.1 = (bf16[1,512,768]{2,1,0:T(8,128)(2,1)S(1)}, bf16[1,512,768]{2,1,0:T(8,128)(2,1)}, u32[]{:S(2)}) copy-start(bf16[1,512,768]{2,1,0:T(8,128)(2,1)} %param.20) | copy-start | bytes 2359300
  34.0 2.4 copy-start.22
  37.4 31.4 %copy-start.11 = (bf16[1,512,768]{2,1,0:T(8,128)(2,1)S(1)}, bf16[1,512,768]{2,1,0:T(8,128)(2,1)}, u32[]{:S(2)}) copy-start(bf16[1,512,768]{2,1,0:T(8,128)(2,1)} %param.21) | copy-start | bytes 2359300
  58.9 9.8 %copy-start.9 = (bf16[512,768]{1,0:T(8,128)(2,1)}, bf16[512,768]{1,0:T(8,128)(2,1)S(1)}, u32[]{:S(2)}) copy-start(bf16[512,768]{1,0:T(8,128)(2,1)S(1)} %get-tuple-element.74.normed_ref) | copy-start | bytes 2359300
  68.8 57.2 %copy-start.13 = (f32[4,1792]{1,0:T(4,128)S(1)}, f32[4,1792]{1,0:T(4,128)}, u32[]{:S(2)}) copy-start(f32[4,1792]{1,0:T(4,128)} %taps_ref.3) | copy-start | bytes 86020
  68.8 57.2 %copy-start.16 = (f32[1,128]{1,0:T(1,128)S(1)}, f32[1,128]{1,0:T(1,128)}, u32[]{:S(2)}) copy-start(f32[1,128]{1,0:T(1,128)} %copy-done.15) | copy-start | bytes 1540
  102.3 23.7 %copy-start.4 = (bf16[512,768]{1,0:T(8,128)(2,1)}, bf16[512,768]{1,0:T(8,128)(2,1)S(1)}, u32[]{:S(2)}) copy-start(bf16[512,768]{1,0:T(8,128)(2,1)S(1)} %get-tuple-element.62.out_low_ref) | copy-start | bytes 2359300
  102.3 23.7 %copy-start.8 = (bf16[4,128,1536]{2,1,0:T(8,128)(2,1)S(1)}, bf16[4,128,1536]{2,1,0:T(8,128)(2,1)}, u32[]{:S(2)}) copy-start(bf16[4,128,1536]{2,1,0:T(8,128)(2,1)} %get-tuple-element.68.starts_ref) | copy-start | bytes 4718596
  154.9 0.6 copy-start.14
  155.5 6.0 %collective-permute-start.1 = (bf16[1,8,1792]{2,1,0:T(8,128)(2,1)}, bf16[1,8,1792]{2,1,0:T(8,128)(2,1)S(1)}, u32[]{:S(2)}, u32[]{:S(2)}) collective-permute-start(bf16[1,8,1792]{2,1,0:T(8,128)(2,1)} %get-tuple-element.72), channel_id=1, source_target_pairs={{1,0},{2,1},{3,2},{5,4},{6,5},{7,6},{9,8},{10,9},{11,10},{13,12},{... | collective-permute-start | bytes 86024 | tf_op jit(solution)/shard_map/ppermute | solution.py:1245
  162.3 13.6 %copy-start = (bf16[512,2048]{1,0:T(8,128)(2,1)}, bf16[512,2048]{1,0:T(8,128)(2,1)S(1)}, u32[]{:S(2)}) copy-start(bf16[512,2048]{1,0:T(8,128)(2,1)S(1)} %fusion.7.proj_grad_ref) | copy-start | bytes 6291460
  162.3 2.2 copy-start.2
  164.5 1.1 copy-start.5
  178.5 1.4 copy-start.3
  179.9 1.1 copy-start.6
  181.1 1.4 copy-start.7
  182.5 1.1 copy-start.10
  356.8 1.8 copy-start.18
  358.6 1.8 copy-start.20
  360.3 1.2 copy-start.21

commit v3 on v2

--- a/solution.py
+++ b/solution.py
@@ -18,7 +18,11 @@
     grad_ref,
     weight_ref,
     momentum_ref,
-    small_ref,
+    conv_sums_ref,
+    wide_ref,
+    head_sums_ref,
+    gain_sums_ref,
+    squares_ref,
     gathered_ref,
     small_out_ref,
     *scratch,
@@ -136,7 +140,13 @@
         if k >= 0:
             ag_copy(f, k).start()
 
-    small_acc[0] = small_ref[...]
+    inner, model = wide_ref.shape[1], gain_sums_ref.shape[1]
+    small_acc[0, 0:5] = conv_sums_ref[0:5]
+    small_acc[0, 5:7, :inner] = wide_ref[0:2]
+    small_acc[0, 5:7, inner : inner + 128] = head_sums_ref[0:2]
+    small_acc[0, 5:8, inner + 128 :] = squares_ref[0:3]
+    small_acc[0, 7:8, :model] = gain_sums_ref[0:1]
+    small_acc[0, 7:8, model : inner + 128] = jnp.zeros((1, inner + 128 - model), jnp.float32)
     if bits:
         sm_copy(0).start()
     for f in range(flows):
@@ -195,22 +205,22 @@
             zg_copy(f, j).wait_send()
 
 
-def exchange(rate, grads, weights, momenta, small):
+def exchange(rate, grads, weights, momenta, sums):
     flows, places, pieces, rows, _ = grads.shape
     bits = places.bit_length() - 1
     assert places == 1 << bits and bits >= 1 and pieces >= 2
     twos = (2,) * bits
     grads = grads.reshape((flows,) + twos + (pieces, rows, LANES))
-    small_rows = small.shape[0]
+    small = sums[0].shape
     vmem = pl.BlockSpec(memory_space=pltpu.VMEM)
     dma = pltpu.SemaphoreType.DMA
     gathered, small_out = pl.pallas_call(
         functools.partial(exchange_kernel, bits, pieces, flows),
         out_shape=(
             jax.ShapeDtypeStruct((flows,) + twos + (pieces + 1, rows, LANES), jnp.bfloat16),
-            jax.ShapeDtypeStruct((small_rows, LANES), jnp.float32),
+            jax.ShapeDtypeStruct(small, jnp.float32),
         ),
-        in_specs=[pl.BlockSpec(memory_space=pltpu.SMEM)] + [vmem] * 4,
+        in_specs=[pl.BlockSpec(memory_space=pltpu.SMEM)] + [vmem] * 8,
         out_specs=(vmem, vmem),
         scratch_shapes=[
             pltpu.VMEM((flows,) + twos[k + 1 :] + (pieces, rows, LANES), jnp.bfloat16)
@@ -218,9 +228,9 @@
         ]
         + [
             pltpu.VMEM((flows, pieces, rows, LANES), jnp.bfloat16),
-            pltpu.VMEM((bits + 1, small_rows, LANES), jnp.float32),
-            pltpu.VMEM((bits, small_rows, LANES), jnp.float32),
-            pltpu.VMEM((pieces, small_rows, LANES), jnp.float32),
+            pltpu.VMEM((bits + 1,) + small, jnp.float32),
+            pltpu.VMEM((bits,) + small, jnp.float32),
+            pltpu.VMEM((pieces,) + small, jnp.float32),
         ]
         + [dma((flows, bits))] * 2
         + [dma((flows, pieces))] * 4
@@ -231,7 +241,7 @@
             collective_id=0, has_side_effects=True, vmem_limit_bytes=56 * 1024 * 1024
         ),
         name="exchange",
-    )(rate, grads, weights, momenta, small)
+    )(rate, grads, weights, momenta, *sums)
     return gathered.reshape(flows, places, pieces + 1, rows, LANES), small_out
 
 
@@ -296,11 +306,13 @@
     weight_ref,
     taps_ref,
     bias_ref,
-    masks_ref,
+    seg_ref,
+    valid_ref,
     dt_bias_ref,
     a_log_ref,
     heads_ref,
     normed_ref,
+    masks_ref,
     gate_ref,
     conv_ref,
     halo_out_ref,
@@ -322,6 +334,32 @@
     def _():
         gain = gain_ref[...]
         for n in range(seqs):
+            padded_seg = seg_ref[n : n + 1]
+            seg = padded_seg[:, HALO:]
+
+            def over_chunks(at):
+                return jnp.concatenate(
+                    [
+                        jnp.broadcast_to(
+                            padded_seg[:, c * CHUNK + at : c * CHUNK + at + 1], (1, CHUNK)
+                        )
+                        for c in range(piece // CHUNK)
+                    ],
+                    axis=1,
+                )
+
+            others = [padded_seg[:, HALO - 3 + k : HALO - 3 + k + piece] for k in range(4)] + [
+                over_chunks(HALO - 1),
+                over_chunks(HALO + CHUNK - 1),
+                jnp.broadcast_to(padded_seg[:, HALO - 1 : HALO], (1, piece)),
+                jnp.broadcast_to(padded_seg[:, HALO + piece - 1 :], (1, piece)),
+            ]
+            lines = [(other == seg).astype(F32) for other in others] + [
+                seg,
+                valid_ref[n : n + 1].astype(F32),
+            ]
+            lines = lines + [jnp.zeros_like(seg)] * (16 - len(lines))
+            masks_ref[pl.ds(n * piece, piece)] = jnp.transpose(jnp.concatenate(lines, axis=0))
             for source, start, to, count in (
                 (halo_ref, n * HALO, n * stride, HALO),
                 (tokens_ref, n * piece, n * stride + HALO, piece),
@@ -337,7 +375,7 @@
                 lax.fori_loop(0, count // 16, body, 0)
             normed_ref[pl.ds(n * piece, piece)] = padded[pl.ds(n * stride + HALO, piece)]
 
-    product[...] = mm(padded[...], weight_ref[...])
+    product[...] = mm_nt(padded[...], weight_ref[...])
 
     @pl.when(step < gate_blocks)
     def _():
@@ -386,7 +424,7 @@
             keep_ref[n] = spread(jnp.broadcast_to(keep, (8, 128)), heads_ref)
 
 
-def front(tokens, halo, gain, weight, taps, bias, masks, dt_bias, a_log, heads_map, sizes):
+def front(tokens, halo, gain, weight, taps, bias, segs, valid, dt_bias, a_log, heads_map, sizes):
     seqs, piece, inner, channels, heads = sizes
     total, model = tokens.shape
     stride = seqs * (piece + HALO)
@@ -403,16 +441,18 @@
             full(total, model),
             full(seqs * HALO, model),
             full(1, model),
-            pl.BlockSpec((model, GATE_BLOCK), lambda j: (0, j)),
+            pl.BlockSpec((GATE_BLOCK, model), lambda j: (j, 0)),
             pl.BlockSpec((4, GATE_BLOCK), conv_at),
             pl.BlockSpec((1, GATE_BLOCK), conv_at),
-            full(total, 16),
+            full(*segs.shape),
+            full(*valid.shape),
             full(1, 128),
             full(1, 128),
             full(128, inner),
         ],
         out_specs=(
             full(total, model),
+            full(total, 16),
             pl.BlockSpec((total, GATE_BLOCK), lambda j: (0, jnp.minimum(j, gate_blocks - 1))),
             pl.BlockSpec((total, GATE_BLOCK), conv_at),
             pl.BlockSpec((seqs * HALO, GATE_BLOCK), conv_at),
@@ -424,6 +464,7 @@
         ),
         out_shape=(
             jax.ShapeDtypeStruct((total, model), BF16),
+            jax.ShapeDtypeStruct((total, 16), F32),
             jax.ShapeDtypeStruct((total, inner), F32),
             jax.ShapeDtypeStruct((total, channels), F32),
             jax.ShapeDtypeStruct((seqs * HALO, channels), F32),
@@ -440,7 +481,7 @@
         ],
         compiler_params=pltpu.CompilerParams(vmem_limit_bytes=48 * 1024 * 1024),
         name="front",
-    )(tokens, halo, gain, weight, taps, bias, masks, dt_bias, a_log, heads_map)
+    )(tokens, halo, gain, weight, taps, bias, segs, valid, dt_bias, a_log, heads_map)
 
 
 def chain_kernel(ways, blocks, own_ref, keep_ref, out_ref, sent, taken, send, recv):
@@ -647,8 +688,11 @@
     block_out = tokens_ref[...].astype(F32) + mixed
     output_ref[...] = block_out.astype(BF16)
     valid = masks_ref[:, 9:10]
-    sums_ref[0:1] += jnp.sum(valid * block_out * block_out, axis=0, keepdims=True)
-    sums_ref[1:2] += jnp.sum(valid * mixed * mixed, axis=0, keepdims=True)
+    for i, block in enumerate((block_out, mixed)):
+        squares = jnp.sum(valid * block * block, axis=0, keepdims=True)
+        for at in range(0, squares.shape[1], 128):
+            sums_ref[i : i + 1] += squares[:, at : at + 128]
+    sums_ref[2:3, :16] += jnp.sum(masks_ref[...], axis=0, keepdims=True)
     out_low = (cot_ref[...].astype(F32) * valid).astype(BF16)
     out_low_ref[...] = out_low
     grads[...] = mm_nt(out_low, weight_ref[...])
@@ -727,7 +771,7 @@
             rows(inner),
             pl.BlockSpec((1, 128, inner), lambda n, c: (n * chunks + c, 0, 0)),
             rows(128),
-            full(8, model),
+            full(8, 128),
             full(8, inner),
             each(128),
         ),
@@ -739,7 +783,7 @@
             shape((total, inner), F32),
             shape((seqs * chunks, 128, inner), BF16),
             shape((total, 128), F32),
-            shape((8, model), F32),
+            shape((8, 128), F32),
             shape((8, inner), F32),
             shape((seqs, 128, inner), F32),
         ),
@@ -787,11 +831,35 @@
     moved_grad,
     shifted_rows,
     all_grad,
+    rims,
+    rims_in,
+    rim_send,
+    rim_recv,
 ):
     seqs, piece, inner, channels, heads = sizes
-    c = pl.program_id(1)
-
-    @pl.when((c == 0) & (pl.program_id(0) == 0))
+    n, c = pl.program_id(0), pl.program_id(1)
+    turn, pieces = lax.axis_index("seq"), lax.axis_size("seq")
+    barrier = pltpu.get_barrier_semaphore()
+    rim_copy = pltpu.make_async_remote_copy(
+        src_ref=rims,
+        dst_ref=rims_in,
+        send_sem=rim_send,
+        recv_sem=rim_recv,
+        device_id={"seq": lax.rem(turn + pieces - 1, pieces)},
+        device_id_type=pl.DeviceIdType.MESH,
+    )
+
+    @pl.when((c == 0) & (n == 0) & (turn < pieces - 1))
+    def _():
+        pl.semaphore_signal(
+            barrier, inc=1, device_id={"seq": turn + 1}, device_id_type=pl.DeviceIdType.MESH
+        )
+
+    @pl.when((c == 0) & (n == 0) & (turn > 0))
+    def _():
+        pl.semaphore_wait(barrier, 1)
+
+    @pl.when((c == 0) & (n == 0))
     def _():
         conv_sums_ref[...] = jnp.zeros_like(conv_sums_ref)
         head_sums_ref[...] = jnp.zeros_like(head_sums_ref)
@@ -919,7 +987,23 @@
 
         @pl.when(c == chunks - 1)
         def _():
-            rim_ref[0, :, at] = rim.astype(BF16)
+            rims[n, :, at] = rim.astype(BF16)
+
+    @pl.when((c == chunks - 1) & (n == seqs - 1))
+    def _():
+        @pl.when(turn > 0)
+        def _():
+            rim_copy.start()
+            rim_copy.wait_send()
+
+        @pl.when(turn < pieces - 1)
+        def _():
+            rim_copy.wait_recv()
+            rim_ref[...] = rims_in[...]
+
+        @pl.when(turn == pieces - 1)
+        def _():
+            rim_ref[...] = jnp.zeros_like(rim_ref)
 
 
 def backward(
@@ -971,7 +1055,7 @@
         out_specs=(
             rows(channels + 256),
             each(8, channels),
-            each(8, channels),
+            pl.BlockSpec(memory_space=pltpu.VMEM),
             full(8, channels),
             full(8, 128),
         ),
@@ -990,8 +1074,14 @@
             pltpu.VMEM((CHUNK, inner), F32),
             pltpu.VMEM((CHUNK + 16, GATE_BLOCK), F32),
             pltpu.VMEM((CHUNK, channels), F32),
+            pltpu.VMEM((seqs, 8, channels), BF16),
+            pltpu.VMEM((seqs, 8, channels), BF16),
+            pltpu.SemaphoreType.DMA,
+            pltpu.SemaphoreType.DMA,
         ],
-        compiler_params=pltpu.CompilerParams(vmem_limit_bytes=48 * 1024 * 1024),
+        compiler_params=pltpu.CompilerParams(
+            collective_id=3, has_side_effects=True, vmem_limit_bytes=48 * 1024 * 1024
+        ),
         name="backward",
     )(
         summed,
@@ -1016,14 +1106,14 @@
     tokens_ref, out_low_ref, gate_grad_ref, proj_grad_ref, weight_ref, gain_ref, grad_ref, sums_ref
 ):
     inner = gate_grad_ref.shape[1]
-    rest = weight_ref.shape[1] - inner
+    rest = weight_ref.shape[0] - inner
 
     @pl.when(pl.program_id(0) == 0)
     def _():
         sums_ref[...] = jnp.zeros_like(sums_ref)
 
-    normed_grad = mm_nt(gate_grad_ref[...], weight_ref[:, :inner]) + mm_nt(
-        proj_grad_ref[:, :rest], weight_ref[:, inner:]
+    normed_grad = mm(gate_grad_ref[...], weight_ref[:inner]) + mm(
+        proj_grad_ref[:, :rest], weight_ref[inner:]
     )
     values = tokens_ref[...].astype(F32)
     scale = lax.rsqrt(jnp.mean(values * values, axis=-1, keepdims=True) + EPS)
@@ -1116,6 +1206,122 @@
         compiler_params=pltpu.CompilerParams(vmem_limit_bytes=48 * 1024 * 1024),
         name="weight_gradient",
     )(out_low, normed, low, gate_grad, proj_grad)
+
+
+def piece_kernel(
+    counts, spot_ref, out_weight_ref, weight_ref, out_momentum_ref, momentum_ref, w_ref, m_ref, turned
+):
+    out_tiles, places, limit = counts
+    tile = pl.program_id(0) * places + spot_ref[0]
+    rows = m_ref.shape[1]
+    mine = pl.ds(pl.multiple_of(spot_ref[1] * rows, 16), rows)
+
+    @pl.when(tile < out_tiles)
+    def _():
+        turned[...] = jnp.transpose(out_weight_ref[...])
+        w_ref[0] = turned[mine]
+        m_ref[0] = out_momentum_ref[...]
+
+    @pl.when(tile >= out_tiles)
+    def _():
+        turned[...] = jnp.transpose(weight_ref[...])
+        w_ref[0] = turned[mine]
+        m_ref[0] = momentum_ref[...]
+
+
+def owned(spot, out_weight, weight_t, out_momentum_t, momentum, flows, places):
+    inner, model = out_weight.shape
+    rows, width = momentum.shape
+    out_tiles, in_tiles = inner // LANES, -(-width // LANES)
+
+    def out_at(f, spot):
+        return jnp.clip(f * places + spot[0], 0, out_tiles - 1)
+
+    def in_at(f, spot):
+        return jnp.clip(f * places + spot[0] - out_tiles, 0, in_tiles - 1)
+
+    piece = pl.BlockSpec((1, rows, LANES), lambda f, spot: (f, 0, 0))
+    return pl.pallas_call(
+        functools.partial(piece_kernel, (out_tiles, places, width)),
+        grid_spec=pltpu.PrefetchScalarGridSpec(
+            num_scalar_prefetch=1,
+            grid=(flows,),
+            in_specs=[
+                pl.BlockSpec((LANES, model), lambda f, spot: (out_at(f, spot), 0)),
+                pl.BlockSpec((LANES, model), lambda f, spot: (in_at(f, spot), 0)),
+                pl.BlockSpec((rows, LANES), lambda f, spot: (0, out_at(f, spot))),
+                pl.BlockSpec((rows, LANES), lambda f, spot: (0, in_at(f, spot))),
+            ],
+            out_specs=(piece, piece),
+            scratch_shapes=[pltpu.VMEM((model, LANES), BF16)],
+        ),
+        out_shape=(
+            jax.ShapeDtypeStruct((flows, rows, LANES), BF16),
+            jax.ShapeDtypeStruct((flows, rows, LANES), F32),
+        ),
+        name="owned",
+    )(spot, out_weight, weight_t, out_momentum_t, momentum)
+
+
+def finish_kernel(
+    out_steps,
+    gathered_ref,
+    out_momentum_ref,
+    momentum_ref,
+    out_weight_ref,
+    weight_ref,
+    new_out_momentum_ref,
+    new_momentum_ref,
+):
+    group, slots, rows, _ = gathered_ref.shape
+    step = pl.program_id(0)
+
+    def write(weights, old, new):
+        for i in range(group):
+            at = slice(i * LANES, (i + 1) * LANES)
+            tile = gathered_ref[i, : slots - 1].reshape((slots - 1) * rows, LANES)
+            weights[at] = jnp.transpose(tile)
+            new[:, at] = 0.5 * old[:, at] + gathered_ref[i, slots - 1].astype(F32)
+
+    @pl.when(step < out_steps)
+    def _():
+        write(out_weight_ref, out_momentum_ref, new_out_momentum_ref)
+
+    @pl.when(step >= out_steps)
+    def _():
+        write(weight_ref, momentum_ref, new_momentum_ref)
+
+
+def finish(gathered, out_momentum_t, momentum, group=4):
+    tiles, slots, rows, _ = gathered.shape
+    width, inner = momentum.shape[1], out_momentum_t.shape[1]
+    model = (slots - 1) * rows
+    wide = group * LANES
+    out_steps, in_steps = inner // wide, -(-width // wide)
+    out_at = lambda j: jnp.minimum(j, out_steps - 1)
+    in_at = lambda j: jnp.maximum(j - out_steps, 0)
+    by_column = [
+        pl.BlockSpec((rows, wide), lambda j: (0, out_at(j))),
+        pl.BlockSpec((rows, wide), lambda j: (0, in_at(j))),
+    ]
+    shape = jax.ShapeDtypeStruct
+    return pl.pallas_call(
+        functools.partial(finish_kernel, out_steps),
+        grid=(out_steps + in_steps,),
+        in_specs=[pl.BlockSpec((group, slots, rows, LANES), lambda j: (j, 0, 0, 0))] + by_column,
+        out_specs=[
+            pl.BlockSpec((wide, model), lambda j: (out_at(j), 0)),
+            pl.BlockSpec((wide, model), lambda j: (in_at(j), 0)),
+        ]
+        + by_column,
+        out_shape=(
+            shape((inner, model), BF16),
+            shape((width, model), BF16),
+            shape((rows, inner), F32),
+            shape((rows, width), F32),
+        ),
+        name="finish",
+    )(gathered, out_momentum_t, momentum)
 
 
 def local(
@@ -1160,25 +1366,6 @@
     halo = arrived[:, :, :model_width].reshape(seqs * HALO, model_width)
     early_seg = jnp.where(turn == 0, -1.0, arrived[:, :, model_width].astype(F32))
     seg_pad = jnp.concatenate([early_seg, seg], axis=1)
-
-    def same(other):
-        return (other == seg).astype(F32)
-
-    by_chunk = seg.reshape(seqs, piece // CHUNK, CHUNK)
-    before = seg_pad[:, HALO - 1 : HALO - 1 + piece].reshape(by_chunk.shape)[:, :, :1]
-    chunk_first = jnp.broadcast_to(before, by_chunk.shape).reshape(seqs, piece)
-    chunk_last = jnp.broadcast_to(by_chunk[:, :, -1:], by_chunk.shape).reshape(seqs, piece)
-    valid_float = valid_mask.astype(F32)
-    columns = [same(seg_pad[:, HALO - 3 + k : HALO - 3 + k + piece]) for k in range(4)] + [
-        same(chunk_first),
-        same(chunk_last),
-        same(early_seg[:, -1:]),
-        same(seg[:, -1:]),
-        seg,
-        valid_float,
-    ]
-    columns = columns + [jnp.zeros_like(seg)] * (16 - len(columns))
-    masks = jnp.stack(columns, axis=2).reshape(total, 16)
     seg_row = seg.reshape(1, total)
     heads_map = (
         lax.broadcasted_iota(jnp.int32, (LANES, inner_width), 0)
@@ -1189,18 +1376,21 @@
         return jnp.pad(values, (0, LANES - heads)).reshape(1, LANES)
 
     flat_tokens = tokens.reshape(total, model_width)
+    weight_t = jnp.transpose(in_weight)
+    out_momentum_t = jnp.transpose(out_momentum)
     flat_cot = cotangent.reshape(total, model_width)
     bias_row, decay_row = lanes(dt_bias), lanes(a_log)
     skip_row = jnp.repeat(skip_d, inner_width // heads).reshape(1, inner_width)
     gain_row = gate_gain.reshape(1, inner_width)
-    normed, gate, conv, conv_halo, summed, raw, cum, fresh, keep = front(
+    normed, masks, gate, conv, conv_halo, summed, raw, cum, fresh, keep = front(
         flat_tokens,
         halo,
         norm_gain.reshape(1, model_width),
-        in_weight,
+        weight_t,
         conv_weight,
         conv_bias.reshape(1, channels),
-        masks,
+        seg_pad,
+        valid_mask,
         bias_row,
         decay_row,
         heads_map,
@@ -1242,8 +1432,7 @@
         heads_map,
         sizes,
     )
-    rim_in = lax.ppermute(rim, "seq", [(b, a) for a, b in route])
-    fixed = (tail + rim_in.astype(F32)).astype(BF16)
+    fixed = (tail + rim.astype(F32)).astype(BF16)
     proj_grad = (
         proj_grad.reshape(seqs, piece, -1)
         .at[:, piece - 8 :, :channels]
@@ -1251,96 +1440,45 @@
         .reshape(total, -1)
     )
     input_grad, gain_sums = input_gradient(
-        flat_tokens, out_low, gate_grad, proj_grad, in_weight, norm_gain.reshape(1, model_width)
+        flat_tokens, out_low, gate_grad, proj_grad, weight_t, norm_gain.reshape(1, model_width)
     )
     grad_tiles = weight_gradient(out_low, normed, low, gate_grad, proj_grad)
     share_rows = model_width // pieces
-    width = inner_width + proj_width
     flows = -(-grad_tiles.shape[0] // places)
-    full = flows * places * LANES
     grad_tiles = jnp.pad(
         grad_tiles, ((0, flows * places - grad_tiles.shape[0]), (0, 0), (0, 0))
     )
     grads = grad_tiles.reshape(flows, places, pieces, share_rows, LANES)
-
-    def tiled(block):
-        spread_out = jnp.pad(block, ((0, 0), (0, full - width)))
-        return spread_out.reshape(-1, flows * places, LANES)
-
-    norm_gain_grad = gain_sums[0]
-    conv_weight_grad = conv_sums[:tap_count]
-    conv_bias_grad = conv_sums[tap_count]
-    dt_bias_grad = head_sums[0, :heads]
-    a_log_grad = head_sums[1, :heads]
-    gate_gain_grad = wide[0]
-    skip_grad = wide[1].reshape(heads, -1).sum(axis=1)
-    out_square = squares[0].sum()
-    mix_square = squares[1].sum()
-    valid_count = valid_float.sum()
-    step_float = step_number[0].astype(jnp.float32)
+    step_float = step_number[0].astype(F32)
     rate_now = learn_rate[0] * step_float / (step_float + 16.0)
-    first_row = lax.axis_index("seq") * share_rows
-    own_in = lax.dynamic_slice_in_dim(in_weight, first_row, share_rows, 0)
-    own_out = lax.dynamic_slice_in_dim(out_weight, first_row, share_rows, 1)
-    place = lax.axis_index("dp")
-
-    def own_piece(out_rows, in_rows):
-        block = tiled(jnp.concatenate([jnp.transpose(out_rows), in_rows], axis=1))
-        block = block.reshape(share_rows, flows, places, LANES)
-        return jnp.transpose(lax.dynamic_index_in_dim(block, place, 2, False), (1, 0, 2))
-
-    parts = (
-        norm_gain_grad,
-        conv_weight_grad,
-        conv_bias_grad,
-        dt_bias_grad,
-        a_log_grad,
-        skip_grad,
-        gate_gain_grad,
-        out_square,
-        mix_square,
-        valid_count,
+    spot = jnp.stack([lax.axis_index("dp"), turn]).astype(jnp.int32)
+    own_weight, own_momentum = owned(
+        spot, out_weight, weight_t, out_momentum_t, in_momentum, flows, places
     )
-    flat = jnp.concatenate([p.reshape(-1) for p in parts])
-    small_rows = -(-flat.shape[0] // (8 * LANES)) * 8
-    small = jnp.pad(flat, (0, small_rows * LANES - flat.shape[0])).reshape(small_rows, LANES)
-    gathered, small_total = exchange(
-        rate_now.reshape(1), grads, own_piece(own_out, own_in), own_piece(out_momentum, in_momentum), small
+    gathered, totals = exchange(
+        rate_now.reshape(1),
+        grads,
+        own_weight,
+        own_momentum,
+        (conv_sums, wide, head_sums, gain_sums, squares),
     )
-
-    def untiled(block):
-        return block.reshape(-1, full)[:, :width]
-
-    summed = untiled(
-        gathered[:, :, pieces].reshape(flows * places, share_rows, LANES).transpose(1, 0, 2)
-    ).astype(jnp.float32)
-    new_in_momentum = 0.5 * in_momentum + summed[:, inner_width:]
-    new_out_momentum = 0.5 * out_momentum + jnp.transpose(summed[:, :inner_width])
-    new_weights = untiled(
-        gathered[:, :, :pieces]
-        .reshape(flows * places, pieces, share_rows, LANES)
-        .transpose(1, 2, 0, 3)
+    new_out_weight, new_weight_t, new_out_momentum_t, new_in_momentum = finish(
+        gathered.reshape(flows * places, pieces + 1, share_rows, LANES),
+        out_momentum_t,
+        in_momentum,
     )
-    new_in_weight = new_weights[:, inner_width:]
-    new_out_weight = jnp.transpose(new_weights[:, :inner_width])
-    flat_total = small_total.reshape(-1)
-    totals = []
-    at = 0
-    for p in parts:
-        totals.append(flat_total[at : at + p.size].reshape(p.shape))
-        at += p.size
-    (
-        norm_gain_total,
-        conv_weight_total,
-        conv_bias_total,
-        dt_bias_total,
-        a_log_total,
-        skip_total,
-        gate_gain_total,
-        out_square_total,
-        mix_square_total,
-        valid_total,
-    ) = totals
+    new_in_weight = jnp.transpose(new_weight_t)
+    new_out_momentum = jnp.transpose(new_out_momentum_t)
+    conv_weight_total = totals[:tap_count]
+    conv_bias_total = totals[tap_count]
+    gate_gain_total = totals[5, :inner_width]
+    skip_total = totals[6, :inner_width].reshape(heads, -1).sum(axis=1)
+    norm_gain_total = totals[7, :model_width]
+    dt_bias_total = totals[5, inner_width : inner_width + heads]
+    a_log_total = totals[6, inner_width : inner_width + heads]
+    out_square_total = totals[5, inner_width + LANES :].sum()
+    mix_square_total = totals[6, inner_width + LANES :].sum()
+    valid_total = totals[7, inner_width + LANES + 9]
     denominator = jnp.maximum(valid_total, 1.0) * model_width
     output_rms = jnp.sqrt(out_square_total / denominator).reshape(1)
     mixer_rms = jnp.sqrt(mix_square_total / denominator).reshape(1)

time: 382 us -> 318 us (0.83)
  local copies, waits for them, and re-layouts: 84.5 us -> 12.8 us
  Pallas kernels: 267 us -> 289 us
  other arithmetic: 11.3 us -> 3.56 us
    unnamed x70 -> x26, local copies, waits for them, and re-layouts: 39.2 us -> 0.08 us
    slice x17 -> x5, local copies, waits for them, and re-layouts: 28.8 us -> 6.97 us  [the longest x1 1.51 us: local(): gate_gain_total = totals[5, :inner_width]]
    pallas_call x0 -> x2, Pallas kernels: none -> 17.8 us  [the longest x1 12.5 us: finish(): pl.pallas_call(functools.partial(finish_kernel, out_steps), grid=(out_ste...]
    dynamic_slice x3 -> x0, local copies, waits for them, and re-layouts: 6.25 us -> none  [the longest x1 3.76 us: local(): own_in = lax.dynamic_slice_in_dim(in_weight, first_row, share_rows, 0)]
  transfers between devices with their start and end apart: 2 -> 1, of which waited for: 1 -> 0; matrix products, arithmetic and copies ran while one was open for 7% -> 1% of each run, Pallas kernels for 0% -> 2%
where the time goes in v3:
time: 318 us; the launch traced here: 317 us
  Pallas kernels  289 us (91%)
  local copies, waits for them, and re-layouts  12.8 us (4%)
  between operations  6.53 us (2%)
  starting transfers between devices  4.92 us (2%)
  other arithmetic  3.56 us (1%)
    pallas_call x1, Pallas kernels, exchange(): pl.pallas_call(functools.partial(exchange_kernel, bits, pieces, flows), o...  127 us
    pallas_call x2, Pallas kernels, chain(): pl.pallas_call(functools.partial(chain_kernel, ways, blocks), out_shape=j...  33.4 us
    pallas_call x1, Pallas kernels, forward(): pl.pallas_call(functools.partial(forward_kernel, sizes, chunks), grid=(se...  33.4 us
    pallas_call x1, Pallas kernels, backward(): pl.pallas_call(functools.partial(backward_kernel, sizes, chunks), grid=(s...  32.2 us
    pallas_call x1, Pallas kernels, front(): pl.pallas_call(functools.partial(front_kernel, sizes), grid=(gate_blocks...  22 us
    pallas_call x1, Pallas kernels, weight_gradient(): pl.pallas_call(functools.partial(weight_kernel, (low_count, gate_count)),...  14.9 us
    pallas_call x1, Pallas kernels, finish(): pl.pallas_call(functools.partial(finish_kernel, out_steps), grid=(out_ste...  12.5 us
    pallas_call x1, Pallas kernels, input_gradient(): pl.pallas_call(input_kernel, grid=(total // block,), in_specs=[rows(model...  8.05 us
  transfers between devices with their start and end apart: 1, of which 0 were waited for; matrix products, arithmetic and copies ran while one was open for 1% of the time, Pallas kernels for 2%

profile of v3, /device:TPU:0, one launch (start us, length us, event | category | flops | bytes accessed | tf_op | source)
XLA Modules:
  0.0 316.8 jit_solution(1270631226675722288)
XLA Ops:
  0.6 0.7 convert_element_type.41.seg_row_ref
  1.3 0.1 fusion.6
  1.4 0.7 slice.71
  2.1 0.1 broadcast_in_dim.13
  2.2 4.9 %collective-permute-start = (bf16[1,16,896]{2,1,0:T(8,128)(2,1)S(1)}, bf16[1,16,896]{2,1,0:T(8,128)(2,1)S(1)}, u32[]{:S(2)}, u32[]{:S(2)}) collective-permute-start(bf16[1,16,896]{2,1,0:T(8,128)(2,1)S(1)} %pad_maximum_fusion), channel_id=1, source_target_pairs={{0,1},{1,2},{2,3},{4,5},{5,6},{6,7},{8,9},{9,10},{10,11},{12,13},{... | collective-permute-start | bytes 86024 | tf_op jit(solution)/shard_map/ppermute | solution.py:1365
  7.2 0.7 pad_bitcast_fusion
  7.9 0.1 fusion.heads_ref
  7.9 0.6 pad_add_fusion.spot_ref
  8.5 0.7 reshape.154.gain_ref
  9.2 0.7 reshape.155.bias_ref
  9.9 0.7 broadcast_in_dim.15
  10.6 0.1 reshape_reshape.9.skip_ref
  10.7 0.7 reshape.159.gain_ref
  12.8 0.0 copy-start.1
  12.8 0.0 copy-start.6
  12.8 0.0 copy-start.12
  12.8 5.3 %owned.1 = (bf16[5,192,128]{2,1,0:T(8,128)(2,1)}, f32[5,192,128]{2,1,0:T(8,128)}) custom-call(s32[2]{0:T(128)} %pad_add_fusion.spot_ref, bf16[1536,768]{1,0:T(8,128)(2,1)} %out_weight_ref.1, bf16[3352,768]{1,0:T(8,128)(2,1)} %bitcast.36, f32[192,1536]{1,0:T(8,128)} %bitcast.41, f32[192,3352]{1,0:T(8,128)} %momentum_ref.3), custom_call_target="tpu_custom_call" | custom-call | tf_op jit(solution)/shard_map/owned/pallas_call | solution.py:1244
  18.1 0.0 collective-permute-done
  18.1 0.1 select_reduce_fusion
  18.2 0.1 pad_maximum_fusion.1.seg_ref
  18.3 0.0 copy-done.1
  18.3 0.0 copy-done.6
  18.3 0.0 copy-start.5
  18.3 22.0 %front.1 = (bf16[512,768]{1,0:T(8,128)(2,1)S(1)}, f32[512,16]{1,0:T(8,128)S(1)}, f32[512,1536]{1,0:T(8,128)}, f32[512,1792]{1,0:T(8,128)}, f32[16,1792]{1,0:T(8,...) custom-call(bf16[512,768]{1,0:T(8,128)(2,1)S(1)} %bitcast.32, ...), custom_call_target="tpu_custom_call" | custom-call | tf_op jit(solution)/shard_map/front/pallas_call | solution.py:437
  40.4 9.8 %chain.2.incoming_ref = f32[1,128,1536]{2,1,0:T(8,128)S(1)} custom-call(f32[1,128,1536]{2,1,0:T(8,128)S(1)} %get-tuple-element.67.own_ref, f32[1,8,1536]{2,1,0:T(8,128)S(1)} %get-tuple-element.68.keep_ref), custom_call_target="tpu_custom_call" | custom-call | tf_op jit(solution)/shard_map/chain/pallas_call | solution.py:551
  50.2 0.0 copy-done.5
  50.2 33.4 %forward.1 = (bf16[512,768]{1,0:T(8,128)(2,1)}, bf16[512,1536]{1,0:T(8,128)(2,1)}, bf16[512,768]{1,0:T(8,128)(2,1)S(1)}, bf16[512,1536]{1,0:T(8,128)(2,1)}, f32[...) custom-call(f32[512,1792]{1,0:T(8,128)} %get-tuple-element.62.summed, ...), custom_call_target="tpu_custom_call" | custom-call | tf_op jit(solution)/shard_map/forward/pallas_call | solution.py:748
  83.6 0.0 copy-start.4
  83.6 23.6 %chain.3.later_ref = f32[1,128,1536]{2,1,0:T(8,128)S(1)} custom-call(f32[1,128,1536]{2,1,0:T(8,128)S(1)} %get-tuple-element.74.own_ref, f32[1,8,1536]{2,1,0:T(8,128)S(1)} %get-tuple-element.68.keep_ref), custom_call_target="tpu_custom_call" | custom-call | tf_op jit(solution)/shard_map/chain/pallas_call | solution.py:551
  107.2 32.2 %backward.1 = (bf16[512,2048]{1,0:T(8,128)(2,1)S(1)}, f32[1,8,1792]{2,1,0:T(8,128)S(1)}, bf16[1,8,1792]{2,1,0:T(8,128)(2,1)S(1)}, f32[8,1792]{1,0:T(8,128)S(1)}, f32[8,128]{1,0:T(8,128)S(1)}) custom-call(f32[512,1792]{1,0:T(8,128)} %get-tuple-element.62.summed_ref, f32[512,1792]{1,0:T(8,128)} %get-tuple-element.72.conv_ref, ...), custom_call_target="tpu_custom_call" | custom-call | tf_op jit(solution)/shard_map/backward/pallas_call | solution.py:1035
  139.5 0.0 copy-start.7
  139.5 0.0 copy-start.11
  139.5 0.0 copy-start
  139.5 0.0 copy-start.3
  139.5 8.0 %input_gradient.1 = (bf16[512,768]{1,0:T(8,128)(2,1)}, f32[8,768]{1,0:T(8,128)S(1)}) custom-call(bf16[512,768]{1,0:T(8,128)(2,1)S(1)} %bitcast.34, bf16[512,768]{1,0:T(8,128)(2,1)S(1)} %get-tuple-element.70.out_low_ref, bf16[512,1536]{1,0:T(8,128)(2,1)S(1)} %copy-done.2, bf16[512,2048]{1,0:T(8,128)(2,1)S(1)} %fusion.2.proj_grad_ref, ...), custom_call_target="tpu_custom_call" | custom-call | tf_op jit(solution)/shard_map/input_gradient/pallas_call | solution.py:1135
  147.6 0.0 copy-start.9
  147.6 14.9 %weight_gradient.1 = bf16[40,768,128]{2,1,0:T(8,128)(2,1)} custom-call(bf16[512,768]{1,0:T(8,128)(2,1)S(1)} %get-tuple-element.70.out_low_ref, bf16[512,768]{1,0:T(8,128)(2,1)S(1)} %get-tuple-element.82.normed_ref, bf16[512,1536]{1,0:T(8,128)(2,1)S(1)} %copy-done.3, bf16[512,1536]{1,0:T(8,128)(2,1)S(1)} %copy-done.2, bf16[512,2048]{1,0:T(8,128)(2,1)} %copy-done), custom_call_target="tpu_custom_call" | custom-call | tf_op jit(solution)/shard_map/weight_gradient/pallas_call | solution.py:1191
  162.6 127.1 %exchange.1 = (bf16[5,2,2,2,5,192,128]{6,5,4,3,2,1,0:T(8,128)(2,1)}, f32[8,1792]{1,0:T(8,128)}) custom-call(f32[1]{0:T(128)S(6)} %div.25.rate_ref, bf16[5,2,2,2,4,192,128]{6,5,4,3,2,1,0:T(8,128)(2,1)} %bitcast.39, bf16[5,192,128]{2,1,0:T(8,128)(2,1)} %get-tuple-element.84.weight_ref, f32[5,192,128]{2,1,0:T(8,128)} %get-tuple-element.85.momentum_ref, ...), custom_call_target="tpu_custom_call" | custom-call | tf_op jit(solution)/shard_map/exchange/pallas_call | solution.py:217
  289.7 1.3 slice.83
  290.9 1.4 slice_reduce_fusion.4
  292.3 1.5 slice_reduce_fusion.1
  293.8 1.4 slice.76
  295.2 1.4 slice_reduce_fusion
  296.6 1.3 slice_reduce_fusion.3
  298.0 1.3 slice_bitcast_fusion.1
  301.3 12.5 %finish.1 = (bf16[1536,768]{1,0:T(8,128)(2,1)}, bf16[3352,768]{1,0:T(8,128)(2,1)}, f32[192,1536]{1,0:T(8,128)}, f32[192,3352]{1,0:T(8,128)}) custom-call(bf16[40,5,192,128]{3,2,1,0:T(8,128)(2,1)} %bitcast.40, f32[192,1536]{1,0:T(8,128)} %bitcast.42, f32[192,3352]{1,0:T(8,128)} %momentum_ref.3), custom_call_target="tpu_custom_call" | custom-call | tf_op jit(solution)/shard_map/finish/pallas_call | solution.py:1308
  313.8 0.1 reshape_squeeze.3
  313.9 0.6 reduce_sum.27
  (18 shorter events, 0.1 us)
Async XLA Ops:
  2.2 15.9 %collective-permute-start = (bf16[1,16,896]{2,1,0:T(8,128)(2,1)S(1)}, bf16[1,16,896]{2,1,0:T(8,128)(2,1)S(1)}, u32[]{:S(2)}, u32[]{:S(2)}) collective-permute-start(bf16[1,16,896]{2,1,0:T(8,128)(2,1)S(1)} %pad_maximum_fusion), channel_id=1, source_target_pairs={{0,1},{1,2},{2,3},{4,5},{5,6},{6,7},{8,9},{9,10},{10,11},{12,13},{... | collective-permute-start | bytes 86024 | tf_op jit(solution)/shard_map/ppermute | solution.py:1365
  12.8 5.5 %copy-start.1 = (bf16[1,512,768]{2,1,0:T(8,128)(2,1)S(1)}, bf16[1,512,768]{2,1,0:T(8,128)(2,1)}, u32[]{:S(2)}) copy-start(bf16[1,512,768]{2,1,0:T(8,128)(2,1)} %param.20) | copy-start | bytes 2359300
  12.8 5.5 %copy-start.6 = (f32[4,1792]{1,0:T(4,128)S(1)}, f32[4,1792]{1,0:T(4,128)}, u32[]{:S(2)}) copy-start(f32[4,1792]{1,0:T(4,128)} %taps_ref.3) | copy-start | bytes 86020
  12.8 5.5 %copy-start.12 = (s32[1,512]{1,0:T(1,128)S(1)}, s32[1,512]{1,0:T(1,128)}, u32[]{:S(2)}) copy-start(s32[1,512]{1,0:T(1,128)} %valid_ref.1) | copy-start | bytes 6148
  18.3 31.9 %copy-start.5 = (bf16[1,512,768]{2,1,0:T(8,128)(2,1)S(1)}, bf16[1,512,768]{2,1,0:T(8,128)(2,1)}, u32[]{:S(2)}) copy-start(bf16[1,512,768]{2,1,0:T(8,128)(2,1)} %param.21) | copy-start | bytes 2359300
  83.6 55.9 %copy-start.8 = (f32[8,1536]{1,0:T(8,128)}, f32[8,1536]{1,0:T(8,128)S(1)}, u32[]{:S(2)}) copy-start(f32[8,1536]{1,0:T(8,128)S(1)} %get-tuple-element.87.wide_ref) | copy-start | bytes 147460
  83.6 55.9 %copy-start.10 = (f32[8,128]{1,0:T(8,128)}, f32[8,128]{1,0:T(8,128)S(1)}, u32[]{:S(2)}) copy-start(f32[8,128]{1,0:T(8,128)S(1)} %get-tuple-element.90.squares_ref) | copy-start | bytes 12292
  83.6 23.6 %copy-start.4 = (bf16[4,128,1536]{2,1,0:T(8,128)(2,1)S(1)}, bf16[4,128,1536]{2,1,0:T(8,128)(2,1)}, u32[]{:S(2)}) copy-start(bf16[4,128,1536]{2,1,0:T(8,128)(2,1)} %get-tuple-element.76.starts_ref) | copy-start | bytes 4718596
  107.2 32.3 %copy-start.2 = (bf16[512,1536]{1,0:T(8,128)(2,1)S(1)}, bf16[512,1536]{1,0:T(8,128)(2,1)}, u32[]{:S(2)}) copy-start(bf16[512,1536]{1,0:T(8,128)(2,1)} %get-tuple-element.71.gate_grad_ref) | copy-start | bytes 4718596
  139.5 8.1 %copy-start.7 = (f32[8,1792]{1,0:T(8,128)}, f32[8,1792]{1,0:T(8,128)S(1)}, u32[]{:S(2)}) copy-start(f32[8,1792]{1,0:T(8,128)S(1)} %get-tuple-element.86.conv_sums_ref) | copy-start | bytes 172036
  139.5 8.1 %copy-start.11 = (f32[8,128]{1,0:T(8,128)}, f32[8,128]{1,0:T(8,128)S(1)}, u32[]{:S(2)}) copy-start(f32[8,128]{1,0:T(8,128)S(1)} %get-tuple-element.88.head_sums_ref) | copy-start | bytes 12292
  139.5 8.1 %copy-start = (bf16[512,2048]{1,0:T(8,128)(2,1)}, bf16[512,2048]{1,0:T(8,128)(2,1)S(1)}, u32[]{:S(2)}) copy-start(bf16[512,2048]{1,0:T(8,128)(2,1)S(1)} %fusion.2.proj_grad_ref) | copy-start | bytes 6291460
  139.5 8.1 %copy-start.3 = (bf16[512,1536]{1,0:T(8,128)(2,1)S(1)}, bf16[512,1536]{1,0:T(8,128)(2,1)}, u32[]{:S(2)}) copy-start(bf16[512,1536]{1,0:T(8,128)(2,1)} %get-tuple-element.83.low_ref) | copy-start | bytes 4718596
  147.6 15.0 %copy-start.9 = (f32[8,768]{1,0:T(8,128)}, f32[8,768]{1,0:T(8,128)S(1)}, u32[]{:S(2)}) copy-start(f32[8,768]{1,0:T(8,128)S(1)} %get-tuple-element.89.gain_sums_ref) | copy-start | bytes 73732

commit v4 on v3

--- a/solution.py
+++ b/solution.py
@@ -7,250 +7,203 @@
 from jax.experimental.pallas import tpu as pltpu
 from jax.sharding import PartitionSpec as P
 
-LANES = 128
-
-
-def exchange_kernel(
-    bits,
-    pieces,
-    flows,
-    rate_ref,
-    grad_ref,
-    weight_ref,
-    momentum_ref,
-    conv_sums_ref,
-    wide_ref,
-    head_sums_ref,
-    gain_sums_ref,
-    squares_ref,
-    gathered_ref,
-    small_out_ref,
-    *scratch,
-):
-    halves = scratch[:bits]
-    (piece_parts, small_acc, small_in, small_parts) = scratch[bits : bits + 4]
-    (rs_send, rs_recv, zs_send, zs_recv, zg_send, zg_recv, ag_send, ag_recv) = scratch[
-        bits + 4 : bits + 12
-    ]
-    (sm_send, sm_recv, sz_send, sz_recv) = scratch[bits + 12 :]
-    place = lax.axis_index("dp")
-    turn = lax.axis_index("seq")
-    own = [(place // (1 << b)) % 2 for b in range(bits)]
-    partner = [{"dp": place + (1 - 2 * own[b]) * (1 << b)} for b in range(bits)]
-    others = [{"seq": (turn + j) % pieces} for j in range(pieces)]
-
-    def order_of(f):
-        rest = list(range(1, bits))
-        shift = f % max(len(rest), 1)
-        return ([0] if bits else []) + rest[shift:] + rest[:shift]
-
-    def index_of(fixed):
-        return tuple(fixed.get(b, slice(None)) for b in range(bits - 1, -1, -1))
-
-    barrier = pltpu.get_barrier_semaphore()
-    for target in partner + others[1:]:
-        pl.semaphore_signal(
-            barrier, inc=1, device_id=target, device_id_type=pl.DeviceIdType.MESH
-        )
-    pl.semaphore_wait(barrier, bits + pieces - 1)
-
-    def remote(src, dst, send, recv, target):
-        return pltpu.make_async_remote_copy(
-            src_ref=src,
-            dst_ref=dst,
-            send_sem=send,
-            recv_sem=recv,
-            device_id=target,
-            device_id_type=pl.DeviceIdType.MESH,
-        )
-
-    def held(f, k, other):
-        order = order_of(f)
-        bit = order[k]
-        value = 1 - own[bit] if other else own[bit]
-        if k == 0:
-            return grad_ref.at[(f,) + index_of({bit: value})]
-        free = [b for b in range(bits - 1, -1, -1) if b not in order[:k]]
-        return halves[k - 1].at[
-            (f,) + tuple(value if b == bit else slice(None) for b in free)
-        ]
-
-    def rs_copy(f, k):
-        return remote(
-            held(f, k, True),
-            halves[k].at[f],
-            rs_send.at[f, k],
-            rs_recv.at[f, k],
-            partner[order_of(f)[k]],
-        )
-
-    def rs_add(f, k):
-        kept = held(f, k, False)
-        into = halves[k].at[f]
-        left = bits - k - 1
-        for count in range(1 << left):
-            spot = tuple((count >> (left - 1 - i)) & 1 for i in range(left))
-
-            def body(p, carry):
-                into[spot + (p,)] = (
-                    kept[spot + (p,)].astype(jnp.float32)
-                    + into[spot + (p,)].astype(jnp.float32)
-                ).astype(jnp.bfloat16)
-                return carry
-
-            lax.fori_loop(0, pieces, body, 0)
-
-    mine = index_of({b: own[b] for b in range(bits)})
-
-    def zs_copy(f, j):
-        return remote(
-            halves[bits - 1].at[f, lax.rem(turn + j, pieces)],
-            piece_parts.at[f, j],
-            zs_send.at[f, j],
-            zs_recv.at[f, j],
-            others[j],
-        )
-
-    def zg_copy(f, j):
-        spot = gathered_ref.at[(f,) + mine + (turn,)]
-        return remote(spot, spot, zg_send.at[f, j], zg_recv.at[f, j], others[j])
-
-    def ag_copy(f, k):
-        order = order_of(f)
-        fixed = {order[i]: own[order[i]] for i in range(k + 1)}
-        spot = gathered_ref.at[(f,) + index_of(fixed)]
-        return remote(spot, spot, ag_send.at[f, k], ag_recv.at[f, k], partner[order[k]])
-
-    def sm_copy(k):
-        return remote(small_acc.at[k], small_in.at[k], sm_send.at[k], sm_recv.at[k], partner[k])
-
-    def sz_copy(j):
-        return remote(
-            small_acc.at[bits], small_parts.at[turn], sz_send.at[j], sz_recv.at[j], others[j]
-        )
-
-    def begin(f, k):
-        if k < bits:
-            rs_copy(f, k).start()
-        else:
-            for j in range(1, pieces):
-                zs_copy(f, j).start()
-
-    def begin_back(f, k):
-        if k >= 0:
-            ag_copy(f, k).start()
-
-    inner, model = wide_ref.shape[1], gain_sums_ref.shape[1]
-    small_acc[0, 0:5] = conv_sums_ref[0:5]
-    small_acc[0, 5:7, :inner] = wide_ref[0:2]
-    small_acc[0, 5:7, inner : inner + 128] = head_sums_ref[0:2]
-    small_acc[0, 5:8, inner + 128 :] = squares_ref[0:3]
-    small_acc[0, 7:8, :model] = gain_sums_ref[0:1]
-    small_acc[0, 7:8, model : inner + 128] = jnp.zeros((1, inner + 128 - model), jnp.float32)
-    if bits:
-        sm_copy(0).start()
-    for f in range(flows):
-        begin(f, 0)
-    for k in range(bits):
-        sm_copy(k).wait_recv()
-        small_acc[k + 1] = small_acc[k] + small_in[k]
-        if k + 1 < bits:
-            sm_copy(k + 1).start()
-        else:
-            for j in range(1, pieces):
-                sz_copy(j).start()
-        for f in range(flows):
-            rs_copy(f, k).wait_recv()
-            rs_add(f, k)
-            begin(f, k + 1)
-    small_parts[turn] = small_acc[bits]
-    rate = rate_ref[0]
-    for f in range(flows):
-        for j in range(1, pieces):
-            zs_copy(f, j).wait_recv()
-        total = halves[bits - 1][f, turn].astype(jnp.float32)
-        for j in range(1, pieces):
-            total = total + piece_parts[f, j].astype(jnp.float32)
-        summed = total.astype(jnp.bfloat16)
-        gathered_ref[(f,) + mine + (pieces,)] = summed
-        moved = 0.5 * momentum_ref[f] + summed.astype(jnp.float32)
-        gathered_ref[(f,) + mine + (turn,)] = (
-            weight_ref[f].astype(jnp.float32) - rate * moved
-        ).astype(jnp.bfloat16)
-        for j in range(1, pieces):
-            zg_copy(f, j).start()
-    for j in range(1, pieces):
-        sz_copy(j).wait_recv()
-    whole = small_parts[0]
-    for j in range(1, pieces):
-        whole = whole + small_parts[j]
-    small_out_ref[...] = whole
-    for f in range(flows):
-        for j in range(1, pieces):
-            zg_copy(f, j).wait_recv()
-        begin_back(f, bits - 1)
-    for k in range(bits - 1, -1, -1):
-        for f in range(flows):
-            ag_copy(f, k).wait_recv()
-            begin_back(f, k - 1)
-    for k in range(bits):
-        sm_copy(k).wait_send()
-        for f in range(flows):
-            rs_copy(f, k).wait_send()
-            ag_copy(f, k).wait_send()
-    for j in range(1, pieces):
-        sz_copy(j).wait_send()
-        for f in range(flows):
-            zs_copy(f, j).wait_send()
-            zg_copy(f, j).wait_send()
-
-
-def exchange(rate, grads, weights, momenta, sums):
-    flows, places, pieces, rows, _ = grads.shape
-    bits = places.bit_length() - 1
-    assert places == 1 << bits and bits >= 1 and pieces >= 2
-    twos = (2,) * bits
-    grads = grads.reshape((flows,) + twos + (pieces, rows, LANES))
-    small = sums[0].shape
-    vmem = pl.BlockSpec(memory_space=pltpu.VMEM)
-    dma = pltpu.SemaphoreType.DMA
-    gathered, small_out = pl.pallas_call(
-        functools.partial(exchange_kernel, bits, pieces, flows),
-        out_shape=(
-            jax.ShapeDtypeStruct((flows,) + twos + (pieces + 1, rows, LANES), jnp.bfloat16),
-            jax.ShapeDtypeStruct(small, jnp.float32),
-        ),
-        in_specs=[pl.BlockSpec(memory_space=pltpu.SMEM)] + [vmem] * 8,
-        out_specs=(vmem, vmem),
-        scratch_shapes=[
-            pltpu.VMEM((flows,) + twos[k + 1 :] + (pieces, rows, LANES), jnp.bfloat16)
-            for k in range(bits)
-        ]
-        + [
-            pltpu.VMEM((flows, pieces, rows, LANES), jnp.bfloat16),
-            pltpu.VMEM((bits + 1,) + small, jnp.float32),
-            pltpu.VMEM((bits,) + small, jnp.float32),
-            pltpu.VMEM((pieces,) + small, jnp.float32),
-        ]
-        + [dma((flows, bits))] * 2
-        + [dma((flows, pieces))] * 4
-        + [dma((flows, bits))] * 2
-        + [dma((bits,))] * 2
-        + [dma((pieces,))] * 2,
-        compiler_params=pltpu.CompilerParams(
-            collective_id=0, has_side_effects=True, vmem_limit_bytes=56 * 1024 * 1024
-        ),
-        name="exchange",
-    )(rate, grads, weights, momenta, *sums)
-    return gathered.reshape(flows, places, pieces + 1, rows, LANES), small_out
-
-
 CHUNK = 128
 HALO = 16
 GATE_BLOCK = 256
 EPS = 1e-05
 NEGATIVE = -1e30
 F32, BF16 = jnp.float32, jnp.bfloat16
+LANES = 128
+MESH = pl.DeviceIdType.MESH
+
+
+def remote(src, dst, send, recv, target):
+    return pltpu.make_async_remote_copy(
+        src_ref=src,
+        dst_ref=dst,
+        send_sem=send,
+        recv_sem=recv,
+        device_id=target,
+        device_id_type=MESH,
+    )
+
+
+def greet(targets):
+    barrier = pltpu.get_barrier_semaphore()
+    for target in targets:
+        pl.semaphore_signal(barrier, inc=1, device_id=target, device_id_type=MESH)
+    pl.semaphore_wait(barrier, len(targets))
+
+
+class Exchange:
+    def __init__(self, bits, pieces, flows):
+        self.bits, self.pieces, self.flows = bits, pieces, flows
+        self.parts = 2 if pieces % 2 == 0 else 1
+        self.place, self.turn = lax.axis_index("dp"), lax.axis_index("seq")
+        self.own = [(self.place // (1 << b)) % 2 for b in range(bits)]
+        self.partner = [
+            {"dp": self.place + (1 - 2 * self.own[b]) * (1 << b)} for b in range(bits)
+        ]
+        self.others = [{"seq": lax.rem(self.turn + j, pieces)} for j in range(pieces)]
+        self.mine = self.index_of({b: self.own[b] for b in range(bits)})
+
+    def index_of(self, fixed):
+        return tuple(fixed.get(b, slice(None)) for b in range(self.bits - 1, -1, -1))
+
+    def order_of(self, f, h):
+        rest = list(range(1, self.bits))
+        shift = (f + h) % max(len(rest), 1)
+        return [0] + rest[shift:] + rest[:shift]
+
+    def share(self, h, extra=0):
+        half = self.pieces // self.parts
+        return pl.ds(h * half, half + (extra if h == self.parts - 1 else 0))
+
+    def held(self, f, h, k, other):
+        order = self.order_of(f, h)
+        bit = order[k]
+        value = 1 - self.own[bit] if other else self.own[bit]
+        free = [b for b in range(self.bits - 1, -1, -1) if b not in order[:k]]
+        source = self.grad if k == 0 else self.halves[k - 1]
+        return source.at[
+            (f,) + tuple(value if b == bit else slice(None) for b in free) + (self.share(h),)
+        ]
+
+    def landing(self, f, h, k):
+        free = self.bits - k - 1
+        return self.halves[k].at[(f,) + (slice(None),) * free + (self.share(h),)]
+
+    def rs_copy(self, f, h, k):
+        return remote(
+            self.held(f, h, k, True),
+            self.landing(f, h, k),
+            self.rs_send.at[f, h, k],
+            self.rs_recv.at[f, h, k],
+            self.partner[self.order_of(f, h)[k]],
+        )
+
+    def rs_begin(self, k, flow=None):
+        for f in range(self.flows) if flow is None else (flow,):
+            for h in range(self.parts):
+                self.rs_copy(f, h, k).start()
+
+    def rs_end(self, k, then=None):
+        for f in range(self.flows):
+            for h in range(self.parts):
+                self.rs_copy(f, h, k).wait_recv()
+                kept, into = self.held(f, h, k, False), self.landing(f, h, k)
+                left = self.bits - k - 1
+                for count in range(1 << left):
+                    spot = tuple((count >> (left - 1 - i)) & 1 for i in range(left))
+
+                    def body(p, carry, spot=spot, kept=kept, into=into):
+                        into[spot + (p,)] = (
+                            kept[spot + (p,)].astype(F32) + into[spot + (p,)].astype(F32)
+                        ).astype(BF16)
+                        return carry
+
+                    lax.fori_loop(0, self.pieces // self.parts, body, 0)
+                if k + 1 < self.bits and then:
+                    self.rs_copy(f, h, k + 1).start()
+            if k + 1 == self.bits and then:
+                self.zs_begin(f)
+
+    def rs_done(self, k):
+        for f in range(self.flows):
+            for h in range(self.parts):
+                self.rs_copy(f, h, k).wait_send()
+
+    def zs_copy(self, f, j):
+        return remote(
+            self.halves[self.bits - 1].at[f, lax.rem(self.turn + j, self.pieces)],
+            self.piece_parts.at[f, j],
+            self.zs_send.at[f, j],
+            self.zs_recv.at[f, j],
+            self.others[j],
+        )
+
+    def zs_begin(self, flow=None):
+        for f in range(self.flows) if flow is None else (flow,):
+            for j in range(1, self.pieces):
+                self.zs_copy(f, j).start()
+
+    def zs_end(self, rate, weight, momentum, put):
+        for f in range(self.flows):
+            for j in range(1, self.pieces):
+                self.zs_copy(f, j).wait_recv()
+            total = self.halves[self.bits - 1][f, self.turn].astype(F32)
+            for j in range(1, self.pieces):
+                total = total + self.piece_parts[f, j].astype(F32)
+            summed = total.astype(BF16)
+            moved = 0.5 * momentum[f] + summed.astype(F32)
+            put(f, summed, (weight[f].astype(F32) - rate * moved).astype(BF16))
+
+    def zs_done(self):
+        for f in range(self.flows):
+            for j in range(1, self.pieces):
+                self.zs_copy(f, j).wait_send()
+
+    def put(self, f, summed, updated):
+        self.gathered[(f,) + self.mine + (self.pieces,)] = summed
+        self.gathered[(f,) + self.mine + (self.turn,)] = updated
+
+    def zg_copy(self, f, j):
+        spot = self.gathered.at[(f,) + self.mine + (self.turn,)]
+        return remote(spot, spot, self.zg_send.at[f, j], self.zg_recv.at[f, j], self.others[j])
+
+    def zg_begin(self, flow=None):
+        for f in range(self.flows) if flow is None else (flow,):
+            for j in range(1, self.pieces):
+                self.zg_copy(f, j).start()
+
+    def zg_end(self):
+        for f in range(self.flows):
+            for j in range(1, self.pieces):
+                self.zg_copy(f, j).wait_recv()
+            for h in range(self.parts):
+                self.ag_copy(f, h, self.bits - 1).start()
+
+    def zg_done(self):
+        for f in range(self.flows):
+            for j in range(1, self.pieces):
+                self.zg_copy(f, j).wait_send()
+
+    def ag_copy(self, f, h, k):
+        order = self.order_of(f, h)
+        fixed = {order[i]: self.own[order[i]] for i in range(k + 1)}
+        spot = self.gathered.at[(f,) + self.index_of(fixed) + (self.share(h, 1),)]
+        return remote(
+            spot,
+            spot,
+            self.ag_send.at[f, h, k],
+            self.ag_recv.at[f, h, k],
+            self.partner[order[k]],
+        )
+
+    def ag_end(self, k):
+        for f in range(self.flows):
+            for h in range(self.parts):
+                self.ag_copy(f, h, k).wait_recv()
+                if k > 0:
+                    self.ag_copy(f, h, k - 1).start()
+
+    def ag_done(self):
+        for k in range(self.bits):
+            for f in range(self.flows):
+                for h in range(self.parts):
+                    self.ag_copy(f, h, k).wait_send()
+
+
+def dma_semaphores(*shape):
+    return [pltpu.SemaphoreType.DMA(shape)] * 2
+
+
+def part_count(pieces):
+    return 2 if pieces % 2 == 0 else 1
+
+
+def half_shape(bits, pieces, flows, rows, k):
+    return (flows,) + (2,) * (bits - k - 1) + (pieces, rows, LANES)
 
 
 def mm(a, b):
@@ -803,27 +756,30 @@
 
 def backward_kernel(
     sizes,
-    chunks,
-    summed_ref,
-    conv_ref,
-    halo_ref,
-    raw_ref,
-    cum_ref,
-    masks_ref,
-    seg_row_ref,
+    dims,
+    rate_ref,
+    summed_all,
+    conv_all,
+    halo_all,
+    raw_all,
+    cum_all,
+    masks_all,
+    seg_row_all,
     later_ref,
-    ssm_grad_ref,
-    starts_ref,
-    dot_ref,
+    ssm_grad_all,
+    starts_all,
+    dot_all,
     taps_ref,
     a_log_ref,
     skip_ref,
     heads_ref,
-    proj_grad_ref,
-    tail_ref,
-    rim_ref,
+    half_ref,
+    weight_ref,
+    momentum_ref,
+    proj_grad_all,
     conv_sums_ref,
     head_sums_ref,
+    piece_ref,
     state_grad,
     after,
     active,
@@ -833,238 +789,231 @@
     all_grad,
     rims,
     rims_in,
-    rim_send,
-    rim_recv,
+    tails_out,
+    *scratch,
 ):
     seqs, piece, inner, channels, heads = sizes
-    n, c = pl.program_id(0), pl.program_id(1)
-    turn, pieces = lax.axis_index("seq"), lax.axis_size("seq")
-    barrier = pltpu.get_barrier_semaphore()
-    rim_copy = pltpu.make_async_remote_copy(
-        src_ref=rims,
-        dst_ref=rims_in,
-        send_sem=rim_send,
-        recv_sem=rim_recv,
-        device_id={"seq": lax.rem(turn + pieces - 1, pieces)},
-        device_id_type=pl.DeviceIdType.MESH,
+    bits, pieces, flows = dims
+    chunks = piece // CHUNK
+    ex = Exchange(bits, pieces, flows)
+    ex.halves = [half_ref] + list(scratch[: bits - 1])
+    (ex.piece_parts, ex.rs_send, ex.rs_recv, ex.zs_send, ex.zs_recv) = scratch[bits - 1 : bits + 4]
+    rim_send, rim_recv = scratch[bits + 4 :]
+    turn = ex.turn
+    rim_copy = remote(
+        rims, rims_in, rim_send, rim_recv, {"seq": lax.rem(turn + pieces - 1, pieces)}
     )
-
-    @pl.when((c == 0) & (n == 0) & (turn < pieces - 1))
-    def _():
-        pl.semaphore_signal(
-            barrier, inc=1, device_id={"seq": turn + 1}, device_id_type=pl.DeviceIdType.MESH
-        )
-
-    @pl.when((c == 0) & (n == 0) & (turn > 0))
-    def _():
-        pl.semaphore_wait(barrier, 1)
-
-    @pl.when((c == 0) & (n == 0))
-    def _():
-        conv_sums_ref[...] = jnp.zeros_like(conv_sums_ref)
-        head_sums_ref[...] = jnp.zeros_like(head_sums_ref)
-
-    @pl.when(c == 0)
-    def _():
-        state_grad[...] = later_ref[0]
-        after[...] = jnp.zeros_like(after)
-
-    def activate(i, carry):
-        rows = pl.ds(pl.multiple_of(i * 16, 16), 16)
-        values = summed_ref[rows]
-        active[rows] = values * sigmoid(values)
-        return carry
-
-    lax.fori_loop(0, CHUNK // 16, activate, 0)
-    lane = lax.broadcasted_iota(jnp.int32, (CHUNK, 128), 1)
-    raw = raw_ref[...]
-    steps = jnp.where(lane < heads, softplus(raw), 0.0)
-    cum = cum_ref[...]
-    cum_t = jnp.transpose(cum)
-    final = cum[CHUNK - 1 :]
-    enter = jnp.exp(cum) * masks_ref[:, 4:5]
-    tails = jnp.exp(final - cum) * masks_ref[:, 5:6]
-    for i, block in enumerate((steps, enter, tails)):
-        factors[i] = spread(block, heads_ref)
-    writer = active[:, inner : inner + 128]
-    reader = active[:, inner + 128 : inner + 256]
-    scores = scores_of(reader, writer)
-    bias = mask_bias(masks_ref[:, 8:9], seg_row_ref[0:1])
-    half = lax.broadcasted_iota(jnp.int32, (CHUNK, 128), 1) < 64
-    writer_low, reader_low = writer.astype(BF16), reader.astype(BF16)
-    reader_t = jnp.transpose(reader_low)
-    later = state_grad[...].astype(BF16)
-    kept = jnp.exp(final) * masks_ref[CHUNK - 1 :, 4:5]
-    kept = spread(jnp.broadcast_to(kept, (8, 128)), heads_ref)[0:1]
-    scores_grad = jnp.zeros((CHUNK, CHUNK), F32)
-    reader_grad = jnp.zeros((CHUNK, 128), F32)
-    writer_grad = jnp.zeros((CHUNK, 128), F32)
-    skip = skip_ref[...]
-    for pair in range(heads // 2):
-        at = slice(pair * 128, (pair + 1) * 128)
-        signal = active[:, at]
-        step_x = factors[0, :, at]
-        moved = (signal * step_x).astype(BF16)
-        grad = ssm_grad_ref[:, at]
-        grad_low = grad.astype(BF16)
-        zero = jnp.zeros_like(grad_low)
-        stacked = jnp.concatenate(
-            [jnp.where(half, grad_low, zero), jnp.where(half, zero, grad_low)], axis=0
-        )
-        both_grad = mm_nt(stacked, moved)
-        one = decays_of(cum, cum_t, bias, 2 * pair)
-        two = decays_of(cum, cum_t, bias, 2 * pair + 1)
-        scores_grad = scores_grad + both_grad[:CHUNK] * one + both_grad[CHUNK:] * two
-        both = jnp.concatenate([(scores * one).astype(BF16), (scores * two).astype(BF16)], axis=0)
-        tail_x = factors[2, :, at]
-        from_later = mm(writer_low, later[:, at])
-        total = mm_tn(both, stacked) + from_later * tail_x
-        weighted = (signal * step_x * tail_x).astype(BF16)
-        entered = (grad * factors[1, :, at]).astype(BF16)
-        start = starts_ref[0, :, at]
-        reader_grad = reader_grad + mm_nt(entered, start)
-        writer_grad = writer_grad + mm_nt(weighted, later[:, at])
-        passed = jnp.sum(start.astype(F32) * later[:, at].astype(F32), axis=0, keepdims=True)
-        factors[1, 0:1, at] = kept[:, at] * passed + jnp.sum(
-            moved.astype(F32) * (from_later * tail_x), axis=0, keepdims=True
-        )
-        state_grad[:, at] = state_grad[:, at] * kept[:, at] + mm(reader_t, entered)
-        moved_grad[:, at] = total * signal
-        factors[2, :, at] = total * moved.astype(F32)
-        all_grad[:, at] = total * step_x + skip[:, at] * grad
-    sh, sl = split(scores_grad)
-    reader_grad = reader_grad + mm(sh, writer_low) + mm(sl, writer_low)
-    writer_grad = writer_grad + mm_tn(sh, reader_low) + mm_tn(sl, reader_low)
-    all_grad[:, inner : inner + 128] = writer_grad
-    all_grad[:, inner + 128 : inner + 256] = reader_grad
-    step_grad = gather_heads(moved_grad[...], heads_ref)
-    change = dot_ref[...] - gather_heads(factors[2], heads_ref)
-    at_end = gather_heads(
-        jnp.broadcast_to(factors[1, 0:1], (8, inner)), heads_ref
-    )[0:1]
-    row = lax.broadcasted_iota(jnp.int32, (CHUNK, 128), 0)
-    change = change + jnp.where(row == CHUNK - 1, at_end, 0.0)
-    decay_grad = exact_mm(triangle(CHUNK, True), change)
-    rate = -jnp.exp(a_log_ref[...])
-    raw_grad = jnp.where(lane < heads, (step_grad + decay_grad * rate) * sigmoid(raw), 0.0)
-    head_sums_ref[0:1] += jnp.sum(raw_grad, axis=0, keepdims=True)
-    head_sums_ref[1:2] += jnp.sum(decay_grad * steps * rate, axis=0, keepdims=True)
-    proj_grad_ref[:, channels : channels + 128] = raw_grad.astype(BF16)
-    proj_grad_ref[:, channels + 128 :] = jnp.zeros((CHUNK, 128), BF16)
-
-    for block in range(channels // GATE_BLOCK):
-        at = slice(block * GATE_BLOCK, (block + 1) * GATE_BLOCK)
-        values = summed_ref[:, at]
-        turned = sigmoid(values)
-        grad = all_grad[:, at] * turned * (1.0 + values * (1.0 - turned))
-        conv_sums_ref[4:5, at] += jnp.sum(grad, axis=0, keepdims=True)
-        conv = conv_ref[:, at]
-        result = grad * taps_ref[3:4, at]
-        conv_sums_ref[3:4, at] += jnp.sum(grad * conv, axis=0, keepdims=True)
-        rim = jnp.zeros((8, GATE_BLOCK), F32)
-        shifted_rows[0:8] = jnp.zeros((8, GATE_BLOCK), F32)
-        for k in range(3):
-            shifted_rows[8 : 8 + CHUNK] = grad * masks_ref[:, k : k + 1]
-            shifted_rows[8 + CHUNK :] = after[k, :, at]
-            after[k, :, at] = shifted_rows[8:16]
-            here = shifted_rows[11 - k : 11 - k + CHUNK]
-            result = result + here * taps_ref[k : k + 1, at]
-            conv_sums_ref[k : k + 1, at] += jnp.sum(here * conv, axis=0, keepdims=True)
-            early = shifted_rows[3 - k : 11 - k]
-            rim = rim + early * taps_ref[k : k + 1, at]
+    greet(ex.partner[1:] + ex.others[1:])
+    conv_sums_ref[...] = jnp.zeros_like(conv_sums_ref)
+    head_sums_ref[...] = jnp.zeros_like(head_sums_ref)
+    slots = 2 * seqs * chunks
+    starts_at = [0, 3, 5] if (bits, slots) == (3, 8) else [i * slots // bits for i in range(bits)]
+
+    def begin(k):
+        if k < bits:
+            ex.rs_begin(k)
+        else:
+            ex.zs_begin()
+
+    def hook(spot):
+        for i, at in enumerate(starts_at):
+
+            @pl.when(spot == at)
+            def _(i=i):
+                if i > 0:
+                    ex.rs_end(i)
+                begin(i + 1)
+
+    def one_chunk(index, carry):
+        n, c = index // chunks, lax.rem(index, chunks)
+        spot = n * chunks + chunks - 1 - c
+        rows_at = pl.ds(pl.multiple_of(spot * CHUNK, CHUNK), CHUNK)
+        summed_ref, conv_ref = summed_all.at[rows_at], conv_all.at[rows_at]
+        halo_ref = halo_all.at[pl.ds(pl.multiple_of(n * HALO, HALO), HALO)]
+        raw_ref, cum_ref, masks_ref = raw_all.at[rows_at], cum_all.at[rows_at], masks_all.at[rows_at]
+        seg_row = seg_row_all[0:1, rows_at]
+        ssm_grad_ref, dot_ref = ssm_grad_all.at[rows_at], dot_all.at[rows_at]
+        starts_ref = starts_all.at[pl.ds(spot, 1)]
+        proj_grad_ref = proj_grad_all.at[rows_at]
+
+        @pl.when(c == 0)
+        def _():
+            state_grad[...] = later_ref[n]
+            after[...] = jnp.zeros_like(after)
+
+        def activate(i, carry):
+            rows = pl.ds(pl.multiple_of(i * 16, 16), 16)
+            values = summed_ref[rows]
+            active[rows] = values * sigmoid(values)
+            return carry
+
+        lax.fori_loop(0, CHUNK // 16, activate, 0)
+        lane = lax.broadcasted_iota(jnp.int32, (CHUNK, 128), 1)
+        raw = raw_ref[...]
+        steps = jnp.where(lane < heads, softplus(raw), 0.0)
+        cum = cum_ref[...]
+        cum_t = jnp.transpose(cum)
+        final = cum[CHUNK - 1 :]
+        enter = jnp.exp(cum) * masks_ref[:, 4:5]
+        tails = jnp.exp(final - cum) * masks_ref[:, 5:6]
+        for i, block in enumerate((steps, enter, tails)):
+            factors[i] = spread(block, heads_ref)
+        writer = active[:, inner : inner + 128]
+        reader = active[:, inner + 128 : inner + 256]
+        scores = scores_of(reader, writer)
+        bias = mask_bias(masks_ref[:, 8:9], seg_row)
+        half = lax.broadcasted_iota(jnp.int32, (CHUNK, 128), 1) < 64
+        writer_low, reader_low = writer.astype(BF16), reader.astype(BF16)
+        reader_t = jnp.transpose(reader_low)
+        later = state_grad[...].astype(BF16)
+        kept = jnp.exp(final) * masks_ref[CHUNK - 1 :, 4:5]
+        kept = spread(jnp.broadcast_to(kept, (8, 128)), heads_ref)[0:1]
+        scores_grad = jnp.zeros((CHUNK, CHUNK), F32)
+        reader_grad = jnp.zeros((CHUNK, 128), F32)
+        writer_grad = jnp.zeros((CHUNK, 128), F32)
+        skip = skip_ref[...]
+        hook(2 * index)
+        for pair in range(heads // 2):
+            if pair == heads // 4:
+                hook(2 * index + 1)
+            at = slice(pair * 128, (pair + 1) * 128)
+            signal = active[:, at]
+            step_x = factors[0, :, at]
+            moved = (signal * step_x).astype(BF16)
+            grad = ssm_grad_ref[:, at]
+            grad_low = grad.astype(BF16)
+            zero = jnp.zeros_like(grad_low)
+            stacked = jnp.concatenate(
+                [jnp.where(half, grad_low, zero), jnp.where(half, zero, grad_low)], axis=0
+            )
+            both_grad = mm_nt(stacked, moved)
+            one = decays_of(cum, cum_t, bias, 2 * pair)
+            two = decays_of(cum, cum_t, bias, 2 * pair + 1)
+            scores_grad = scores_grad + both_grad[:CHUNK] * one + both_grad[CHUNK:] * two
+            both = jnp.concatenate([(scores * one).astype(BF16), (scores * two).astype(BF16)], axis=0)
+            tail_x = factors[2, :, at]
+            from_later = mm(writer_low, later[:, at])
+            total = mm_tn(both, stacked) + from_later * tail_x
+            weighted = (signal * step_x * tail_x).astype(BF16)
+            entered = (grad * factors[1, :, at]).astype(BF16)
+            start = starts_ref[0, :, at]
+            reader_grad = reader_grad + mm_nt(entered, start)
+            writer_grad = writer_grad + mm_nt(weighted, later[:, at])
+            passed = jnp.sum(start.astype(F32) * later[:, at].astype(F32), axis=0, keepdims=True)
+            factors[1, 0:1, at] = kept[:, at] * passed + jnp.sum(
+                moved.astype(F32) * (from_later * tail_x), axis=0, keepdims=True
+            )
+            state_grad[:, at] = state_grad[:, at] * kept[:, at] + mm(reader_t, entered)
+            moved_grad[:, at] = total * signal
+            factors[2, :, at] = total * moved.astype(F32)
+            all_grad[:, at] = total * step_x + skip[:, at] * grad
+        sh, sl = split(scores_grad)
+        reader_grad = reader_grad + mm(sh, writer_low) + mm(sl, writer_low)
+        writer_grad = writer_grad + mm_tn(sh, reader_low) + mm_tn(sl, reader_low)
+        all_grad[:, inner : inner + 128] = writer_grad
+        all_grad[:, inner + 128 : inner + 256] = reader_grad
+        step_grad = gather_heads(moved_grad[...], heads_ref)
+        change = dot_ref[...] - gather_heads(factors[2], heads_ref)
+        at_end = gather_heads(
+            jnp.broadcast_to(factors[1, 0:1], (8, inner)), heads_ref
+        )[0:1]
+        row = lax.broadcasted_iota(jnp.int32, (CHUNK, 128), 0)
+        change = change + jnp.where(row == CHUNK - 1, at_end, 0.0)
+        decay_grad = exact_mm(triangle(CHUNK, True), change)
+        rate = -jnp.exp(a_log_ref[...])
+        raw_grad = jnp.where(lane < heads, (step_grad + decay_grad * rate) * sigmoid(raw), 0.0)
+        head_sums_ref[0:1] += jnp.sum(raw_grad, axis=0, keepdims=True)
+        head_sums_ref[1:2] += jnp.sum(decay_grad * steps * rate, axis=0, keepdims=True)
+        proj_grad_ref[:, channels : channels + 128] = raw_grad.astype(BF16)
+        proj_grad_ref[:, channels + 128 :] = jnp.zeros((CHUNK, 128), BF16)
+
+        for block in range(channels // GATE_BLOCK):
+            at = slice(block * GATE_BLOCK, (block + 1) * GATE_BLOCK)
+            values = summed_ref[:, at]
+            turned = sigmoid(values)
+            grad = all_grad[:, at] * turned * (1.0 + values * (1.0 - turned))
+            conv_sums_ref[4:5, at] += jnp.sum(grad, axis=0, keepdims=True)
+            conv = conv_ref[:, at]
+            result = grad * taps_ref[3:4, at]
+            conv_sums_ref[3:4, at] += jnp.sum(grad * conv, axis=0, keepdims=True)
+            rim = jnp.zeros((8, GATE_BLOCK), F32)
+            shifted_rows[0:8] = jnp.zeros((8, GATE_BLOCK), F32)
+            for k in range(3):
+                shifted_rows[8 : 8 + CHUNK] = grad * masks_ref[:, k : k + 1]
+                shifted_rows[8 + CHUNK :] = after[k, :, at]
+                after[k, :, at] = shifted_rows[8:16]
+                here = shifted_rows[11 - k : 11 - k + CHUNK]
+                result = result + here * taps_ref[k : k + 1, at]
+                conv_sums_ref[k : k + 1, at] += jnp.sum(here * conv, axis=0, keepdims=True)
+                early = shifted_rows[3 - k : 11 - k]
+                rim = rim + early * taps_ref[k : k + 1, at]
+
+                @pl.when(c == chunks - 1)
+                def _():
+                    conv_sums_ref[k : k + 1, at] += jnp.sum(
+                        early * halo_ref[HALO - 8 :, at], axis=0, keepdims=True
+                    )
+
+            proj_grad_ref[:, at] = result.astype(BF16)
+
+            @pl.when(c == 0)
+            def _():
+                tails_out[n, :, at] = result[CHUNK - 8 :]
 
             @pl.when(c == chunks - 1)
             def _():
-                conv_sums_ref[k : k + 1, at] += jnp.sum(
-                    early * halo_ref[HALO - 8 :, at], axis=0, keepdims=True
-                )
-
-        proj_grad_ref[:, at] = result.astype(BF16)
-
-        @pl.when(c == 0)
-        def _():
-            tail_ref[0, :, at] = result[CHUNK - 8 :]
-
-        @pl.when(c == chunks - 1)
-        def _():
-            rims[n, :, at] = rim.astype(BF16)
-
-    @pl.when((c == chunks - 1) & (n == seqs - 1))
-    def _():
-        @pl.when(turn > 0)
-        def _():
-            rim_copy.start()
-            rim_copy.wait_send()
-
-        @pl.when(turn < pieces - 1)
-        def _():
-            rim_copy.wait_recv()
-            rim_ref[...] = rims_in[...]
-
-        @pl.when(turn == pieces - 1)
-        def _():
-            rim_ref[...] = jnp.zeros_like(rim_ref)
-
-
-def backward(
-    summed,
-    conv,
-    halo,
-    raw,
-    cum,
-    masks,
-    seg_row,
-    later,
-    ssm_grad,
-    starts,
-    dots,
-    taps,
-    a_log,
-    skip,
-    heads_map,
-    sizes,
-):
+                rims[n, :, at] = rim.astype(BF16)
+
+        return carry
+
+    lax.fori_loop(0, seqs * chunks, one_chunk, 0)
+
+    @pl.when(turn > 0)
+    def _():
+        rim_copy.start()
+
+    def put(f, summed, updated):
+        piece_ref[f, 0] = summed
+        piece_ref[f, 1] = updated
+
+    ex.zs_end(rate_ref[0], weight_ref, momentum_ref, put)
+
+    @pl.when(turn < pieces - 1)
+    def _():
+        rim_copy.wait_recv()
+        for n in range(seqs):
+            for at in range(0, channels, GATE_BLOCK):
+                columns = slice(at, at + GATE_BLOCK)
+                rows = slice((n + 1) * piece - 8, (n + 1) * piece)
+                proj_grad_all[rows, columns] = (
+                    tails_out[n, :, columns] + rims_in[n, :, columns].astype(F32)
+                ).astype(BF16)
+
+    @pl.when(turn > 0)
+    def _():
+        rim_copy.wait_send()
+
+    for k in range(1, bits):
+        ex.rs_done(k)
+    ex.zs_done()
+
+
+def backward(rate, inputs, half, weights, momenta, sizes, places, pieces):
     seqs, piece, inner, channels, heads = sizes
-    total = summed.shape[0]
-    chunks = piece // CHUNK
-    full = lambda *shape: pl.BlockSpec(shape, lambda n, c: (0,) * len(shape))
-    spot = lambda n, c: n * chunks + chunks - 1 - c
-    rows = lambda width: pl.BlockSpec((CHUNK, width), lambda n, c: (spot(n, c), 0))
-    each = lambda depth, width: pl.BlockSpec((1, depth, width), lambda n, c: (n, 0, 0))
+    total = inputs[0].shape[0]
+    bits = places.bit_length() - 1
+    flows, rows = half.shape[0], half.shape[-2]
+    vmem = pl.BlockSpec(memory_space=pltpu.VMEM)
     shape = jax.ShapeDtypeStruct
     return pl.pallas_call(
-        functools.partial(backward_kernel, sizes, chunks),
-        grid=(seqs, chunks),
-        in_specs=[
-            rows(channels),
-            rows(channels),
-            pl.BlockSpec((HALO, channels), lambda n, c: (n, 0)),
-            rows(128),
-            rows(128),
-            rows(16),
-            pl.BlockSpec((1, CHUNK), lambda n, c: (0, spot(n, c))),
-            each(128, inner),
-            rows(inner),
-            pl.BlockSpec((1, 128, inner), lambda n, c: (spot(n, c), 0, 0)),
-            rows(128),
-            full(4, channels),
-            full(1, 128),
-            full(1, inner),
-            full(128, inner),
-        ],
-        out_specs=(
-            rows(channels + 256),
-            each(8, channels),
-            pl.BlockSpec(memory_space=pltpu.VMEM),
-            full(8, channels),
-            full(8, 128),
-        ),
+        functools.partial(backward_kernel, sizes, (bits, pieces, flows)),
+        in_specs=[pl.BlockSpec(memory_space=pltpu.SMEM)] + [vmem] * (len(inputs) + 3),
+        out_specs=(vmem,) * 4,
         out_shape=(
             shape((total, channels + 256), BF16),
-            shape((seqs, 8, channels), F32),
-            shape((seqs, 8, channels), BF16),
             shape((8, channels), F32),
             shape((8, 128), F32),
+            shape((flows, 2, rows, LANES), BF16),
         ),
         scratch_shapes=[
             pltpu.VMEM((128, inner), F32),
@@ -1076,143 +1025,400 @@
             pltpu.VMEM((CHUNK, channels), F32),
             pltpu.VMEM((seqs, 8, channels), BF16),
             pltpu.VMEM((seqs, 8, channels), BF16),
-            pltpu.SemaphoreType.DMA,
-            pltpu.SemaphoreType.DMA,
-        ],
+            pltpu.VMEM((seqs, 8, channels), F32),
+        ]
+        + [
+            pltpu.VMEM(half_shape(bits, pieces, flows, rows, k), BF16) for k in range(1, bits)
+        ]
+        + [pltpu.VMEM((flows, pieces, rows, LANES), BF16)]
+        + dma_semaphores(flows, part_count(pieces), bits)
+        + dma_semaphores(flows, pieces)
+        + [pltpu.SemaphoreType.DMA] * 2,
         compiler_params=pltpu.CompilerParams(
             collective_id=3, has_side_effects=True, vmem_limit_bytes=48 * 1024 * 1024
         ),
         name="backward",
+    )(rate, *inputs, half, weights, momenta)
+
+
+def turn_kernel(
+    dims,
+    own_ref,
+    keep_ref,
+    out_low_ref,
+    normed_ref,
+    low_ref,
+    gate_grad_ref,
+    later_ref,
+    half_ref,
+    sent,
+    taken,
+    turned,
+    grad,
+    send,
+    recv,
+    rs_send,
+    rs_recv,
+):
+    bits, pieces, flows, blocks, real = dims
+    places = 1 << bits
+    ex = Exchange(bits, pieces, flows)
+    ex.grad, ex.halves = grad, [half_ref]
+    ex.rs_send, ex.rs_recv = rs_send, rs_recv
+    turn = ex.turn
+    first, final = turn == pieces - 1, turn == 0
+    ahead, behind = lax.rem(turn + pieces - 1, pieces), lax.rem(turn + 1, pieces)
+    barrier = pltpu.get_barrier_semaphore()
+    pl.semaphore_signal(barrier, inc=1, device_id=ex.partner[0], device_id_type=MESH)
+
+    @pl.when(jnp.logical_not(first))
+    def _():
+        pl.semaphore_signal(barrier, inc=1, device_id={"seq": behind}, device_id_type=MESH)
+
+    @pl.when(final)
+    def _():
+        pl.semaphore_wait(barrier, 1)
+
+    @pl.when(jnp.logical_not(final))
+    def _():
+        pl.semaphore_wait(barrier, 2)
+
+    width = own_ref.shape[2] // blocks
+    rows = grad.shape[-2]
+
+    def copy(c):
+        return remote(sent.at[c], taken.at[c], send.at[c], recv.at[c], {"seq": ahead})
+
+    @pl.when(first)
+    def _():
+        later_ref[...] = jnp.zeros_like(later_ref)
+        for c in range(blocks):
+            sent[c] = own_ref[:, :, c * width : (c + 1) * width].astype(BF16)
+            copy(c).start()
+
+    turned[0] = jnp.transpose(out_low_ref[...])
+    turned[1] = jnp.transpose(normed_ref[...])
+    low_tiles = low_ref.shape[1] // LANES
+
+    def store(tile, values):
+        f, d = tile // places, tile % places
+        spot = (f,) + tuple((d >> b) & 1 for b in range(bits - 1, -1, -1))
+        for p in range(pieces):
+            grad[spot + (p,)] = values[p * rows : (p + 1) * rows]
+
+    def tiles(tile):
+        if tile >= real:
+            result = jnp.zeros((pieces * rows, 2 * LANES), F32)
+        elif tile < low_tiles:
+            result = mm(turned[0], low_ref[:, tile * LANES : (tile + 2) * LANES])
+        else:
+            at = (tile - low_tiles) * LANES
+            result = mm(turned[1], gate_grad_ref[:, at : at + 2 * LANES])
+        result = result.astype(BF16)
+        store(tile, result[:, :LANES])
+        store(tile + 1, result[:, LANES:])
+
+    pairs = flows * places // 2
+    done = 0
+    for c in range(blocks):
+        until = pairs * (c + 1) // blocks
+        for pair in range(done, until):
+            tiles(2 * pair)
+            if (2 * pair + 2) % places == 0:
+                ex.rs_begin(0, (2 * pair) // places)
+        done = until
+
+        @pl.when(jnp.logical_not(first))
+        def _():
+            at = slice(c * width, (c + 1) * width)
+            copy(c).wait_recv()
+
+            @pl.when(jnp.logical_not(final))
+            def _():
+                sent[c] = (
+                    own_ref[:, :, at] + keep_ref[:, 0:1, at] * taken[c].astype(F32)
+                ).astype(BF16)
+                copy(c).start()
+
+            later_ref[:, :, at] = taken[c].astype(F32)
+
+    ex.rs_end(0)
+    ex.rs_done(0)
+
+    @pl.when(jnp.logical_not(final))
+    def _():
+        for c in range(blocks):
+            copy(c).wait_send()
+
+
+def turn_back(own, keep, out_low, normed, low, gate_grad, places, pieces, blocks=6):
+    seqs, depth, inner = own.shape
+    total, model = out_low.shape
+    bits = places.bit_length() - 1
+    assert places == 1 << bits and bits >= 1 and pieces >= 2
+    real = 2 * inner // LANES
+    flows = -(-real // places)
+    rows = model // pieces
+    vmem = pl.BlockSpec(memory_space=pltpu.VMEM)
+    part = (blocks, seqs, depth, inner // blocks)
+    return pl.pallas_call(
+        functools.partial(turn_kernel, (bits, pieces, flows, blocks, real)),
+        out_shape=(
+            jax.ShapeDtypeStruct(own.shape, F32),
+            jax.ShapeDtypeStruct(half_shape(bits, pieces, flows, rows, 0), BF16),
+        ),
+        in_specs=[vmem] * 6,
+        out_specs=(vmem, vmem),
+        scratch_shapes=[pltpu.VMEM(part, BF16)] * 2
+        + [
+            pltpu.VMEM((2, model, total), BF16),
+            pltpu.VMEM(half_shape(bits, pieces, flows, rows, -1), BF16),
+        ]
+        + dma_semaphores(blocks)
+        + dma_semaphores(flows, part_count(pieces), 1),
+        compiler_params=pltpu.CompilerParams(
+            collective_id=2, has_side_effects=True, vmem_limit_bytes=32 * 1024 * 1024
+        ),
+        name="turn_back",
+    )(own, keep, out_low, normed, low, gate_grad)
+
+
+def last_kernel(
+    dims,
+    rate_ref,
+    tokens_ref,
+    out_low_ref,
+    normed_ref,
+    gate_grad_ref,
+    proj_grad_ref,
+    weight_t_ref,
+    gain_ref,
+    piece_ref,
+    weight_ref,
+    momentum_ref,
+    conv_sums_ref,
+    wide_ref,
+    head_sums_ref,
+    squares_ref,
+    input_grad_ref,
+    gathered_a_ref,
+    gathered_b_ref,
+    small_out_ref,
+    *scratch,
+):
+    bits, pieces, flows_a, flows_b, real = dims
+    places = 1 << bits
+    a, b = Exchange(bits, pieces, flows_a), Exchange(bits, pieces, flows_b)
+    b.halves, scratch = scratch[:bits], scratch[bits:]
+    (b.grad, b.piece_parts, turned, gain_sums, small_acc, small_in, small_parts) = scratch[:7]
+    (b.rs_send, b.rs_recv, b.zs_send, b.zs_recv) = scratch[7:11]
+    (b.zg_send, b.zg_recv, b.ag_send, b.ag_recv) = scratch[11:15]
+    (a.zg_send, a.zg_recv, a.ag_send, a.ag_recv) = scratch[15:19]
+    (sm_send, sm_recv, sz_send, sz_recv) = scratch[19:]
+    a.gathered, b.gathered = gathered_a_ref, gathered_b_ref
+    turn = a.turn
+    rows = b.grad.shape[-2]
+    greet(a.partner + a.others[1:])
+
+    for f in range(flows_a):
+        a.put(f, piece_ref[f, 0], piece_ref[f, 1])
+        a.zg_begin(f)
+
+    turned[...] = jnp.transpose(normed_ref[...])
+
+    def tiles(tile):
+        if tile >= real:
+            result = jnp.zeros((pieces * rows, 2 * LANES), BF16)
+        else:
+            at = tile * LANES
+            result = mm(turned[...], proj_grad_ref[:, at : at + 2 * LANES]).astype(BF16)
+        for i in range(2):
+            f, d = (tile + i) // places, (tile + i) % places
+            spot = (f,) + tuple((d >> k) & 1 for k in range(bits - 1, -1, -1))
+            for p in range(pieces):
+                b.grad[spot + (p,)] = result[
+                    p * rows : (p + 1) * rows, i * LANES : (i + 1) * LANES
+                ]
+
+    for f in range(flows_b):
+        for d in range(0, places, 2):
+            tiles(f * places + d)
+        b.rs_begin(0, f)
+
+    inner = gate_grad_ref.shape[1]
+    rest = weight_t_ref.shape[0] - inner
+    gain_sums[...] = jnp.zeros_like(gain_sums)
+
+    def input_rows(i, carry):
+        at = pl.ds(pl.multiple_of(i * 128, 128), 128)
+        normed_grad = mm(gate_grad_ref[at], weight_t_ref[:inner]) + mm(
+            proj_grad_ref[at, :rest], weight_t_ref[inner:]
+        )
+        values = tokens_ref[at].astype(F32)
+        scale = lax.rsqrt(jnp.mean(values * values, axis=-1, keepdims=True) + EPS)
+        gain_sums[0:1] += jnp.sum(normed_grad * values * scale, axis=0, keepdims=True)
+        pushed = normed_grad * gain_ref[...]
+        inside = jnp.mean(pushed * values, axis=-1, keepdims=True)
+        input_grad_ref[at] = (
+            out_low_ref[at].astype(F32)
+            + scale * pushed
+            - values * (scale * scale * scale * inside)
+        ).astype(BF16)
+        return carry
+
+    blocks = tokens_ref.shape[0] // 128
+    lax.fori_loop(0, blocks // 2, input_rows, 0)
+    b.rs_end(0, then=True)
+    lax.fori_loop(blocks // 2, blocks, input_rows, 0)
+
+    def sm_copy(k):
+        return remote(
+            small_acc.at[k], small_in.at[k], sm_send.at[k], sm_recv.at[k], a.partner[k]
+        )
+
+    def sz_copy(j):
+        return remote(
+            small_acc.at[bits], small_parts.at[turn], sz_send.at[j], sz_recv.at[j], a.others[j]
+        )
+
+    model = gain_sums.shape[1]
+    small_acc[0, 0:5] = conv_sums_ref[0:5]
+    small_acc[0, 5:7, :inner] = wide_ref[0:2]
+    small_acc[0, 5:7, inner : inner + 128] = head_sums_ref[0:2]
+    small_acc[0, 5:8, inner + 128 :] = squares_ref[0:3]
+    small_acc[0, 7:8, :model] = gain_sums[0:1]
+    small_acc[0, 7:8, model : inner + 128] = jnp.zeros((1, inner + 128 - model), F32)
+    sm_copy(0).start()
+
+    def small_step(k):
+        sm_copy(k).wait_recv()
+        small_acc[k + 1] = small_acc[k] + small_in[k]
+        if k + 1 < bits:
+            sm_copy(k + 1).start()
+        else:
+            small_parts[turn] = small_acc[bits]
+            for j in range(1, pieces):
+                sz_copy(j).start()
+
+    a.zg_end()
+    for k in range(1, bits):
+        b.rs_end(k, then=True)
+        small_step(k - 1)
+        if k == 1:
+            a.ag_end(bits - 1)
+    small_step(bits - 1)
+
+    def put(f, summed, updated):
+        b.put(f, summed, updated)
+        b.zg_begin(f)
+
+    b.zs_end(rate_ref[0], weight_ref, momentum_ref, put)
+    for k in range(bits - 2, 0, -1):
+        a.ag_end(k)
+    b.zg_end()
+    for k in range(bits - 1, 0, -1):
+        b.ag_end(k)
+    for j in range(1, pieces):
+        sz_copy(j).wait_recv()
+    whole = small_parts[0]
+    for j in range(1, pieces):
+        whole = whole + small_parts[j]
+    small_out_ref[...] = whole
+    a.ag_end(0)
+    b.ag_end(0)
+    for k in range(bits):
+        sm_copy(k).wait_send()
+        b.rs_done(k)
+    for j in range(1, pieces):
+        sz_copy(j).wait_send()
+    b.zs_done()
+    for ex in (a, b):
+        ex.zg_done()
+        ex.ag_done()
+
+
+def last(
+    rate,
+    tokens,
+    out_low,
+    normed,
+    gate_grad,
+    proj_grad,
+    weight_t,
+    gain,
+    piece,
+    weights,
+    momenta,
+    sums,
+    places,
+    pieces,
+):
+    total, model = tokens.shape
+    bits = places.bit_length() - 1
+    real = proj_grad.shape[1] // LANES
+    flows_a, flows_b = piece.shape[0], weights.shape[0]
+    rows = model // pieces
+    small = sums[0].shape
+    parts = part_count(pieces)
+    vmem = pl.BlockSpec(memory_space=pltpu.VMEM)
+    shape = jax.ShapeDtypeStruct
+    gathered = lambda flows: (flows,) + (2,) * bits + (pieces + 1, rows, LANES)
+    sem = dma_semaphores
+    return pl.pallas_call(
+        functools.partial(last_kernel, (bits, pieces, flows_a, flows_b, real)),
+        out_shape=(
+            shape((total, model), BF16),
+            shape(gathered(flows_a), BF16),
+            shape(gathered(flows_b), BF16),
+            shape(small, F32),
+        ),
+        in_specs=[pl.BlockSpec(memory_space=pltpu.SMEM)] + [vmem] * 14,
+        out_specs=(vmem,) * 4,
+        scratch_shapes=[
+            pltpu.VMEM(half_shape(bits, pieces, flows_b, rows, k), BF16) for k in range(bits)
+        ]
+        + [
+            pltpu.VMEM(half_shape(bits, pieces, flows_b, rows, -1), BF16),
+            pltpu.VMEM((flows_b, pieces, rows, LANES), BF16),
+            pltpu.VMEM((model, total), BF16),
+            pltpu.VMEM((8, model), F32),
+            pltpu.VMEM((bits + 1,) + small, F32),
+            pltpu.VMEM((bits,) + small, F32),
+            pltpu.VMEM((pieces,) + small, F32),
+        ]
+        + sem(flows_b, parts, bits)
+        + sem(flows_b, pieces)
+        + sem(flows_b, pieces)
+        + sem(flows_b, parts, bits)
+        + sem(flows_a, pieces)
+        + sem(flows_a, parts, bits)
+        + sem(bits)
+        + sem(pieces),
+        compiler_params=pltpu.CompilerParams(
+            collective_id=0, has_side_effects=True, vmem_limit_bytes=48 * 1024 * 1024
+        ),
+        name="last",
     )(
-        summed,
-        conv,
-        halo,
-        raw,
-        cum,
-        masks,
-        seg_row,
-        later,
-        ssm_grad,
-        starts,
-        dots,
-        taps,
-        a_log,
-        skip,
-        heads_map,
+        rate,
+        tokens,
+        out_low,
+        normed,
+        gate_grad,
+        proj_grad,
+        weight_t,
+        gain,
+        piece,
+        weights,
+        momenta,
+        *sums,
     )
-
-
-def input_kernel(
-    tokens_ref, out_low_ref, gate_grad_ref, proj_grad_ref, weight_ref, gain_ref, grad_ref, sums_ref
-):
-    inner = gate_grad_ref.shape[1]
-    rest = weight_ref.shape[0] - inner
-
-    @pl.when(pl.program_id(0) == 0)
-    def _():
-        sums_ref[...] = jnp.zeros_like(sums_ref)
-
-    normed_grad = mm(gate_grad_ref[...], weight_ref[:inner]) + mm(
-        proj_grad_ref[:, :rest], weight_ref[inner:]
-    )
-    values = tokens_ref[...].astype(F32)
-    scale = lax.rsqrt(jnp.mean(values * values, axis=-1, keepdims=True) + EPS)
-    sums_ref[0:1] += jnp.sum(normed_grad * values * scale, axis=0, keepdims=True)
-    pushed = normed_grad * gain_ref[...]
-    inside = jnp.mean(pushed * values, axis=-1, keepdims=True)
-    grad_ref[...] = (
-        out_low_ref[...].astype(F32)
-        + scale * pushed
-        - values * (scale * scale * scale * inside)
-    ).astype(BF16)
-
-
-def input_gradient(tokens, out_low, gate_grad, proj_grad, weight, gain):
-    total, model = tokens.shape
-    block = 128
-    rows = lambda width: pl.BlockSpec((block, width), lambda i: (i, 0))
-    full = lambda *shape: pl.BlockSpec(shape, lambda i: (0,) * len(shape))
-    return pl.pallas_call(
-        input_kernel,
-        grid=(total // block,),
-        in_specs=[
-            rows(model),
-            rows(model),
-            rows(gate_grad.shape[1]),
-            rows(proj_grad.shape[1]),
-            full(*weight.shape),
-            full(1, model),
-        ],
-        out_specs=(rows(model), full(8, model)),
-        out_shape=(
-            jax.ShapeDtypeStruct((total, model), BF16),
-            jax.ShapeDtypeStruct((8, model), F32),
-        ),
-        compiler_params=pltpu.CompilerParams(vmem_limit_bytes=48 * 1024 * 1024),
-        name="input_gradient",
-    )(tokens, out_low, gate_grad, proj_grad, weight, gain)
-
-
-def weight_kernel(counts, out_low_ref, normed_ref, low_ref, gate_grad_ref, proj_grad_ref, grad_ref, turned):
-    low_count, gate_count = counts
-    step = pl.program_id(0)
-
-    @pl.when(step == 0)
-    def _():
-        turned[0] = jnp.transpose(out_low_ref[...])
-        turned[1] = jnp.transpose(normed_ref[...])
-
-    def put(result):
-        grad_ref[0] = result[:, :LANES].astype(BF16)
-        grad_ref[1] = result[:, LANES:].astype(BF16)
-
-    @pl.when(step < low_count)
-    def _():
-        put(mm(turned[0], low_ref[...]))
-
-    @pl.when((step >= low_count) & (step < low_count + gate_count))
-    def _():
-        put(mm(turned[1], gate_grad_ref[...]))
-
-    @pl.when(step >= low_count + gate_count)
-    def _():
-        put(mm(turned[1], proj_grad_ref[...]))
-
-
-def weight_gradient(out_low, normed, low, gate_grad, proj_grad):
-    total, model = normed.shape
-    wide = 2 * LANES
-    low_count, gate_count, proj_count = (a.shape[1] // wide for a in (low, gate_grad, proj_grad))
-    full = lambda *shape: pl.BlockSpec(shape, lambda j: (0,) * len(shape))
-
-    def columns(before, count):
-        return pl.BlockSpec((total, wide), lambda j: (0, jnp.clip(j - before, 0, count - 1)))
-
-    return pl.pallas_call(
-        functools.partial(weight_kernel, (low_count, gate_count)),
-        grid=(low_count + gate_count + proj_count,),
-        in_specs=[
-            full(total, model),
-            full(total, model),
-            columns(0, low_count),
-            columns(low_count, gate_count),
-            columns(low_count + gate_count, proj_count),
-        ],
-        out_specs=pl.BlockSpec((2, model, LANES), lambda j: (j, 0, 0)),
-        out_shape=jax.ShapeDtypeStruct(
-            (2 * (low_count + gate_count + proj_count), model, LANES), BF16
-        ),
-        scratch_shapes=[pltpu.VMEM((2, model, total), BF16)],
-        compiler_params=pltpu.CompilerParams(vmem_limit_bytes=48 * 1024 * 1024),
-        name="weight_gradient",
-    )(out_low, normed, low, gate_grad, proj_grad)
 
 
 def piece_kernel(
     counts, spot_ref, out_weight_ref, weight_ref, out_momentum_ref, momentum_ref, w_ref, m_ref, turned
 ):
-    out_tiles, places, limit = counts
-    tile = pl.program_id(0) * places + spot_ref[0]
+    out_tiles, tile_of = counts
+    tile = tile_of(pl.program_id(0), spot_ref)
     rows = m_ref.shape[1]
     mine = pl.ds(pl.multiple_of(spot_ref[1] * rows, 16), rows)
 
@@ -1229,20 +1435,27 @@
         m_ref[0] = momentum_ref[...]
 
 
-def owned(spot, out_weight, weight_t, out_momentum_t, momentum, flows, places):
+def owned(spot, out_weight, weight_t, out_momentum_t, momentum, flows_a, flows_b, places):
     inner, model = out_weight.shape
     rows, width = momentum.shape
     out_tiles, in_tiles = inner // LANES, -(-width // LANES)
 
+    flows = flows_a + flows_b
+
+    def tile_of(f, spot):
+        early = jnp.minimum(f * places + spot[0], 2 * out_tiles - 1)
+        late = 2 * out_tiles + (f - flows_a) * places + spot[0]
+        return jnp.where(f < flows_a, early, late)
+
     def out_at(f, spot):
-        return jnp.clip(f * places + spot[0], 0, out_tiles - 1)
+        return jnp.clip(tile_of(f, spot), 0, out_tiles - 1)
 
     def in_at(f, spot):
-        return jnp.clip(f * places + spot[0] - out_tiles, 0, in_tiles - 1)
+        return jnp.clip(tile_of(f, spot) - out_tiles, 0, in_tiles - 1)
 
     piece = pl.BlockSpec((1, rows, LANES), lambda f, spot: (f, 0, 0))
     return pl.pallas_call(
-        functools.partial(piece_kernel, (out_tiles, places, width)),
+        functools.partial(piece_kernel, (out_tiles, tile_of)),
         grid_spec=pltpu.PrefetchScalarGridSpec(
             num_scalar_prefetch=1,
             grid=(flows,),
@@ -1265,7 +1478,8 @@
 
 def finish_kernel(
     out_steps,
-    gathered_ref,
+    gathered_a_ref,
+    gathered_b_ref,
     out_momentum_ref,
     momentum_ref,
     out_weight_ref,
@@ -1273,10 +1487,10 @@
     new_out_momentum_ref,
     new_momentum_ref,
 ):
-    group, slots, rows, _ = gathered_ref.shape
+    group, slots, rows, _ = gathered_a_ref.shape
     step = pl.program_id(0)
 
-    def write(weights, old, new):
+    def write(gathered_ref, weights, old, new):
         for i in range(group):
             at = slice(i * LANES, (i + 1) * LANES)
             tile = gathered_ref[i, : slots - 1].reshape((slots - 1) * rows, LANES)
@@ -1285,15 +1499,19 @@
 
     @pl.when(step < out_steps)
     def _():
-        write(out_weight_ref, out_momentum_ref, new_out_momentum_ref)
-
-    @pl.when(step >= out_steps)
-    def _():
-        write(weight_ref, momentum_ref, new_momentum_ref)
-
-
-def finish(gathered, out_momentum_t, momentum, group=4):
-    tiles, slots, rows, _ = gathered.shape
+        write(gathered_a_ref, out_weight_ref, out_momentum_ref, new_out_momentum_ref)
+
+    @pl.when((step >= out_steps) & (step < 2 * out_steps))
+    def _():
+        write(gathered_a_ref, weight_ref, momentum_ref, new_momentum_ref)
+
+    @pl.when(step >= 2 * out_steps)
+    def _():
+        write(gathered_b_ref, weight_ref, momentum_ref, new_momentum_ref)
+
+
+def finish(gathered_a, gathered_b, out_momentum_t, momentum, group=4):
+    _, slots, rows, _ = gathered_a.shape
     width, inner = momentum.shape[1], out_momentum_t.shape[1]
     model = (slots - 1) * rows
     wide = group * LANES
@@ -1308,7 +1526,15 @@
     return pl.pallas_call(
         functools.partial(finish_kernel, out_steps),
         grid=(out_steps + in_steps,),
-        in_specs=[pl.BlockSpec((group, slots, rows, LANES), lambda j: (j, 0, 0, 0))] + by_column,
+        in_specs=[
+            pl.BlockSpec(
+                (group, slots, rows, LANES), lambda j: (jnp.minimum(j, 2 * out_steps - 1), 0, 0, 0)
+            ),
+            pl.BlockSpec(
+                (group, slots, rows, LANES), lambda j: (jnp.maximum(j - 2 * out_steps, 0), 0, 0, 0)
+            ),
+        ]
+        + by_column,
         out_specs=[
             pl.BlockSpec((wide, model), lambda j: (out_at(j), 0)),
             pl.BlockSpec((wide, model), lambda j: (in_at(j), 0)),
@@ -1321,7 +1547,7 @@
             shape((rows, width), F32),
         ),
         name="finish",
-    )(gathered, out_momentum_t, momentum)
+    )(gathered_a, gathered_b, out_momentum_t, momentum)
 
 
 def local(
@@ -1413,57 +1639,61 @@
         heads_map,
         sizes,
     )
-    later = chain(state_grad, keep, -1)
-    proj_grad, tail, rim, conv_sums, head_sums = backward(
-        summed,
-        conv,
-        conv_halo,
-        raw,
-        cum,
-        masks,
-        seg_row,
-        later,
-        ssm_grad,
-        starts,
-        dots,
-        conv_weight,
-        decay_row,
-        skip_row,
-        heads_map,
+    later, half = turn_back(state_grad, keep, out_low, normed, low, gate_grad, places, pieces)
+    step_float = step_number[0].astype(F32)
+    rate = (learn_rate[0] * step_float / (step_float + 16.0)).reshape(1)
+    flows_a = half.shape[0]
+    flows_b = -(-(channels + 2 * LANES) // (LANES * places))
+    spot = jnp.stack([lax.axis_index("dp"), turn]).astype(jnp.int32)
+    weights, momenta = owned(
+        spot, out_weight, weight_t, out_momentum_t, in_momentum, flows_a, flows_b, places
+    )
+    proj_grad, conv_sums, head_sums, piece_a = backward(
+        rate,
+        (
+            summed,
+            conv,
+            conv_halo,
+            raw,
+            cum,
+            masks,
+            seg_row,
+            later,
+            ssm_grad,
+            starts,
+            dots,
+            conv_weight,
+            decay_row,
+            skip_row,
+            heads_map,
+        ),
+        half,
+        weights[:flows_a],
+        momenta[:flows_a],
         sizes,
+        places,
+        pieces,
     )
-    fixed = (tail + rim.astype(F32)).astype(BF16)
-    proj_grad = (
-        proj_grad.reshape(seqs, piece, -1)
-        .at[:, piece - 8 :, :channels]
-        .set(fixed)
-        .reshape(total, -1)
+    input_grad, gathered_a, gathered_b, totals = last(
+        rate,
+        flat_tokens,
+        out_low,
+        normed,
+        gate_grad,
+        proj_grad,
+        weight_t,
+        norm_gain.reshape(1, model_width),
+        piece_a,
+        weights[flows_a:],
+        momenta[flows_a:],
+        (conv_sums, wide, head_sums, squares),
+        places,
+        pieces,
     )
-    input_grad, gain_sums = input_gradient(
-        flat_tokens, out_low, gate_grad, proj_grad, weight_t, norm_gain.reshape(1, model_width)
-    )
-    grad_tiles = weight_gradient(out_low, normed, low, gate_grad, proj_grad)
-    share_rows = model_width // pieces
-    flows = -(-grad_tiles.shape[0] // places)
-    grad_tiles = jnp.pad(
-        grad_tiles, ((0, flows * places - grad_tiles.shape[0]), (0, 0), (0, 0))
-    )
-    grads = grad_tiles.reshape(flows, places, pieces, share_rows, LANES)
-    step_float = step_number[0].astype(F32)
-    rate_now = learn_rate[0] * step_float / (step_float + 16.0)
-    spot = jnp.stack([lax.axis_index("dp"), turn]).astype(jnp.int32)
-    own_weight, own_momentum = owned(
-        spot, out_weight, weight_t, out_momentum_t, in_momentum, flows, places
-    )
-    gathered, totals = exchange(
-        rate_now.reshape(1),
-        grads,
-        own_weight,
-        own_momentum,
-        (conv_sums, wide, head_sums, gain_sums, squares),
-    )
+    share = (pieces + 1, model_width // pieces, LANES)
     new_out_weight, new_weight_t, new_out_momentum_t, new_in_momentum = finish(
-        gathered.reshape(flows * places, pieces + 1, share_rows, LANES),
+        gathered_a.reshape((-1,) + share),
+        gathered_b.reshape((-1,) + share),
         out_momentum_t,
         in_momentum,
     )

time: 318 us -> 273 us (0.86)
  Pallas kernels: 289 us -> 244 us
    pallas_call x2 -> x1, Pallas kernels: 33.4 us -> 9.83 us  [chain(): pl.pallas_call(functools.partial(chain_kernel, ways, blocks), out_shape=j...]
    pallas_call x5 -> x4, Pallas kernels: 188 us -> 166 us  [the longest x1 85.2 us: last(): pl.pallas_call(functools.partial(last_kernel, (bits, pieces, flows_a, flo...]
    unnamed x26 -> x27, local copies, waits for them, and re-layouts: 0.08 us -> 5.14 us
    slice x0 -> x4, local copies, waits for them, and re-layouts: none -> 3.75 us  [the longest x1 0.98 us: local(): momenta[:flows_a]]
  transfers between devices with their start and end apart: 1 -> 1, of which waited for: 0 -> 0; matrix products, arithmetic and copies ran while one was open for 1% -> 2% of each run, Pallas kernels for 2% -> 2%
where the time goes in v4:
time: 273 us; the launch traced here: 272 us
  Pallas kernels  244 us (89%)
  local copies, waits for them, and re-layouts  14.3 us (5%)
  between operations  6.5 us (2%)
  starting transfers between devices  4.92 us (2%)
  other arithmetic  2.79 us (1%)
    pallas_call x1, Pallas kernels, last(): pl.pallas_call(functools.partial(last_kernel, (bits, pieces, flows_a, flo...  85.2 us
    pallas_call x1, Pallas kernels, backward(): pl.pallas_call(functools.partial(backward_kernel, sizes, (bits, pieces, f...  47.6 us
    pallas_call x1, Pallas kernels, forward(): pl.pallas_call(functools.partial(forward_kernel, sizes, chunks), grid=(se...  33.3 us
    pallas_call x1, Pallas kernels, turn_back(): pl.pallas_call(functools.partial(turn_kernel, (bits, pieces, flows, block...  28 us
    pallas_call x1, Pallas kernels, front(): pl.pallas_call(functools.partial(front_kernel, sizes), grid=(gate_blocks...  22 us
    pallas_call x1, Pallas kernels, finish(): pl.pallas_call(functools.partial(finish_kernel, out_steps), grid=(out_ste...  12.4 us
    pallas_call x1, Pallas kernels, chain(): pl.pallas_call(functools.partial(chain_kernel, ways, blocks), out_shape=j...  9.83 us
  transfers between devices with their start and end apart: 1, of which 0 were waited for; matrix products, arithmetic and copies ran while one was open for 2% of the time, Pallas kernels for 2%

profile of v4, /device:TPU:0, one launch (start us, length us, event | category | flops | bytes accessed | tf_op | source)
XLA Modules:
  0.0 272.0 jit_solution(3958906352635477614)
XLA Ops:
  0.6 0.7 convert_element_type.35.seg_row_ref.seg_row_all
  1.3 0.1 fusion.4
  1.4 0.7 slice.55
  2.1 0.1 broadcast_in_dim.13
  2.2 4.9 %collective-permute-start = (bf16[1,16,896]{2,1,0:T(8,128)(2,1)S(1)}, bf16[1,16,896]{2,1,0:T(8,128)(2,1)S(1)}, u32[]{:S(2)}, u32[]{:S(2)}) collective-permute-start(bf16[1,16,896]{2,1,0:T(8,128)(2,1)S(1)} %pad_maximum_fusion), channel_id=1, source_target_pairs={{0,1},{1,2},{2,3},{4,5},{5,6},{6,7},{8,9},{9,10},{10,11},{12,13},{... | collective-permute-start | bytes 86024 | tf_op jit(solution)/shard_map/ppermute | solution.py:1591
  7.2 0.7 pad_bitcast_fusion
  7.9 0.1 fusion.heads_ref
  7.9 0.6 pad_add_fusion.spot_ref
  8.5 0.0 copy-start
  8.6 0.0 copy-start.7
  8.6 0.0 copy-start.8
  8.6 5.3 %owned.1 = (bf16[5,192,128]{2,1,0:T(8,128)(2,1)}, f32[5,192,128]{2,1,0:T(8,128)}) custom-call(s32[2]{0:T(128)} %pad_add_fusion.spot_ref, bf16[1536,768]{1,0:T(8,128)(2,1)} %out_weight_ref.1, bf16[3352,768]{1,0:T(8,128)(2,1)} %bitcast.33, f32[192,1536]{1,0:T(8,128)} %bitcast.37, f32[192,3352]{1,0:T(8,128)} %momentum_ref.3), custom_call_target="tpu_custom_call" | custom-call | tf_op jit(solution)/shard_map/owned/pallas_call | solution.py:1457
  13.9 1.0 slice.60.momentum_ref
  14.9 0.9 slice.62.momentum_ref
  15.8 0.9 slice.59.weight_ref
  16.7 0.9 slice.61.weight_ref
  17.7 0.0 copy-done.10
  17.7 0.1 broadcast_in_dim.15
  17.8 0.1 reshape_reshape.3.skip_ref
  19.2 0.0 collective-permute-done
  19.2 0.1 select_reduce_fusion
  19.3 0.1 pad_maximum_fusion.1.seg_ref
  19.4 0.0 copy-done.7
  19.4 0.0 copy-done.8
  19.4 0.0 copy-start.6
  19.5 22.0 %front.1 = (bf16[512,768]{1,0:T(8,128)(2,1)S(1)}, f32[512,16]{1,0:T(8,128)S(1)}, f32[512,1536]{1,0:T(8,128)}, f32[512,1792]{1,0:T(8,128)}, f32[16,1792]{1,0:T(8,...) custom-call(bf16[512,768]{1,0:T(8,128)(2,1)S(1)} %bitcast.28, ...), custom_call_target="tpu_custom_call" | custom-call | tf_op jit(solution)/shard_map/front/pallas_call | solution.py:390
  41.5 9.8 %chain.1.incoming_ref = f32[1,128,1536]{2,1,0:T(8,128)S(1)} custom-call(f32[1,128,1536]{2,1,0:T(8,128)S(1)} %get-tuple-element.56.own_ref, f32[1,8,1536]{2,1,0:T(8,128)S(1)} %get-tuple-element.57.keep_ref), custom_call_target="tpu_custom_call" | custom-call | tf_op jit(solution)/shard_map/chain/pallas_call | solution.py:504
  51.3 0.0 copy-done.6
  51.3 33.3 %forward.1 = (bf16[512,768]{1,0:T(8,128)(2,1)}, bf16[512,1536]{1,0:T(8,128)(2,1)}, bf16[512,768]{1,0:T(8,128)(2,1)S(1)}, bf16[512,1536]{1,0:T(8,128)(2,1)}, f32[...) custom-call(f32[512,1792]{1,0:T(8,128)} %get-tuple-element.51.summed, ...), custom_call_target="tpu_custom_call" | custom-call | tf_op jit(solution)/shard_map/forward/pallas_call | solution.py:701
  84.6 1.4 copy-done.1
  86.0 1.4 copy-done.5
  87.4 28.0 %turn_back.1 = (f32[1,128,1536]{2,1,0:T(8,128)S(1)}, bf16[3,2,2,4,192,128]{5,4,3,2,1,0:T(8,128)(2,1)S(1)}) custom-call(f32[1,128,1536]{2,1,0:T(8,128)S(1)} %get-tuple-element.64.own_ref, f32[1,8,1536]{2,1,0:T(8,128)S(1)} %get-tuple-element.57.keep_ref, bf16[512,768]{1,0:T(8,128)(2,1)S(1)} %get-tuple-element.59.out_low_ref, ...), custom_call_target="tpu_custom_call" | custom-call | tf_op jit(solution)/shard_map/turn_back/pallas_call | solution.py:1164
  115.4 0.0 copy-start.3
  115.4 1.4 copy-done.3
  116.8 47.6 %backward.1 = (bf16[512,2048]{1,0:T(8,128)(2,1)}, f32[8,1792]{1,0:T(8,128)S(1)}, f32[8,128]{1,0:T(8,128)S(1)}, bf16[3,2,192,128]{3,2,1,0:T(8,128)(2,1)S(1)}) custom-call(f32[1]{0:T(128)S(6)} %div.25.rate_ref, f32[512,1792]{1,0:T(8,128)} %get-tuple-element.51.summed_ref.summed_all, f32[512,1792]{1,0:T(8,128)} %get-tuple-element.62.conv_all, ...), custom_call_target="tpu_custom_call" | custom-call | tf_op jit(solution)/shard_map/backward/pallas_call | solution.py:1008
  164.4 0.0 copy-done.2
  164.4 85.2 %last.1 = (bf16[512,768]{1,0:T(8,128)(2,1)S(1)}, bf16[3,2,2,2,5,192,128]{6,5,4,3,2,1,0:T(8,128)(2,1)}, bf16[2,2,2,2,5,192,128]{6,5,4,3,2,1,0:T(8,128)(2,1)}, f32[8,1792]{1,0:T(8,128)S(1)}) custom-call(f32[1]{0:T(128)S(6)} %div.25.rate_ref, bf16[512,768]{1,0:T(8,128)(2,1)S(1)} %bitcast.30, bf16[512,768]{1,0:T(8,128)(2,1)S(1)} %get-tuple-element.59.out_low_ref, ...), custom_call_target="tpu_custom_call" | custom-call | tf_op jit(solution)/shard_map/last/pallas_call | solution.py:1367
  249.6 0.6 slice.71
  250.2 0.6 slice_reduce_fusion.4
  250.8 0.6 slice_reduce_fusion.1
  251.4 0.6 slice.64
  252.0 0.6 slice_reduce_fusion
  252.6 0.6 slice_reduce_fusion.3
  253.3 0.5 slice_bitcast_fusion.1
  255.8 0.1 reshape_squeeze.3
  255.9 12.4 %finish.1 = (bf16[1536,768]{1,0:T(8,128)(2,1)}, bf16[3352,768]{1,0:T(8,128)(2,1)}, f32[192,1536]{1,0:T(8,128)}, f32[192,3352]{1,0:T(8,128)}) custom-call(bf16[24,5,192,128]{3,2,1,0:T(8,128)(2,1)} %bitcast.36, bf16[16,5,192,128]{3,2,1,0:T(8,128)(2,1)} %bitcast.39, f32[192,1536]{1,0:T(8,128)} %bitcast.38, f32[192,3352]{1,0:T(8,128)} %momentum_ref.3), custom_call_target="tpu_custom_call" | custom-call | tf_op jit(solution)/shard_map/finish/pallas_call | solution.py:1526
  268.3 0.6 reduce_sum.27
  268.9 0.9 copy.35
  (20 shorter events, 0.1 us)
Async XLA Ops:
  2.2 17.0 %collective-permute-start = (bf16[1,16,896]{2,1,0:T(8,128)(2,1)S(1)}, bf16[1,16,896]{2,1,0:T(8,128)(2,1)S(1)}, u32[]{:S(2)}, u32[]{:S(2)}) collective-permute-start(bf16[1,16,896]{2,1,0:T(8,128)(2,1)S(1)} %pad_maximum_fusion), channel_id=1, source_target_pairs={{0,1},{1,2},{2,3},{4,5},{5,6},{6,7},{8,9},{9,10},{10,11},{12,13},{... | collective-permute-start | bytes 86024 | tf_op jit(solution)/shard_map/ppermute | solution.py:1591
  8.5 9.1 %copy-start.11 = (f32[768]{0:T(1024)S(1)}, f32[768]{0:T(1024)}, u32[]{:S(2)}) copy-start(f32[768]{0:T(1024)} %param.24) | copy-start | bytes 9220
  8.5 9.1 %copy-start.10 = (f32[1792]{0:T(1024)S(1)}, f32[1792]{0:T(1024)}, u32[]{:S(2)}) copy-start(f32[1792]{0:T(1024)} %param.27) | copy-start | bytes 21508
  8.5 9.2 %copy-start.12 = (f32[24]{0:T(128)S(1)}, f32[24]{0:T(128)}, u32[]{:S(2)}) copy-start(f32[24]{0:T(128)} %param.30) | copy-start | bytes 292
  8.5 9.3 %copy-start.9 = (f32[1536]{0:T(1024)S(1)}, f32[1536]{0:T(1024)}, u32[]{:S(2)}) copy-start(f32[1536]{0:T(1024)} %param.31) | copy-start | bytes 18436
  8.5 10.9 %copy-start = (bf16[1,512,768]{2,1,0:T(8,128)(2,1)S(1)}, bf16[1,512,768]{2,1,0:T(8,128)(2,1)}, u32[]{:S(2)}) copy-start(bf16[1,512,768]{2,1,0:T(8,128)(2,1)} %param.18) | copy-start | bytes 2359300
  8.6 10.9 %copy-start.7 = (f32[4,1792]{1,0:T(4,128)S(1)}, f32[4,1792]{1,0:T(4,128)}, u32[]{:S(2)}) copy-start(f32[4,1792]{1,0:T(4,128)} %taps_ref.3) | copy-start | bytes 86020
  8.6 10.9 %copy-start.8 = (s32[1,512]{1,0:T(1,128)S(1)}, s32[1,512]{1,0:T(1,128)}, u32[]{:S(2)}) copy-start(s32[1,512]{1,0:T(1,128)} %valid_ref.1) | copy-start | bytes 6148
  19.4 31.9 %copy-start.6 = (bf16[1,512,768]{2,1,0:T(8,128)(2,1)S(1)}, bf16[1,512,768]{2,1,0:T(8,128)(2,1)}, u32[]{:S(2)}) copy-start(bf16[1,512,768]{2,1,0:T(8,128)(2,1)} %param.19) | copy-start | bytes 2359300
  84.6 1.4 copy-start.1
  86.0 1.4 copy-start.5
  87.4 29.5 %copy-start.4 = (bf16[4,128,1536]{2,1,0:T(8,128)(2,1)S(1)}, bf16[4,128,1536]{2,1,0:T(8,128)(2,1)}, u32[]{:S(2)}) copy-start(bf16[4,128,1536]{2,1,0:T(8,128)(2,1)} %get-tuple-element.68.starts_all) | copy-start | bytes 4718596
  115.4 1.4 copy-start.3
  116.8 47.6 %copy-start.2 = (bf16[512,1536]{1,0:T(8,128)(2,1)S(1)}, bf16[512,1536]{1,0:T(8,128)(2,1)}, u32[]{:S(2)}) copy-start(bf16[512,1536]{1,0:T(8,128)(2,1)} %get-tuple-element.61.gate_grad_ref) | copy-start | bytes 4718596

commit v5 on v3

v5 whole, which is shorter than its diff:
```python
import functools

import jax
import jax.numpy as jnp
from jax import lax
from jax.experimental import pallas as pl
from jax.experimental.pallas import tpu as pltpu
from jax.sharding import PartitionSpec as P

CHUNK = 128
HALO = 16
GATE_BLOCK = 256
EPS = 1e-05
NEGATIVE = -1e30
F32, BF16 = jnp.float32, jnp.bfloat16
LANES = 128
MESH = pl.DeviceIdType.MESH


def remote(src, dst, send, recv, target):
    return pltpu.make_async_remote_copy(
        src_ref=src,
        dst_ref=dst,
        send_sem=send,
        recv_sem=recv,
        device_id=target,
        device_id_type=MESH,
    )


def greet(targets):
    barrier = pltpu.get_barrier_semaphore()
    for target in targets:
        pl.semaphore_signal(barrier, inc=1, device_id=target, device_id_type=MESH)
    pl.semaphore_wait(barrier, len(targets))


def dma_semaphores(*shape):
    return [pltpu.SemaphoreType.DMA(shape)] * 2


def part_count(pieces):
    return 2 if pieces % 2 == 0 else 1


def half_shape(bits, pieces, flows, rows, k):
    return (flows,) + (2,) * (bits - k - 1) + (pieces, rows, LANES)


def mm(a, b):
    return jnp.dot(a, b, preferred_element_type=F32)


def mm_nt(a, b):
    return lax.dot_general(a, b, (((1,), (1,)), ((), ())), preferred_element_type=F32)


def mm_tn(a, b):
    return lax.dot_general(a, b, (((0,), (0,)), ((), ())), preferred_element_type=F32)


def split(a):
    high = a.astype(BF16)
    return high, (a - high.astype(F32)).astype(BF16)


def exact_mm(a, b):
    return jnp.dot(a, b, preferred_element_type=F32, precision=lax.Precision.HIGHEST)


def spread(a, heads_ref):
    high, low = split(a)
    return mm(high, heads_ref[...]) + mm(low, heads_ref[...])


def gather_heads(a, heads_ref):
    high, low = split(a)
    return mm_nt(high, heads_ref[...]) + mm_nt(low, heads_ref[...])


def sigmoid(v):
    return 1.0 / (1.0 + jnp.exp(-v))


def softplus(v):
    return jnp.maximum(v, 0.0) + jnp.log1p(jnp.exp(-jnp.abs(v)))


def triangle(size, upper):
    row = lax.broadcasted_iota(jnp.int32, (size, size), 0)
    column = lax.broadcasted_iota(jnp.int32, (size, size), 1)
    return ((row <= column) if upper else (row >= column)).astype(F32)


def front_kernel(
    sizes,
    tokens_ref,
    halo_ref,
    gain_ref,
    weight_ref,
    taps_ref,
    bias_ref,
    seg_ref,
    valid_ref,
    dt_bias_ref,
    a_log_ref,
    heads_ref,
    normed_ref,
    masks_ref,
    gate_ref,
    conv_ref,
    halo_out_ref,
    summed_ref,
    raw_ref,
    cum_ref,
    state_ref,
    keep_ref,
    padded,
    product,
    active,
):
    seqs, piece, inner, channels, heads = sizes
    gate_blocks, conv_blocks = inner // GATE_BLOCK, channels // GATE_BLOCK
    step = pl.program_id(0)
    stride = piece + HALO

    @pl.when(step == 0)
    def _():
        gain = gain_ref[...]
        for n in range(seqs):
            padded_seg = seg_ref[n : n + 1]
            seg = padded_seg[:, HALO:]

            def over_chunks(at):
                return jnp.concatenate(
                    [
                        jnp.broadcast_to(
                            padded_seg[:, c * CHUNK + at : c * CHUNK + at + 1], (1, CHUNK)
                        )
                        for c in range(piece // CHUNK)
                    ],
                    axis=1,
                )

            others = [padded_seg[:, HALO - 3 + k : HALO - 3 + k + piece] for k in range(4)] + [
                over_chunks(HALO - 1),
                over_chunks(HALO + CHUNK - 1),
                jnp.broadcast_to(padded_seg[:, HALO - 1 : HALO], (1, piece)),
                jnp.broadcast_to(padded_seg[:, HALO + piece - 1 :], (1, piece)),
            ]
            lines = [(other == seg).astype(F32) for other in others] + [
                seg,
                valid_ref[n : n + 1].astype(F32),
            ]
            lines = lines + [jnp.zeros_like(seg)] * (16 - len(lines))
            masks_ref[pl.ds(n * piece, piece)] = jnp.transpose(jnp.concatenate(lines, axis=0))
            for source, start, to, count in (
                (halo_ref, n * HALO, n * stride, HALO),
                (tokens_ref, n * piece, n * stride + HALO, piece),
            ):

                def body(i, carry):
                    values = source[pl.ds(pl.multiple_of(start + i * 16, 16), 16)].astype(F32)
                    scale = lax.rsqrt(jnp.mean(values * values, axis=-1, keepdims=True) + EPS)
                    low = (values * scale * gain).astype(BF16)
                    padded[pl.ds(pl.multiple_of(to + i * 16, 16), 16)] = low
                    return carry

                lax.fori_loop(0, count // 16, body, 0)
            normed_ref[pl.ds(n * piece, piece)] = padded[pl.ds(n * stride + HALO, piece)]

    product[...] = mm_nt(padded[...], weight_ref[...])

    @pl.when(step < gate_blocks)
    def _():
        for n in range(seqs):
            gate_ref[pl.ds(n * piece, piece)] = product[pl.ds(n * stride + HALO, piece)]

    @pl.when((step >= gate_blocks) & (step < gate_blocks + conv_blocks))
    def _():
        at = pl.multiple_of((step - gate_blocks) * GATE_BLOCK, GATE_BLOCK)
        for n in range(seqs):
            conv_ref[pl.ds(n * piece, piece)] = product[pl.ds(n * stride + HALO, piece)]
            halo_out_ref[pl.ds(n * HALO, HALO)] = product[pl.ds(n * stride, HALO)]
            for i in range(piece // 64):
                rows = pl.ds(n * piece + i * 64, 64)
                total = jnp.broadcast_to(bias_ref[...], (64, GATE_BLOCK))
                for k in range(4):
                    source = product[pl.ds(n * stride + HALO - 3 + k + i * 64, 64)]
                    total = total + source * masks_ref[rows, k : k + 1] * taps_ref[k : k + 1]
                summed_ref[rows] = total
                active[rows, pl.ds(at, GATE_BLOCK)] = (total * sigmoid(total)).astype(BF16)

    @pl.when(step == gate_blocks + conv_blocks)
    def _():
        lane = lax.broadcasted_iota(jnp.int32, (piece, 128), 1)
        lower = triangle(CHUNK, False)
        for n in range(seqs):
            rows = pl.ds(n * piece, piece)
            raw = jnp.where(lane < heads, product[pl.ds(n * stride + HALO, piece), :128], 0.0)
            raw = raw + dt_bias_ref[...]
            raw_ref[rows] = raw
            steps = jnp.where(lane < heads, softplus(raw), 0.0)
            decay = -jnp.exp(a_log_ref[...]) * steps
            total = jnp.zeros((1, 128), F32)
            pieces = []
            for c in range(piece // CHUNK):
                cumulative = exact_mm(lower, decay[c * CHUNK : (c + 1) * CHUNK])
                cum_ref[pl.ds(n * piece + c * CHUNK, CHUNK)] = cumulative
                pieces.append(cumulative + total)
                total = total + cumulative[CHUNK - 1 :]
            whole = jnp.concatenate(pieces, axis=0) if len(pieces) > 1 else pieces[0]
            tails = jnp.exp(total - whole) * steps * masks_ref[rows, 7:8]
            weighted = (spread(tails, heads_ref) * active[rows, :inner].astype(F32)).astype(BF16)
            state_ref[n] = mm_tn(active[rows, inner : inner + 128], weighted)
            last = masks_ref[n * piece + piece - 1 : n * piece + piece, 6:7]
            keep = jnp.exp(total) * last
            keep_ref[n] = spread(jnp.broadcast_to(keep, (8, 128)), heads_ref)


def front(tokens, halo, gain, weight, taps, bias, segs, valid, dt_bias, a_log, heads_map, sizes):
    seqs, piece, inner, channels, heads = sizes
    total, model = tokens.shape
    stride = seqs * (piece + HALO)
    gate_blocks, conv_blocks = inner // GATE_BLOCK, channels // GATE_BLOCK
    full = lambda *shape: pl.BlockSpec(shape, lambda j: (0,) * len(shape))

    def conv_at(j):
        return (0, jnp.clip(j - gate_blocks, 0, conv_blocks - 1))

    return pl.pallas_call(
        functools.partial(front_kernel, sizes),
        grid=(gate_blocks + conv_blocks + 1,),
        in_specs=[
            full(total, model),
            full(seqs * HALO, model),
            full(1, model),
            pl.BlockSpec((GATE_BLOCK, model), lambda j: (j, 0)),
            pl.BlockSpec((4, GATE_BLOCK), conv_at),
            pl.BlockSpec((1, GATE_BLOCK), conv_at),
            full(*segs.shape),
            full(*valid.shape),
            full(1, 128),
            full(1, 128),
            full(128, inner),
        ],
        out_specs=(
            full(total, model),
            full(total, 16),
            pl.BlockSpec((total, GATE_BLOCK), lambda j: (0, jnp.minimum(j, gate_blocks - 1))),
            pl.BlockSpec((total, GATE_BLOCK), conv_at),
            pl.BlockSpec((seqs * HALO, GATE_BLOCK), conv_at),
            pl.BlockSpec((total, GATE_BLOCK), conv_at),
            full(total, 128),
            full(total, 128),
            full(seqs, 128, inner),
            full(seqs, 8, inner),
        ),
        out_shape=(
            jax.ShapeDtypeStruct((total, model), BF16),
            jax.ShapeDtypeStruct((total, 16), F32),
            jax.ShapeDtypeStruct((total, inner), F32),
            jax.ShapeDtypeStruct((total, channels), F32),
            jax.ShapeDtypeStruct((seqs * HALO, channels), F32),
            jax.ShapeDtypeStruct((total, channels), F32),
            jax.ShapeDtypeStruct((total, 128), F32),
            jax.ShapeDtypeStruct((total, 128), F32),
            jax.ShapeDtypeStruct((seqs, 128, inner), F32),
            jax.ShapeDtypeStruct((seqs, 8, inner), F32),
        ),
        scratch_shapes=[
            pltpu.VMEM((stride, model), BF16),
            pltpu.VMEM((stride, GATE_BLOCK), F32),
            pltpu.VMEM((total, channels), BF16),
        ],
        compiler_params=pltpu.CompilerParams(vmem_limit_bytes=48 * 1024 * 1024),
        name="front",
    )(tokens, halo, gain, weight, taps, bias, segs, valid, dt_bias, a_log, heads_map)


def chain_kernel(ways, blocks, own_ref, keep_ref, out_ref, sent, taken, send, recv):
    size = lax.axis_size("seq")
    turn = lax.axis_index("seq")
    first = turn == (0 if ways > 0 else size - 1)
    final = turn == (size - 1 if ways > 0 else 0)
    ahead = {"seq": lax.rem(turn + ways + size, size)}
    behind = {"seq": lax.rem(turn - ways + size, size)}
    barrier = pltpu.get_barrier_semaphore()

    @pl.when(jnp.logical_not(first))
    def _():
        pl.semaphore_signal(
            barrier, inc=1, device_id=behind, device_id_type=pl.DeviceIdType.MESH
        )

    @pl.when(jnp.logical_not(final))
    def _():
        pl.semaphore_wait(barrier, 1)

    width = own_ref.shape[2] // blocks

    def copy(c):
        return pltpu.make_async_remote_copy(
            src_ref=sent.at[c],
            dst_ref=taken.at[c],
            send_sem=send.at[c],
            recv_sem=recv.at[c],
            device_id=ahead,
            device_id_type=pl.DeviceIdType.MESH,
        )

    @pl.when(first)
    def _():
        out_ref[...] = jnp.zeros_like(out_ref)
        for c in range(blocks):
            at = slice(c * width, (c + 1) * width)
            sent[c] = own_ref[:, :, at].astype(BF16)
            copy(c).start()

    @pl.when(jnp.logical_not(first))
    def _():
        for c in range(blocks):
            at = slice(c * width, (c + 1) * width)
            copy(c).wait_recv()

            @pl.when(jnp.logical_not(final))
            def _():
                sent[c] = (
                    own_ref[:, :, at] + keep_ref[:, 0:1, at] * taken[c].astype(F32)
                ).astype(BF16)
                copy(c).start()

            out_ref[:, :, at] = taken[c].astype(F32)

    @pl.when(jnp.logical_not(final))
    def _():
        for c in range(blocks):
            copy(c).wait_send()


def chain(own, keep, ways, blocks=6):
    seqs, depth, inner = own.shape
    vmem = pl.BlockSpec(memory_space=pltpu.VMEM)
    part = (blocks, seqs, depth, inner // blocks)
    return pl.pallas_call(
        functools.partial(chain_kernel, ways, blocks),
        out_shape=jax.ShapeDtypeStruct(own.shape, F32),
        in_specs=[vmem, vmem],
        out_specs=vmem,
        scratch_shapes=[pltpu.VMEM(part, BF16)] * 2 + [pltpu.SemaphoreType.DMA((blocks,))] * 2,
        compiler_params=pltpu.CompilerParams(
            collective_id=1 if ways > 0 else 2,
            has_side_effects=True,
            vmem_limit_bytes=32 * 1024 * 1024,
        ),
        name="chain",
    )(own, keep)


def decays_of(cum, cum_t, bias, h):
    return jnp.exp(cum[:, h : h + 1] - cum_t[h : h + 1, :] + bias)


def mask_bias(seg_col, seg_row):
    row = lax.broadcasted_iota(jnp.int32, (CHUNK, CHUNK), 0)
    column = lax.broadcasted_iota(jnp.int32, (CHUNK, CHUNK), 1)
    return jnp.where((row >= column) & (seg_col == seg_row), 0.0, NEGATIVE)


def scores_of(reader, writer):
    rh, rl = split(reader)
    wh, wl = split(writer)
    return mm_nt(rh, wh) + (mm_nt(rh, wl) + mm_nt(rl, wh))


def forward_kernel(
    sizes,
    chunks,
    summed_ref,
    gate_ref,
    raw_ref,
    cum_ref,
    masks_ref,
    seg_row_ref,
    incoming_ref,
    tokens_ref,
    cot_ref,
    weight_ref,
    gain_ref,
    skip_ref,
    heads_ref,
    output_ref,
    low_ref,
    out_low_ref,
    gate_grad_ref,
    ssm_grad_ref,
    starts_ref,
    dot_ref,
    sums_ref,
    wide_ref,
    state_grad_ref,
    state,
    prefix,
    active,
    mixed_in,
    factors,
    grads,
    inv,
):
    seqs, piece, inner, channels, heads = sizes
    c = pl.program_id(1)

    @pl.when((c == 0) & (pl.program_id(0) == 0))
    def _():
        sums_ref[...] = jnp.zeros_like(sums_ref)
        wide_ref[...] = jnp.zeros_like(wide_ref)

    @pl.when(c == 0)
    def _():
        state[...] = incoming_ref[0]
        prefix[...] = jnp.zeros_like(prefix)
        state_grad_ref[...] = jnp.zeros_like(state_grad_ref)

    def activate(i, carry):
        rows = pl.ds(pl.multiple_of(i * 16, 16), 16)
        values = summed_ref[rows]
        active[rows] = values * sigmoid(values)
        return carry

    lax.fori_loop(0, CHUNK // 16, activate, 0)
    lane = lax.broadcasted_iota(jnp.int32, (CHUNK, 128), 1)
    steps = jnp.where(lane < heads, softplus(raw_ref[...]), 0.0)
    cum = cum_ref[...]
    cum_t = jnp.transpose(cum)
    final = cum[CHUNK - 1 :]
    enter = jnp.exp(cum) * masks_ref[:, 4:5]
    tails = jnp.exp(final - cum) * steps * masks_ref[:, 5:6]
    from_start = jnp.exp(cum + prefix[0:1]) * masks_ref[:, 6:7]
    prefix[...] = prefix[...] + final
    for i, block in enumerate((steps, enter, tails, from_start)):
        factors[i] = spread(block, heads_ref)
    writer = active[:, inner : inner + 128]
    reader = active[:, inner + 128 : inner + 256]
    scores = scores_of(reader, writer)
    bias = mask_bias(masks_ref[:, 8:9], seg_row_ref[0:1])
    half = lax.broadcasted_iota(jnp.int32, (CHUNK, 128), 1) < 64
    state_low = state[...].astype(BF16)
    starts_ref[0] = state_low
    reader_low = reader.astype(BF16)
    for pair in range(heads // 2):
        at = slice(pair * 128, (pair + 1) * 128)
        moved = (active[:, at] * factors[0, :, at]).astype(BF16)
        zero = jnp.zeros_like(moved)
        one = (scores * decays_of(cum, cum_t, bias, 2 * pair)).astype(BF16)
        two = (scores * decays_of(cum, cum_t, bias, 2 * pair + 1)).astype(BF16)
        both = jnp.concatenate([one, two], axis=1)
        stacked = jnp.concatenate(
            [jnp.where(half, moved, zero), jnp.where(half, zero, moved)], axis=0
        )
        carried = mm(reader_low, state_low[:, at]) * factors[1, :, at]
        mixed_in[:, at] = mm(both, stacked) + carried
    weighted = (active[:, :inner] * factors[2]).astype(BF16)
    kept = jnp.exp(final) * masks_ref[CHUNK - 1 :, 4:5]
    kept = spread(jnp.broadcast_to(kept, (8, 128)), heads_ref)[0:1]
    state[...] = state[...] * kept + mm_tn(writer.astype(BF16), weighted)

    gain = gain_ref[...]
    skip = skip_ref[...]

    def gating(i, carry):
        rows = pl.ds(pl.multiple_of(i * 16, 16), 16)
        gate = gate_ref[rows]
        mixer = mixed_in[rows] + skip * active[rows, :inner]
        gated = mixer * gate * sigmoid(gate)
        scale = lax.rsqrt(jnp.mean(gated * gated, axis=-1, keepdims=True) + EPS)
        inv[rows] = jnp.broadcast_to(scale, (16, 128))
        low_ref[rows] = (gated * scale * gain).astype(BF16)
        return carry

    lax.fori_loop(0, CHUNK // 16, gating, 0)
    mixed = mm(low_ref[...], weight_ref[...])
    block_out = tokens_ref[...].astype(F32) + mixed
    output_ref[...] = block_out.astype(BF16)
    valid = masks_ref[:, 9:10]
    for i, block in enumerate((block_out, mixed)):
        squares = jnp.sum(valid * block * block, axis=0, keepdims=True)
        for at in range(0, squares.shape[1], 128):
            sums_ref[i : i + 1] += squares[:, at : at + 128]
    sums_ref[2:3, :16] += jnp.sum(masks_ref[...], axis=0, keepdims=True)
    out_low = (cot_ref[...].astype(F32) * valid).astype(BF16)
    out_low_ref[...] = out_low
    grads[...] = mm_nt(out_low, weight_ref[...])

    def backing(i, carry):
        gain_sum, skip_sum = carry
        rows = pl.ds(pl.multiple_of(i * 16, 16), 16)
        gate = gate_ref[rows]
        turned = sigmoid(gate)
        silu = gate * turned
        signal = active[rows, :inner]
        mixer = mixed_in[rows] + skip * signal
        gated = mixer * silu
        scale = inv[rows, 0:1]
        grad = grads[rows]
        gain_sum = gain_sum + grad * gated * scale
        grad = grad * gain
        inside = jnp.mean(grad * gated, axis=-1, keepdims=True)
        gated_grad = scale * grad - gated * (scale * scale * scale * inside)
        ssm_grad = gated_grad * silu
        ssm_grad_ref[rows] = ssm_grad
        grads[rows] = ssm_grad
        skip_sum = skip_sum + ssm_grad * signal
        gate_grad_ref[rows] = (gated_grad * mixer * turned * (1.0 + gate * (1.0 - turned))).astype(
            BF16
        )
        return gain_sum, skip_sum

    start = jnp.zeros((16, inner), F32)
    gain_sum, skip_sum = lax.fori_loop(0, CHUNK // 16, backing, (start, start))
    wide_ref[0:1] += jnp.sum(gain_sum, axis=0, keepdims=True)
    wide_ref[1:2] += jnp.sum(skip_sum, axis=0, keepdims=True)
    reader_t = jnp.transpose(reader_low)
    for pair in range(heads // 2):
        at = slice(pair * 128, (pair + 1) * 128)
        state_grad_ref[0, :, at] += mm(
            reader_t, (grads[:, at] * factors[3, :, at]).astype(BF16)
        )
        mixed_in[:, at] = mixed_in[:, at] * grads[:, at].astype(BF16).astype(F32)
    dot_ref[...] = gather_heads(mixed_in[...], heads_ref)


def forward(
    summed, gate, raw, cum, masks, seg_row, incoming, tokens, cot, weight, gain, skip, heads_map, sizes
):
    seqs, piece, inner, channels, heads = sizes
    total, model = tokens.shape
    chunks = piece // CHUNK
    full = lambda *shape: pl.BlockSpec(shape, lambda n, c: (0,) * len(shape))
    rows = lambda width: pl.BlockSpec((CHUNK, width), lambda n, c: (n * chunks + c, 0))
    each = lambda depth: pl.BlockSpec((1, depth, inner), lambda n, c: (n, 0, 0))
    shape = jax.ShapeDtypeStruct
    return pl.pallas_call(
        functools.partial(forward_kernel, sizes, chunks),
        grid=(seqs, chunks),
        in_specs=[
            rows(channels),
            rows(inner),
            rows(128),
            rows(128),
            rows(16),
            pl.BlockSpec((1, CHUNK), lambda n, c: (0, n * chunks + c)),
            each(128),
            rows(model),
            rows(model),
            full(inner, model),
            full(1, inner),
            full(1, inner),
            full(128, inner),
        ],
        out_specs=(
            rows(model),
            rows(inner),
            rows(model),
            rows(inner),
            rows(inner),
            pl.BlockSpec((1, 128, inner), lambda n, c: (n * chunks + c, 0, 0)),
            rows(128),
            full(8, 128),
            full(8, inner),
            each(128),
        ),
        out_shape=(
            shape((total, model), BF16),
            shape((total, inner), BF16),
            shape((total, model), BF16),
            shape((total, inner), BF16),
            shape((total, inner), F32),
            shape((seqs * chunks, 128, inner), BF16),
            shape((total, 128), F32),
            shape((8, 128), F32),
            shape((8, inner), F32),
            shape((seqs, 128, inner), F32),
        ),
        scratch_shapes=[
            pltpu.VMEM((128, inner), F32),
            pltpu.VMEM((8, 128), F32),
            pltpu.VMEM((CHUNK, channels), F32),
            pltpu.VMEM((CHUNK, inner), F32),
            pltpu.VMEM((4, CHUNK, inner), F32),
            pltpu.VMEM((CHUNK, inner), F32),
            pltpu.VMEM((CHUNK, 128), F32),
        ],
        compiler_params=pltpu.CompilerParams(vmem_limit_bytes=48 * 1024 * 1024),
        name="forward",
    )(summed, gate, raw, cum, masks, seg_row, incoming, tokens, cot, weight, gain, skip, heads_map)


TILE = 256


class Exchange:
    def __init__(self, bits, pieces, flows):
        self.bits, self.pieces, self.flows = bits, pieces, flows
        self.parts = part_count(pieces)
        self.place, self.turn = lax.axis_index("dp"), lax.axis_index("seq")
        self.own = [(self.place // (1 << b)) % 2 for b in range(bits)]
        self.partner = [
            {"dp": self.place + (1 - 2 * self.own[b]) * (1 << b)} for b in range(bits)
        ]
        self.others = [{"seq": lax.rem(self.turn + j, pieces)} for j in range(pieces)]
        self.mine = self.index_of({b: self.own[b] for b in range(bits)})

    def index_of(self, fixed):
        return tuple(fixed.get(b, slice(None)) for b in range(self.bits - 1, -1, -1))

    def spot_of(self, d):
        return tuple((d // (1 << b)) % 2 for b in range(self.bits - 1, -1, -1))

    def order_of(self, f, h):
        rest = list(range(1, self.bits))
        shift = (f + h) % max(len(rest), 1)
        return [0] + rest[shift:] + rest[:shift]

    def share(self, h, extra=0):
        half = self.pieces // self.parts
        return pl.ds(h * half, half + (extra if h == self.parts - 1 else 0))

    def held(self, f, h, k, other):
        order = self.order_of(f, h)
        bit = order[k]
        value = 1 - self.own[bit] if other else self.own[bit]
        free = [b for b in range(self.bits - 1, -1, -1) if b not in order[:k]]
        source = self.grad if k == 0 else self.halves[k - 1]
        return source.at[
            (f,) + tuple(value if b == bit else slice(None) for b in free) + (self.share(h),)
        ]

    def landing(self, f, h, k):
        free = self.bits - k - 1
        return self.halves[k].at[(f,) + (slice(None),) * free + (self.share(h),)]

    def rs_copy(self, f, h, k):
        return remote(
            self.held(f, h, k, True),
            self.landing(f, h, k),
            self.rs_send.at[f, h, k],
            self.rs_recv.at[f, h, k],
            self.partner[self.order_of(f, h)[k]],
        )

    def rs_begin(self, f):
        for h in range(self.parts):
            self.rs_copy(f, h, 0).start()

    def rs_end(self, f, k):
        for h in range(self.parts):
            self.rs_copy(f, h, k).wait_recv()
            kept, into = self.held(f, h, k, False), self.landing(f, h, k)
            left = self.bits - k - 1
            for count in range(1 << left):
                spot = tuple((count >> (left - 1 - i)) & 1 for i in range(left))

                def body(p, carry, spot=spot, kept=kept, into=into):
                    into[spot + (p,)] = (
                        kept[spot + (p,)].astype(F32) + into[spot + (p,)].astype(F32)
                    ).astype(BF16)
                    return carry

                lax.fori_loop(0, self.pieces // self.parts, body, 0)
            if k + 1 < self.bits:
                self.rs_copy(f, h, k + 1).start()
        if k + 1 == self.bits:
            for j in range(1, self.pieces):
                self.zs_copy(f, j).start()

    def zs_copy(self, f, j):
        return remote(
            self.halves[self.bits - 1].at[f, lax.rem(self.turn + j, self.pieces)],
            self.piece_parts.at[f, j],
            self.zs_send.at[f, j],
            self.zs_recv.at[f, j],
            self.others[j],
        )

    def zs_end(self, f, rate, weight, momentum):
        for j in range(1, self.pieces):
            self.zs_copy(f, j).wait_recv()
        total = self.halves[self.bits - 1][f, self.turn].astype(F32)
        for j in range(1, self.pieces):
            total = total + self.piece_parts[f, j].astype(F32)
        summed = total.astype(BF16)
        moved = 0.5 * momentum + summed.astype(F32)
        self.gathered[(f,) + self.mine + (self.pieces,)] = summed
        self.gathered[(f,) + self.mine + (self.turn,)] = (
            weight.astype(F32) - rate * moved
        ).astype(BF16)
        for j in range(1, self.pieces):
            self.zg_copy(f, j).start()

    def zg_copy(self, f, j):
        spot = self.gathered.at[(f,) + self.mine + (self.turn,)]
        return remote(spot, spot, self.zg_send.at[f, j], self.zg_recv.at[f, j], self.others[j])

    def zg_end(self, f):
        for j in range(1, self.pieces):
            self.zg_copy(f, j).wait_recv()
        for h in range(self.parts):
            self.ag_copy(f, h, self.bits - 1).start()

    def ag_copy(self, f, h, k):
        order = self.order_of(f, h)
        fixed = {order[i]: self.own[order[i]] for i in range(k + 1)}
        spot = self.gathered.at[(f,) + self.index_of(fixed) + (self.share(h, 1),)]
        return remote(
            spot,
            spot,
            self.ag_send.at[f, h, k],
            self.ag_recv.at[f, h, k],
            self.partner[order[k]],
        )

    def ag_end(self, f, k):
        for h in range(self.parts):
            self.ag_copy(f, h, k).wait_recv()
            if k > 0:
                self.ag_copy(f, h, k - 1).start()

    def tiles_sent(self):
        for f in range(self.flows):
            for h in range(self.parts):
                self.rs_copy(f, h, 0).wait_send()

    def sent(self):
        for f in range(self.flows):
            for h in range(self.parts):
                for k in range(self.bits):
                    if k > 0:
                        self.rs_copy(f, h, k).wait_send()
                    self.ag_copy(f, h, k).wait_send()
            for j in range(1, self.pieces):
                self.zs_copy(f, j).wait_send()
                self.zg_copy(f, j).wait_send()

    def actions(self, f, rate, weights, momenta, after):
        steps = [functools.partial(self.rs_end, f, k) for k in range(self.bits)]
        steps.append(lambda: self.zs_end(f, rate, weights[f], momenta[f]))
        steps.append(functools.partial(self.zg_end, f))
        steps += [functools.partial(self.ag_end, f, k) for k in range(self.bits - 1, 0, -1)]

        def finish():
            self.ag_end(f, 0)
            after(f)

        return steps + [finish]


def exchange_scratch(bits, pieces, flows, rows, first=-1):
    parts = part_count(pieces)
    return (
        [pltpu.VMEM(half_shape(bits, pieces, flows, rows, k), BF16) for k in range(first, bits)]
        + [
            pltpu.VMEM((flows, pieces, rows, LANES), BF16),
            pltpu.VMEM((flows,) + (2,) * bits + (pieces + 1, rows, LANES), BF16),
        ]
        + dma_semaphores(flows, parts, bits)
        + dma_semaphores(flows, pieces)
        + dma_semaphores(flows, pieces)
        + dma_semaphores(flows, parts, bits)
        + [pltpu.SemaphoreType.DMA((flows,))]
    )


def give(ex, scratch, grad=None):
    if grad is None:
        grad, scratch = scratch[0], scratch[1:]
    ex.grad, ex.halves = grad, scratch[: ex.bits]
    scratch = scratch[ex.bits :]
    (ex.piece_parts, ex.gathered, ex.rs_send, ex.rs_recv, ex.zs_send, ex.zs_recv) = scratch[:6]
    (ex.zg_send, ex.zg_recv, ex.ag_send, ex.ag_recv, ex.out_sem) = scratch[6:11]
    return scratch[11:]


def tail_kernel(sizes, dims, *refs):
    seqs, piece, inner, channels, heads = sizes
    bits, pieces, flows_a, flows_b, split_rows, blocks = dims
    (
        rate_ref,
        summed_ref,
        conv_ref,
        halo_ref,
        taps_ref,
        ssm_grad_ref,
        starts_ref,
        heads_ref,
        skip_ref,
        summed_rw_ref,
        raw_ref,
        cum_ref,
        masks_ref,
        seg_row_ref,
        dot_ref,
        a_log_ref,
        own_ref,
        keep_ref,
        out_low_ref,
        normed_ref,
        low_ref,
        gate_grad_ref,
        weight_t_ref,
        tokens_ref,
        gain_ref,
        weight_ref,
        momentum_ref,
        wide_ref,
        squares_ref,
        input_grad_ref,
        small_out_ref,
        out_a_ref,
        out_b_ref,
    ) = refs[:33]
    scratch = refs[33:]
    a, b = Exchange(bits, pieces, flows_a), Exchange(bits, pieces, flows_b)
    scratch = give(a, scratch)
    scratch = give(b, scratch, a.grad)
    (
        sent,
        taken,
        chain_send,
        chain_recv,
        later,
        out_turned,
        normed_turned,
        writer_low,
        reader_low,
        reader_turned,
        scores,
        cum_turned,
        biases,
        scores_grad,
        reader_grad,
        writer_grad,
        active,
        bent,
        step_x,
        cum_x,
        total,
        state_grad,
        ends,
        step_sum,
        move_sum,
        end_sum,
        shifted_rows,
        proj_grad,
        tails,
        rims,
        rims_in,
        rim_send,
        rim_recv,
        conv_sums,
        head_sums,
        gain_sums,
        small_acc,
        small_in,
        small_parts,
        sm_send,
        sm_recv,
        sz_send,
        sz_recv,
    ) = scratch
    j = pl.program_id(0)
    steps = inner // TILE
    final_step = steps + 1
    places = 1 << bits
    per_flow = places // split_rows
    turn = a.turn
    chunk_count = seqs * piece // CHUNK
    rows = a.grad.shape[-2]
    chunks = piece // CHUNK
    rate = rate_ref[0]
    real = 2 * inner // LANES

    def out_copy(ex, out, f):
        return pltpu.make_async_copy(ex.gathered.at[f], out.at[f], ex.out_sem.at[f])

    a_actions = [
        a.actions(f, rate, weight_ref, momentum_ref, lambda f: out_copy(a, out_a_ref, f).start())
        for f in range(flows_a)
    ]
    late = [weight_ref.at[pl.ds(flows_a, flows_b)], momentum_ref.at[pl.ds(flows_a, flows_b)]]
    b_actions = [
        b.actions(f, rate, *late, lambda f: out_copy(b, out_b_ref, f).start())
        for f in range(flows_b)
    ]

    def store(ex, tile, values):
        for part in range(split_rows):
            d = (tile % per_flow) * split_rows + part
            spot = (tile // per_flow,) + ex.spot_of(d)
            for p in range(pieces):
                at = (p * split_rows + part) * rows
                ex.grad[spot + (p,)] = values[at : at + rows]

    def rim_copy(slot):
        return remote(
            rims.at[slot],
            rims_in.at[slot],
            rim_send.at[slot],
            rim_recv.at[slot],
            {"seq": lax.rem(turn + pieces - 1, pieces)},
        )

    def fix_rim(slot, at):
        @pl.when(turn < pieces - 1)
        def _():
            rim_copy(slot).wait_recv()
            for n in range(seqs):
                proj_grad[(n + 1) * piece - 8 : (n + 1) * piece, at] = (
                    tails[n] + rims_in[slot, n].astype(F32)
                ).astype(BF16)

    def conv_back(slot, at):
        for n in range(seqs):
            here_rows = pl.ds(n * piece, piece)
            grad = total[here_rows] * bent[here_rows]
            conv = conv_ref[here_rows]
            sums = [None] * 5
            sums[4] = jnp.sum(grad, axis=0, keepdims=True)
            sums[3] = jnp.sum(grad * conv, axis=0, keepdims=True)
            result = grad * taps_ref[3:4]
            rim = jnp.zeros((8, TILE), F32)
            shifted_rows[0:8] = jnp.zeros((8, TILE), F32)
            shifted_rows[8 + piece :] = jnp.zeros((8, TILE), F32)
            for k in range(3):
                shifted_rows[8 : 8 + piece] = grad * masks_ref[here_rows, k : k + 1]
                here = shifted_rows[11 - k : 11 - k + piece]
                result = result + here * taps_ref[k : k + 1]
                early = shifted_rows[3 - k : 11 - k]
                rim = rim + early * taps_ref[k : k + 1]
                sums[k] = jnp.sum(here * conv, axis=0, keepdims=True) + jnp.sum(
                    early * halo_ref[(n + 1) * HALO - 8 : (n + 1) * HALO], axis=0, keepdims=True
                )
            for i in range(5):
                if n == 0:
                    conv_sums[i : i + 1, at] = sums[i]
                else:
                    conv_sums[i : i + 1, at] += sums[i]
            proj_grad[here_rows, at] = result.astype(BF16)
            tails[n] = result[piece - 8 :]
            rims[slot, n] = rim.astype(BF16)

        @pl.when(turn > 0)
        def _():
            rim_copy(slot).start()

    @pl.when(j == 0)
    def _():
        greet(a.partner + a.others[1:])
        first, final = turn == pieces - 1, turn == 0
        width = inner // blocks

        def copy(c):
            ahead = {"seq": lax.rem(turn + pieces - 1, pieces)}
            return remote(sent.at[c], taken.at[c], chain_send.at[c], chain_recv.at[c], ahead)

        @pl.when(first)
        def _():
            later[...] = jnp.zeros_like(later)
            for c in range(blocks):
                sent[c] = own_ref[:, :, c * width : (c + 1) * width].astype(BF16)
                copy(c).start()

        out_turned[...] = jnp.transpose(out_low_ref[...])
        normed_turned[...] = jnp.transpose(normed_ref[...])
        low_tiles = inner // LANES

        def tiles(tile):
            if tile >= real:
                result = jnp.zeros((out_turned.shape[0], 2 * LANES), BF16)
            elif tile < low_tiles:
                at = tile * LANES
                result = mm(out_turned[...], low_ref[:, at : at + 2 * LANES]).astype(BF16)
            else:
                at = (tile - low_tiles) * LANES
                result = mm(normed_turned[...], gate_grad_ref[:, at : at + 2 * LANES])
                result = result.astype(BF16)
            store(a, tile, result[:, :LANES])
            store(a, tile + 1, result[:, LANES:])

        pairs = flows_a * per_flow // 2
        done = 0
        for c in range(blocks):
            until = pairs * (c + 1) // blocks
            for pair in range(done, until):
                tiles(2 * pair)
                if (2 * pair + 2) % per_flow == 0:
                    a.rs_begin(2 * pair // per_flow)
            done = until

            @pl.when(jnp.logical_not(first))
            def _():
                at = slice(c * width, (c + 1) * width)
                copy(c).wait_recv()

                @pl.when(jnp.logical_not(final))
                def _():
                    sent[c] = (
                        own_ref[:, :, at] + keep_ref[:, 0:1, at] * taken[c].astype(F32)
                    ).astype(BF16)
                    copy(c).start()

                later[:, :, at] = taken[c].astype(F32)

        for f in range(flows_a):
            a_actions[f][0]()
        a.tiles_sent()
        for ck in range(chunk_count):
            at = slice(ck * CHUNK, (ck + 1) * CHUNK)
            values = summed_rw_ref[at]
            values = values * sigmoid(values)
            writer, reader = values[:, :128], values[:, 128:]
            scores[ck] = scores_of(reader, writer)
            writer_low[at] = writer.astype(BF16)
            reader_low[at] = reader.astype(BF16)
            reader_turned[ck] = jnp.transpose(reader.astype(BF16))
            cum_turned[ck] = jnp.transpose(cum_ref[at])
            biases[ck] = mask_bias(masks_ref[at, 8:9], seg_row_ref[0:1, at])
        for ref in (
            scores_grad,
            reader_grad,
            writer_grad,
            step_sum,
            move_sum,
            end_sum,
            ends,
            gain_sums,
        ):
            ref[...] = jnp.zeros_like(ref)

        @pl.when(jnp.logical_not(final))
        def _():
            for c in range(blocks):
                copy(c).wait_send()

    agenda = {}

    def plan(step, act):
        agenda.setdefault(min(max(step, 1), steps), []).append(act)

    last_b = [((f + 1) * per_flow * LANES - 1) // TILE + 1 for f in range(flows_b)]
    a_steps = {1: 3, 2: 4} if bits == 3 else {k: 1 + k for k in range(1, bits)}
    a_done = b_ready = None
    for k in range(1, bits):
        for f in range(flows_a):
            plan(a_steps[k], a_actions[f][k])
    b_taken = []
    for f in range(flows_b):
        taken_steps = 0
        if last_b[f] + 1 <= steps:
            plan(last_b[f] + 1, functools.partial(b.rs_begin, f))
            for i in range(bits):
                if last_b[f] + 2 + i <= steps:
                    plan(last_b[f] + 2 + i, b_actions[f][i])
                    taken_steps = i + 1
            b_taken.append(taken_steps)
        else:
            b_taken.append(None)

    def weight_tiles(tile, at):
        result = mm(normed_turned[...], proj_grad[:, at]).astype(BF16)
        store(b, tile, result[:, :LANES])
        store(b, tile + 1, result[:, LANES:])

    @pl.when((j > 0) & (j < final_step))
    def _():
        at = pl.ds(pl.multiple_of((j - 1) * TILE, TILE), TILE)

        @pl.when(j > 1)
        def _():
            before = pl.ds(pl.multiple_of((j - 2) * TILE, TILE), TILE)
            fix_rim(j - 2, before)
            weight_tiles((j - 2) * (TILE // LANES), before)

        def activate(i, carry):
            rows_at = pl.ds(pl.multiple_of(i * 32, 32), 32)
            values = summed_ref[rows_at]
            turned = sigmoid(values)
            active[rows_at] = values * turned
            bent[rows_at] = turned * (1.0 + values * (1.0 - turned))
            return carry

        lax.fori_loop(0, seqs * piece // 32, activate, 0)
        raw = raw_ref[...]
        lane = lax.broadcasted_iota(jnp.int32, raw.shape, 1)
        step_x[...] = spread(jnp.where(lane < heads, softplus(raw), 0.0), heads_ref)
        cum = cum_ref[...]
        high, low = split(cum)
        lowest = (cum - high.astype(F32) - low.astype(F32)).astype(BF16)
        cum_x[...] = (
            mm(high, heads_ref[...]) + mm(low, heads_ref[...]) + mm(lowest, heads_ref[...])
        )
        half = lax.broadcasted_iota(jnp.int32, (CHUNK, 128), 1) < 64
        head = (j - 1) * (TILE // 64)
        skip = skip_ref[...]
        for n in range(seqs):
            state_grad[...] = later[n, :, at]
            for c in range(chunks - 1, -1, -1):
                ck = n * chunks + c
                here = slice(ck * CHUNK, (ck + 1) * CHUNK)
                cum_here = cum_x[here]
                final_cum = cum_here[CHUNK - 1 :]
                enter_x = jnp.exp(cum_here) * masks_ref[here, 4:5]
                tail_x = jnp.exp(final_cum - cum_here) * masks_ref[here, 5:6]
                kept = jnp.exp(final_cum) * masks_ref[(ck + 1) * CHUNK - 1 : (ck + 1) * CHUNK, 4:5]
                signal = active[here]
                grad = ssm_grad_ref[here]
                moved = (signal * step_x[here]).astype(BF16)
                grad_low = grad.astype(BF16)
                later_low = state_grad[...].astype(BF16)
                from_later = mm(writer_low[here], later_low) * tail_x
                parts = []
                score = scores[ck]
                bias = biases[ck]
                grad_of_scores = scores_grad[ck]
                for pair in range(TILE // 128):
                    col = slice(pair * 128, (pair + 1) * 128)
                    ones = []
                    for i in range(2):
                        lane_at = pair * 128 + i * 64
                        ones.append(
                            jnp.exp(
                                cum_here[:, lane_at : lane_at + 1]
                                - cum_turned[ck, pl.ds(head + 2 * pair + i, 1), :]
                                + bias
                            )
                        )
                    zero = jnp.zeros((CHUNK, 128), BF16)
                    stacked = jnp.concatenate(
                        [
                            jnp.where(half, grad_low[:, col], zero),
                            jnp.where(half, zero, grad_low[:, col]),
                        ],
                        axis=0,
                    )
                    both_grad = mm_nt(stacked, moved[:, col])
                    grad_of_scores = (
                        grad_of_scores + both_grad[:CHUNK] * ones[0] + both_grad[CHUNK:] * ones[1]
                    )
                    both = jnp.concatenate([(score * one).astype(BF16) for one in ones], axis=0)
                    parts.append(mm_tn(both, stacked))
                scores_grad[ck] = grad_of_scores
                moved_grad = jnp.concatenate(parts, axis=1) + from_later
                wide_moved = moved.astype(F32)
                weighted = (wide_moved * tail_x).astype(BF16)
                entered = (grad * enter_x).astype(BF16)
                start = starts_ref[ck]
                reader_grad[here] += mm_nt(entered, start)
                writer_grad[here] += mm_nt(weighted, later_low)
                passed = jnp.sum(
                    start.astype(F32) * later_low.astype(F32), axis=0, keepdims=True
                )
                ends[ck : ck + 1] = kept * passed + jnp.sum(
                    wide_moved * from_later, axis=0, keepdims=True
                )
                state_grad[...] = state_grad[...] * kept + mm(reader_turned[ck], entered)
                step_sum[here] += gather_heads(moved_grad * signal, heads_ref)
                move_sum[here] += gather_heads(moved_grad * wide_moved, heads_ref)
                total[here] = moved_grad * step_x[here] + skip * grad
        end_sum[...] += gather_heads(ends[...], heads_ref)
        conv_back(j - 1, at)
        for step in sorted(agenda):

            @pl.when(j == step)
            def _(step=step):
                for act in agenda[step]:
                    act()

    @pl.when(j == final_step)
    def _():
        before = slice((steps - 1) * TILE, steps * TILE)
        fix_rim(steps - 1, before)
        weight_tiles((steps - 1) * (TILE // LANES), before)
        pending = []
        for f in range(flows_b):
            if last_b[f] == steps and b_taken[f] is None:
                b.rs_begin(f)
                b_taken[f] = 0
        at = slice(inner, channels)
        lane = lax.broadcasted_iota(jnp.int32, (CHUNK, 128), 1)
        row = lax.broadcasted_iota(jnp.int32, (CHUNK, 128), 0)
        upper = triangle(CHUNK, True)
        decay_rate = -jnp.exp(a_log_ref[...])
        raw_sum = jnp.zeros((1, 128), F32)
        decay_sum = jnp.zeros((1, 128), F32)
        values = summed_rw_ref[...]
        turned = sigmoid(values)
        bent[...] = turned * (1.0 + values * (1.0 - turned))
        for ck in range(chunk_count):
            here = slice(ck * CHUNK, (ck + 1) * CHUNK)
            high, low = split(scores_grad[ck])
            total[here, 128:] = (
                reader_grad[here] + mm(high, writer_low[here]) + mm(low, writer_low[here])
            )
            total[here, :128] = (
                writer_grad[here] + mm_tn(high, reader_low[here]) + mm_tn(low, reader_low[here])
            )
            raw = raw_ref[here]
            taken_steps = jnp.where(lane < heads, softplus(raw), 0.0)
            change = dot_ref[here] - move_sum[here]
            change = change + jnp.where(row == CHUNK - 1, end_sum[ck : ck + 1], 0.0)
            decay_grad = exact_mm(upper, change)
            raw_grad = jnp.where(
                lane < heads, (step_sum[here] + decay_grad * decay_rate) * sigmoid(raw), 0.0
            )
            raw_sum = raw_sum + jnp.sum(raw_grad, axis=0, keepdims=True)
            decay_sum = decay_sum + jnp.sum(
                decay_grad * taken_steps * decay_rate, axis=0, keepdims=True
            )
            proj_grad[here, channels : channels + 128] = raw_grad.astype(BF16)
            proj_grad[here, channels + 128 :] = jnp.zeros((CHUNK, 128), BF16)
        head_sums[0:1] = raw_sum
        head_sums[1:2] = decay_sum
        conv_back(steps, at)
        fix_rim(steps, at)
        for tile in range(inner // LANES, flows_b * per_flow, 2):
            if tile * LANES < channels + 256:
                weight_tiles(tile, slice(tile * LANES, (tile + 2) * LANES))
            else:
                for i in range(2):
                    store(b, tile + i, jnp.zeros((pieces * split_rows * rows, LANES), BF16))
        for f in range(flows_b):
            if b_taken[f] is None:
                b.rs_begin(f)
                b_taken[f] = 0

        rest = weight_t_ref.shape[0] - inner

        def input_rows(i, carry):
            rows_at = pl.ds(pl.multiple_of(i * 128, 128), 128)
            normed_grad = mm(gate_grad_ref[rows_at], weight_t_ref[:inner]) + mm(
                proj_grad[rows_at, :rest], weight_t_ref[inner:]
            )
            values = tokens_ref[rows_at].astype(F32)
            scale = lax.rsqrt(jnp.mean(values * values, axis=-1, keepdims=True) + EPS)
            gain_sums[0:1] += jnp.sum(normed_grad * values * scale, axis=0, keepdims=True)
            pushed = normed_grad * gain_ref[...]
            inside = jnp.mean(pushed * values, axis=-1, keepdims=True)
            input_grad_ref[rows_at] = (
                out_low_ref[rows_at].astype(F32)
                + scale * pushed
                - values * (scale * scale * scale * inside)
            ).astype(BF16)
            return carry

        def sm_copy(k):
            return remote(
                small_acc.at[k], small_in.at[k], sm_send.at[k], sm_recv.at[k], a.partner[k]
            )

        def sz_copy(k):
            return remote(
                small_acc.at[bits],
                small_parts.at[turn],
                sz_send.at[k],
                sz_recv.at[k],
                a.others[k],
            )

        def small_begin():
            model = gain_sums.shape[1]
            small_acc[0, 0:5] = conv_sums[0:5]
            small_acc[0, 5:7, :inner] = wide_ref[0:2]
            small_acc[0, 5:7, inner : inner + 128] = head_sums[0:2]
            small_acc[0, 5:8, inner + 128 :] = squares_ref[0:3]
            small_acc[0, 7:8, :model] = gain_sums[0:1]
            small_acc[0, 7:8, model : inner + 128] = jnp.zeros((1, inner + 128 - model), F32)
            sm_copy(0).start()

        def small_step(k):
            sm_copy(k).wait_recv()
            small_acc[k + 1] = small_acc[k] + small_in[k]
            if k + 1 < bits:
                sm_copy(k + 1).start()
            else:
                small_parts[turn] = small_acc[bits]
                for i in range(1, pieces):
                    sz_copy(i).start()

        def small_end():
            for i in range(1, pieces):
                sz_copy(i).wait_recv()
            whole = small_parts[0]
            for i in range(1, pieces):
                whole = whole + small_parts[i]
            small_out_ref[...] = whole

        lines = [a_actions[f][bits:] for f in range(flows_a)]
        lines += [b_actions[f][b_taken[f] :] for f in range(flows_b)]
        blocks_of_rows = tokens_ref.shape[0] // 128
        extra = [
            lambda: lax.fori_loop(0, blocks_of_rows // 2, input_rows, 0),
            lambda: lax.fori_loop(blocks_of_rows // 2, blocks_of_rows, input_rows, 0),
            small_begin,
        ]
        extra += [functools.partial(small_step, k) for k in range(bits)] + [small_end]
        while any(lines) or extra:
            if extra:
                extra.pop(0)()
            for line in lines:
                if line:
                    line.pop(0)()
        b.tiles_sent()
        a.sent()
        b.sent()
        for k in range(bits):
            sm_copy(k).wait_send()
        for i in range(1, pieces):
            sz_copy(i).wait_send()

        @pl.when(turn > 0)
        def _():
            for slot in range(steps + 1):
                rim_copy(slot).wait_send()

        for f in range(flows_a):
            out_copy(a, out_a_ref, f).wait()
        for f in range(flows_b):
            out_copy(b, out_b_ref, f).wait()


def row_split(places, rows):
    return 2 if places > 2 and rows % 32 == 0 else 1


def tail(
    rate,
    tiled,
    summed_rw_source,
    whole,
    weights,
    momenta,
    wide,
    squares,
    sizes,
    places,
    pieces,
    flows,
    blocks=6,
):
    seqs, piece, inner, channels, heads = sizes
    summed, conv, halo, taps, ssm_grad, starts, heads_map, skip = tiled
    total_rows = summed.shape[0]
    own = whole[6]
    tokens, weight_t = whole[13], whole[12]
    model = tokens.shape[1]
    flows_a, flows_b = flows
    assert flows_b <= flows_a
    bits = places.bit_length() - 1
    assert places == 1 << bits and bits >= 1 and pieces >= 2
    share = model // pieces
    split_rows = row_split(places, share)
    rows = share // split_rows
    steps = inner // TILE
    small = (8, channels)
    shape = jax.ShapeDtypeStruct
    any_space = pl.BlockSpec(memory_space=pl.ANY)
    sem = dma_semaphores

    def constant(array):
        count = array.ndim
        return pl.BlockSpec(
            array.shape, lambda j: (0,) * count, pipeline_mode=pl.Buffered(1)
        )

    def columns(height, last):
        return pl.BlockSpec((height, TILE), lambda j: (0, jnp.clip(j - 1, 0, last)))

    gathered = lambda count: (count,) + (2,) * bits + (pieces + 1, rows, LANES)
    chunk_count = total_rows // CHUNK
    square = (chunk_count, CHUNK, CHUNK)
    per_tile = (total_rows, TILE)
    per_head = (total_rows, 128)
    constants = list(whole) + [weights, momenta, wide, squares]
    return pl.pallas_call(
        functools.partial(
            tail_kernel, sizes, (bits, pieces, flows_a, flows_b, split_rows, blocks)
        ),
        grid=(steps + 2,),
        in_specs=[
            pl.BlockSpec(memory_space=pltpu.SMEM),
            columns(total_rows, steps),
            columns(total_rows, steps),
            columns(halo.shape[0], steps),
            columns(4, steps),
            columns(total_rows, steps - 1),
            pl.BlockSpec(
                (chunk_count, 128, TILE), lambda j: (0, 0, jnp.clip(j - 1, 0, steps - 1))
            ),
            columns(128, steps - 1),
            columns(1, steps - 1),
            pl.BlockSpec((total_rows, TILE), lambda j: (0, steps), pipeline_mode=pl.Buffered(1)),
        ]
        + [constant(array) for array in constants],
        out_specs=(
            pl.BlockSpec((total_rows, model), lambda j: (0, 0)),
            pl.BlockSpec(small, lambda j: (0, 0)),
            any_space,
            any_space,
        ),
        out_shape=(
            shape((total_rows, model), BF16),
            shape(small, F32),
            shape(gathered(flows_a), BF16),
            shape(gathered(flows_b), BF16),
        ),
        scratch_shapes=exchange_scratch(bits, pieces, flows_a, rows)
        + exchange_scratch(bits, pieces, flows_b, rows, 0)
        + [pltpu.VMEM((blocks, seqs, 128, inner // blocks), BF16)] * 2
        + sem(blocks)
        + [
            pltpu.VMEM((seqs, 128, inner), F32),
            pltpu.VMEM((model, total_rows), BF16),
            pltpu.VMEM((model, total_rows), BF16),
            pltpu.VMEM(per_head, BF16),
            pltpu.VMEM(per_head, BF16),
            pltpu.VMEM(square, BF16),
            pltpu.VMEM(square, F32),
            pltpu.VMEM(square, F32),
            pltpu.VMEM(square, F32),
            pltpu.VMEM(square, F32),
            pltpu.VMEM(per_head, F32),
            pltpu.VMEM(per_head, F32),
            pltpu.VMEM(per_tile, F32),
            pltpu.VMEM(per_tile, F32),
            pltpu.VMEM(per_tile, F32),
            pltpu.VMEM(per_tile, F32),
            pltpu.VMEM(per_tile, F32),
            pltpu.VMEM((128, TILE), F32),
            pltpu.VMEM((max(chunk_count, 8), TILE), F32),
            pltpu.VMEM(per_head, F32),
            pltpu.VMEM(per_head, F32),
            pltpu.VMEM((max(chunk_count, 8), 128), F32),
            pltpu.VMEM((piece + 16, TILE), F32),
            pltpu.VMEM((total_rows, channels + 256), BF16),
            pltpu.VMEM((seqs, 8, TILE), F32),
            pltpu.VMEM((steps + 1, seqs, 8, TILE), BF16),
            pltpu.VMEM((steps + 1, seqs, 8, TILE), BF16),
        ]
        + sem(steps + 1)
        + [
            pltpu.VMEM(small, F32),
            pltpu.VMEM((8, 128), F32),
            pltpu.VMEM((8, model), F32),
            pltpu.VMEM((bits + 1,) + small, F32),
            pltpu.VMEM((bits,) + small, F32),
            pltpu.VMEM((pieces,) + small, F32),
        ]
        + sem(bits)
        + sem(pieces),
        compiler_params=pltpu.CompilerParams(
            collective_id=2, has_side_effects=True, vmem_limit_bytes=62 * 1024 * 1024
        ),
        name="tail",
    )(rate, *tiled, summed_rw_source, *constants)


def piece_kernel(
    counts, spot_ref, out_weight_ref, weight_ref, out_momentum_ref, momentum_ref, w_ref, m_ref, turned
):
    out_tiles, tile_of, split_rows = counts
    tile = tile_of(pl.program_id(0), spot_ref)
    rows = m_ref.shape[1]
    part = lax.rem(spot_ref[0], split_rows)
    mine = pl.ds(pl.multiple_of((spot_ref[1] * split_rows + part) * rows, 16), rows)
    half = pl.ds(pl.multiple_of(part * rows, 16), rows)

    @pl.when(tile < out_tiles)
    def _():
        turned[...] = jnp.transpose(out_weight_ref[...])
        w_ref[0] = turned[mine]
        m_ref[0] = out_momentum_ref[half]

    @pl.when(tile >= out_tiles)
    def _():
        turned[...] = jnp.transpose(weight_ref[...])
        w_ref[0] = turned[mine]
        m_ref[0] = momentum_ref[half]


def owned(spot, out_weight, weight_t, out_momentum_t, momentum, flows_a, flows_b, places):
    inner, model = out_weight.shape
    share, width = momentum.shape
    out_tiles, in_tiles = inner // LANES, -(-width // LANES)
    split_rows = row_split(places, share)
    rows, per_flow = share // split_rows, places // split_rows

    flows = flows_a + flows_b

    def tile_of(f, spot):
        early = jnp.minimum(f * per_flow + spot[0] // split_rows, 2 * out_tiles - 1)
        late = 2 * out_tiles + (f - flows_a) * per_flow + spot[0] // split_rows
        return jnp.where(f < flows_a, early, late)

    def out_at(f, spot):
        return jnp.clip(tile_of(f, spot), 0, out_tiles - 1)

    def in_at(f, spot):
        return jnp.clip(tile_of(f, spot) - out_tiles, 0, in_tiles - 1)

    piece = pl.BlockSpec((1, rows, LANES), lambda f, spot: (f, 0, 0))
    return pl.pallas_call(
        functools.partial(piece_kernel, (out_tiles, tile_of, split_rows)),
        grid_spec=pltpu.PrefetchScalarGridSpec(
            num_scalar_prefetch=1,
            grid=(flows,),
            in_specs=[
                pl.BlockSpec((LANES, model), lambda f, spot: (out_at(f, spot), 0)),
                pl.BlockSpec((LANES, model), lambda f, spot: (in_at(f, spot), 0)),
                pl.BlockSpec((share, LANES), lambda f, spot: (0, out_at(f, spot))),
                pl.BlockSpec((share, LANES), lambda f, spot: (0, in_at(f, spot))),
            ],
            out_specs=(piece, piece),
            scratch_shapes=[pltpu.VMEM((model, LANES), BF16)],
        ),
        out_shape=(
            jax.ShapeDtypeStruct((flows, rows, LANES), BF16),
            jax.ShapeDtypeStruct((flows, rows, LANES), F32),
        ),
        name="owned",
    )(spot, out_weight, weight_t, out_momentum_t, momentum)


def finish_kernel(
    out_steps,
    split_rows,
    gathered_a_ref,
    gathered_b_ref,
    out_momentum_ref,
    momentum_ref,
    out_weight_ref,
    weight_ref,
    new_out_momentum_ref,
    new_momentum_ref,
    joined,
):
    group, slots, rows, _ = gathered_a_ref.shape
    step = pl.program_id(0)

    def write(gathered_ref, weights, old, new):
        for i in range(group // split_rows):
            at = slice(i * LANES, (i + 1) * LANES)
            for part in range(split_rows):
                for p in range(slots - 1):
                    to = (p * split_rows + part) * rows
                    joined[to : to + rows] = gathered_ref[i * split_rows + part, p]
                own = slice(part * rows, (part + 1) * rows)
                summed = gathered_ref[i * split_rows + part, slots - 1].astype(F32)
                new[own, at] = 0.5 * old[own, at] + summed
            weights[at] = jnp.transpose(joined[...])

    @pl.when(step < out_steps)
    def _():
        write(gathered_a_ref, out_weight_ref, out_momentum_ref, new_out_momentum_ref)

    @pl.when((step >= out_steps) & (step < 2 * out_steps))
    def _():
        write(gathered_a_ref, weight_ref, momentum_ref, new_momentum_ref)

    @pl.when(step >= 2 * out_steps)
    def _():
        write(gathered_b_ref, weight_ref, momentum_ref, new_momentum_ref)


def finish(gathered_a, gathered_b, out_momentum_t, momentum, split_rows, group=4):
    _, slots, rows, _ = gathered_a.shape
    share, width = momentum.shape
    inner = out_momentum_t.shape[1]
    model = (slots - 1) * share
    wide = group * LANES
    group = group * split_rows
    out_steps, in_steps = inner // wide, -(-width // wide)
    out_at = lambda j: jnp.minimum(j, out_steps - 1)
    in_at = lambda j: jnp.maximum(j - out_steps, 0)
    by_column = [
        pl.BlockSpec((share, wide), lambda j: (0, out_at(j))),
        pl.BlockSpec((share, wide), lambda j: (0, in_at(j))),
    ]
    shape = jax.ShapeDtypeStruct
    return pl.pallas_call(
        functools.partial(finish_kernel, out_steps, split_rows),
        grid=(out_steps + in_steps,),
        in_specs=[
            pl.BlockSpec(
                (group, slots, rows, LANES), lambda j: (jnp.minimum(j, 2 * out_steps - 1), 0, 0, 0)
            ),
            pl.BlockSpec(
                (group, slots, rows, LANES), lambda j: (jnp.maximum(j - 2 * out_steps, 0), 0, 0, 0)
            ),
        ]
        + by_column,
        out_specs=[
            pl.BlockSpec((wide, model), lambda j: (out_at(j), 0)),
            pl.BlockSpec((wide, model), lambda j: (in_at(j), 0)),
        ]
        + by_column,
        out_shape=(
            shape((inner, model), BF16),
            shape((width, model), BF16),
            shape((share, inner), F32),
            shape((share, width), F32),
        ),
        scratch_shapes=[pltpu.VMEM((model, LANES), BF16)],
        name="finish",
    )(gathered_a, gathered_b, out_momentum_t, momentum)


def local(
    tokens,
    cotangent,
    segment_ids,
    doc_starts,
    valid_mask,
    step_number,
    learn_rate,
    norm_gain,
    in_weight,
    conv_weight,
    conv_bias,
    dt_bias,
    a_log,
    skip_d,
    gate_gain,
    out_weight,
    in_momentum,
    out_momentum,
):
    seqs, piece, model_width = tokens.shape
    heads = dt_bias.shape[0]
    tap_count, channels = conv_weight.shape
    inner_width = gate_gain.shape[0]
    proj_width = in_weight.shape[1]
    total = seqs * piece
    sizes = (seqs, piece, inner_width, channels, heads)
    places, pieces = lax.axis_size("dp"), lax.axis_size("seq")
    turn = lax.axis_index("seq")
    seg = segment_ids.astype(F32)
    sent = jnp.concatenate(
        [
            tokens[:, piece - HALO :],
            jnp.broadcast_to(seg[:, piece - HALO :, None], (seqs, HALO, LANES)).astype(BF16),
        ],
        axis=2,
    )
    route = [(i, i + 1) for i in range(pieces - 1)]
    arrived = lax.ppermute(sent, "seq", route)
    halo = arrived[:, :, :model_width].reshape(seqs * HALO, model_width)
    early_seg = jnp.where(turn == 0, -1.0, arrived[:, :, model_width].astype(F32))
    seg_pad = jnp.concatenate([early_seg, seg], axis=1)
    seg_row = seg.reshape(1, total)
    heads_map = (
        lax.broadcasted_iota(jnp.int32, (LANES, inner_width), 0)
        == lax.broadcasted_iota(jnp.int32, (LANES, inner_width), 1) // (inner_width // heads)
    ).astype(BF16)

    def lanes(values):
        return jnp.pad(values, (0, LANES - heads)).reshape(1, LANES)

    flat_tokens = tokens.reshape(total, model_width)
    weight_t = jnp.transpose(in_weight)
    out_momentum_t = jnp.transpose(out_momentum)
    flat_cot = cotangent.reshape(total, model_width)
    bias_row, decay_row = lanes(dt_bias), lanes(a_log)
    skip_row = jnp.repeat(skip_d, inner_width // heads).reshape(1, inner_width)
    gain_row = gate_gain.reshape(1, inner_width)
    normed, masks, gate, conv, conv_halo, summed, raw, cum, fresh, keep = front(
        flat_tokens,
        halo,
        norm_gain.reshape(1, model_width),
        weight_t,
        conv_weight,
        conv_bias.reshape(1, channels),
        seg_pad,
        valid_mask,
        bias_row,
        decay_row,
        heads_map,
        sizes,
    )
    incoming = chain(fresh, keep, 1)
    output, low, out_low, gate_grad, ssm_grad, starts, dots, squares, wide, state_grad = forward(
        summed,
        gate,
        raw,
        cum,
        masks,
        seg_row,
        incoming,
        flat_tokens,
        flat_cot,
        out_weight,
        gain_row,
        skip_row,
        heads_map,
        sizes,
    )
    step_float = step_number[0].astype(F32)
    rate = (learn_rate[0] * step_float / (step_float + 16.0)).reshape(1)
    share_rows = model_width // pieces
    split_rows = row_split(places, share_rows)
    per_flow = places // split_rows
    flows_a = -(-2 * inner_width // (LANES * per_flow))
    flows_b = -(-(channels + 2 * LANES) // (LANES * per_flow))
    spot = jnp.stack([lax.axis_index("dp"), turn]).astype(jnp.int32)
    weights, momenta = owned(
        spot, out_weight, weight_t, out_momentum_t, in_momentum, flows_a, flows_b, places
    )
    input_grad, totals, gathered_a, gathered_b = tail(
        rate,
        (summed, conv, conv_halo, conv_weight, ssm_grad, starts, heads_map, skip_row),
        summed,
        (
            raw,
            cum,
            masks,
            seg_row,
            dots,
            decay_row,
            state_grad,
            keep,
            out_low,
            normed,
            low,
            gate_grad,
            weight_t,
            flat_tokens,
            norm_gain.reshape(1, model_width),
        ),
        weights,
        momenta,
        wide,
        squares,
        sizes,
        places,
        pieces,
        (flows_a, flows_b),
    )
    share = (pieces + 1, share_rows // split_rows, LANES)
    new_out_weight, new_weight_t, new_out_momentum_t, new_in_momentum = finish(
        gathered_a.reshape((-1,) + share),
        gathered_b.reshape((-1,) + share),
        out_momentum_t,
        in_momentum,
        split_rows,
    )
    new_in_weight = jnp.transpose(new_weight_t)
    new_out_momentum = jnp.transpose(new_out_momentum_t)
    conv_weight_total = totals[:tap_count]
    conv_bias_total = totals[tap_count]
    gate_gain_total = totals[5, :inner_width]
    skip_total = totals[6, :inner_width].reshape(heads, -1).sum(axis=1)
    norm_gain_total = totals[7, :model_width]
    dt_bias_total = totals[5, inner_width : inner_width + heads]
    a_log_total = totals[6, inner_width : inner_width + heads]
    out_square_total = totals[5, inner_width + LANES :].sum()
    mix_square_total = totals[6, inner_width + LANES :].sum()
    valid_total = totals[7, inner_width + LANES + 9]
    denominator = jnp.maximum(valid_total, 1.0) * model_width
    output_rms = jnp.sqrt(out_square_total / denominator).reshape(1)
    mixer_rms = jnp.sqrt(mix_square_total / denominator).reshape(1)
    return (
        output.reshape(tokens.shape),
        input_grad.reshape(tokens.shape),
        new_in_weight,
        new_out_weight,
        new_in_momentum,
        new_out_momentum,
        norm_gain_total,
        conv_weight_total,
        conv_bias_total,
        dt_bias_total,
        a_log_total,
        skip_total,
        gate_gain_total,
        output_rms,
        mixer_rms,
    )


def solution(mesh):
    placed = (
        P("dp", "seq", None),
        P("dp", "seq", None),
        P("dp", "seq"),
        P("dp", "seq"),
        P("dp", "seq"),
        P(),
        P(),
        P(),
        P(),
        P(),
        P(),
        P(),
        P(),
        P(),
        P(),
        P(),
        P("seq", None),
        P(None, "seq"),
    )
    return jax.shard_map(
        local,
        mesh=mesh,
        in_specs=placed,
        out_specs=(
            P("dp", "seq", None),
            P("dp", "seq", None),
            P(),
            P(),
            P("seq", None),
            P(None, "seq"),
            P(),
            P(),
            P(),
            P(),
            P(),
            P(),
            P(),
            P(),
            P(),
        ),
        check_vma=False,
    )
```

time: 318 us -> 249 us (0.78)
  Pallas kernels: 289 us -> 213 us
  local copies, waits for them, and re-layouts: 12.8 us -> 17.4 us
    pallas_call x6 -> x3, Pallas kernels: 200 us -> 148 us  [the longest x1 127 us: tail(): pl.pallas_call(functools.partial(tail_kernel, sizes, (bits, pieces, flows...]
    pallas_call x2 -> x1, Pallas kernels: 33.4 us -> 9.87 us  [chain(): pl.pallas_call(functools.partial(chain_kernel, ways, blocks), out_shape=j...]
    unnamed x26 -> x43, local copies, waits for them, and re-layouts: 0.08 us -> 4.65 us
  transfers between devices with their start and end apart: 1 -> 1, of which waited for: 0 -> 0; matrix products, arithmetic and copies ran while one was open for 1% -> 2% of each run, Pallas kernels for 2% -> 3%
where the time goes in v5:
time: 249 us; the launch traced here: 246 us
  Pallas kernels  213 us (86%)
  local copies, waits for them, and re-layouts  17.4 us (7%)
  between operations  6.55 us (3%)
  starting transfers between devices  4.92 us (2%)
  other arithmetic  3.59 us (1%)
    pallas_call x1, Pallas kernels, tail(): pl.pallas_call(functools.partial(tail_kernel, sizes, (bits, pieces, flows...  127 us
    pallas_call x1, Pallas kernels, forward(): pl.pallas_call(functools.partial(forward_kernel, sizes, chunks), grid=(se...  33.4 us
    pallas_call x1, Pallas kernels, front(): pl.pallas_call(functools.partial(front_kernel, sizes), grid=(gate_blocks...  22 us
    pallas_call x1, Pallas kernels, finish(): pl.pallas_call(functools.partial(finish_kernel, out_steps, split_rows), g...  12.5 us
    pallas_call x1, Pallas kernels, chain(): pl.pallas_call(functools.partial(chain_kernel, ways, blocks), out_shape=j...  9.87 us
    pallas_call x1, Pallas kernels, owned(): pl.pallas_call(functools.partial(piece_kernel, (out_tiles, tile_of, split...  8.15 us
  transfers between devices with their start and end apart: 1, of which 0 were waited for; matrix products, arithmetic and copies ran while one was open for 2% of the time, Pallas kernels for 3%

profile of v5, /device:TPU:0, one launch (start us, length us, event | category | flops | bytes accessed | tf_op | source)
XLA Modules:
  0.0 245.8 jit_solution(5588451933499734541)
XLA Ops:
  0.6 0.7 convert_element_type.35.seg_row_ref.refs_13_
  1.3 0.1 fusion.4
  1.4 0.7 slice.43
  2.1 0.1 broadcast_in_dim.13
  2.2 4.9 %collective-permute-start = (bf16[1,16,896]{2,1,0:T(8,128)(2,1)S(1)}, bf16[1,16,896]{2,1,0:T(8,128)(2,1)S(1)}, u32[]{:S(2)}, u32[]{:S(2)}) collective-permute-start(bf16[1,16,896]{2,1,0:T(8,128)(2,1)S(1)} %pad_maximum_fusion), channel_id=1, source_target_pairs={{0,1},{1,2},{2,3},{4,5},{5,6},{6,7},{8,9},{9,10},{10,11},{12,13},{... | collective-permute-start | bytes 86024 | tf_op jit(solution)/shard_map/ppermute | solution.py:1654
  7.2 0.7 pad_bitcast_fusion
  7.9 0.1 fusion.heads_ref.refs_7_
  7.9 0.0 copy-start.1
  8.0 0.6 pad_add_fusion.spot_ref
  9.9 0.7 reshape.111.gain_ref.refs_24_
  10.6 0.7 reshape.116.gain_ref
  11.3 0.7 reshape.112.bias_ref
  12.0 0.7 broadcast_in_dim.15
  12.7 0.1 reshape_reshape.3.skip_ref.refs_8_
  12.8 0.0 copy-start
  12.9 0.0 copy-start.12
  12.9 0.0 copy-start.19
  12.9 8.1 %owned.1 = (bf16[10,96,128]{2,1,0:T(8,128)(2,1)}, f32[10,96,128]{2,1,0:T(8,128)}) custom-call(s32[2]{0:T(128)} %pad_add_fusion.spot_ref, bf16[1536,768]{1,0:T(8,128)(2,1)} %out_weight_ref.1, bf16[3352,768]{1,0:T(8,128)(2,1)} %bitcast.32, f32[192,1536]{1,0:T(8,128)} %bitcast.36, f32[192,3352]{1,0:T(8,128)} %momentum_ref.3), custom_call_target="tpu_custom_call" | custom-call | tf_op jit(solution)/shard_map/owned/pallas_call | solution.py:1510
  21.0 0.0 collective-permute-done
  21.0 0.1 select_reduce_fusion
  21.1 0.1 pad_maximum_fusion.1.seg_ref
  21.2 0.0 copy-done.17
  21.2 0.0 copy-done.16
  21.2 0.0 copy-done
  21.2 0.0 copy-done.12
  21.3 0.0 copy-done.19
  21.3 0.0 copy-start.5
  21.3 22.0 %front.1 = (bf16[512,768]{1,0:T(8,128)(2,1)S(1)}, f32[512,16]{1,0:T(8,128)S(1)}, f32[512,1536]{1,0:T(8,128)}, f32[512,1792]{1,0:T(8,128)}, f32[16,1792]{1,0:T(8,...) custom-call(bf16[512,768]{1,0:T(8,128)(2,1)S(1)} %bitcast.29, ...), custom_call_target="tpu_custom_call" | custom-call | tf_op jit(solution)/shard_map/front/pallas_call | solution.py:231
  43.4 9.9 %chain.1.incoming_ref = f32[1,128,1536]{2,1,0:T(8,128)S(1)} custom-call(f32[1,128,1536]{2,1,0:T(8,128)S(1)} %get-tuple-element.50.own_ref, f32[1,8,1536]{2,1,0:T(8,128)S(1)} %get-tuple-element.51.keep_ref.refs_17_), custom_call_target="tpu_custom_call" | custom-call | tf_op jit(solution)/shard_map/chain/pallas_call | solution.py:345
  53.3 33.4 %forward.1 = (bf16[512,768]{1,0:T(8,128)(2,1)}, bf16[512,1536]{1,0:T(8,128)(2,1)}, bf16[512,768]{1,0:T(8,128)(2,1)S(1)}, bf16[512,1536]{1,0:T(8,128)(2,1)}, f32[...) custom-call(f32[512,1792]{1,0:T(8,128)} %get-tuple-element.45.summed, ...), custom_call_target="tpu_custom_call" | custom-call | tf_op jit(solution)/shard_map/forward/pallas_call | solution.py:542
  86.7 0.0 copy-start.7
  86.7 0.9 copy-done.7
  87.6 0.9 copy-done.8
  88.5 0.7 copy-done.9
  89.2 0.6 copy-done.14
  89.8 0.6 copy-done.18
  90.4 127.4 %tail.1 = (bf16[512,768]{1,0:T(8,128)(2,1)}, f32[8,1792]{1,0:T(8,128)}, bf16[6,2,2,2,5,96,128]{6,5,4,3,2,1,0:T(8,128)(2,1)}, bf16[4,2,2,2,5,96,128]{6,5,4,3,2,1,0:T(8,128)(2,1)}) custom-call(f32[1]{0:T(128)S(6)} %div.25.refs_0_, f32[512,1792]{1,0:T(8,128)} %get-tuple-element.45.summed_ref.refs_1_.refs_9_, f32[512,1792]{1,0:T(8,128)} %get-tuple-element.53.refs_2_, ...), custom_call_target="tpu_custom_call" | custom-call | tf_op jit(solution)/shard_map/tail/pallas_call | solution.py:1383
  217.8 1.3 slice.55
  219.1 1.3 slice_bitcast_fusion.1
  220.3 1.4 slice_reduce_fusion.4
  221.7 1.3 slice_reduce_fusion.3
  223.0 1.4 slice_reduce_fusion
  224.5 1.5 slice_reduce_fusion.1
  226.0 1.4 slice.48
  229.4 0.1 reshape_squeeze.3
  229.5 0.6 reduce_sum.27
  230.2 12.5 %finish.1 = (bf16[1536,768]{1,0:T(8,128)(2,1)}, bf16[3352,768]{1,0:T(8,128)(2,1)}, f32[192,1536]{1,0:T(8,128)}, f32[192,3352]{1,0:T(8,128)}) custom-call(bf16[48,5,96,128]{3,2,1,0:T(8,128)(2,1)} %bitcast.35, bf16[32,5,96,128]{3,2,1,0:T(8,128)(2,1)} %bitcast.38, f32[192,1536]{1,0:T(8,128)} %bitcast.37, f32[192,3352]{1,0:T(8,128)} %momentum_ref.3), custom_call_target="tpu_custom_call" | custom-call | tf_op jit(solution)/shard_map/finish/pallas_call | solution.py:1588
  242.7 0.9 copy.35
  (30 shorter events, 0.1 us)
Async XLA Ops:
  1.3 51.9 %copy-start.15 = (f32[1,512]{1,0:T(1,128)}, f32[1,512]{1,0:T(1,128)S(1)}, u32[]{:S(2)}) copy-start(f32[1,512]{1,0:T(1,128)S(1)} %convert_element_type.35.seg_row_ref.refs_13_) | copy-start | bytes 6148
  2.2 18.8 %collective-permute-start = (bf16[1,16,896]{2,1,0:T(8,128)(2,1)S(1)}, bf16[1,16,896]{2,1,0:T(8,128)(2,1)S(1)}, u32[]{:S(2)}, u32[]{:S(2)}) collective-permute-start(bf16[1,16,896]{2,1,0:T(8,128)(2,1)S(1)} %pad_maximum_fusion), channel_id=1, source_target_pairs={{0,1},{1,2},{2,3},{4,5},{5,6},{6,7},{8,9},{9,10},{10,11},{12,13},{... | collective-permute-start | bytes 86024 | tf_op jit(solution)/shard_map/ppermute | solution.py:1654
  7.9 13.4 %copy-start.17 = (f32[1,128]{1,0:T(1,128)}, f32[1,128]{1,0:T(1,128)S(1)}, u32[]{:S(2)}) copy-start(f32[1,128]{1,0:T(1,128)S(1)} %get-tuple-element.83.a_log_ref.refs_15_) | copy-start | bytes 1540
  7.9 45.3 %copy-start.1 = (bf16[128,1536]{1,0:T(8,128)(2,1)}, bf16[128,1536]{1,0:T(8,128)(2,1)S(1)}, u32[]{:S(2)}) copy-start(bf16[128,1536]{1,0:T(8,128)(2,1)S(1)} %fusion.heads_ref.refs_7_) | copy-start | bytes 1179652
  10.6 10.7 %copy-start.16 = (f32[1,768]{1,0:T(1,128)}, f32[1,768]{1,0:T(1,128)S(1)}, u32[]{:S(2)}) copy-start(f32[1,768]{1,0:T(1,128)S(1)} %reshape.111.gain_ref.refs_24_) | copy-start | bytes 9220
  12.8 40.5 %copy-start.13 = (f32[1,1536]{1,0:T(1,128)}, f32[1,1536]{1,0:T(1,128)S(1)}, u32[]{:S(2)}) copy-start(f32[1,1536]{1,0:T(1,128)S(1)} %reshape_reshape.3.skip_ref.refs_8_) | copy-start | bytes 18436
  12.8 8.4 %copy-start = (bf16[1,512,768]{2,1,0:T(8,128)(2,1)S(1)}, bf16[1,512,768]{2,1,0:T(8,128)(2,1)}, u32[]{:S(2)}) copy-start(bf16[1,512,768]{2,1,0:T(8,128)(2,1)} %param.18) | copy-start | bytes 2359300
  12.9 8.4 %copy-start.12 = (f32[4,1792]{1,0:T(4,128)S(1)}, f32[4,1792]{1,0:T(4,128)}, u32[]{:S(2)}) copy-start(f32[4,1792]{1,0:T(4,128)} %refs_4_.1) | copy-start | bytes 86020
  12.9 8.4 %copy-start.19 = (s32[1,512]{1,0:T(1,128)S(1)}, s32[1,512]{1,0:T(1,128)}, u32[]{:S(2)}) copy-start(s32[1,512]{1,0:T(1,128)} %valid_ref.1) | copy-start | bytes 6148
  21.3 32.0 %copy-start.5 = (bf16[1,512,768]{2,1,0:T(8,128)(2,1)S(1)}, bf16[1,512,768]{2,1,0:T(8,128)(2,1)}, u32[]{:S(2)}) copy-start(bf16[1,512,768]{2,1,0:T(8,128)(2,1)} %param.19) | copy-start | bytes 2359300
  43.3 43.3 %copy-start.2 = (f32[512,16]{1,0:T(8,128)}, f32[512,16]{1,0:T(8,128)S(1)}, u32[]{:S(2)}) copy-start(f32[512,16]{1,0:T(8,128)S(1)} %get-tuple-element.49.masks_ref.refs_12_) | copy-start | bytes 98308
  43.3 43.3 %copy-start.3 = (f32[512,128]{1,0:T(8,128)}, f32[512,128]{1,0:T(8,128)S(1)}, u32[]{:S(2)}) copy-start(f32[512,128]{1,0:T(8,128)S(1)} %get-tuple-element.47.raw_ref.refs_10_) | copy-start | bytes 786436
  43.3 43.3 %copy-start.4 = (f32[512,128]{1,0:T(8,128)}, f32[512,128]{1,0:T(8,128)S(1)}, u32[]{:S(2)}) copy-start(f32[512,128]{1,0:T(8,128)S(1)} %get-tuple-element.48.cum_ref.refs_11_) | copy-start | bytes 786436
  43.3 43.3 %copy-start.6 = (bf16[512,768]{1,0:T(8,128)(2,1)}, bf16[512,768]{1,0:T(8,128)(2,1)S(1)}, u32[]{:S(2)}) copy-start(bf16[512,768]{1,0:T(8,128)(2,1)S(1)} %get-tuple-element.60.refs_19_) | copy-start | bytes 2359300
  43.3 43.3 %copy-start.10 = (f32[1,8,1536]{2,1,0:T(8,128)}, f32[1,8,1536]{2,1,0:T(8,128)S(1)}, u32[]{:S(2)}) copy-start(f32[1,8,1536]{2,1,0:T(8,128)S(1)} %get-tuple-element.51.keep_ref.refs_17_) | copy-start | bytes 147460
  43.3 43.3 %copy-start.11 = (f32[16,1792]{1,0:T(8,128)}, f32[16,1792]{1,0:T(8,128)S(1)}, u32[]{:S(2)}) copy-start(f32[16,1792]{1,0:T(8,128)S(1)} %get-tuple-element.54.refs_3_) | copy-start | bytes 344068
  86.7 0.9 copy-start.7
  87.6 0.9 copy-start.8
  88.5 0.7 copy-start.9
  89.2 0.6 copy-start.14
  89.8 0.6 copy-start.18
  230.1 12.5 %copy-start.20 = (bf16[512,768]{1,0:T(8,128)(2,1)S(1)}, bf16[512,768]{1,0:T(8,128)(2,1)}, u32[]{:S(2)}) copy-start(bf16[512,768]{1,0:T(8,128)(2,1)} %get-tuple-element.67) | copy-start | bytes 2359300

commit v6 on v5

--- a/solution.py
+++ b/solution.py
@@ -80,6 +80,10 @@
 
 def sigmoid(v):
     return 1.0 / (1.0 + jnp.exp(-v))
+
+
+def gate_of(v):
+    return 0.5 + 0.5 * jnp.tanh(0.5 * v)
 
 
 def softplus(v):
@@ -189,7 +193,7 @@
                     source = product[pl.ds(n * stride + HALO - 3 + k + i * 64, 64)]
                     total = total + source * masks_ref[rows, k : k + 1] * taps_ref[k : k + 1]
                 summed_ref[rows] = total
-                active[rows, pl.ds(at, GATE_BLOCK)] = (total * sigmoid(total)).astype(BF16)
+                active[rows, pl.ds(at, GATE_BLOCK)] = (total * gate_of(total)).astype(BF16)
 
     @pl.when(step == gate_blocks + conv_blocks)
     def _():
@@ -406,6 +410,7 @@
     factors,
     grads,
     inv,
+    totals,
 ):
     seqs, piece, inner, channels, heads = sizes
     c = pl.program_id(1)
@@ -424,7 +429,7 @@
     def activate(i, carry):
         rows = pl.ds(pl.multiple_of(i * 16, 16), 16)
         values = summed_ref[rows]
-        active[rows] = values * sigmoid(values)
+        active[rows] = values * gate_of(values)
         return carry
 
     lax.fori_loop(0, CHUNK // 16, activate, 0)
@@ -467,14 +472,25 @@
     gain = gain_ref[...]
     skip = skip_ref[...]
 
+    column_blocks = [slice(at, at + 512) for at in range(0, inner, 512)]
+
     def gating(i, carry):
         rows = pl.ds(pl.multiple_of(i * 16, 16), 16)
-        gate = gate_ref[rows]
-        mixer = mixed_in[rows] + skip * active[rows, :inner]
-        gated = mixer * gate * sigmoid(gate)
-        scale = lax.rsqrt(jnp.mean(gated * gated, axis=-1, keepdims=True) + EPS)
+        squares = jnp.zeros((16, 512), F32)
+        for at in column_blocks:
+            gate = gate_ref[rows, at]
+            turned = gate_of(gate)
+            mixer = mixed_in[rows, at] + skip[:, at] * active[rows, at]
+            product = mixer * gate * turned
+            factors[0, rows, at] = product
+            factors[1, rows, at] = turned
+            factors[2, rows, at] = mixer
+            squares = squares + product * product
+        mean = jnp.sum(squares, axis=-1, keepdims=True) / inner
+        scale = lax.rsqrt(mean + EPS)
         inv[rows] = jnp.broadcast_to(scale, (16, 128))
-        low_ref[rows] = (gated * scale * gain).astype(BF16)
+        for at in column_blocks:
+            low_ref[rows, at] = (factors[0, rows, at] * scale * gain[:, at]).astype(BF16)
         return carry
 
     lax.fori_loop(0, CHUNK // 16, gating, 0)
@@ -491,34 +507,42 @@
     out_low_ref[...] = out_low
     grads[...] = mm_nt(out_low, weight_ref[...])
 
+    @pl.when((c == 0) & (pl.program_id(0) == 0))
+    def _():
+        totals[...] = jnp.zeros_like(totals)
+
     def backing(i, carry):
-        gain_sum, skip_sum = carry
         rows = pl.ds(pl.multiple_of(i * 16, 16), 16)
-        gate = gate_ref[rows]
-        turned = sigmoid(gate)
-        silu = gate * turned
-        signal = active[rows, :inner]
-        mixer = mixed_in[rows] + skip * signal
-        gated = mixer * silu
         scale = inv[rows, 0:1]
-        grad = grads[rows]
-        gain_sum = gain_sum + grad * gated * scale
-        grad = grad * gain
-        inside = jnp.mean(grad * gated, axis=-1, keepdims=True)
-        gated_grad = scale * grad - gated * (scale * scale * scale * inside)
-        ssm_grad = gated_grad * silu
-        ssm_grad_ref[rows] = ssm_grad
-        grads[rows] = ssm_grad
-        skip_sum = skip_sum + ssm_grad * signal
-        gate_grad_ref[rows] = (gated_grad * mixer * turned * (1.0 + gate * (1.0 - turned))).astype(
-            BF16
-        )
-        return gain_sum, skip_sum
-
-    start = jnp.zeros((16, inner), F32)
-    gain_sum, skip_sum = lax.fori_loop(0, CHUNK // 16, backing, (start, start))
-    wide_ref[0:1] += jnp.sum(gain_sum, axis=0, keepdims=True)
-    wide_ref[1:2] += jnp.sum(skip_sum, axis=0, keepdims=True)
+        inside = jnp.zeros((16, 512), F32)
+        for at in column_blocks:
+            grad = grads[rows, at]
+            gated = factors[0, rows, at]
+            totals[0, :, at] += grad * gated * scale
+            inside = inside + grad * gain[:, at] * gated
+        inside = jnp.sum(inside, axis=-1, keepdims=True) / inner
+        inside = scale * scale * scale * inside
+        for at in column_blocks:
+            gate, turned = gate_ref[rows, at], factors[1, rows, at]
+            gated_grad = scale * (grads[rows, at] * gain[:, at]) - factors[0, rows, at] * inside
+            ssm_grad = gated_grad * (gate * turned)
+            ssm_grad_ref[rows, at] = ssm_grad
+            grads[rows, at] = ssm_grad
+            totals[1, :, at] += ssm_grad * active[rows, at]
+            gate_grad_ref[rows, at] = (
+                gated_grad * factors[2, rows, at] * turned * (1.0 + gate * (1.0 - turned))
+            ).astype(BF16)
+        return carry
+
+    lax.fori_loop(0, CHUNK // 16, backing, 0)
+
+    @pl.when((c == chunks - 1) & (pl.program_id(0) == seqs - 1))
+    def _():
+        wide_ref[0:1] = jnp.sum(totals[0], axis=0, keepdims=True)
+        skips = jnp.sum(totals[1], axis=0, keepdims=True)
+        skips = gather_heads(jnp.broadcast_to(skips, (8, inner)), heads_ref)
+        wide_ref[1:2, :128] = skips[0:1]
+
     reader_t = jnp.transpose(reader_low)
     for pair in range(heads // 2):
         at = slice(pair * 128, (pair + 1) * 128)
@@ -589,6 +613,7 @@
             pltpu.VMEM((4, CHUNK, inner), F32),
             pltpu.VMEM((CHUNK, inner), F32),
             pltpu.VMEM((CHUNK, 128), F32),
+            pltpu.VMEM((2, 16, inner), F32),
         ],
         compiler_params=pltpu.CompilerParams(vmem_limit_bytes=48 * 1024 * 1024),
         name="forward",
@@ -1083,7 +1108,7 @@
         def activate(i, carry):
             rows_at = pl.ds(pl.multiple_of(i * 32, 32), 32)
             values = summed_ref[rows_at]
-            turned = sigmoid(values)
+            turned = gate_of(values)
             active[rows_at] = values * turned
             bent[rows_at] = turned * (1.0 + values * (1.0 - turned))
             return carry
@@ -1470,18 +1495,21 @@
     tile = tile_of(pl.program_id(0), spot_ref)
     rows = m_ref.shape[1]
     part = lax.rem(spot_ref[0], split_rows)
-    mine = pl.ds(pl.multiple_of((spot_ref[1] * split_rows + part) * rows, 16), rows)
+    first = (spot_ref[1] * split_rows + part) * rows
+    start = jnp.minimum(lax.div(first, 128) * 128, out_weight_ref.shape[1] - 256)
+    window = pl.ds(pl.multiple_of(start, 128), 256)
+    mine = pl.ds(pl.multiple_of(first - start, 16), rows)
     half = pl.ds(pl.multiple_of(part * rows, 16), rows)
 
     @pl.when(tile < out_tiles)
     def _():
-        turned[...] = jnp.transpose(out_weight_ref[...])
+        turned[...] = jnp.transpose(out_weight_ref[:, window])
         w_ref[0] = turned[mine]
         m_ref[0] = out_momentum_ref[half]
 
     @pl.when(tile >= out_tiles)
     def _():
-        turned[...] = jnp.transpose(weight_ref[...])
+        turned[...] = jnp.transpose(weight_ref[:, window])
         w_ref[0] = turned[mine]
         m_ref[0] = momentum_ref[half]
 
@@ -1519,7 +1547,7 @@
                 pl.BlockSpec((share, LANES), lambda f, spot: (0, in_at(f, spot))),
             ],
             out_specs=(piece, piece),
-            scratch_shapes=[pltpu.VMEM((model, LANES), BF16)],
+            scratch_shapes=[pltpu.VMEM((256, LANES), BF16)],
         ),
         out_shape=(
             jax.ShapeDtypeStruct((flows, rows, LANES), BF16),
@@ -1536,14 +1564,40 @@
     gathered_b_ref,
     out_momentum_ref,
     momentum_ref,
+    totals_ref,
     out_weight_ref,
     weight_ref,
     new_out_momentum_ref,
     new_momentum_ref,
+    conv_weight_ref,
+    conv_bias_ref,
+    gate_gain_ref,
+    norm_gain_ref,
+    skip_ref,
+    dt_bias_ref,
+    a_log_ref,
+    output_rms_ref,
+    mixer_rms_ref,
     joined,
 ):
     group, slots, rows, _ = gathered_a_ref.shape
     step = pl.program_id(0)
+
+    @pl.when(step == 0)
+    def _():
+        heads, inner, model = skip_ref.shape[0], gate_gain_ref.shape[0], norm_gain_ref.shape[0]
+        side = inner + 128
+        conv_weight_ref[...] = totals_ref[0:4]
+        conv_bias_ref[...] = totals_ref[4]
+        gate_gain_ref[...] = totals_ref[5, :inner]
+        norm_gain_ref[...] = totals_ref[7, :model]
+        skip_ref[...] = totals_ref[6, :heads]
+        dt_bias_ref[...] = totals_ref[5, inner : inner + heads]
+        a_log_ref[...] = totals_ref[6, inner : inner + heads]
+        count = jnp.maximum(totals_ref[7:8, side + 9 : side + 10], 1.0) * model
+        squares = jnp.sum(totals_ref[5:7, side:], axis=1, keepdims=True)
+        output_rms_ref[...] = jnp.sqrt(squares[0:1] / count)
+        mixer_rms_ref[...] = jnp.sqrt(squares[1:2] / count)
 
     def write(gathered_ref, weights, old, new):
         for i in range(group // split_rows):
@@ -1570,7 +1624,7 @@
         write(gathered_b_ref, weight_ref, momentum_ref, new_momentum_ref)
 
 
-def finish(gathered_a, gathered_b, out_momentum_t, momentum, split_rows, group=4):
+def finish(gathered_a, gathered_b, out_momentum_t, momentum, totals, heads, split_rows, group=4):
     _, slots, rows, _ = gathered_a.shape
     share, width = momentum.shape
     inner = out_momentum_t.shape[1]
@@ -1585,6 +1639,20 @@
         pl.BlockSpec((share, wide), lambda j: (0, in_at(j))),
     ]
     shape = jax.ShapeDtypeStruct
+    smalls = [
+        shape(size, F32)
+        for size in (
+            (4, totals.shape[1]),
+            (totals.shape[1],),
+            (inner,),
+            (model,),
+            (heads,),
+            (heads,),
+            (heads,),
+            (1, 1),
+            (1, 1),
+        )
+    ]
     return pl.pallas_call(
         functools.partial(finish_kernel, out_steps, split_rows),
         grid=(out_steps + in_steps,),
@@ -1596,21 +1664,27 @@
                 (group, slots, rows, LANES), lambda j: (jnp.maximum(j - 2 * out_steps, 0), 0, 0, 0)
             ),
         ]
-        + by_column,
+        + by_column
+        + [pl.BlockSpec(totals.shape, lambda j: (0, 0))],
         out_specs=[
             pl.BlockSpec((wide, model), lambda j: (out_at(j), 0)),
             pl.BlockSpec((wide, model), lambda j: (in_at(j), 0)),
         ]
-        + by_column,
-        out_shape=(
+        + by_column
+        + [
+            pl.BlockSpec(small.shape, lambda j, count=len(small.shape): (0,) * count)
+            for small in smalls
+        ],
+        out_shape=[
             shape((inner, model), BF16),
             shape((width, model), BF16),
             shape((share, inner), F32),
             shape((share, width), F32),
-        ),
+        ]
+        + smalls,
         scratch_shapes=[pltpu.VMEM((model, LANES), BF16)],
         name="finish",
-    )(gathered_a, gathered_b, out_momentum_t, momentum)
+    )(gathered_a, gathered_b, out_momentum_t, momentum, totals)
 
 
 def local(
@@ -1744,28 +1818,32 @@
         (flows_a, flows_b),
     )
     share = (pieces + 1, share_rows // split_rows, LANES)
-    new_out_weight, new_weight_t, new_out_momentum_t, new_in_momentum = finish(
+    (
+        new_out_weight,
+        new_weight_t,
+        new_out_momentum_t,
+        new_in_momentum,
+        conv_weight_total,
+        conv_bias_total,
+        gate_gain_total,
+        norm_gain_total,
+        skip_total,
+        dt_bias_total,
+        a_log_total,
+        output_rms,
+        mixer_rms,
+    ) = finish(
         gathered_a.reshape((-1,) + share),
         gathered_b.reshape((-1,) + share),
         out_momentum_t,
         in_momentum,
+        totals,
+        heads,
         split_rows,
     )
     new_in_weight = jnp.transpose(new_weight_t)
     new_out_momentum = jnp.transpose(new_out_momentum_t)
-    conv_weight_total = totals[:tap_count]
-    conv_bias_total = totals[tap_count]
-    gate_gain_total = totals[5, :inner_width]
-    skip_total = totals[6, :inner_width].reshape(heads, -1).sum(axis=1)
-    norm_gain_total = totals[7, :model_width]
-    dt_bias_total = totals[5, inner_width : inner_width + heads]
-    a_log_total = totals[6, inner_width : inner_width + heads]
-    out_square_total = totals[5, inner_width + LANES :].sum()
-    mix_square_total = totals[6, inner_width + LANES :].sum()
-    valid_total = totals[7, inner_width + LANES + 9]
-    denominator = jnp.maximum(valid_total, 1.0) * model_width
-    output_rms = jnp.sqrt(out_square_total / denominator).reshape(1)
-    mixer_rms = jnp.sqrt(mix_square_total / denominator).reshape(1)
+    output_rms, mixer_rms = output_rms.reshape(1), mixer_rms.reshape(1)
     return (
         output.reshape(tokens.shape),
         input_grad.reshape(tokens.shape),

time: 249 us -> 230 us (0.924)
  local copies, waits for them, and re-layouts: 17.4 us -> 9.08 us
  between operations: 6.55 us -> 2.26 us
  Pallas kernels: 213 us -> 210 us
    slice x5 -> x0, local copies, waits for them, and re-layouts: 6.97 us -> none  [the longest x1 1.51 us: local(): gate_gain_total = totals[5, :inner_width]]
    pallas_call x1, Pallas kernels: 33.4 us -> 30.3 us  [forward(): pl.pallas_call(functools.partial(forward_kernel, sizes, chunks), grid=(se...]
where the time goes in v6:
time: 230 us; the launch traced here: 228 us
  Pallas kernels  210 us (91%)
  local copies, waits for them, and re-layouts  9.08 us (4%)
  starting transfers between devices  4.92 us (2%)
    pallas_call x1, Pallas kernels, tail(): pl.pallas_call(functools.partial(tail_kernel, sizes, (bits, pieces, flows...  127 us
    pallas_call x1, Pallas kernels, forward(): pl.pallas_call(functools.partial(forward_kernel, sizes, chunks), grid=(se...  30.3 us
    pallas_call x1, Pallas kernels, front(): pl.pallas_call(functools.partial(front_kernel, sizes), grid=(gate_blocks...  21.9 us
    pallas_call x1, Pallas kernels, finish(): pl.pallas_call(functools.partial(finish_kernel, out_steps, split_rows), g...  12.8 us
    pallas_call x1, Pallas kernels, chain(): pl.pallas_call(functools.partial(chain_kernel, ways, blocks), out_shape=j...  9.88 us
    pallas_call x1, Pallas kernels, owned(): pl.pallas_call(functools.partial(piece_kernel, (out_tiles, tile_of, split...  7.98 us
    ppermute x1, starting transfers between devices, local(): arrived = lax.ppermute(sent, 'seq', route)  4.92 us
    unnamed x43, local copies, waits for them, and re-layouts  4.61 us
  transfers between devices with their start and end apart: 1, of which 0 were waited for; matrix products, arithmetic and copies ran while one was open for 2% of the time, Pallas kernels for 3%

profile of v6, /device:TPU:0, one launch (start us, length us, event | category | flops | bytes accessed | tf_op | source)
XLA Modules:
  0.0 228.1 jit_solution(4664858790621440127)
XLA Ops:
  0.6 0.7 convert_element_type.35.seg_row_ref.refs_13_
  1.3 0.1 fusion.4
  1.4 0.7 slice.13
  2.1 0.1 broadcast_in_dim.13
  2.2 4.9 %collective-permute-start = (bf16[1,16,896]{2,1,0:T(8,128)(2,1)S(1)}, bf16[1,16,896]{2,1,0:T(8,128)(2,1)S(1)}, u32[]{:S(2)}, u32[]{:S(2)}) collective-permute-start(bf16[1,16,896]{2,1,0:T(8,128)(2,1)S(1)} %pad_maximum_fusion), channel_id=1, source_target_pairs={{0,1},{1,2},{2,3},{4,5},{5,6},{6,7},{8,9},{9,10},{10,11},{12,13},{... | collective-permute-start | bytes 86024 | tf_op jit(solution)/shard_map/ppermute | solution.py:1728
  7.2 0.7 pad_bitcast_fusion
  7.9 0.1 fusion.heads_ref.refs_7_
  7.9 0.0 copy-start.1
  8.0 0.6 pad_add_fusion.spot_ref
  9.9 0.7 reshape.107.gain_ref.refs_24_
  10.6 0.7 reshape.112.gain_ref
  11.3 0.7 reshape.108.bias_ref
  12.0 0.7 broadcast_in_dim.15
  12.7 0.1 reshape_reshape.3.skip_ref.refs_8_
  12.8 0.0 copy-start
  12.9 0.0 copy-start.12
  12.9 0.0 copy-start.19
  12.9 8.0 %owned.1 = (bf16[10,96,128]{2,1,0:T(8,128)(2,1)}, f32[10,96,128]{2,1,0:T(8,128)}) custom-call(s32[2]{0:T(128)} %pad_add_fusion.spot_ref, bf16[1536,768]{1,0:T(8,128)(2,1)} %out_weight_ref.1, bf16[3352,768]{1,0:T(8,128)(2,1)} %bitcast.27, f32[192,1536]{1,0:T(8,128)} %bitcast.31, f32[192,3352]{1,0:T(8,128)} %momentum_ref.3), custom_call_target="tpu_custom_call" | custom-call | tf_op jit(solution)/shard_map/owned/pallas_call | solution.py:1538
  20.9 0.0 collective-permute-done
  20.9 0.1 select_reduce_fusion
  21.0 0.1 pad_maximum_fusion.1.seg_ref
  21.1 0.0 copy-done.17
  21.1 0.0 copy-done.16
  21.1 0.0 copy-done
  21.1 0.0 copy-done.12
  21.1 0.0 copy-done.19
  21.1 0.0 copy-start.5
  21.1 21.9 %front.1 = (bf16[512,768]{1,0:T(8,128)(2,1)S(1)}, f32[512,16]{1,0:T(8,128)S(1)}, f32[512,1536]{1,0:T(8,128)}, f32[512,1792]{1,0:T(8,128)}, f32[16,1792]{1,0:T(8,...) custom-call(bf16[512,768]{1,0:T(8,128)(2,1)S(1)} %bitcast.24, ...), custom_call_target="tpu_custom_call" | custom-call | tf_op jit(solution)/shard_map/front/pallas_call | solution.py:235
  43.0 0.0 copy-start.6
  43.0 0.0 copy-start.10
  43.0 0.0 copy-start.11
  43.0 9.9 %chain.1.incoming_ref = f32[1,128,1536]{2,1,0:T(8,128)S(1)} custom-call(f32[1,128,1536]{2,1,0:T(8,128)S(1)} %get-tuple-element.59.own_ref, f32[1,8,1536]{2,1,0:T(8,128)S(1)} %get-tuple-element.60.keep_ref.refs_17_), custom_call_target="tpu_custom_call" | custom-call | tf_op jit(solution)/shard_map/chain/pallas_call | solution.py:349
  52.9 0.0 copy-done.15
  52.9 0.0 copy-done.1
  52.9 0.0 copy-done.13
  52.9 0.0 copy-done.5
  52.9 30.3 %forward.1 = (bf16[512,768]{1,0:T(8,128)(2,1)}, bf16[512,1536]{1,0:T(8,128)(2,1)}, bf16[512,768]{1,0:T(8,128)(2,1)S(1)}, bf16[512,1536]{1,0:T(8,128)(2,1)}, f32[...) custom-call(f32[512,1792]{1,0:T(8,128)} %get-tuple-element.54.summed, ...), custom_call_target="tpu_custom_call" | custom-call | tf_op jit(solution)/shard_map/forward/pallas_call | solution.py:566
  83.2 0.0 copy-done.2
  83.2 0.0 copy-done.3
  83.2 0.0 copy-start.7
  83.3 0.9 copy-done.7
  84.1 0.9 copy-done.8
  85.0 0.7 copy-done.9
  85.7 0.6 copy-done.14
  86.3 0.6 copy-done.18
  86.9 127.4 %tail.1 = (bf16[512,768]{1,0:T(8,128)(2,1)}, f32[8,1792]{1,0:T(8,128)}, bf16[6,2,2,2,5,96,128]{6,5,4,3,2,1,0:T(8,128)(2,1)}, bf16[4,2,2,2,5,96,128]{6,5,4,3,2,1,0:T(8,128)(2,1)}) custom-call(f32[1]{0:T(128)S(6)} %div.19.refs_0_, f32[512,1792]{1,0:T(8,128)} %get-tuple-element.54.summed_ref.refs_1_.refs_9_, f32[512,1792]{1,0:T(8,128)} %get-tuple-element.62.refs_2_, ...), custom_call_target="tpu_custom_call" | custom-call | tf_op jit(solution)/shard_map/tail/pallas_call | solution.py:1408
  214.4 12.8 %finish.1 = (bf16[1536,768]{1,0:T(8,128)(2,1)}, bf16[3352,768]{1,0:T(8,128)(2,1)}, f32[192,1536]{1,0:T(8,128)}, f32[192,3352]{1,0:T(8,128)}, f32[4,1792]{1,0:T(4...) custom-call(bf16[48,5,96,128]{3,2,1,0:T(8,128)(2,1)} %bitcast.30, ...), custom_call_target="tpu_custom_call" | custom-call | tf_op jit(solution)/shard_map/finish/pallas_call | solution.py:1656
  227.2 0.9 copy.35
  (21 shorter events, 0.1 us)
Async XLA Ops:
  1.3 51.6 %copy-start.15 = (f32[1,512]{1,0:T(1,128)}, f32[1,512]{1,0:T(1,128)S(1)}, u32[]{:S(2)}) copy-start(f32[1,512]{1,0:T(1,128)S(1)} %convert_element_type.35.seg_row_ref.refs_13_) | copy-start | bytes 6148
  2.2 18.6 %collective-permute-start = (bf16[1,16,896]{2,1,0:T(8,128)(2,1)S(1)}, bf16[1,16,896]{2,1,0:T(8,128)(2,1)S(1)}, u32[]{:S(2)}, u32[]{:S(2)}) collective-permute-start(bf16[1,16,896]{2,1,0:T(8,128)(2,1)S(1)} %pad_maximum_fusion), channel_id=1, source_target_pairs={{0,1},{1,2},{2,3},{4,5},{5,6},{6,7},{8,9},{9,10},{10,11},{12,13},{... | collective-permute-start | bytes 86024 | tf_op jit(solution)/shard_map/ppermute | solution.py:1728
  7.9 13.2 %copy-start.17 = (f32[1,128]{1,0:T(1,128)}, f32[1,128]{1,0:T(1,128)S(1)}, u32[]{:S(2)}) copy-start(f32[1,128]{1,0:T(1,128)S(1)} %get-tuple-element.95.a_log_ref.refs_15_) | copy-start | bytes 1540
  7.9 45.0 %copy-start.1 = (bf16[128,1536]{1,0:T(8,128)(2,1)}, bf16[128,1536]{1,0:T(8,128)(2,1)S(1)}, u32[]{:S(2)}) copy-start(bf16[128,1536]{1,0:T(8,128)(2,1)S(1)} %fusion.heads_ref.refs_7_) | copy-start | bytes 1179652
  10.6 10.5 %copy-start.16 = (f32[1,768]{1,0:T(1,128)}, f32[1,768]{1,0:T(1,128)S(1)}, u32[]{:S(2)}) copy-start(f32[1,768]{1,0:T(1,128)S(1)} %reshape.107.gain_ref.refs_24_) | copy-start | bytes 9220
  12.8 40.1 %copy-start.13 = (f32[1,1536]{1,0:T(1,128)}, f32[1,1536]{1,0:T(1,128)S(1)}, u32[]{:S(2)}) copy-start(f32[1,1536]{1,0:T(1,128)S(1)} %reshape_reshape.3.skip_ref.refs_8_) | copy-start | bytes 18436
  12.8 8.2 %copy-start = (bf16[1,512,768]{2,1,0:T(8,128)(2,1)S(1)}, bf16[1,512,768]{2,1,0:T(8,128)(2,1)}, u32[]{:S(2)}) copy-start(bf16[1,512,768]{2,1,0:T(8,128)(2,1)} %param.18) | copy-start | bytes 2359300
  12.9 8.2 %copy-start.12 = (f32[4,1792]{1,0:T(4,128)S(1)}, f32[4,1792]{1,0:T(4,128)}, u32[]{:S(2)}) copy-start(f32[4,1792]{1,0:T(4,128)} %refs_4_.1) | copy-start | bytes 86020
  12.9 8.2 %copy-start.19 = (s32[1,512]{1,0:T(1,128)S(1)}, s32[1,512]{1,0:T(1,128)}, u32[]{:S(2)}) copy-start(s32[1,512]{1,0:T(1,128)} %valid_ref.1) | copy-start | bytes 6148
  21.1 31.8 %copy-start.5 = (bf16[1,512,768]{2,1,0:T(8,128)(2,1)S(1)}, bf16[1,512,768]{2,1,0:T(8,128)(2,1)}, u32[]{:S(2)}) copy-start(bf16[1,512,768]{2,1,0:T(8,128)(2,1)} %param.19) | copy-start | bytes 2359300
  43.0 40.2 %copy-start.2 = (f32[512,16]{1,0:T(8,128)}, f32[512,16]{1,0:T(8,128)S(1)}, u32[]{:S(2)}) copy-start(f32[512,16]{1,0:T(8,128)S(1)} %get-tuple-element.58.masks_ref.refs_12_) | copy-start | bytes 98308
  43.0 40.2 %copy-start.3 = (f32[512,128]{1,0:T(8,128)}, f32[512,128]{1,0:T(8,128)S(1)}, u32[]{:S(2)}) copy-start(f32[512,128]{1,0:T(8,128)S(1)} %get-tuple-element.56.raw_ref.refs_10_) | copy-start | bytes 786436
  43.0 40.2 %copy-start.4 = (f32[512,128]{1,0:T(8,128)}, f32[512,128]{1,0:T(8,128)S(1)}, u32[]{:S(2)}) copy-start(f32[512,128]{1,0:T(8,128)S(1)} %get-tuple-element.57.cum_ref.refs_11_) | copy-start | bytes 786436
  43.0 40.2 %copy-start.6 = (bf16[512,768]{1,0:T(8,128)(2,1)}, bf16[512,768]{1,0:T(8,128)(2,1)S(1)}, u32[]{:S(2)}) copy-start(bf16[512,768]{1,0:T(8,128)(2,1)S(1)} %get-tuple-element.69.refs_19_) | copy-start | bytes 2359300
  43.0 40.2 %copy-start.10 = (f32[1,8,1536]{2,1,0:T(8,128)}, f32[1,8,1536]{2,1,0:T(8,128)S(1)}, u32[]{:S(2)}) copy-start(f32[1,8,1536]{2,1,0:T(8,128)S(1)} %get-tuple-element.60.keep_ref.refs_17_) | copy-start | bytes 147460
  43.0 40.2 %copy-start.11 = (f32[16,1792]{1,0:T(8,128)}, f32[16,1792]{1,0:T(8,128)S(1)}, u32[]{:S(2)}) copy-start(f32[16,1792]{1,0:T(8,128)S(1)} %get-tuple-element.63.refs_3_) | copy-start | bytes 344068
  83.2 0.9 copy-start.7
  84.1 0.9 copy-start.8
  85.0 0.7 copy-start.9
  85.7 0.6 copy-start.14
  86.3 0.6 copy-start.18
  214.3 12.8 %copy-start.20 = (bf16[512,768]{1,0:T(8,128)(2,1)S(1)}, bf16[512,768]{1,0:T(8,128)(2,1)}, u32[]{:S(2)}) copy-start(bf16[512,768]{1,0:T(8,128)(2,1)} %get-tuple-element.76) | copy-start | bytes 2359300

commit v7 on v6

--- a/solution.py
+++ b/solution.py
@@ -438,12 +438,13 @@
     cum = cum_ref[...]
     cum_t = jnp.transpose(cum)
     final = cum[CHUNK - 1 :]
-    enter = jnp.exp(cum) * masks_ref[:, 4:5]
     tails = jnp.exp(final - cum) * steps * masks_ref[:, 5:6]
-    from_start = jnp.exp(cum + prefix[0:1]) * masks_ref[:, 6:7]
+    before = spread(jnp.exp(prefix[...]), heads_ref)[0:1]
     prefix[...] = prefix[...] + final
-    for i, block in enumerate((steps, enter, tails, from_start)):
+    for i, block in enumerate((steps, jnp.exp(cum), tails)):
         factors[i] = spread(block, heads_ref)
+    factors[3] = factors[1] * before * masks_ref[:, 6:7]
+    factors[1] = factors[1] * masks_ref[:, 4:5]
     writer = active[:, inner : inner + 128]
     reader = active[:, inner + 128 : inner + 256]
     scores = scores_of(reader, writer)
@@ -831,7 +832,7 @@
         normed_ref,
         low_ref,
         gate_grad_ref,
-        weight_t_ref,
+        weight_t_hbm,
         tokens_ref,
         gain_ref,
         weight_ref,
@@ -891,7 +892,10 @@
         sm_recv,
         sz_send,
         sz_recv,
+        weight_t_ref,
+        weight_sem,
     ) = scratch
+    weight_copy = pltpu.make_async_copy(weight_t_hbm, weight_t_ref, weight_sem)
     j = pl.program_id(0)
     steps = inner // TILE
     final_step = steps + 1
@@ -994,6 +998,7 @@
                 sent[c] = own_ref[:, :, c * width : (c + 1) * width].astype(BF16)
                 copy(c).start()
 
+        weight_copy.start()
         out_turned[...] = jnp.transpose(out_low_ref[...])
         normed_turned[...] = jnp.transpose(normed_ref[...])
         low_tiles = inner // LANES
@@ -1258,6 +1263,7 @@
                 b_taken[f] = 0
 
         rest = weight_t_ref.shape[0] - inner
+        weight_copy.wait()
 
         def input_rows(i, carry):
             rows_at = pl.ds(pl.multiple_of(i * 128, 128), 128)
@@ -1330,7 +1336,7 @@
         while any(lines) or extra:
             if extra:
                 extra.pop(0)()
-            for line in lines:
+            for line in lines[flows_a:] + lines[:flows_a]:
                 if line:
                     line.pop(0)()
         b.tiles_sent()
@@ -1424,7 +1430,7 @@
             columns(1, steps - 1),
             pl.BlockSpec((total_rows, TILE), lambda j: (0, steps), pipeline_mode=pl.Buffered(1)),
         ]
-        + [constant(array) for array in constants],
+        + [any_space if array is weight_t else constant(array) for array in constants],
         out_specs=(
             pl.BlockSpec((total_rows, model), lambda j: (0, 0)),
             pl.BlockSpec(small, lambda j: (0, 0)),
@@ -1480,7 +1486,8 @@
             pltpu.VMEM((pieces,) + small, F32),
         ]
         + sem(bits)
-        + sem(pieces),
+        + sem(pieces)
+        + [pltpu.VMEM(weight_t.shape, BF16), pltpu.SemaphoreType.DMA],
         compiler_params=pltpu.CompilerParams(
             collective_id=2, has_side_effects=True, vmem_limit_bytes=62 * 1024 * 1024
         ),

time: 230 us -> 227 us (0.987)
  Pallas kernels: 210 us -> 207 us
    pallas_call x1, Pallas kernels: 127 us -> 125 us  [tail(): pl.pallas_call(functools.partial(tail_kernel, sizes, (bits, pieces, flows...]
  transfers between devices with their start and end apart: 1 -> 1, of which waited for: 0 -> 0; matrix products, arithmetic and copies ran while one was open for 2% -> 2% of each run, Pallas kernels for 3% -> 4%
where the time goes in v7:
time: 227 us; the launch traced here: 225 us
  Pallas kernels  207 us (91%)
  local copies, waits for them, and re-layouts  9.08 us (4%)
  starting transfers between devices  4.92 us (2%)
    pallas_call x1, Pallas kernels, tail(): pl.pallas_call(functools.partial(tail_kernel, sizes, (bits, pieces, flows...  125 us
    pallas_call x1, Pallas kernels, forward(): pl.pallas_call(functools.partial(forward_kernel, sizes, chunks), grid=(se...  29.7 us
    pallas_call x1, Pallas kernels, front(): pl.pallas_call(functools.partial(front_kernel, sizes), grid=(gate_blocks...  21.9 us
    pallas_call x1, Pallas kernels, finish(): pl.pallas_call(functools.partial(finish_kernel, out_steps, split_rows), g...  12.8 us
    pallas_call x1, Pallas kernels, chain(): pl.pallas_call(functools.partial(chain_kernel, ways, blocks), out_shape=j...  9.88 us
    pallas_call x1, Pallas kernels, owned(): pl.pallas_call(functools.partial(piece_kernel, (out_tiles, tile_of, split...  7.98 us
    ppermute x1, starting transfers between devices, local(): arrived = lax.ppermute(sent, 'seq', route)  4.92 us
    unnamed x43, local copies, waits for them, and re-layouts  4.61 us
  transfers between devices with their start and end apart: 1, of which 0 were waited for; matrix products, arithmetic and copies ran while one was open for 2% of the time, Pallas kernels for 4%

profile of v7, /device:TPU:0, one launch (start us, length us, event | category | flops | bytes accessed | tf_op | source)
XLA Modules:
  0.0 225.0 jit_solution(4372238502299584264)
XLA Ops:
  0.6 0.7 convert_element_type.35.seg_row_ref.refs_13_
  1.3 0.1 fusion.4
  1.4 0.7 slice.13
  2.1 0.1 broadcast_in_dim.13
  2.2 4.9 %collective-permute-start = (bf16[1,16,896]{2,1,0:T(8,128)(2,1)S(1)}, bf16[1,16,896]{2,1,0:T(8,128)(2,1)S(1)}, u32[]{:S(2)}, u32[]{:S(2)}) collective-permute-start(bf16[1,16,896]{2,1,0:T(8,128)(2,1)S(1)} %pad_maximum_fusion), channel_id=1, source_target_pairs={{0,1},{1,2},{2,3},{4,5},{5,6},{6,7},{8,9},{9,10},{10,11},{12,13},{... | collective-permute-start | bytes 86024 | tf_op jit(solution)/shard_map/ppermute | solution.py:1735
  7.2 0.7 pad_bitcast_fusion
  7.9 0.1 fusion.heads_ref.refs_7_
  7.9 0.0 copy-start.1
  8.0 0.6 pad_add_fusion.spot_ref
  9.9 0.7 reshape.107.gain_ref.refs_24_
  10.6 0.7 reshape.112.gain_ref
  11.3 0.7 reshape.108.bias_ref
  12.0 0.7 broadcast_in_dim.15
  12.7 0.1 reshape_reshape.3.skip_ref.refs_8_
  12.8 0.0 copy-start
  12.9 0.0 copy-start.12
  12.9 0.0 copy-start.19
  12.9 8.0 %owned.1 = (bf16[10,96,128]{2,1,0:T(8,128)(2,1)}, f32[10,96,128]{2,1,0:T(8,128)}) custom-call(s32[2]{0:T(128)} %pad_add_fusion.spot_ref, bf16[1536,768]{1,0:T(8,128)(2,1)} %out_weight_ref.1, bf16[3352,768]{1,0:T(8,128)(2,1)} %bitcast.27, f32[192,1536]{1,0:T(8,128)} %bitcast.31, f32[192,3352]{1,0:T(8,128)} %momentum_ref.3), custom_call_target="tpu_custom_call" | custom-call | tf_op jit(solution)/shard_map/owned/pallas_call | solution.py:1545
  20.9 0.0 collective-permute-done
  20.9 0.1 select_reduce_fusion
  21.0 0.1 pad_maximum_fusion.1.seg_ref
  21.1 0.0 copy-done.17
  21.1 0.0 copy-done.16
  21.1 0.0 copy-done
  21.1 0.0 copy-done.12
  21.1 0.0 copy-done.19
  21.1 0.0 copy-start.5
  21.1 21.9 %front.1 = (bf16[512,768]{1,0:T(8,128)(2,1)S(1)}, f32[512,16]{1,0:T(8,128)S(1)}, f32[512,1536]{1,0:T(8,128)}, f32[512,1792]{1,0:T(8,128)}, f32[16,1792]{1,0:T(8,...) custom-call(bf16[512,768]{1,0:T(8,128)(2,1)S(1)} %bitcast.24, ...), custom_call_target="tpu_custom_call" | custom-call | tf_op jit(solution)/shard_map/front/pallas_call | solution.py:235
  43.0 0.0 copy-start.6
  43.0 0.0 copy-start.10
  43.0 0.0 copy-start.11
  43.0 9.9 %chain.1.incoming_ref = f32[1,128,1536]{2,1,0:T(8,128)S(1)} custom-call(f32[1,128,1536]{2,1,0:T(8,128)S(1)} %get-tuple-element.59.own_ref, f32[1,8,1536]{2,1,0:T(8,128)S(1)} %get-tuple-element.60.keep_ref.refs_17_), custom_call_target="tpu_custom_call" | custom-call | tf_op jit(solution)/shard_map/chain/pallas_call | solution.py:349
  52.9 0.0 copy-done.15
  52.9 0.0 copy-done.1
  52.9 0.0 copy-done.13
  52.9 0.0 copy-done.5
  52.9 29.7 %forward.1 = (bf16[512,768]{1,0:T(8,128)(2,1)}, bf16[512,1536]{1,0:T(8,128)(2,1)}, bf16[512,768]{1,0:T(8,128)(2,1)S(1)}, bf16[512,1536]{1,0:T(8,128)(2,1)}, f32[...) custom-call(f32[512,1792]{1,0:T(8,128)} %get-tuple-element.54.summed, ...), custom_call_target="tpu_custom_call" | custom-call | tf_op jit(solution)/shard_map/forward/pallas_call | solution.py:567
  82.6 0.0 copy-done.3
  82.6 0.0 copy-start.7
  82.7 0.9 copy-done.7
  83.5 0.9 copy-done.8
  84.4 0.7 copy-done.9
  85.1 0.6 copy-done.14
  85.7 0.6 copy-done.18
  86.3 125.0 %tail.1 = (bf16[512,768]{1,0:T(8,128)(2,1)}, f32[8,1792]{1,0:T(8,128)}, bf16[6,2,2,2,5,96,128]{6,5,4,3,2,1,0:T(8,128)(2,1)}, bf16[4,2,2,2,5,96,128]{6,5,4,3,2,1,0:T(8,128)(2,1)}) custom-call(f32[1]{0:T(128)S(6)} %div.19.refs_0_, f32[512,1792]{1,0:T(8,128)} %get-tuple-element.54.summed_ref.refs_1_.refs_9_, f32[512,1792]{1,0:T(8,128)} %get-tuple-element.62.refs_2_, ...), custom_call_target="tpu_custom_call" | custom-call | tf_op jit(solution)/shard_map/tail/pallas_call | solution.py:1414
  211.3 0.0 copy-start.20
  211.3 12.8 %finish.1 = (bf16[1536,768]{1,0:T(8,128)(2,1)}, bf16[3352,768]{1,0:T(8,128)(2,1)}, f32[192,1536]{1,0:T(8,128)}, f32[192,3352]{1,0:T(8,128)}, f32[4,1792]{1,0:T(4...) custom-call(bf16[48,5,96,128]{3,2,1,0:T(8,128)(2,1)} %bitcast.30, ...), custom_call_target="tpu_custom_call" | custom-call | tf_op jit(solution)/shard_map/finish/pallas_call | solution.py:1663
  224.2 0.9 copy.35
  (21 shorter events, 0.1 us)
Async XLA Ops:
  1.3 51.6 %copy-start.15 = (f32[1,512]{1,0:T(1,128)}, f32[1,512]{1,0:T(1,128)S(1)}, u32[]{:S(2)}) copy-start(f32[1,512]{1,0:T(1,128)S(1)} %convert_element_type.35.seg_row_ref.refs_13_) | copy-start | bytes 6148
  2.2 18.6 %collective-permute-start = (bf16[1,16,896]{2,1,0:T(8,128)(2,1)S(1)}, bf16[1,16,896]{2,1,0:T(8,128)(2,1)S(1)}, u32[]{:S(2)}, u32[]{:S(2)}) collective-permute-start(bf16[1,16,896]{2,1,0:T(8,128)(2,1)S(1)} %pad_maximum_fusion), channel_id=1, source_target_pairs={{0,1},{1,2},{2,3},{4,5},{5,6},{6,7},{8,9},{9,10},{10,11},{12,13},{... | collective-permute-start | bytes 86024 | tf_op jit(solution)/shard_map/ppermute | solution.py:1735
  7.9 13.2 %copy-start.17 = (f32[1,128]{1,0:T(1,128)}, f32[1,128]{1,0:T(1,128)S(1)}, u32[]{:S(2)}) copy-start(f32[1,128]{1,0:T(1,128)S(1)} %get-tuple-element.95.a_log_ref.refs_15_) | copy-start | bytes 1540
  7.9 45.0 %copy-start.1 = (bf16[128,1536]{1,0:T(8,128)(2,1)}, bf16[128,1536]{1,0:T(8,128)(2,1)S(1)}, u32[]{:S(2)}) copy-start(bf16[128,1536]{1,0:T(8,128)(2,1)S(1)} %fusion.heads_ref.refs_7_) | copy-start | bytes 1179652
  10.6 10.5 %copy-start.16 = (f32[1,768]{1,0:T(1,128)}, f32[1,768]{1,0:T(1,128)S(1)}, u32[]{:S(2)}) copy-start(f32[1,768]{1,0:T(1,128)S(1)} %reshape.107.gain_ref.refs_24_) | copy-start | bytes 9220
  12.8 40.1 %copy-start.13 = (f32[1,1536]{1,0:T(1,128)}, f32[1,1536]{1,0:T(1,128)S(1)}, u32[]{:S(2)}) copy-start(f32[1,1536]{1,0:T(1,128)S(1)} %reshape_reshape.3.skip_ref.refs_8_) | copy-start | bytes 18436
  12.8 8.2 %copy-start = (bf16[1,512,768]{2,1,0:T(8,128)(2,1)S(1)}, bf16[1,512,768]{2,1,0:T(8,128)(2,1)}, u32[]{:S(2)}) copy-start(bf16[1,512,768]{2,1,0:T(8,128)(2,1)} %param.18) | copy-start | bytes 2359300
  12.9 8.2 %copy-start.12 = (f32[4,1792]{1,0:T(4,128)S(1)}, f32[4,1792]{1,0:T(4,128)}, u32[]{:S(2)}) copy-start(f32[4,1792]{1,0:T(4,128)} %refs_4_.1) | copy-start | bytes 86020
  12.9 8.2 %copy-start.19 = (s32[1,512]{1,0:T(1,128)S(1)}, s32[1,512]{1,0:T(1,128)}, u32[]{:S(2)}) copy-start(s32[1,512]{1,0:T(1,128)} %valid_ref.1) | copy-start | bytes 6148
  21.1 31.8 %copy-start.5 = (bf16[1,512,768]{2,1,0:T(8,128)(2,1)S(1)}, bf16[1,512,768]{2,1,0:T(8,128)(2,1)}, u32[]{:S(2)}) copy-start(bf16[1,512,768]{2,1,0:T(8,128)(2,1)} %param.19) | copy-start | bytes 2359300
  43.0 39.6 %copy-start.2 = (f32[512,16]{1,0:T(8,128)}, f32[512,16]{1,0:T(8,128)S(1)}, u32[]{:S(2)}) copy-start(f32[512,16]{1,0:T(8,128)S(1)} %get-tuple-element.58.masks_ref.refs_12_) | copy-start | bytes 98308
  43.0 39.6 %copy-start.3 = (f32[512,128]{1,0:T(8,128)}, f32[512,128]{1,0:T(8,128)S(1)}, u32[]{:S(2)}) copy-start(f32[512,128]{1,0:T(8,128)S(1)} %get-tuple-element.56.raw_ref.refs_10_) | copy-start | bytes 786436
  43.0 39.6 %copy-start.4 = (f32[512,128]{1,0:T(8,128)}, f32[512,128]{1,0:T(8,128)S(1)}, u32[]{:S(2)}) copy-start(f32[512,128]{1,0:T(8,128)S(1)} %get-tuple-element.57.cum_ref.refs_11_) | copy-start | bytes 786436
  43.0 39.6 %copy-start.6 = (bf16[512,768]{1,0:T(8,128)(2,1)}, bf16[512,768]{1,0:T(8,128)(2,1)S(1)}, u32[]{:S(2)}) copy-start(bf16[512,768]{1,0:T(8,128)(2,1)S(1)} %get-tuple-element.69.refs_19_) | copy-start | bytes 2359300
  43.0 39.6 %copy-start.10 = (f32[1,8,1536]{2,1,0:T(8,128)}, f32[1,8,1536]{2,1,0:T(8,128)S(1)}, u32[]{:S(2)}) copy-start(f32[1,8,1536]{2,1,0:T(8,128)S(1)} %get-tuple-element.60.keep_ref.refs_17_) | copy-start | bytes 147460
  43.0 39.6 %copy-start.11 = (f32[16,1792]{1,0:T(8,128)}, f32[16,1792]{1,0:T(8,128)S(1)}, u32[]{:S(2)}) copy-start(f32[16,1792]{1,0:T(8,128)S(1)} %get-tuple-element.63.refs_3_) | copy-start | bytes 344068
  82.6 0.9 copy-start.7
  83.5 0.9 copy-start.8
  84.4 0.7 copy-start.9
  85.1 0.6 copy-start.14
  85.7 0.6 copy-start.18
  211.3 12.8 %copy-start.20 = (bf16[512,768]{1,0:T(8,128)(2,1)S(1)}, bf16[512,768]{1,0:T(8,128)(2,1)}, u32[]{:S(2)}) copy-start(bf16[512,768]{1,0:T(8,128)(2,1)} %get-tuple-element.76) | copy-start | bytes 2359300

commit v8 on v7

--- a/solution.py
+++ b/solution.py
@@ -1496,72 +1496,120 @@
 
 
 def piece_kernel(
-    counts, spot_ref, out_weight_ref, weight_ref, out_momentum_ref, momentum_ref, w_ref, m_ref, turned
+    dims,
+    out_weight_ref,
+    weight_ref,
+    out_momentum_ref,
+    momentum_ref,
+    last_momentum_ref,
+    w_ref,
+    m_ref,
+    tiles,
+    halves,
+    turned,
+    w_sem,
+    m_sem,
 ):
-    out_tiles, tile_of, split_rows = counts
-    tile = tile_of(pl.program_id(0), spot_ref)
-    rows = m_ref.shape[1]
-    part = lax.rem(spot_ref[0], split_rows)
-    first = (spot_ref[1] * split_rows + part) * rows
-    start = jnp.minimum(lax.div(first, 128) * 128, out_weight_ref.shape[1] - 256)
+    flows_a, flows_b, places, split_rows = dims
+    place, turn = lax.axis_index("dp"), lax.axis_index("seq")
+    rows, per_flow = m_ref.shape[1], places // split_rows
+    inner, model = out_weight_ref.shape
+    width = weight_ref.shape[0]
+    out_tiles, in_tiles, rest = inner // LANES, width // LANES, width % LANES
+    part = lax.rem(place, split_rows)
+    first = (turn * split_rows + part) * rows
+    start = jnp.minimum(lax.div(first, 128) * 128, model - 256)
     window = pl.ds(pl.multiple_of(start, 128), 256)
     mine = pl.ds(pl.multiple_of(first - start, 16), rows)
-    half = pl.ds(pl.multiple_of(part * rows, 16), rows)
-
-    @pl.when(tile < out_tiles)
-    def _():
-        turned[...] = jnp.transpose(out_weight_ref[:, window])
-        w_ref[0] = turned[mine]
-        m_ref[0] = out_momentum_ref[half]
-
-    @pl.when(tile >= out_tiles)
-    def _():
-        turned[...] = jnp.transpose(weight_ref[:, window])
-        w_ref[0] = turned[mine]
-        m_ref[0] = momentum_ref[half]
-
-
-def owned(spot, out_weight, weight_t, out_momentum_t, momentum, flows_a, flows_b, places):
-    inner, model = out_weight.shape
+    half = pl.ds(pl.multiple_of(part * rows, 8), rows)
+    within = lax.div(place, split_rows)
+    flows = flows_a + flows_b
+
+    def each(act):
+        for f in range(flows):
+            if f < flows_a:
+                tile = f * per_flow + within
+            else:
+                tile = 2 * out_tiles + (f - flows_a) * per_flow + within
+            act(f, tile)
+
+    def copies(source, momentum, at, count, f):
+        yield pltpu.make_async_copy(
+            source.at[pl.ds(pl.multiple_of(at, 8), count), window],
+            tiles.at[f, pl.ds(0, count)],
+            w_sem.at[f],
+        )
+        if count == LANES:
+            lanes = pl.ds(pl.multiple_of(at, LANES), LANES)
+            yield pltpu.make_async_copy(momentum.at[half, lanes], halves.at[f], m_sem.at[f])
+
+    def moves(f, tile, act):
+        in_limit = out_tiles + in_tiles
+        if f < flows_a:
+            in_limit = min(in_limit, 2 * out_tiles)
+
+        @pl.when(tile < out_tiles)
+        def _():
+            for copy in copies(out_weight_ref, out_momentum_ref, tile * LANES, LANES, f):
+                act(copy)
+
+        @pl.when((tile >= out_tiles) & (tile < in_limit))
+        def _():
+            at = (tile - out_tiles) * LANES
+            for copy in copies(weight_ref, momentum_ref, at, LANES, f):
+                act(copy)
+
+        if rest and f >= flows_a:
+
+            @pl.when(tile == in_limit)
+            def _():
+                for copy in copies(weight_ref, momentum_ref, in_tiles * LANES, rest, f):
+                    act(copy)
+
+    tiles[...] = jnp.zeros_like(tiles)
+    halves[...] = jnp.zeros_like(halves)
+    each(lambda f, tile: moves(f, tile, lambda copy: copy.start()))
+    each(lambda f, tile: moves(f, tile, lambda copy: copy.wait()))
+
+    def take(f, tile):
+        turned[...] = jnp.transpose(tiles[f])
+        w_ref[f] = turned[mine]
+        m_ref[f] = halves[f]
+        if rest and f >= flows_a:
+
+            @pl.when(tile == out_tiles + in_tiles)
+            def _():
+                m_ref[f] = last_momentum_ref[half]
+
+    each(take)
+
+
+def owned(out_weight, weight_t, out_momentum_t, momentum, flows_a, flows_b, places):
+    model = out_weight.shape[1]
     share, width = momentum.shape
-    out_tiles, in_tiles = inner // LANES, -(-width // LANES)
     split_rows = row_split(places, share)
-    rows, per_flow = share // split_rows, places // split_rows
-
-    flows = flows_a + flows_b
-
-    def tile_of(f, spot):
-        early = jnp.minimum(f * per_flow + spot[0] // split_rows, 2 * out_tiles - 1)
-        late = 2 * out_tiles + (f - flows_a) * per_flow + spot[0] // split_rows
-        return jnp.where(f < flows_a, early, late)
-
-    def out_at(f, spot):
-        return jnp.clip(tile_of(f, spot), 0, out_tiles - 1)
-
-    def in_at(f, spot):
-        return jnp.clip(tile_of(f, spot) - out_tiles, 0, in_tiles - 1)
-
-    piece = pl.BlockSpec((1, rows, LANES), lambda f, spot: (f, 0, 0))
+    rows, flows = share // split_rows, flows_a + flows_b
+    whole = width // LANES * LANES
+    last_momentum = jnp.pad(momentum[:, whole:], ((0, 0), (0, LANES - (width - whole))))
+    any_space = pl.BlockSpec(memory_space=pl.ANY)
+    vmem = pl.BlockSpec(memory_space=pltpu.VMEM)
     return pl.pallas_call(
-        functools.partial(piece_kernel, (out_tiles, tile_of, split_rows)),
-        grid_spec=pltpu.PrefetchScalarGridSpec(
-            num_scalar_prefetch=1,
-            grid=(flows,),
-            in_specs=[
-                pl.BlockSpec((LANES, model), lambda f, spot: (out_at(f, spot), 0)),
-                pl.BlockSpec((LANES, model), lambda f, spot: (in_at(f, spot), 0)),
-                pl.BlockSpec((share, LANES), lambda f, spot: (0, out_at(f, spot))),
-                pl.BlockSpec((share, LANES), lambda f, spot: (0, in_at(f, spot))),
-            ],
-            out_specs=(piece, piece),
-            scratch_shapes=[pltpu.VMEM((256, LANES), BF16)],
-        ),
+        functools.partial(piece_kernel, (flows_a, flows_b, places, split_rows)),
+        in_specs=[any_space] * 4 + [vmem],
+        out_specs=(vmem, vmem),
         out_shape=(
             jax.ShapeDtypeStruct((flows, rows, LANES), BF16),
             jax.ShapeDtypeStruct((flows, rows, LANES), F32),
         ),
+        scratch_shapes=[
+            pltpu.VMEM((flows, LANES, 256), BF16),
+            pltpu.VMEM((flows, rows, LANES), F32),
+            pltpu.VMEM((256, LANES), BF16),
+            pltpu.SemaphoreType.DMA((flows,)),
+            pltpu.SemaphoreType.DMA((flows,)),
+        ],
         name="owned",
-    )(spot, out_weight, weight_t, out_momentum_t, momentum)
+    )(out_weight, weight_t, out_momentum_t, momentum, last_momentum)
 
 
 def finish_kernel(
@@ -1790,9 +1838,8 @@
     per_flow = places // split_rows
     flows_a = -(-2 * inner_width // (LANES * per_flow))
     flows_b = -(-(channels + 2 * LANES) // (LANES * per_flow))
-    spot = jnp.stack([lax.axis_index("dp"), turn]).astype(jnp.int32)
     weights, momenta = owned(
-        spot, out_weight, weight_t, out_momentum_t, in_momentum, flows_a, flows_b, places
+        out_weight, weight_t, out_momentum_t, in_momentum, flows_a, flows_b, places
     )
     input_grad, totals, gathered_a, gathered_b = tail(
         rate,

time: 227 us -> 224 us (0.987)
  Pallas kernels: 207 us -> 203 us
    pallas_call x1, Pallas kernels: 7.98 us -> 3.79 us  [owned(): pl.pallas_call(functools.partial(piece_kernel, (flows_a, flows_b, places,...]
  transfers between devices with their start and end apart: 1 -> 1, of which waited for: 0 -> 0; matrix products, arithmetic and copies ran while one was open for 2% -> 2% of each run, Pallas kernels for 4% -> 2%
where the time goes in v8:
time: 224 us; the launch traced here: 222 us
  Pallas kernels  203 us (91%)
  local copies, waits for them, and re-layouts  10.7 us (5%)
  starting transfers between devices  4.92 us (2%)
  between operations  2.25 us (1%)
    pallas_call x1, Pallas kernels, tail(): pl.pallas_call(functools.partial(tail_kernel, sizes, (bits, pieces, flows...  124 us
    pallas_call x1, Pallas kernels, forward(): pl.pallas_call(functools.partial(forward_kernel, sizes, chunks), grid=(se...  30 us
    pallas_call x1, Pallas kernels, front(): pl.pallas_call(functools.partial(front_kernel, sizes), grid=(gate_blocks...  21.9 us
    pallas_call x1, Pallas kernels, finish(): pl.pallas_call(functools.partial(finish_kernel, out_steps, split_rows), g...  12.8 us
    pallas_call x1, Pallas kernels, chain(): pl.pallas_call(functools.partial(chain_kernel, ways, blocks), out_shape=j...  9.89 us
    ppermute x1, starting transfers between devices, local(): arrived = lax.ppermute(sent, 'seq', route)  4.92 us
    unnamed x43, local copies, waits for them, and re-layouts  4.61 us
  transfers between devices with their start and end apart: 1, of which 0 were waited for; matrix products, arithmetic and copies ran while one was open for 2% of the time, Pallas kernels for 2%

profile of v8, /device:TPU:0, one launch (start us, length us, event | category | flops | bytes accessed | tf_op | source)
XLA Modules:
  0.0 221.6 jit_solution(921119733977298364)
XLA Ops:
  0.6 0.7 convert_element_type.37.seg_row_ref.refs_13_
  1.3 0.1 fusion.4
  1.4 0.7 slice.16
  2.1 0.1 broadcast_in_dim.13
  2.2 4.9 %collective-permute-start = (bf16[1,16,896]{2,1,0:T(8,128)(2,1)S(1)}, bf16[1,16,896]{2,1,0:T(8,128)(2,1)S(1)}, u32[]{:S(2)}, u32[]{:S(2)}) collective-permute-start(bf16[1,16,896]{2,1,0:T(8,128)(2,1)S(1)} %pad_maximum_fusion), channel_id=1, source_target_pairs={{0,1},{1,2},{2,3},{4,5},{5,6},{6,7},{8,9},{9,10},{10,11},{12,13},{... | collective-permute-start | bytes 86024 | tf_op jit(solution)/shard_map/ppermute | solution.py:1783
  7.2 0.1 fusion.heads_ref.refs_7_
  7.3 0.0 copy-start.1
  7.3 0.7 pad_bitcast_fusion
  9.3 0.7 reshape.107.gain_ref.refs_24_
  10.0 0.7 reshape.112.gain_ref
  10.7 0.7 reshape.108.bias_ref
  11.4 0.7 broadcast_in_dim.15
  12.2 0.1 reshape_reshape.3.skip_ref.refs_8_
  12.2 0.9 slice.20
  13.2 0.7 pad.13.last_momentum_ref
  13.8 3.8 %owned.1 = (bf16[10,96,128]{2,1,0:T(8,128)(2,1)}, f32[10,96,128]{2,1,0:T(8,128)}) custom-call(bf16[1536,768]{1,0:T(8,128)(2,1)} %out_weight_ref.1, bf16[3352,768]{1,0:T(8,128)(2,1)} %bitcast.25, f32[192,1536]{1,0:T(8,128)} %bitcast.29, f32[192,3352]{1,0:T(8,128)} %momentum_ref.3, f32[192,128]{1,0:T(8,128)} %pad.13.last_momentum_ref), custom_call_target="tpu_custom_call" | custom-call | tf_op jit(solution)/shard_map/owned/pallas_call | solution.py:1596
  17.6 0.0 collective-permute-done
  17.7 0.1 select_reduce_fusion
  17.8 0.1 pad_maximum_fusion.1.seg_ref
  17.9 0.0 copy-done.17
  17.9 0.0 copy-done.16
  17.9 0.0 copy-done
  17.9 0.0 copy-done.12
  17.9 0.0 copy-done.19
  17.9 0.0 copy-start.5
  17.9 21.9 %front.1 = (bf16[512,768]{1,0:T(8,128)(2,1)S(1)}, f32[512,16]{1,0:T(8,128)S(1)}, f32[512,1536]{1,0:T(8,128)}, f32[512,1792]{1,0:T(8,128)}, f32[16,1792]{1,0:T(8,...) custom-call(bf16[512,768]{1,0:T(8,128)(2,1)S(1)} %bitcast.22, ...), custom_call_target="tpu_custom_call" | custom-call | tf_op jit(solution)/shard_map/front/pallas_call | solution.py:235
  39.8 0.0 copy-start.6
  39.8 0.0 copy-start.10
  39.8 0.0 copy-start.11
  39.8 9.9 %chain.1.incoming_ref = f32[1,128,1536]{2,1,0:T(8,128)S(1)} custom-call(f32[1,128,1536]{2,1,0:T(8,128)S(1)} %get-tuple-element.59.own_ref, f32[1,8,1536]{2,1,0:T(8,128)S(1)} %get-tuple-element.60.keep_ref.refs_17_), custom_call_target="tpu_custom_call" | custom-call | tf_op jit(solution)/shard_map/chain/pallas_call | solution.py:349
  49.7 0.0 copy-done.15
  49.7 0.0 copy-done.1
  49.7 0.0 copy-done.13
  49.8 0.0 copy-done.5
  49.8 30.0 %forward.1 = (bf16[512,768]{1,0:T(8,128)(2,1)}, bf16[512,1536]{1,0:T(8,128)(2,1)}, bf16[512,768]{1,0:T(8,128)(2,1)S(1)}, bf16[512,1536]{1,0:T(8,128)(2,1)}, f32[...) custom-call(f32[512,1792]{1,0:T(8,128)} %get-tuple-element.54.summed, ...), custom_call_target="tpu_custom_call" | custom-call | tf_op jit(solution)/shard_map/forward/pallas_call | solution.py:567
  79.7 0.0 copy-done.2
  79.7 0.0 copy-done.3
  79.7 0.0 copy-done.4
  79.8 0.0 copy-done.6
  79.8 0.0 copy-start.7
  79.8 0.9 copy-done.7
  80.7 0.9 copy-done.8
  81.5 0.7 copy-done.9
  82.2 0.6 copy-done.14
  82.9 0.6 copy-done.18
  83.5 124.4 %tail.1 = (bf16[512,768]{1,0:T(8,128)(2,1)}, f32[8,1792]{1,0:T(8,128)}, bf16[6,2,2,2,5,96,128]{6,5,4,3,2,1,0:T(8,128)(2,1)}, bf16[4,2,2,2,5,96,128]{6,5,4,3,2,1,0:T(8,128)(2,1)}) custom-call(f32[1]{0:T(128)S(6)} %div.19.refs_0_, f32[512,1792]{1,0:T(8,128)} %get-tuple-element.54.summed_ref.refs_1_.refs_9_, f32[512,1792]{1,0:T(8,128)} %get-tuple-element.62.refs_2_, ...), custom_call_target="tpu_custom_call" | custom-call | tf_op jit(solution)/shard_map/tail/pallas_call | solution.py:1414
  207.9 12.8 %finish.1 = (bf16[1536,768]{1,0:T(8,128)(2,1)}, bf16[3352,768]{1,0:T(8,128)(2,1)}, f32[192,1536]{1,0:T(8,128)}, f32[192,3352]{1,0:T(8,128)}, f32[4,1792]{1,0:T(4...) custom-call(bf16[48,5,96,128]{3,2,1,0:T(8,128)(2,1)} %bitcast.28, ...), custom_call_target="tpu_custom_call" | custom-call | tf_op jit(solution)/shard_map/finish/pallas_call | solution.py:1711
  220.7 0.9 copy.35
  (22 shorter events, 0.1 us)
Async XLA Ops:
  1.3 48.4 %copy-start.15 = (f32[1,512]{1,0:T(1,128)}, f32[1,512]{1,0:T(1,128)S(1)}, u32[]{:S(2)}) copy-start(f32[1,512]{1,0:T(1,128)S(1)} %convert_element_type.37.seg_row_ref.refs_13_) | copy-start | bytes 6148
  2.2 15.4 %collective-permute-start = (bf16[1,16,896]{2,1,0:T(8,128)(2,1)S(1)}, bf16[1,16,896]{2,1,0:T(8,128)(2,1)S(1)}, u32[]{:S(2)}, u32[]{:S(2)}) collective-permute-start(bf16[1,16,896]{2,1,0:T(8,128)(2,1)S(1)} %pad_maximum_fusion), channel_id=1, source_target_pairs={{0,1},{1,2},{2,3},{4,5},{5,6},{6,7},{8,9},{9,10},{10,11},{12,13},{... | collective-permute-start | bytes 86024 | tf_op jit(solution)/shard_map/ppermute | solution.py:1783
  7.3 42.5 %copy-start.1 = (bf16[128,1536]{1,0:T(8,128)(2,1)}, bf16[128,1536]{1,0:T(8,128)(2,1)S(1)}, u32[]{:S(2)}) copy-start(bf16[128,1536]{1,0:T(8,128)(2,1)S(1)} %fusion.heads_ref.refs_7_) | copy-start | bytes 1179652
  8.0 9.8 %copy-start.17 = (f32[1,128]{1,0:T(1,128)}, f32[1,128]{1,0:T(1,128)S(1)}, u32[]{:S(2)}) copy-start(f32[1,128]{1,0:T(1,128)S(1)} %get-tuple-element.95.a_log_ref.refs_15_) | copy-start | bytes 1540
  10.0 7.8 %copy-start.16 = (f32[1,768]{1,0:T(1,128)}, f32[1,768]{1,0:T(1,128)S(1)}, u32[]{:S(2)}) copy-start(f32[1,768]{1,0:T(1,128)S(1)} %reshape.107.gain_ref.refs_24_) | copy-start | bytes 9220
  12.2 37.5 %copy-start.13 = (f32[1,1536]{1,0:T(1,128)}, f32[1,1536]{1,0:T(1,128)S(1)}, u32[]{:S(2)}) copy-start(f32[1,1536]{1,0:T(1,128)S(1)} %reshape_reshape.3.skip_ref.refs_8_) | copy-start | bytes 18436
  13.8 4.0 %copy-start = (bf16[1,512,768]{2,1,0:T(8,128)(2,1)S(1)}, bf16[1,512,768]{2,1,0:T(8,128)(2,1)}, u32[]{:S(2)}) copy-start(bf16[1,512,768]{2,1,0:T(8,128)(2,1)} %param.18) | copy-start | bytes 2359300
  13.8 4.0 %copy-start.12 = (f32[4,1792]{1,0:T(4,128)S(1)}, f32[4,1792]{1,0:T(4,128)}, u32[]{:S(2)}) copy-start(f32[4,1792]{1,0:T(4,128)} %refs_4_.1) | copy-start | bytes 86020
  13.8 4.0 %copy-start.19 = (s32[1,512]{1,0:T(1,128)S(1)}, s32[1,512]{1,0:T(1,128)}, u32[]{:S(2)}) copy-start(s32[1,512]{1,0:T(1,128)} %valid_ref.1) | copy-start | bytes 6148
  17.9 31.9 %copy-start.5 = (bf16[1,512,768]{2,1,0:T(8,128)(2,1)S(1)}, bf16[1,512,768]{2,1,0:T(8,128)(2,1)}, u32[]{:S(2)}) copy-start(bf16[1,512,768]{2,1,0:T(8,128)(2,1)} %param.19) | copy-start | bytes 2359300
  39.8 39.9 %copy-start.2 = (f32[512,16]{1,0:T(8,128)}, f32[512,16]{1,0:T(8,128)S(1)}, u32[]{:S(2)}) copy-start(f32[512,16]{1,0:T(8,128)S(1)} %get-tuple-element.58.masks_ref.refs_12_) | copy-start | bytes 98308
  39.8 39.9 %copy-start.3 = (f32[512,128]{1,0:T(8,128)}, f32[512,128]{1,0:T(8,128)S(1)}, u32[]{:S(2)}) copy-start(f32[512,128]{1,0:T(8,128)S(1)} %get-tuple-element.56.raw_ref.refs_10_) | copy-start | bytes 786436
  39.8 40.0 %copy-start.4 = (f32[512,128]{1,0:T(8,128)}, f32[512,128]{1,0:T(8,128)S(1)}, u32[]{:S(2)}) copy-start(f32[512,128]{1,0:T(8,128)S(1)} %get-tuple-element.57.cum_ref.refs_11_) | copy-start | bytes 786436
  39.8 40.0 %copy-start.6 = (bf16[512,768]{1,0:T(8,128)(2,1)}, bf16[512,768]{1,0:T(8,128)(2,1)S(1)}, u32[]{:S(2)}) copy-start(bf16[512,768]{1,0:T(8,128)(2,1)S(1)} %get-tuple-element.69.refs_19_) | copy-start | bytes 2359300
  39.8 40.0 %copy-start.10 = (f32[1,8,1536]{2,1,0:T(8,128)}, f32[1,8,1536]{2,1,0:T(8,128)S(1)}, u32[]{:S(2)}) copy-start(f32[1,8,1536]{2,1,0:T(8,128)S(1)} %get-tuple-element.60.keep_ref.refs_17_) | copy-start | bytes 147460
  39.8 40.0 %copy-start.11 = (f32[16,1792]{1,0:T(8,128)}, f32[16,1792]{1,0:T(8,128)S(1)}, u32[]{:S(2)}) copy-start(f32[16,1792]{1,0:T(8,128)S(1)} %get-tuple-element.63.refs_3_) | copy-start | bytes 344068
  79.8 0.9 copy-start.7
  80.7 0.9 copy-start.8
  81.5 0.7 copy-start.9
  82.2 0.6 copy-start.14
  82.9 0.6 copy-start.18
  207.9 12.8 %copy-start.20 = (bf16[512,768]{1,0:T(8,128)(2,1)S(1)}, bf16[512,768]{1,0:T(8,128)(2,1)}, u32[]{:S(2)}) copy-start(bf16[512,768]{1,0:T(8,128)(2,1)} %get-tuple-element.76) | copy-start | bytes 2359300

commit v9 on v8

--- a/solution.py
+++ b/solution.py
@@ -342,7 +342,7 @@
             copy(c).wait_send()
 
 
-def chain(own, keep, ways, blocks=6):
+def chain(own, keep, ways, blocks=12):
     seqs, depth, inner = own.shape
     vmem = pl.BlockSpec(memory_space=pltpu.VMEM)
     part = (blocks, seqs, depth, inner // blocks)
@@ -1660,11 +1660,11 @@
             for part in range(split_rows):
                 for p in range(slots - 1):
                     to = (p * split_rows + part) * rows
-                    joined[to : to + rows] = gathered_ref[i * split_rows + part, p]
+                    joined[i, to : to + rows] = gathered_ref[i * split_rows + part, p]
                 own = slice(part * rows, (part + 1) * rows)
                 summed = gathered_ref[i * split_rows + part, slots - 1].astype(F32)
                 new[own, at] = 0.5 * old[own, at] + summed
-            weights[at] = jnp.transpose(joined[...])
+            weights[at] = jnp.transpose(joined[i])
 
     @pl.when(step < out_steps)
     def _():
@@ -1737,7 +1737,7 @@
             shape((share, width), F32),
         ]
         + smalls,
-        scratch_shapes=[pltpu.VMEM((model, LANES), BF16)],
+        scratch_shapes=[pltpu.VMEM((group // split_rows, model, LANES), BF16)],
         name="finish",
     )(gathered_a, gathered_b, out_momentum_t, momentum, totals)
 

time: 224 us -> 223 us (level)
  no operation moved by 1% of the time
where the time goes in v9:
time: 223 us; the launch traced here: 221 us
  Pallas kernels  202 us (91%)
  local copies, waits for them, and re-layouts  10.7 us (5%)
  starting transfers between devices  4.92 us (2%)
  between operations  2.25 us (1%)
    pallas_call x1, Pallas kernels, tail(): pl.pallas_call(functools.partial(tail_kernel, sizes, (bits, pieces, flows...  124 us
    pallas_call x1, Pallas kernels, forward(): pl.pallas_call(functools.partial(forward_kernel, sizes, chunks), grid=(se...  30 us
    pallas_call x1, Pallas kernels, front(): pl.pallas_call(functools.partial(front_kernel, sizes), grid=(gate_blocks...  21.9 us
    pallas_call x1, Pallas kernels, finish(): pl.pallas_call(functools.partial(finish_kernel, out_steps, split_rows), g...  12.7 us
    pallas_call x1, Pallas kernels, chain(): pl.pallas_call(functools.partial(chain_kernel, ways, blocks), out_shape=j...  10 us
    ppermute x1, starting transfers between devices, local(): arrived = lax.ppermute(sent, 'seq', route)  4.92 us
    unnamed x43, local copies, waits for them, and re-layouts  4.61 us
  transfers between devices with their start and end apart: 1, of which 0 were waited for; matrix products, arithmetic and copies ran while one was open for 2% of the time, Pallas kernels for 2%

profile of v9, /device:TPU:0, one launch (start us, length us, event | category | flops | bytes accessed | tf_op | source)
XLA Modules:
  0.0 221.2 jit_solution(13901052280530958253)
XLA Ops:
  0.6 0.7 convert_element_type.37.seg_row_ref.refs_13_
  1.3 0.1 fusion.4
  1.4 0.7 slice.16
  2.1 0.1 broadcast_in_dim.13
  2.2 4.9 %collective-permute-start = (bf16[1,16,896]{2,1,0:T(8,128)(2,1)S(1)}, bf16[1,16,896]{2,1,0:T(8,128)(2,1)S(1)}, u32[]{:S(2)}, u32[]{:S(2)}) collective-permute-start(bf16[1,16,896]{2,1,0:T(8,128)(2,1)S(1)} %pad_maximum_fusion), channel_id=1, source_target_pairs={{0,1},{1,2},{2,3},{4,5},{5,6},{6,7},{8,9},{9,10},{10,11},{12,13},{... | collective-permute-start | bytes 86024 | tf_op jit(solution)/shard_map/ppermute | solution.py:1783
  7.2 0.1 fusion.heads_ref.refs_7_
  7.3 0.0 copy-start.1
  7.3 0.7 pad_bitcast_fusion
  9.3 0.7 reshape.107.gain_ref.refs_24_
  10.0 0.7 reshape.112.gain_ref
  10.7 0.7 reshape.108.bias_ref
  11.4 0.7 broadcast_in_dim.15
  12.2 0.1 reshape_reshape.3.skip_ref.refs_8_
  12.2 0.9 slice.20
  13.2 0.7 pad.13.last_momentum_ref
  13.8 3.8 %owned.1 = (bf16[10,96,128]{2,1,0:T(8,128)(2,1)}, f32[10,96,128]{2,1,0:T(8,128)}) custom-call(bf16[1536,768]{1,0:T(8,128)(2,1)} %out_weight_ref.1, bf16[3352,768]{1,0:T(8,128)(2,1)} %bitcast.25, f32[192,1536]{1,0:T(8,128)} %bitcast.29, f32[192,3352]{1,0:T(8,128)} %momentum_ref.3, f32[192,128]{1,0:T(8,128)} %pad.13.last_momentum_ref), custom_call_target="tpu_custom_call" | custom-call | tf_op jit(solution)/shard_map/owned/pallas_call | solution.py:1596
  17.6 0.0 collective-permute-done
  17.7 0.1 select_reduce_fusion
  17.8 0.1 pad_maximum_fusion.1.seg_ref
  17.9 0.0 copy-done.17
  17.9 0.0 copy-done.16
  17.9 0.0 copy-done
  17.9 0.0 copy-done.12
  17.9 0.0 copy-done.19
  17.9 0.0 copy-start.5
  17.9 21.9 %front.1 = (bf16[512,768]{1,0:T(8,128)(2,1)S(1)}, f32[512,16]{1,0:T(8,128)S(1)}, f32[512,1536]{1,0:T(8,128)}, f32[512,1792]{1,0:T(8,128)}, f32[16,1792]{1,0:T(8,...) custom-call(bf16[512,768]{1,0:T(8,128)(2,1)S(1)} %bitcast.22, ...), custom_call_target="tpu_custom_call" | custom-call | tf_op jit(solution)/shard_map/front/pallas_call | solution.py:235
  39.8 0.0 copy-start.6
  39.8 10.0 %chain.1.incoming_ref = f32[1,128,1536]{2,1,0:T(8,128)S(1)} custom-call(f32[1,128,1536]{2,1,0:T(8,128)S(1)} %get-tuple-element.59.own_ref, f32[1,8,1536]{2,1,0:T(8,128)S(1)} %get-tuple-element.60.keep_ref.refs_17_), custom_call_target="tpu_custom_call" | custom-call | tf_op jit(solution)/shard_map/chain/pallas_call | solution.py:349
  49.8 0.0 copy-done.15
  49.8 0.0 copy-done.1
  49.9 0.0 copy-done.13
  49.9 0.0 copy-done.5
  49.9 30.0 %forward.1 = (bf16[512,768]{1,0:T(8,128)(2,1)}, bf16[512,1536]{1,0:T(8,128)(2,1)}, bf16[512,768]{1,0:T(8,128)(2,1)S(1)}, bf16[512,1536]{1,0:T(8,128)(2,1)}, f32[...) custom-call(f32[512,1792]{1,0:T(8,128)} %get-tuple-element.54.summed, ...), custom_call_target="tpu_custom_call" | custom-call | tf_op jit(solution)/shard_map/forward/pallas_call | solution.py:567
  79.8 0.0 copy-done.3
  79.8 0.0 copy-done.4
  79.9 0.0 copy-done.6
  79.9 0.0 copy-done.10
  79.9 0.0 copy-done.11
  79.9 0.0 copy-start.7
  79.9 0.9 copy-done.7
  80.8 0.9 copy-done.8
  81.7 0.7 copy-done.9
  82.3 0.6 copy-done.14
  83.0 0.6 copy-done.18
  83.6 124.0 %tail.1 = (bf16[512,768]{1,0:T(8,128)(2,1)}, f32[8,1792]{1,0:T(8,128)}, bf16[6,2,2,2,5,96,128]{6,5,4,3,2,1,0:T(8,128)(2,1)}, bf16[4,2,2,2,5,96,128]{6,5,4,3,2,1,0:T(8,128)(2,1)}) custom-call(f32[1]{0:T(128)S(6)} %div.19.refs_0_, f32[512,1792]{1,0:T(8,128)} %get-tuple-element.54.summed_ref.refs_1_.refs_9_, f32[512,1792]{1,0:T(8,128)} %get-tuple-element.62.refs_2_, ...), custom_call_target="tpu_custom_call" | custom-call | tf_op jit(solution)/shard_map/tail/pallas_call | solution.py:1414
  207.5 0.0 copy-start.20
  207.6 12.7 %finish.1 = (bf16[1536,768]{1,0:T(8,128)(2,1)}, bf16[3352,768]{1,0:T(8,128)(2,1)}, f32[192,1536]{1,0:T(8,128)}, f32[192,3352]{1,0:T(8,128)}, f32[4,1792]{1,0:T(4...) custom-call(bf16[48,5,96,128]{3,2,1,0:T(8,128)(2,1)} %bitcast.28, ...), custom_call_target="tpu_custom_call" | custom-call | tf_op jit(solution)/shard_map/finish/pallas_call | solution.py:1711
  220.3 0.9 copy.35
  (22 shorter events, 0.1 us)
Async XLA Ops:
  1.3 48.5 %copy-start.15 = (f32[1,512]{1,0:T(1,128)}, f32[1,512]{1,0:T(1,128)S(1)}, u32[]{:S(2)}) copy-start(f32[1,512]{1,0:T(1,128)S(1)} %convert_element_type.37.seg_row_ref.refs_13_) | copy-start | bytes 6148
  2.2 15.4 %collective-permute-start = (bf16[1,16,896]{2,1,0:T(8,128)(2,1)S(1)}, bf16[1,16,896]{2,1,0:T(8,128)(2,1)S(1)}, u32[]{:S(2)}, u32[]{:S(2)}) collective-permute-start(bf16[1,16,896]{2,1,0:T(8,128)(2,1)S(1)} %pad_maximum_fusion), channel_id=1, source_target_pairs={{0,1},{1,2},{2,3},{4,5},{5,6},{6,7},{8,9},{9,10},{10,11},{12,13},{... | collective-permute-start | bytes 86024 | tf_op jit(solution)/shard_map/ppermute | solution.py:1783
  7.3 42.6 %copy-start.1 = (bf16[128,1536]{1,0:T(8,128)(2,1)}, bf16[128,1536]{1,0:T(8,128)(2,1)S(1)}, u32[]{:S(2)}) copy-start(bf16[128,1536]{1,0:T(8,128)(2,1)S(1)} %fusion.heads_ref.refs_7_) | copy-start | bytes 1179652
  8.0 9.8 %copy-start.17 = (f32[1,128]{1,0:T(1,128)}, f32[1,128]{1,0:T(1,128)S(1)}, u32[]{:S(2)}) copy-start(f32[1,128]{1,0:T(1,128)S(1)} %get-tuple-element.95.a_log_ref.refs_15_) | copy-start | bytes 1540
  10.0 7.8 %copy-start.16 = (f32[1,768]{1,0:T(1,128)}, f32[1,768]{1,0:T(1,128)S(1)}, u32[]{:S(2)}) copy-start(f32[1,768]{1,0:T(1,128)S(1)} %reshape.107.gain_ref.refs_24_) | copy-start | bytes 9220
  12.2 37.6 %copy-start.13 = (f32[1,1536]{1,0:T(1,128)}, f32[1,1536]{1,0:T(1,128)S(1)}, u32[]{:S(2)}) copy-start(f32[1,1536]{1,0:T(1,128)S(1)} %reshape_reshape.3.skip_ref.refs_8_) | copy-start | bytes 18436
  13.8 4.0 %copy-start = (bf16[1,512,768]{2,1,0:T(8,128)(2,1)S(1)}, bf16[1,512,768]{2,1,0:T(8,128)(2,1)}, u32[]{:S(2)}) copy-start(bf16[1,512,768]{2,1,0:T(8,128)(2,1)} %param.18) | copy-start | bytes 2359300
  13.8 4.0 %copy-start.12 = (f32[4,1792]{1,0:T(4,128)S(1)}, f32[4,1792]{1,0:T(4,128)}, u32[]{:S(2)}) copy-start(f32[4,1792]{1,0:T(4,128)} %refs_4_.1) | copy-start | bytes 86020
  13.8 4.0 %copy-start.19 = (s32[1,512]{1,0:T(1,128)S(1)}, s32[1,512]{1,0:T(1,128)}, u32[]{:S(2)}) copy-start(s32[1,512]{1,0:T(1,128)} %valid_ref.1) | copy-start | bytes 6148
  17.9 32.0 %copy-start.5 = (bf16[1,512,768]{2,1,0:T(8,128)(2,1)S(1)}, bf16[1,512,768]{2,1,0:T(8,128)(2,1)}, u32[]{:S(2)}) copy-start(bf16[1,512,768]{2,1,0:T(8,128)(2,1)} %param.19) | copy-start | bytes 2359300
  39.8 40.1 %copy-start.2 = (f32[512,16]{1,0:T(8,128)}, f32[512,16]{1,0:T(8,128)S(1)}, u32[]{:S(2)}) copy-start(f32[512,16]{1,0:T(8,128)S(1)} %get-tuple-element.58.masks_ref.refs_12_) | copy-start | bytes 98308
  39.8 40.1 %copy-start.3 = (f32[512,128]{1,0:T(8,128)}, f32[512,128]{1,0:T(8,128)S(1)}, u32[]{:S(2)}) copy-start(f32[512,128]{1,0:T(8,128)S(1)} %get-tuple-element.56.raw_ref.refs_10_) | copy-start | bytes 786436
  39.8 40.1 %copy-start.4 = (f32[512,128]{1,0:T(8,128)}, f32[512,128]{1,0:T(8,128)S(1)}, u32[]{:S(2)}) copy-start(f32[512,128]{1,0:T(8,128)S(1)} %get-tuple-element.57.cum_ref.refs_11_) | copy-start | bytes 786436
  39.8 40.1 %copy-start.6 = (bf16[512,768]{1,0:T(8,128)(2,1)}, bf16[512,768]{1,0:T(8,128)(2,1)S(1)}, u32[]{:S(2)}) copy-start(bf16[512,768]{1,0:T(8,128)(2,1)S(1)} %get-tuple-element.69.refs_19_) | copy-start | bytes 2359300
  39.8 40.1 %copy-start.10 = (f32[1,8,1536]{2,1,0:T(8,128)}, f32[1,8,1536]{2,1,0:T(8,128)S(1)}, u32[]{:S(2)}) copy-start(f32[1,8,1536]{2,1,0:T(8,128)S(1)} %get-tuple-element.60.keep_ref.refs_17_) | copy-start | bytes 147460
  39.8 40.1 %copy-start.11 = (f32[16,1792]{1,0:T(8,128)}, f32[16,1792]{1,0:T(8,128)S(1)}, u32[]{:S(2)}) copy-start(f32[16,1792]{1,0:T(8,128)S(1)} %get-tuple-element.63.refs_3_) | copy-start | bytes 344068
  79.9 0.9 copy-start.7
  80.8 0.9 copy-start.8
  81.7 0.7 copy-start.9
  82.3 0.6 copy-start.14
  83.0 0.6 copy-start.18
  207.5 12.8 %copy-start.20 = (bf16[512,768]{1,0:T(8,128)(2,1)S(1)}, bf16[512,768]{1,0:T(8,128)(2,1)}, u32[]{:S(2)}) copy-start(bf16[512,768]{1,0:T(8,128)(2,1)} %get-tuple-element.76) | copy-start | bytes 2359300
